TPU v7x, 128 devices: a whole 4x4x4 slice. The times are simulated.
128 devices in a mesh: seq: 16 (over z, y_hi, core), tensor: 8 (over x, y_lo).
Axes of the slice: x: 4, y: 4 (y_hi: 2, y_lo: 2; y = y_hi * 2 + y_lo), z: 4, core: 2. Of those that a mesh axis runs over, the one named last changes fastest.
Arguments:
- queries: bfloat16 [3, 48, 40, 5120], P(None, 'seq', None, 'tensor'), may hold values from -16 to 16
- keys_values: bfloat16 [2, 3, 48, 40, 5120], P(None, None, 'seq', None, 'tensor'), may hold values from -16 to 16
- out_weight: bfloat16 [5120, 5120], P('tensor'), may hold values from -0.078125 to 0.078125
- grad_out: bfloat16 [3, 48, 40, 5120], P(None, 'seq', 'tensor'), may hold values from -6 to 6
- window: int32 [40, 3], P('tensor'), may hold values from 0 to 3, as said below
- block_mask: int32 [1, 16, 5, 63], replicated, may hold values from 0 to 1, as said below
Outputs:
- layer_out: bfloat16 [3, 48, 40, 5120], P(None, 'seq', 'tensor')
- grad_queries: bfloat16 [3, 48, 40, 5120], P(None, 'seq', None, 'tensor')
- grad_keys_values: bfloat16 [2, 3, 48, 40, 5120], P(None, None, 'seq', None, 'tensor')
- grad_weight: bfloat16 [5120, 5120], P('tensor', 'seq')
Inputs may be any that keep to these rules, and one draw needn't show every extreme that they name: `window`: in every group of 5 consecutive heads one head has the reach (1, 1, 3). `block_mask`: the middle entry of every tile's row (the tile itself) is 1.
All inputs are finite; a program needn't handle non-finite values.
Results may differ from a plain program's by a relative error of at most 0.014.
Values may be sent and summed in bfloat16 or wider, within the bound.
No kernel may reach another device: no remote copies, remote signals or barrier semaphores. Data moves between devices by JAX's collectives and lax.ppermute only.
A program may use at most 128 MiB of HBM per device.

v0:
```python
import jax
import jax.numpy as jnp
import numpy as np
from jax import lax
from jax.experimental import pallas as pl
from jax.experimental.pallas import tpu as pltpu
from jax.sharding import PartitionSpec as P

HEAD_DIM = 128
TILE_W = 8
REACH_W = 3
OFFSETS = 63
SCALE = HEAD_DIM ** (-0.5)
OUTSIDE = -1e30
F32 = jnp.float32
BF16 = jnp.bfloat16


def dot(a, b, dims):
    return lax.dot_general(a, b, (dims, ((), ())), preferred_element_type=F32)


def tensor_shift(value, dx, dy):
    pairs = [
        (x * 2 + y, (x + dx) % 4 * 2 + (y + dy) % 2) for x in range(4) for y in range(2)
    ]
    return lax.ppermute(value, "tensor", pairs)


def seq_shift(value, dz, dy, core=0):
    pairs = [
        ((z * 2 + y) * 2 + c, ((z + dz) % 4 * 2 + (y + dy) % 2) * 2 + (c + core) % 2)
        for z in range(4)
        for y in range(2)
        for c in range(2)
    ]
    return lax.ppermute(value, "seq", pairs)


def added(*terms):
    total = terms[0].astype(F32)
    for term in terms[1:]:
        total = total + term.astype(F32)
    return total


def tops(room):
    upper = room // 2 // 16 * 16
    return upper, room - upper


def gathered(own, shift):
    t0, t1 = tops(own.shape[0])
    c01 = shift(own, 0, 1)
    c10 = shift(own, -1, 0)
    c30 = shift(own, 1, 0)
    c11 = shift(c01, -1, 0)
    c31 = shift(c01, 1, 0)
    c20 = [shift(c10[:t0], -1, 0), shift(c30[t0:], 1, 0)]
    c21 = [shift(c11[:t1], -1, 0), shift(c31[t1:], 1, 0)]
    return [own, c01, c10, c11, *c20, *c21, c30, c31], (c11, c31)


ANYWHERE = pl.BlockSpec(memory_space=pl.ANY)


def kernel(body, outs, args, specs=None, out_specs=None, grid=(), after=(), flops=0, moved=0, scratch=()):
    count = len(args)

    def run(*refs):
        return body(*refs[:count], *refs[count + len(after) :])

    vector = pl.BlockSpec(memory_space=pltpu.VMEM)
    specs = [vector] * count if specs is None else specs
    out_specs = [vector] * len(outs) if out_specs is None else out_specs
    return pl.pallas_call(
        run,
        grid=grid,
        in_specs=[*specs, *[ANYWHERE] * len(after)],
        out_specs=out_specs,
        out_shape=[jax.ShapeDtypeStruct(shape, kind) for shape, kind in outs],
        scratch_shapes=scratch,
        cost_estimate=pl.CostEstimate(flops=flops, transcendentals=0, bytes_accessed=moved),
    )(*args, *after)


def join_total(zero_ref, plus_ref, minus_ref, plus_sum_ref, minus_sum_ref):
    upper, lower = plus_sum_ref.shape[0], minus_sum_ref.shape[0]
    first = added(zero_ref[:upper], plus_sum_ref[...], minus_ref[lower:])
    second = added(zero_ref[upper:], plus_ref[upper:], minus_sum_ref[...])
    return jnp.concatenate([first, second], axis=0)


def side_kernel(*refs):
    refs[-1][...] = join_total(*refs[:5]).astype(BF16)


def relay_kernel(kept_plus_ref, kept_minus_ref, plus_ref, minus_ref, plus_out, minus_out):
    plus_out[...] = added(kept_plus_ref[...], plus_ref[: plus_out.shape[0]]).astype(BF16)
    minus_out[...] = added(kept_minus_ref[...], minus_ref[: minus_out.shape[0]]).astype(BF16)


def mixed_kernel(*refs):
    out_ref = refs[-1]
    total = (join_total(*refs[:5]) + refs[5][...].astype(F32)).astype(BF16).astype(F32)
    rows = out_ref.shape[1]
    for i in range(out_ref.shape[0]):
        out_ref[i] = total[i * rows : (i + 1) * rows].astype(BF16)


def split_kernel(*refs):
    core_ref, mine_ref, other_ref = refs[6:]
    total = join_total(*refs[:5]) + refs[5][...].astype(F32)
    half = mine_ref.shape[1]
    low, high = total[:, :half], total[:, half:]
    first = core_ref[0] == 0
    mine_ref[...] = jnp.where(first, low, high).astype(BF16)
    other_ref[...] = jnp.where(first, high, low).astype(BF16)


def stack_kernel(mine_ref, came_ref, core_ref, out_ref):
    first = core_ref[0] == 0
    mine, came = mine_ref[...].astype(F32), came_ref[...].astype(F32)
    step = HEAD_DIM // 2
    for i in range(mine.shape[0] // step):
        rows = slice(i * step, (i + 1) * step)
        here = 2 * i * step
        out_ref[here : here + step] = jnp.where(first, mine[rows], came[rows]).astype(BF16)
        out_ref[here + step : here + 2 * step] = jnp.where(first, came[rows], mine[rows]).astype(BF16)


SCALAR = pl.BlockSpec(memory_space=pltpu.SMEM)
VECTOR = pl.BlockSpec(memory_space=pltpu.VMEM)


def hop(shift, arrays):
    return [shift(arrays[i], 1 - 2 * i, 0) for i in range(2)]


def forward_kernel(
    q_ref, own_ref, up_ref, down_ref, bias_ref, hot_ref, perm_ref, core_ref, p_ref, att_ref, turned_ref
):
    qa = jnp.concatenate([q_ref[...], hot_ref[...]], axis=1)
    scores = []
    for b, ref in enumerate((up_ref, own_ref, down_ref)):
        bias = jnp.concatenate([bias_ref[0, b]] * 9, axis=0).astype(BF16)
        ka = jnp.concatenate([ref[0], bias], axis=1)
        scores.append(dot(ka, qa, ((1,), (1,))))
    top = jnp.max(scores[0], axis=0, keepdims=True)
    for s in scores[1:]:
        top = jnp.maximum(top, jnp.max(s, axis=0, keepdims=True))
    weights = [jnp.exp((s - top) * SCALE) for s in scores]
    total = jnp.sum(weights[0], axis=0, keepdims=True)
    for w in weights[1:]:
        total = total + jnp.sum(w, axis=0, keepdims=True)
    inverse = 1.0 / total
    attended = None
    for b, ref in enumerate((up_ref, own_ref, down_ref)):
        probs = (weights[b] * inverse).astype(BF16)
        p_ref[0, b] = probs
        part = dot(ref[1], probs, ((0,), (0,)))
        attended = part if attended is None else attended + part
    attended = attended.astype(BF16)
    att_ref[...] = dot(perm_ref[...], attended, ((1,), (1,))).astype(BF16)
    turned = dot(attended, perm_ref[...], ((1,), (1,)))
    low, high = turned[: HEAD_DIM // 2], turned[HEAD_DIM // 2 :]
    first = core_ref[0] == 0
    turned_ref[0, 0] = jnp.where(first, low, high).astype(BF16)
    turned_ref[1, 0] = jnp.where(first, high, low).astype(BF16)


def backward_kernel(
    q_ref, own_ref, up_ref, down_ref, p_ref, ga_ref, perm_ref, gq_ref, gown_ref, gup_ref, gdown_ref
):
    q = q_ref[...]
    g = dot(perm_ref[...], ga_ref[...], ((1,), (0,))).astype(BF16)
    refs = (up_ref, own_ref, down_ref)
    outs = (gup_ref, gown_ref, gdown_ref)
    grads = []
    delta = None
    for b in range(3):
        gp = dot(refs[b][1], g, ((1,), (1,)))
        part = jnp.sum(p_ref[0, b].astype(F32) * gp, axis=0, keepdims=True)
        delta = part if delta is None else delta + part
        grads.append(gp)
    gq = None
    for b in range(3):
        probs = p_ref[0, b]
        ds = (probs.astype(F32) * (grads[b] - delta) * SCALE).astype(BF16)
        outs[b][0] = dot(ds, q, ((1,), (0,))).astype(outs[b].dtype)
        outs[b][1] = dot(probs, g, ((1,), (0,))).astype(outs[b].dtype)
        part = dot(refs[b][0], ds, ((0,), (0,)))
        gq = part if gq is None else gq + part
    gq_ref[...] = gq.T.astype(BF16)


def weight_kernel(order_ref, turned_ref, *refs):
    *pieces, after_ref, keep_ref, send_ref = refs
    g = jnp.concatenate([p[...] for p in pieces], axis=0)
    grad = dot(turned_ref[...], g, ((1,), (0,))).astype(BF16)
    half = keep_ref.shape[1]
    keep_ref[0] = grad[:half]
    send_ref[0] = grad[half:]


def place_parts(rows, room, upper, refs):
    plus, minus, kept_plus, kept_minus, zero = refs
    plus[...] = jnp.concatenate([rows(2, 0, upper), rows(1, upper, room)], axis=0).astype(BF16)
    minus[...] = jnp.concatenate([rows(2, upper, room), rows(3, 0, upper)], axis=0).astype(BF16)
    kept_plus[...] = rows(1, 0, upper).astype(BF16)
    kept_minus[...] = rows(3, upper, room).astype(BF16)
    zero[...] = rows(0, 0, room).astype(BF16)


def part_rows(room, upper):
    return [room, room, upper, room - upper, room]


def fold_kernel(keep_ref, came_ref, *outs):
    room = keep_ref.shape[1]

    def rows(d, start, end):
        return added(keep_ref[d, start:end], came_ref[d, start:end])

    place_parts(rows, room, outs[2].shape[0], outs)


def project_kernel(att_ref, w_ref, *outs):
    mixed = dot(att_ref[...], w_ref[...], ((1,), (0,)))
    room = outs[0].shape[0]
    for i, e in enumerate((1, 0)):
        refs = outs[5 * i : 5 * i + 5]

        def rows(d, start, end, e=e):
            base = (d * 2 + e) * room
            return mixed[base + start : base + end]

        place_parts(rows, room, refs[2].shape[0], refs)


def attn_grad_kernel(w_ref, *refs):
    *pieces, ga_ref, total_ref = refs
    step = pl.program_id(0)
    g = jnp.concatenate([p[...] for p in pieces], axis=0)
    part = dot(g, w_ref[...], ((1,), (1,)))

    @pl.when(step == 0)
    def _():
        total_ref[...] = part

    @pl.when(step > 0)
    def _():
        total_ref[...] += part

    @pl.when(step == pl.num_programs(0) - 1)
    def _():
        ga_ref[...] = total_ref[...].astype(BF16)


def total_kernel(*refs):
    out_ref = refs[-1]
    start = 0
    for i in range(0, len(refs) - 1, 3):
        part = added(refs[i][...], refs[i + 1][...], refs[i + 2][...]).astype(BF16)
        out_ref[:, :, start : start + part.shape[2]] = part
        start += part.shape[2]


def mask_bias(window, own_mask, seq_place, row_tiles):
    heads = window.shape[0]
    columns = own_mask.shape[0]
    rows = own_mask.reshape(columns, 3, 3, 7)[:, 1]
    query = np.arange(columns)
    delta = query[:, None] - query[None, :]
    pick = (delta[:, :, None] + REACH_W == np.arange(7)).astype(np.int32)
    bits = jnp.sum(rows.transpose(1, 0, 2)[:, None] * pick[None], axis=-1)
    dh = jnp.arange(3, dtype=jnp.int32) - 1
    tile_row = dh + seq_place
    row_ok = (tile_row >= 0) & (tile_row < row_tiles)
    inside = (jnp.abs(dh)[None, :] <= window[:, 1:2]) & row_ok[None, :] & (window[:, :1] >= 0)
    near = np.abs(delta)[None] <= window[:, 2][:, None, None]
    ok = inside[:, :, None, None] & near[:, None] & (bits > 0)[None]
    bias = jnp.where(ok, 0.0, OUTSIDE).astype(F32)
    bias = jnp.pad(bias, ((0, 0), (0, 0), (0, 0), (0, 128 - columns)))
    wide = jnp.broadcast_to(bias[:, :, :, None], (heads, 3, columns, TILE_W, 128))
    return wide.reshape(heads, 3, columns * TILE_W, 128)


def layer(queries, keys_values, out_weight, grad_out, window, block_mask):
    frames, tile_rows, columns, channels = queries.shape
    model_width = grad_out.shape[3]
    local_columns = grad_out.shape[2]
    tokens = frames * tile_rows * columns
    heads = channels // HEAD_DIM
    strips = frames * tile_rows
    row_tiles = lax.axis_size("seq")
    seq_place = lax.axis_index("seq")
    tensor_place = lax.axis_index("tensor")
    spot_z, spot_y, core = seq_place // 4, seq_place // 2 % 2, seq_place % 2
    spot_x, spot_low = tensor_place // 2, tensor_place % 2
    core = core[None].astype(jnp.int32)

    onward = [(i, i + 1) for i in range(row_tiles - 1)]
    back = [(i + 1, i) for i in range(row_tiles - 1)]
    up = lax.ppermute(keys_values, "seq", onward)
    down = lax.ppermute(keys_values, "seq", back)

    piece = strips * local_columns
    room = -(-piece // 16) * 16
    own_grad = jnp.pad(grad_out.reshape(piece, model_width), ((0, room - piece), (0, 0)))
    pieces, last_hops = gathered(own_grad, tensor_shift)
    slots = 8 * room

    slot = lax.iota(jnp.int32, slots)
    block, row = slot // room, slot % room
    owner = (spot_x + block // 2) % 4 * 2 + (spot_low + block % 2) % 2
    place = row // local_columns * columns + owner * local_columns + row % local_columns
    place = jnp.where(row < piece, place, -1)
    cell = lax.iota(jnp.int32, tokens)
    perm = (place[:, None] == cell[None, :]).astype(BF16)
    perm_back = (cell[:, None] == place[None, :]).astype(BF16)
    hot = (cell[:, None] % columns // TILE_W == lax.iota(jnp.int32, 128)[None, :]).astype(BF16)

    own_mask = lax.dynamic_slice_in_dim(block_mask, seq_place, 1, 1).reshape(-1, OFFSETS)
    bias = mask_bias(window, own_mask, seq_place, row_tiles)

    flat_q = queries.reshape(tokens, channels)
    flat = [v.reshape(2, tokens, channels) for v in (keys_values, up, down)]

    def whole(shape):
        return pl.BlockSpec(shape, lambda h: (0,) * len(shape))

    q_spec = pl.BlockSpec((tokens, HEAD_DIM), lambda h: (0, h))
    kv_spec = pl.BlockSpec((2, tokens, HEAD_DIM), lambda h: (0, 0, h))
    half = channels // 2
    pairs = heads * tokens * 3 * tokens
    probs, attended, turned = kernel(
        forward_kernel,
        [
            ((heads, 3, tokens, tokens), BF16),
            ((slots, channels), BF16),
            ((2, heads, HEAD_DIM // 2, slots), BF16),
        ],
        [flat_q, *flat, bias, hot, perm, core],
        [
            q_spec,
            kv_spec,
            kv_spec,
            kv_spec,
            pl.BlockSpec((1, 3, columns, 128), lambda h: (h, 0, 0, 0)),
            whole((tokens, 128)),
            whole((slots, tokens)),
            SCALAR,
        ],
        [
            pl.BlockSpec((1, 3, tokens, tokens), lambda h: (h, 0, 0, 0)),
            pl.BlockSpec((slots, HEAD_DIM), lambda h: (0, h)),
            pl.BlockSpec((2, 1, HEAD_DIM // 2, slots), lambda h: (0, h, 0, 0)),
        ],
        grid=(heads,),
        after=last_hops,
        flops=pairs * 1500,
        moved=8 << 20,
    )
    turned = turned.reshape(channels, slots)

    wide = model_width // 8
    step = lax.iota(jnp.int32, 8)
    chips = (spot_z + step // 2) % 4 * 2 + (spot_y + step % 2) % 2

    def weight_half(e, after):
        spec = pl.BlockSpec((1, half, wide), lambda i, o: (i, 0, 0))
        return pl.pallas_call(
            weight_kernel,
            grid_spec=pltpu.PrefetchScalarGridSpec(
                num_scalar_prefetch=1,
                grid=(4,),
                in_specs=[pl.BlockSpec((channels, slots), lambda i, o: (0, 0))]
                + [pl.BlockSpec((p.shape[0], wide), lambda i, o: (0, o[i])) for p in pieces]
                + [ANYWHERE],
                out_specs=[spec] * 2,
            ),
            out_shape=[jax.ShapeDtypeStruct((4, half, wide), BF16)] * 2,
            cost_estimate=pl.CostEstimate(
                flops=slots * model_width * channels * 2,
                transcendentals=0,
                bytes_accessed=6 << 20,
            ),
        )(chips[e::2].astype(jnp.int32), turned, *pieces, after)

    keep1, send1 = weight_half(1, attended)
    came1 = seq_shift(send1, 0, 0, 1)
    keep0, send0 = weight_half(0, send1)
    came0 = seq_shift(send0, 0, 0, 1)

    uppers = tops(room)
    shapes = [((n, model_width), BF16) for e in (1, 0) for n in part_rows(room, uppers[e])]
    broad = 2 * wide
    mixed_parts = kernel(
        project_kernel,
        shapes,
        [attended, out_weight],
        [whole((slots, channels)), pl.BlockSpec((channels, broad), lambda i: (0, i))],
        [pl.BlockSpec((n[0][0], broad), lambda i: (0, i)) for n in shapes],
        grid=(4,),
        after=[send0],
        flops=slots * model_width * channels * 3,
        moved=12 << 20,
    )
    mixed_parts = {1: mixed_parts[:5], 0: mixed_parts[5:]}
    mixed_came = {e: hop(tensor_shift, mixed_parts[e]) for e in (1, 0)}

    def fold(keep, came, after):
        return kernel(
            fold_kernel,
            [((n, wide), BF16) for n in part_rows(half, half // 2)],
            [keep, came],
            after=[after],
            flops=1 << 20,
            moved=5 << 20,
        )

    weight_parts = {1: fold(keep1, came1, mixed_parts[0][0])}
    weight_parts[0] = fold(keep0, came0, weight_parts[1][0])
    weight_came = {e: hop(seq_shift, weight_parts[e]) for e in (1, 0)}

    (grad_attn,) = kernel(
        attn_grad_kernel,
        [((slots, channels), BF16)],
        [out_weight, *pieces],
        [pl.BlockSpec((channels, broad), lambda i: (0, i))]
        + [pl.BlockSpec((p.shape[0], broad), lambda i: (0, i)) for p in pieces],
        [whole((slots, channels))],
        grid=(4,),
        after=[weight_parts[0][0]],
        flops=slots * model_width * channels * 3,
        moved=12 << 20,
        scratch=[pltpu.VMEM((slots, channels), F32)],
    )

    def differentiate(first, count, after):
        def spec(shape, at):
            def index(h):
                return tuple(h + first if i == at else 0 for i in range(len(shape)))

            return pl.BlockSpec(shape, index)

        width = count * HEAD_DIM
        kv_in = spec((2, tokens, HEAD_DIM), 2)
        return kernel(
            backward_kernel,
            [
                ((tokens, width), BF16),
                ((2, tokens, width), F32),
                ((2, tokens, width), BF16),
                ((2, tokens, width), BF16),
            ],
            [flat_q, *flat, probs, grad_attn, perm_back],
            [
                spec((tokens, HEAD_DIM), 1),
                kv_in,
                kv_in,
                kv_in,
                spec((1, 3, tokens, tokens), 0),
                spec((slots, HEAD_DIM), 1),
                whole((tokens, slots)),
            ],
            [q_spec, kv_spec, kv_spec, kv_spec],
            grid=(count,),
            after=after,
            flops=pairs * 2000 * count // heads,
            moved=2 * count << 20,
        )

    def send_halo(grad_up, grad_down):
        from_below = lax.ppermute(grad_up, "seq", back)
        from_above = lax.ppermute(grad_down, "seq", onward)
        return from_below, from_above

    def relay(parts, came, shift, after):
        sums = kernel(
            relay_kernel,
            [(parts[2].shape, BF16), (parts[3].shape, BF16)],
            [parts[2], parts[3], *came],
            after=after,
            moved=1 << 20,
        )
        return hop(shift, sums), sums[0]

    def side(parts, came, sums, shift, after):
        (total,) = kernel(
            side_kernel,
            [(parts[4].shape, BF16)],
            [parts[4], *came, *sums],
            after=after,
            moved=2 << 20,
        )
        return shift(total, 0, 1), total

    split = (heads + 1) // 2
    gq_a, own_a, up_a, down_a = differentiate(0, split, [])
    below_a, above_a = send_halo(up_a, down_a)
    mixed_sum1, mark = relay(mixed_parts[1], mixed_came[1], tensor_shift, [up_a])
    weight_sum1, mark = relay(weight_parts[1], weight_came[1], seq_shift, [mark])
    gq_b, own_b, up_b, down_b = differentiate(split, heads - split, [mark])
    below_b, above_b = send_halo(up_b, down_b)
    mixed_sum0, mark = relay(mixed_parts[0], mixed_came[0], tensor_shift, [up_b])
    weight_sum0, mark = relay(weight_parts[0], weight_came[0], seq_shift, [mark])
    mixed_side, mark = side(mixed_parts[1], mixed_came[1], mixed_sum1, tensor_shift, [mark])
    weight_side, mark = side(weight_parts[1], weight_came[1], weight_sum1, seq_shift, [mark])

    quarter = ((half, wide // 2), BF16)
    mine, other = kernel(
        split_kernel,
        [quarter, quarter],
        [weight_parts[0][4], *weight_came[0], *weight_sum0, weight_side, core],
        [VECTOR] * 6 + [SCALAR],
        after=[mark],
        moved=2 << 20,
    )
    other = seq_shift(other, 0, 0, 1)
    (layer_out,) = kernel(
        mixed_kernel,
        [((strips, local_columns, model_width), BF16)],
        [mixed_parts[0][4], *mixed_came[0], *mixed_sum0, mixed_side],
        after=[mine],
        moved=3 << 20,
    )
    (grad_weight,) = kernel(
        stack_kernel,
        [((channels, wide // 2), BF16)],
        [mine, other, core],
        [VECTOR] * 2 + [SCALAR],
        moved=1 << 20,
    )
    (grad_kv,) = kernel(
        total_kernel,
        [((2, tokens, channels), BF16)],
        [own_a, below_a, above_a, own_b, below_b, above_b],
        moved=5 << 20,
    )
    grad_q = jnp.concatenate([gq_a, gq_b], axis=1)
    return (
        layer_out.reshape(frames, tile_rows, local_columns, model_width),
        grad_q.reshape(queries.shape),
        grad_kv.reshape(keys_values.shape),
        grad_weight,
    )


def solution(mesh):
    return jax.shard_map(
        layer,
        mesh=mesh,
        in_specs=(
            P(None, "seq", None, "tensor"),
            P(None, None, "seq", None, "tensor"),
            P("tensor", None),
            P(None, "seq", "tensor", None),
            P("tensor", None),
            P(),
        ),
        out_specs=(
            P(None, "seq", "tensor", None),
            P(None, "seq", None, "tensor"),
            P(None, None, "seq", None, "tensor"),
            P("tensor", "seq"),
        ),
        check_vma=False,
    )
```

profile of v0, /device:TPU:32, one launch (start us, length us, event | category | flops | bytes accessed | tf_op | source)
XLA Modules:
  0.0 207.0 jit_solution(16878240868297699306)
XLA Ops:
  0.7 2.1 collective-permute-start
  2.7 6.0 %collective-permute-start.1 = (bf16[2,3,3,40,640]{4,3,2,1,0:T(8,128)(2,1)}, bf16[2,3,3,40,640]{4,3,2,1,0:T(8,128)(2,1)S(1)}, u32[]{:S(2)}, u32[]{:S(2)}) collective-permute-start(bf16[2,3,3,40,640]{4,3,2,1,0:T(8,128)(2,1)} %param.9), channel_id=1, source_target_pairs={{8,0},{16,8},{24,16},{32,24},{40,32},{48,40},{56,48},{64,56},{72,6... | collective-permute-start | bytes 2764808 | tf_op jit(solution)/shard_map/ppermute | solution.py:306
  8.8 1.3 copy.21
  10.4 1.7 collective-permute-start.2
  12.0 1.5 collective-permute-start.7
  13.5 1.7 collective-permute-start.5
  16.4 0.8 fusion.refs_6_
  17.3 20.9 %collective-permute-done.2.refs_1_.refs_2_ = bf16[48,5120]{1,0:T(8,128)(2,1)} collective-permute-done((bf16[48,5120]{1,0:T(8,128)(2,1)S(1)}, bf16[48,5120]{1,0:T(8,128)(2,1)}, u32[]{:S(2)}, u32[]{:S(2)}) %collective-permute-start.2) | collective-permute-done | bytes 491552 | tf_op jit(solution)/shard_map/ppermute | solution.py:27
  38.1 2.8 %collective-permute-start.3 = (bf16[48,5120]{1,0:T(8,128)(2,1)}, bf16[48,5120]{1,0:T(8,128)(2,1)}, u32[]{:S(2)}, u32[]{:S(2)}) collective-permute-start(bf16[48,5120]{1,0:T(8,128)(2,1)} %collective-permute-done.2.refs_1_.refs_2_), channel_id=1, source_target_pairs={{0,6},{1,7},{2,0},{3,1},{4,2},{5,3},{6,4},{7,5},{8,14},{9,15},{10,... | collective-permute-start | bytes 1474568 | tf_op jit(solution)/shard_map/ppermute | solution.py:27
  41.1 0.8 fusion.2.refs_5_
  41.8 0.7 broadcast_bitcast_fusion.refs_4_
  42.6 1.0 slice.45
  43.6 4.2 %collective-permute-done.3.refs_8_.refs_3_.refs_4_ = bf16[48,5120]{1,0:T(8,128)(2,1)} collective-permute-done((bf16[48,5120]{1,0:T(8,128)(2,1)}, bf16[48,5120]{1,0:T(8,128)(2,1)}, u32[]{:S(2)}, u32[]{:S(2)}) %collective-permute-start.3) | collective-permute-done | bytes 491552 | tf_op jit(solution)/shard_map/ppermute | solution.py:27
  47.7 1.1 collective-permute-start.8
  48.8 1.0 slice.46
  49.8 2.6 %collective-permute-start.9 = (bf16[32,5120]{1,0:T(8,128)(2,1)S(1)}, bf16[32,5120]{1,0:T(8,128)(2,1)}, u32[]{:S(2)}, u32[]{:S(2)}) collective-permute-start(bf16[32,5120]{1,0:T(8,128)(2,1)S(1)} %slice.46), channel_id=1, source_target_pairs={{0,6},{1,7},{2,0},{3,1},{4,2},{5,3},{6,4},{7,5},{8,14},{9,15},{10,... | collective-permute-start | bytes 983048 | tf_op jit(solution)/shard_map/ppermute | solution.py:27
  53.8 0.9 slice.44
  54.9 1.9 collective-permute-start.6
  56.8 0.9 slice.47
  59.0 10.6 %shard_map.111 = (bf16[5,3,360,360]{3,2,1,0:T(8,128)(2,1)}, bf16[384,640]{1,0:T(8,128)(2,1)}, bf16[2,5,64,384]{3,2,1,0:T(8,128)(2,1)}) custom-call(bf16[360,640]{1,0:T(8,128)(2,1)} %bitcast.33, bf16[2,360,640]{2,1,0:T(8,128)(2,1)} %bitcast.22, bf16[2,360,640]{2,1,0:T(8,128)(2,1)} %bitcast.25, bf16[2,360,640]{2,1,0:T(8,128)(2,1)} %bitcast.28, ...), custom_call_target="tpu_custom_call" | custom-call | flops 2916000000 | bytes 8388608 | tf_op jit(solution)/shard_map/pallas_call | solution.py:76
  69.7 6.4 %shard_map.112 = (bf16[4,320,640]{2,1,0:T(8,128)(2,1)}, bf16[4,320,640]{2,1,0:T(8,128)(2,1)}) custom-call(s32[4]{0:T(128)} %slice.42.order_ref, bf16[640,384]{1,0:T(8,128)(2,1)} %bitcast.36, bf16[48,5120]{1,0:T(8,128)(2,1)} %copy-done.14, bf16[48,5120]{1,0:T(8,128)(2,1)} %collective-permute-done.2.refs_1_.refs_2_, ...), custom_call_target="tpu_custom_call" | custom-call | flops 2516582400 | bytes 6291456 | tf_op jit(solution)/shard_map/pallas_call | solution.py:373
  76.2 6.3 %shard_map.113 = (bf16[4,320,640]{2,1,0:T(8,128)(2,1)}, bf16[4,320,640]{2,1,0:T(8,128)(2,1)}) custom-call(s32[4]{0:T(128)} %slice.37.order_ref, bf16[640,384]{1,0:T(8,128)(2,1)} %bitcast.37, bf16[48,5120]{1,0:T(8,128)(2,1)} %copy-done.14, bf16[48,5120]{1,0:T(8,128)(2,1)} %collective-permute-done.2.refs_1_.refs_2_, ...), custom_call_target="tpu_custom_call" | custom-call | flops 2516582400 | bytes 6291456 | tf_op jit(solution)/shard_map/pallas_call | solution.py:373
  83.1 7.2 %shard_map.114 = (bf16[48,5120]{1,0:T(8,128)(2,1)}, bf16[48,5120]{1,0:T(8,128)(2,1)}, bf16[32,5120]{1,0:T(8,128)(2,1)}, bf16[16,5120]{1,0:T(8,128)(2,1)}, bf16[4...) custom-call(bf16[384,640]{1,0:T(8,128)(2,1)} %get-tuple-element.49.r, ...), custom_call_target="tpu_custom_call" | custom-call | flops 3774873600 | bytes 12582912 | tf_op jit(solution)/shard_map/pallas_call | solution.py:76
  90.5 3.1 %collective-permute-start.18 = (bf16[48,5120]{1,0:T(8,128)(2,1)}, bf16[48,5120]{1,0:T(8,128)(2,1)S(1)}, u32[]{:S(2)}, u32[]{:S(2)}) collective-permute-start(bf16[48,5120]{1,0:T(8,128)(2,1)} %get-tuple-element.69), channel_id=1, source_target_pairs={{0,6},{1,7},{2,0},{3,1},{4,2},{5,3},{6,4},{7,5},{8,14},{9,15},{10,... | collective-permute-start | bytes 1474568 | tf_op jit(solution)/shard_map/ppermute | solution.py:27
  93.6 0.8 fusion.1.refs_6_
  94.4 3.2 %collective-permute-start.12 = (bf16[48,5120]{1,0:T(8,128)(2,1)}, bf16[48,5120]{1,0:T(8,128)(2,1)S(1)}, u32[]{:S(2)}, u32[]{:S(2)}) collective-permute-start(bf16[48,5120]{1,0:T(8,128)(2,1)} %get-tuple-element.55), channel_id=1, source_target_pairs={{0,6},{1,7},{2,0},{3,1},{4,2},{5,3},{6,4},{7,5},{8,14},{9,15},{10,... | collective-permute-start | bytes 1474568 | tf_op jit(solution)/shard_map/ppermute | solution.py:27
  97.6 3.2 %shard_map.115 = (bf16[320,640]{1,0:T(8,128)(2,1)}, bf16[320,640]{1,0:T(8,128)(2,1)}, bf16[160,640]{1,0:T(8,128)(2,1)}, bf16[160,640]{1,0:T(8,128)(2,1)}, bf16[320,640]{1,0:T(8,128)(2,1)}) custom-call(bf16[4,320,640]{2,1,0:T(8,128)(2,1)} %get-tuple-element.60.refs_0_, bf16[4,320,640]{2,1,0:T(8,128)(2,1)} %collective-permute-done.14.refs_1_, ...), custom_call_target="tpu_custom_call" | custom-call | flops 1048576 | bytes 5242880 | tf_op jit(solution)/shard_map/pallas_call | solution.py:76
  100.8 1.9 collective-permute-start.15
  102.7 3.2 %shard_map.116 = (bf16[320,640]{1,0:T(8,128)(2,1)}, bf16[320,640]{1,0:T(8,128)(2,1)}, bf16[160,640]{1,0:T(8,128)(2,1)}, bf16[160,640]{1,0:T(8,128)(2,1)}, bf16[320,640]{1,0:T(8,128)(2,1)}) custom-call(bf16[4,320,640]{2,1,0:T(8,128)(2,1)} %get-tuple-element.59.refs_0_, bf16[4,320,640]{2,1,0:T(8,128)(2,1)} %collective-permute-done.13.refs_1_, ...), custom_call_target="tpu_custom_call" | custom-call | flops 1048576 | bytes 5242880 | tf_op jit(solution)/shard_map/pallas_call | solution.py:76
  106.1 1.9 collective-permute-start.23
  108.0 7.7 %shard_map.117.refs_5_ = bf16[384,640]{1,0:T(8,128)(2,1)} custom-call(bf16[640,5120]{1,0:T(8,128)(2,1)} %refs_0_.1, bf16[48,5120]{1,0:T(8,128)(2,1)} %copy-done.14, bf16[48,5120]{1,0:T(8,128)(2,1)} %collective-permute-done.2.refs_1_.refs_2_, bf16[48,5120]{1,0:T(8,128)(2,1)} %collective-permute-done.5.refs_2_.refs_3_, ...), custom_call_target="tpu_custom_call" | custom-call | flops 3774873600 | bytes 12582912 | tf_op jit(solution)/shard_map/pallas_call | solution.py:76
  115.7 2.3 %collective-permute-start.24 = (bf16[320,640]{1,0:T(8,128)(2,1)}, bf16[320,640]{1,0:T(8,128)(2,1)S(1)}, u32[]{:S(2)}, u32[]{:S(2)}) collective-permute-start(bf16[320,640]{1,0:T(8,128)(2,1)} %get-tuple-element.80), channel_id=1, source_target_pairs={{0,96},{8,104},{16,112},{24,120},{32,0},{40,8},{48,16},{56,24},{64... | collective-permute-start | bytes 1228808 | tf_op jit(solution)/shard_map/ppermute | solution.py:37
  118.0 8.1 %shard_map.118 = (bf16[360,384]{1,0:T(8,128)(2,1)}, f32[2,360,384]{2,1,0:T(8,128)}, bf16[2,360,384]{2,1,0:T(8,128)(2,1)}, bf16[2,360,384]{2,1,0:T(8,128)(2,1)}) custom-call(bf16[360,640]{1,0:T(8,128)(2,1)} %bitcast.34, bf16[2,360,640]{2,1,0:T(8,128)(2,1)} %bitcast.23, bf16[2,360,640]{2,1,0:T(8,128)(2,1)} %bitcast.26, bf16[2,360,640]{2,1,0:T(8,128)(2,1)} %bitcast.29, ...), custom_call_target="tpu_custom_call" | custom-call | flops 2332800000 | bytes 6291456 | tf_op jit(solution)/shard_map/pallas_call | solution.py:76
  126.1 2.3 %shard_map.119 = (bf16[32,5120]{1,0:T(8,128)(2,1)}, bf16[16,5120]{1,0:T(8,128)(2,1)}) custom-call(bf16[32,5120]{1,0:T(8,128)(2,1)} %get-tuple-element.66.refs_0_, bf16[16,5120]{1,0:T(8,128)(2,1)} %get-tuple-element.67.refs_1_, bf16[48,5120]{1,0:T(8,128)(2,1)} %copy-done.4, bf16[48,5120]{1,0:T(8,128)(2,1)} %copy-done.5, ...), custom_call_target="tpu_custom_call" | custom-call | bytes 1048576 | tf_op jit(solution)/shard_map/pallas_call | solution.py:76
  128.4 1.9 collective-permute-start.22
  130.3 2.8 %collective-permute-start.31 = (bf16[2,360,384]{2,1,0:T(8,128)(2,1)S(1)}, bf16[2,360,384]{2,1,0:T(8,128)(2,1)}, u32[]{:S(2)}, u32[]{:S(2)}) collective-permute-start(bf16[2,360,384]{2,1,0:T(8,128)(2,1)S(1)} %copy-done.12), channel_id=1, source_target_pairs={{8,0},{16,8},{24,16},{32,24},{40,32},{48,40},{56,48},{64,56},{72,6... | collective-permute-start | bytes 1658888 | tf_op jit(solution)/shard_map/ppermute | solution.py:476
  133.1 0.8 collective-permute-start.21
  133.9 2.1 %shard_map.120 = (bf16[160,640]{1,0:T(8,128)(2,1)}, bf16[160,640]{1,0:T(8,128)(2,1)}) custom-call(bf16[160,640]{1,0:T(8,128)(2,1)} %get-tuple-element.63.refs_0_, bf16[160,640]{1,0:T(8,128)(2,1)} %get-tuple-element.64.refs_1_, bf16[320,640]{1,0:T(8,128)(2,1)} %copy-done.6, bf16[320,640]{1,0:T(8,128)(2,1)} %copy-done.7, ...), custom_call_target="tpu_custom_call" | custom-call | bytes 1048576 | tf_op jit(solution)/shard_map/pallas_call | solution.py:76
  136.1 1.0 collective-permute-start.28
  137.1 1.1 collective-permute-start.29
  138.2 2.3 %collective-permute-start.32 = (bf16[2,360,384]{2,1,0:T(8,128)(2,1)}, bf16[2,360,384]{2,1,0:T(8,128)(2,1)S(1)}, u32[]{:S(2)}, u32[]{:S(2)}) collective-permute-start(bf16[2,360,384]{2,1,0:T(8,128)(2,1)} %get-tuple-element.90), channel_id=1, source_target_pairs={{0,8},{8,16},{16,24},{24,32},{32,40},{40,48},{48,56},{56,64},{64,7... | collective-permute-start | bytes 1658888 | tf_op jit(solution)/shard_map/ppermute | solution.py:477
  140.5 6.2 %shard_map.121 = (bf16[360,256]{1,0:T(8,128)(2,1)}, f32[2,360,256]{2,1,0:T(8,128)}, bf16[2,360,256]{2,1,0:T(8,128)(2,1)}, bf16[2,360,256]{2,1,0:T(8,128)(2,1)}) custom-call(bf16[360,640]{1,0:T(8,128)(2,1)} %bitcast.35, bf16[2,360,640]{2,1,0:T(8,128)(2,1)} %bitcast.24, bf16[2,360,640]{2,1,0:T(8,128)(2,1)} %bitcast.27, bf16[2,360,640]{2,1,0:T(8,128)(2,1)} %bitcast.30, ...), custom_call_target="tpu_custom_call" | custom-call | flops 1555200000 | bytes 4194304 | tf_op jit(solution)/shard_map/pallas_call | solution.py:76
  146.7 2.2 %shard_map.122 = (bf16[16,5120]{1,0:T(8,128)(2,1)}, bf16[32,5120]{1,0:T(8,128)(2,1)}) custom-call(bf16[16,5120]{1,0:T(8,128)(2,1)} %get-tuple-element.56.refs_0_, bf16[32,5120]{1,0:T(8,128)(2,1)} %get-tuple-element.57.refs_1_, bf16[48,5120]{1,0:T(8,128)(2,1)} %copy-done.2, bf16[48,5120]{1,0:T(8,128)(2,1)} %copy-done.3, ...), custom_call_target="tpu_custom_call" | custom-call | bytes 1048576 | tf_op jit(solution)/shard_map/pallas_call | solution.py:76
  148.9 2.2 %shard_map.123 = (bf16[160,640]{1,0:T(8,128)(2,1)}, bf16[160,640]{1,0:T(8,128)(2,1)}) custom-call(bf16[160,640]{1,0:T(8,128)(2,1)} %get-tuple-element.78.refs_0_, bf16[160,640]{1,0:T(8,128)(2,1)} %get-tuple-element.79.refs_1_, bf16[320,640]{1,0:T(8,128)(2,1)} %copy-done.8, bf16[320,640]{1,0:T(8,128)(2,1)} %copy-done.9, ...), custom_call_target="tpu_custom_call" | custom-call | bytes 1048576 | tf_op jit(solution)/shard_map/pallas_call | solution.py:76
  151.1 0.7 copy-done.21
  151.8 2.4 %shard_map.124.refs_5_ = bf16[48,5120]{1,0:T(8,128)(2,1)} custom-call(bf16[48,5120]{1,0:T(8,128)(2,1)} %get-tuple-element.76.refs_0_, bf16[48,5120]{1,0:T(8,128)(2,1)} %copy-done.4, bf16[48,5120]{1,0:T(8,128)(2,1)} %copy-done.5, bf16[32,5120]{1,0:T(8,128)(2,1)} %copy-done.21, bf16[16,5120]{1,0:T(8,128)(2,1)} %copy-done.27, ...), custom_call_target="tpu_custom_call" | custom-call | bytes 2097152 | tf_op jit(solution)/shard_map/pallas_call | solution.py:76
  155.0 2.3 %shard_map.125.refs_7_ = bf16[320,640]{1,0:T(8,128)(2,1)} custom-call(bf16[320,640]{1,0:T(8,128)(2,1)} %get-tuple-element.84.refs_0_, bf16[320,640]{1,0:T(8,128)(2,1)} %copy-done.6, bf16[320,640]{1,0:T(8,128)(2,1)} %copy-done.7, bf16[160,640]{1,0:T(8,128)(2,1)} %copy-done.23, bf16[160,640]{1,0:T(8,128)(2,1)} %copy-done.24, bf16[48,5120]{1,0:T(8,128)(2,1)} %shard_map.124.refs_5_), custom_call_target="tpu_custom_call" | custom-call | bytes 2097152 | tf_op jit(solution)/shard_map/pallas_call | solution.py:76
  157.3 2.1 %collective-permute-start.30 = (bf16[320,640]{1,0:T(8,128)(2,1)}, bf16[320,640]{1,0:T(8,128)(2,1)S(1)}, u32[]{:S(2)}, u32[]{:S(2)}) collective-permute-start(bf16[320,640]{1,0:T(8,128)(2,1)} %shard_map.125.refs_7_), channel_id=1, source_target_pairs={{0,16},{8,24},{16,0},{24,8},{32,48},{40,56},{48,32},{56,40},{64,80... | collective-permute-start | bytes 1228808 | tf_op jit(solution)/shard_map/ppermute | solution.py:37
  159.4 1.3 collective-permute-start.26
  160.7 1.3 collective-permute-start.27
  162.0 6.9 %collective-permute-start.33 = (bf16[2,360,256]{2,1,0:T(8,128)(2,1)S(1)}, bf16[2,360,256]{2,1,0:T(8,128)(2,1)S(1)}, u32[]{:S(2)}, u32[]{:S(2)}) collective-permute-start(bf16[2,360,256]{2,1,0:T(8,128)(2,1)S(1)} %copy-done.17), channel_id=1, source_target_pairs={{8,0},{16,8},{24,16},{32,24},{40,32},{48,40},{56,48},{64,56},{72,6... | collective-permute-start | bytes 1105928 | tf_op jit(solution)/shard_map/ppermute | solution.py:476
  169.0 0.8 collective-permute-start.25
  169.8 1.9 collective-permute-start.34
  171.8 2.6 %collective-permute-start.20 = (bf16[32,5120]{1,0:T(8,128)(2,1)}, bf16[32,5120]{1,0:T(8,128)(2,1)S(1)}, u32[]{:S(2)}, u32[]{:S(2)}) collective-permute-start(bf16[32,5120]{1,0:T(8,128)(2,1)} %get-tuple-element.75), channel_id=1, source_target_pairs={{0,6},{1,7},{2,0},{3,1},{4,2},{5,3},{6,4},{7,5},{8,14},{9,15},{10,... | collective-permute-start | bytes 983048 | tf_op jit(solution)/shard_map/ppermute | solution.py:27
  174.4 2.6 %shard_map.126 = (bf16[320,320]{1,0:T(8,128)(2,1)}, bf16[320,320]{1,0:T(8,128)(2,1)}) custom-call(bf16[320,640]{1,0:T(8,128)(2,1)} %get-tuple-element.82.refs_0_, bf16[320,640]{1,0:T(8,128)(2,1)} %copy-done.8, bf16[320,640]{1,0:T(8,128)(2,1)} %copy-done.9, bf16[160,640]{1,0:T(8,128)(2,1)} %collective-permute-done.26.refs_3_, bf16[160,640]{1,0:T(8,128)(2,1)} %copy-done.26, ...), custom_call_target="tpu_custom_call" | custom-call | bytes 2097152 | tf_op jit(solution)/shard_map/pallas_call | solution.py:76
  177.0 2.1 %collective-permute-start.35 = (bf16[320,320]{1,0:T(8,128)(2,1)}, bf16[320,320]{1,0:T(8,128)(2,1)S(1)}, u32[]{:S(2)}, u32[]{:S(2)}) collective-permute-start(bf16[320,320]{1,0:T(8,128)(2,1)} %get-tuple-element.93), channel_id=1, source_target_pairs={{0,8},{8,0},{16,24},{24,16},{32,40},{40,32},{48,56},{56,48},{64,72... | collective-permute-start | bytes 614408 | tf_op jit(solution)/shard_map/ppermute | solution.py:37
  179.2 2.0 pad_maximum_fusion
  181.2 11.0 %collective-permute-done.34.refs_5_ = bf16[2,360,256]{2,1,0:T(8,128)(2,1)S(1)} collective-permute-done((bf16[2,360,256]{2,1,0:T(8,128)(2,1)}, bf16[2,360,256]{2,1,0:T(8,128)(2,1)S(1)}, u32[]{:S(2)}, u32[]{:S(2)}) %collective-permute-start.34) | collective-permute-done | bytes 368672 | tf_op jit(solution)/shard_map/ppermute | solution.py:477
  192.1 0.7 copy-done.19
  192.9 3.2 %shard_map.128 = bf16[2,360,640]{2,1,0:T(8,128)(2,1)} custom-call(f32[2,360,384]{2,1,0:T(8,128)} %get-tuple-element.89.refs_0_, bf16[2,360,384]{2,1,0:T(8,128)(2,1)} %collective-permute-done.31.refs_1_, bf16[2,360,384]{2,1,0:T(8,128)(2,1)} %copy-done.13, f32[2,360,256]{2,1,0:T(8,128)} %get-tuple-element.91.refs_3_, bf16[2,360,256]{2,1,0:T(8,128)(2,1)} %copy-done.18, ...), custom_call_target="tpu_custom_call" | custom-call | bytes 5242880 | tf_op jit(solution)/shard_map/pallas_call | solution.py:76
  197.0 3.0 %shard_map.127 = bf16[9,5,5120]{2,1,0:T(8,128)(2,1)} custom-call(bf16[48,5120]{1,0:T(8,128)(2,1)} %get-tuple-element.53.refs_0_, bf16[48,5120]{1,0:T(8,128)(2,1)} %copy-done.2, bf16[48,5120]{1,0:T(8,128)(2,1)} %copy-done.3, bf16[16,5120]{1,0:T(8,128)(2,1)} %copy-done.28, bf16[32,5120]{1,0:T(8,128)(2,1)} %copy-done.20, bf16[48,5120]{1,0:T(8,128)(2,1)} %copy-done.15, ...), custom_call_target="tpu_custom_call" | custom-call | bytes 3145728 | tf_op jit(solution)/shard_map/pallas_call | solution.py:76
  200.0 2.4 %copy.22 = bf16[3,3,5,5120]{3,1,2,0:T(4,128)(2,1)} copy(bf16[3,3,5,5120]{3,2,1,0:T(8,128)(2,1)} %bitcast.21) | data formatting | bytes 921600
  203.0 2.0 shard_map.129
  205.0 2.0 copy.23
  (126 shorter events, 7.7 us)
Async XLA Ops:
  0.6 14.7 %copy-start = (s32[1,16,5,63]{3,1,2,0:T(8,128)S(1)}, s32[1,16,5,63]{3,1,2,0:T(8,128)}, u32[]{:S(2)}) copy-start(s32[1,16,5,63]{3,1,2,0:T(8,128)} %param.13) | copy-start | bytes 60484
  0.6 14.8 %copy-start.29 = (s32[5,5,7]{2,1,0:T(8,128)S(1)}, s32[5,5,7]{2,1,0:T(8,128)}, u32[]{:S(2)}) copy-start(s32[5,5,7]{2,1,0:T(8,128)} %constant.210) | copy-start | bytes 2104
  0.7 15.5 %copy-start.30 = (s32[5,5]{1,0:T(8,128)S(1)}, s32[5,5]{1,0:T(8,128)}, u32[]{:S(2)}) copy-start(s32[5,5]{1,0:T(8,128)} %constant.209) | copy-start | bytes 304
  0.7 14.6 %copy-start.31 = (s32[5,3]{0,1:T(4,128)S(1)}, s32[5,3]{0,1:T(4,128)}, u32[]{:S(2)}) copy-start(s32[5,3]{0,1:T(4,128)} %param.12) | copy-start | bytes 184
  0.7 57.1 %collective-permute-start = (bf16[2,3,3,40,640]{4,3,2,1,0:T(8,128)(2,1)}, bf16[2,3,3,40,640]{4,3,2,1,0:T(8,128)(2,1)S(1)}, u32[]{:S(2)}, u32[]{:S(2)}) collective-permute-start(bf16[2,3,3,40,640]{4,3,2,1,0:T(8,128)(2,1)} %param.9), channel_id=1, source_target_pairs={{0,8},{8,16},{16,24},{24,32},{32,40},{40,48},{48,56},{56,64},{64,7... | collective-permute-start | bytes 2764808 | tf_op jit(solution)/shard_map/ppermute | solution.py:305
  2.7 55.2 %collective-permute-start.1 = (bf16[2,3,3,40,640]{4,3,2,1,0:T(8,128)(2,1)}, bf16[2,3,3,40,640]{4,3,2,1,0:T(8,128)(2,1)S(1)}, u32[]{:S(2)}, u32[]{:S(2)}) collective-permute-start(bf16[2,3,3,40,640]{4,3,2,1,0:T(8,128)(2,1)} %param.9), channel_id=1, source_target_pairs={{8,0},{16,8},{24,16},{32,24},{40,32},{48,40},{56,48},{64,56},{72,6... | collective-permute-start | bytes 2764808 | tf_op jit(solution)/shard_map/ppermute | solution.py:306
  10.3 59.3 %copy-start.14 = (bf16[48,5120]{1,0:T(8,128)(2,1)}, bf16[48,5120]{1,0:T(8,128)(2,1)S(1)}, u32[]{:S(2)}) copy-start(bf16[48,5120]{1,0:T(8,128)(2,1)S(1)} %pad.9.refs_0_.refs_1_) | copy-start | bytes 1474564
  10.4 27.8 %collective-permute-start.2 = (bf16[48,5120]{1,0:T(8,128)(2,1)S(1)}, bf16[48,5120]{1,0:T(8,128)(2,1)}, u32[]{:S(2)}, u32[]{:S(2)}) collective-permute-start(bf16[48,5120]{1,0:T(8,128)(2,1)S(1)} %pad.9.refs_0_.refs_1_), channel_id=1, source_target_pairs={{0,1},{1,0},{2,3},{3,2},{4,5},{5,4},{6,7},{7,6},{8,9},{9,8},{10,11... | collective-permute-start | bytes 1474568 | tf_op jit(solution)/shard_map/ppermute | solution.py:27
  12.0 29.0 %collective-permute-start.7 = (bf16[48,5120]{1,0:T(8,128)(2,1)S(1)}, bf16[48,5120]{1,0:T(8,128)(2,1)}, u32[]{:S(2)}, u32[]{:S(2)}) collective-permute-start(bf16[48,5120]{1,0:T(8,128)(2,1)S(1)} %pad.9.refs_0_.refs_1_), channel_id=1, source_target_pairs={{0,2},{1,3},{2,4},{3,5},{4,6},{5,7},{6,0},{7,1},{8,10},{9,11},{10,... | collective-permute-start | bytes 1474568 | tf_op jit(solution)/shard_map/ppermute | solution.py:27
  13.5 36.3 %collective-permute-start.5 = (bf16[48,5120]{1,0:T(8,128)(2,1)S(1)}, bf16[48,5120]{1,0:T(8,128)(2,1)}, u32[]{:S(2)}, u32[]{:S(2)}) collective-permute-start(bf16[48,5120]{1,0:T(8,128)(2,1)S(1)} %pad.9.refs_0_.refs_1_), channel_id=1, source_target_pairs={{0,6},{1,7},{2,0},{3,1},{4,2},{5,3},{6,4},{7,5},{8,14},{9,15},{10,... | collective-permute-start | bytes 1474568 | tf_op jit(solution)/shard_map/ppermute | solution.py:27
  38.1 9.6 %collective-permute-start.3 = (bf16[48,5120]{1,0:T(8,128)(2,1)}, bf16[48,5120]{1,0:T(8,128)(2,1)}, u32[]{:S(2)}, u32[]{:S(2)}) collective-permute-start(bf16[48,5120]{1,0:T(8,128)(2,1)} %collective-permute-done.2.refs_1_.refs_2_), channel_id=1, source_target_pairs={{0,6},{1,7},{2,0},{3,1},{4,2},{5,3},{6,4},{7,5},{8,14},{9,15},{10,... | collective-permute-start | bytes 1474568 | tf_op jit(solution)/shard_map/ppermute | solution.py:27
  41.0 13.9 %collective-permute-start.4 = (bf16[48,5120]{1,0:T(8,128)(2,1)}, bf16[48,5120]{1,0:T(8,128)(2,1)}, u32[]{:S(2)}, u32[]{:S(2)}) collective-permute-start(bf16[48,5120]{1,0:T(8,128)(2,1)} %collective-permute-done.2.refs_1_.refs_2_), channel_id=1, source_target_pairs={{0,2},{1,3},{2,4},{3,5},{4,6},{5,7},{6,0},{7,1},{8,10},{9,11},{10,... | collective-permute-start | bytes 1474568 | tf_op jit(solution)/shard_map/ppermute | solution.py:27
  47.7 22.0 %collective-permute-start.8 = (bf16[32,5120]{1,0:T(8,128)(2,1)S(1)}, bf16[32,5120]{1,0:T(8,128)(2,1)}, u32[]{:S(2)}, u32[]{:S(2)}) collective-permute-start(bf16[32,5120]{1,0:T(8,128)(2,1)S(1)} %slice.45), channel_id=1, source_target_pairs={{0,2},{1,3},{2,4},{3,5},{4,6},{5,7},{6,0},{7,1},{8,10},{9,11},{10,... | collective-permute-start | bytes 983048 | tf_op jit(solution)/shard_map/ppermute | solution.py:27
  49.8 19.9 %collective-permute-start.9 = (bf16[32,5120]{1,0:T(8,128)(2,1)S(1)}, bf16[32,5120]{1,0:T(8,128)(2,1)}, u32[]{:S(2)}, u32[]{:S(2)}) collective-permute-start(bf16[32,5120]{1,0:T(8,128)(2,1)S(1)} %slice.46), channel_id=1, source_target_pairs={{0,6},{1,7},{2,0},{3,1},{4,2},{5,3},{6,4},{7,5},{8,14},{9,15},{10,... | collective-permute-start | bytes 983048 | tf_op jit(solution)/shard_map/ppermute | solution.py:27
  54.9 14.8 %collective-permute-start.6 = (bf16[16,5120]{1,0:T(8,128)(2,1)S(1)}, bf16[16,5120]{1,0:T(8,128)(2,1)}, u32[]{:S(2)}, u32[]{:S(2)}) collective-permute-start(bf16[16,5120]{1,0:T(8,128)(2,1)S(1)} %slice.44), channel_id=1, source_target_pairs={{0,6},{1,7},{2,0},{3,1},{4,2},{5,3},{6,4},{7,5},{8,14},{9,15},{10,... | collective-permute-start | bytes 491528 | tf_op jit(solution)/shard_map/ppermute | solution.py:27
  57.8 0.9 copy-start.10
  57.8 11.9 %collective-permute-start.10 = (bf16[16,5120]{1,0:T(8,128)(2,1)S(1)}, bf16[16,5120]{1,0:T(8,128)(2,1)}, u32[]{:S(2)}, u32[]{:S(2)}) collective-permute-start(bf16[16,5120]{1,0:T(8,128)(2,1)S(1)} %slice.47), channel_id=1, source_target_pairs={{0,2},{1,3},{2,4},{3,5},{4,6},{5,7},{6,0},{7,1},{8,10},{9,11},{10,... | collective-permute-start | bytes 491528 | tf_op jit(solution)/shard_map/ppermute | solution.py:27
  58.0 1.1 copy-start.11
  76.1 18.3 %collective-permute-start.14 = (bf16[4,320,640]{2,1,0:T(8,128)(2,1)}, bf16[4,320,640]{2,1,0:T(8,128)(2,1)}, u32[]{:S(2)}, u32[]{:S(2)}) collective-permute-start(bf16[4,320,640]{2,1,0:T(8,128)(2,1)} %get-tuple-element.51.refs_10_), channel_id=1, source_target_pairs={{0,8},{8,0},{16,24},{24,16},{32,40},{40,32},{48,56},{56,48},{64,72... | collective-permute-start | bytes 4915208 | tf_op jit(solution)/shard_map/ppermute | solution.py:37
  82.5 18.3 %collective-permute-start.13 = (bf16[4,320,640]{2,1,0:T(8,128)(2,1)}, bf16[4,320,640]{2,1,0:T(8,128)(2,1)}, u32[]{:S(2)}, u32[]{:S(2)}) collective-permute-start(bf16[4,320,640]{2,1,0:T(8,128)(2,1)} %get-tuple-element.52.refs_2_), channel_id=1, source_target_pairs={{0,8},{8,0},{16,24},{24,16},{32,40},{40,32},{48,56},{56,48},{64,72... | collective-permute-start | bytes 4915208 | tf_op jit(solution)/shard_map/ppermute | solution.py:37
  90.3 15.6 %collective-permute-start.17 = (bf16[48,5120]{1,0:T(8,128)(2,1)}, bf16[48,5120]{1,0:T(8,128)(2,1)S(1)}, u32[]{:S(2)}, u32[]{:S(2)}) collective-permute-start(bf16[48,5120]{1,0:T(8,128)(2,1)} %get-tuple-element.68), channel_id=1, source_target_pairs={{0,2},{1,3},{2,4},{3,5},{4,6},{5,7},{6,0},{7,1},{8,10},{9,11},{10,... | collective-permute-start | bytes 1474568 | tf_op jit(solution)/shard_map/ppermute | solution.py:27
  90.5 15.6 %collective-permute-start.18 = (bf16[48,5120]{1,0:T(8,128)(2,1)}, bf16[48,5120]{1,0:T(8,128)(2,1)S(1)}, u32[]{:S(2)}, u32[]{:S(2)}) collective-permute-start(bf16[48,5120]{1,0:T(8,128)(2,1)} %get-tuple-element.69), channel_id=1, source_target_pairs={{0,6},{1,7},{2,0},{3,1},{4,2},{5,3},{6,4},{7,5},{8,14},{9,15},{10,... | collective-permute-start | bytes 1474568 | tf_op jit(solution)/shard_map/ppermute | solution.py:27
  93.6 22.1 %collective-permute-start.11 = (bf16[48,5120]{1,0:T(8,128)(2,1)}, bf16[48,5120]{1,0:T(8,128)(2,1)S(1)}, u32[]{:S(2)}, u32[]{:S(2)}) collective-permute-start(bf16[48,5120]{1,0:T(8,128)(2,1)} %get-tuple-element.54.refs_2_), channel_id=1, source_target_pairs={{0,2},{1,3},{2,4},{3,5},{4,6},{5,7},{6,0},{7,1},{8,10},{9,11},{10,... | collective-permute-start | bytes 1474568 | tf_op jit(solution)/shard_map/ppermute | solution.py:27
  94.4 34.1 %collective-permute-start.12 = (bf16[48,5120]{1,0:T(8,128)(2,1)}, bf16[48,5120]{1,0:T(8,128)(2,1)S(1)}, u32[]{:S(2)}, u32[]{:S(2)}) collective-permute-start(bf16[48,5120]{1,0:T(8,128)(2,1)} %get-tuple-element.55), channel_id=1, source_target_pairs={{0,6},{1,7},{2,0},{3,1},{4,2},{5,3},{6,4},{7,5},{8,14},{9,15},{10,... | collective-permute-start | bytes 1474568 | tf_op jit(solution)/shard_map/ppermute | solution.py:27
  100.8 29.5 %collective-permute-start.15 = (bf16[320,640]{1,0:T(8,128)(2,1)}, bf16[320,640]{1,0:T(8,128)(2,1)S(1)}, u32[]{:S(2)}, u32[]{:S(2)}) collective-permute-start(bf16[320,640]{1,0:T(8,128)(2,1)} %get-tuple-element.61.refs_2_), channel_id=1, source_target_pairs={{0,32},{8,40},{16,48},{24,56},{32,64},{40,72},{48,80},{56,88},{64,... | collective-permute-start | bytes 1228808 | tf_op jit(solution)/shard_map/ppermute | solution.py:37
  105.9 9.7 %copy-start.4 = (bf16[48,5120]{1,0:T(8,128)(2,1)}, bf16[48,5120]{1,0:T(8,128)(2,1)S(1)}, u32[]{:S(2)}) copy-start(bf16[48,5120]{1,0:T(8,128)(2,1)S(1)} %collective-permute-done.17.refs_2_.refs_1_) | copy-start | bytes 1474564
  105.9 27.2 %collective-permute-start.16 = (bf16[320,640]{1,0:T(8,128)(2,1)}, bf16[320,640]{1,0:T(8,128)(2,1)S(1)}, u32[]{:S(2)}, u32[]{:S(2)}) collective-permute-start(bf16[320,640]{1,0:T(8,128)(2,1)} %get-tuple-element.65), channel_id=1, source_target_pairs={{0,96},{8,104},{16,112},{24,120},{32,0},{40,8},{48,16},{56,24},{64... | collective-permute-start | bytes 1228808 | tf_op jit(solution)/shard_map/ppermute | solution.py:37
  106.1 9.6 %copy-start.5 = (bf16[48,5120]{1,0:T(8,128)(2,1)}, bf16[48,5120]{1,0:T(8,128)(2,1)S(1)}, u32[]{:S(2)}) copy-start(bf16[48,5120]{1,0:T(8,128)(2,1)S(1)} %collective-permute-done.18.refs_3_.refs_2_) | copy-start | bytes 1474564
  106.1 31.0 %collective-permute-start.23 = (bf16[320,640]{1,0:T(8,128)(2,1)}, bf16[320,640]{1,0:T(8,128)(2,1)S(1)}, u32[]{:S(2)}, u32[]{:S(2)}) collective-permute-start(bf16[320,640]{1,0:T(8,128)(2,1)} %get-tuple-element.62.refs_11_), channel_id=1, source_target_pairs={{0,32},{8,40},{16,48},{24,56},{32,64},{40,72},{48,80},{56,88},{64,... | collective-permute-start | bytes 1228808 | tf_op jit(solution)/shard_map/ppermute | solution.py:37
  115.7 10.4 %copy-start.2 = (bf16[48,5120]{1,0:T(8,128)(2,1)}, bf16[48,5120]{1,0:T(8,128)(2,1)S(1)}, u32[]{:S(2)}) copy-start(bf16[48,5120]{1,0:T(8,128)(2,1)S(1)} %collective-permute-done.11.refs_2_.refs_1_) | copy-start | bytes 1474564
  115.7 22.5 %collective-permute-start.24 = (bf16[320,640]{1,0:T(8,128)(2,1)}, bf16[320,640]{1,0:T(8,128)(2,1)S(1)}, u32[]{:S(2)}, u32[]{:S(2)}) collective-permute-start(bf16[320,640]{1,0:T(8,128)(2,1)} %get-tuple-element.80), channel_id=1, source_target_pairs={{0,96},{8,104},{16,112},{24,120},{32,0},{40,8},{48,16},{56,24},{64... | collective-permute-start | bytes 1228808 | tf_op jit(solution)/shard_map/ppermute | solution.py:37
  126.1 4.2 %copy-start.12 = (bf16[2,360,384]{2,1,0:T(8,128)(2,1)S(1)}, bf16[2,360,384]{2,1,0:T(8,128)(2,1)}, u32[]{:S(2)}) copy-start(bf16[2,360,384]{2,1,0:T(8,128)(2,1)} %get-tuple-element.70.refs_4_) | copy-start | bytes 1658884
  128.4 18.2 %copy-start.3 = (bf16[48,5120]{1,0:T(8,128)(2,1)}, bf16[48,5120]{1,0:T(8,128)(2,1)S(1)}, u32[]{:S(2)}) copy-start(bf16[48,5120]{1,0:T(8,128)(2,1)S(1)} %collective-permute-done.12.refs_3_.refs_2_) | copy-start | bytes 1474564
  128.4 7.6 %collective-permute-start.22 = (bf16[16,5120]{1,0:T(8,128)(2,1)}, bf16[16,5120]{1,0:T(8,128)(2,1)S(1)}, u32[]{:S(2)}, u32[]{:S(2)}) collective-permute-start(bf16[16,5120]{1,0:T(8,128)(2,1)} %get-tuple-element.77), channel_id=1, source_target_pairs={{0,6},{1,7},{2,0},{3,1},{4,2},{5,3},{6,4},{7,5},{8,14},{9,15},{10,... | collective-permute-start | bytes 491528 | tf_op jit(solution)/shard_map/ppermute | solution.py:27
  130.3 3.6 %copy-start.6 = (bf16[320,640]{1,0:T(8,128)(2,1)}, bf16[320,640]{1,0:T(8,128)(2,1)S(1)}, u32[]{:S(2)}) copy-start(bf16[320,640]{1,0:T(8,128)(2,1)S(1)} %collective-permute-done.15.refs_2_.refs_1_) | copy-start | bytes 1228804
  130.3 31.7 %collective-permute-start.31 = (bf16[2,360,384]{2,1,0:T(8,128)(2,1)S(1)}, bf16[2,360,384]{2,1,0:T(8,128)(2,1)}, u32[]{:S(2)}, u32[]{:S(2)}) collective-permute-start(bf16[2,360,384]{2,1,0:T(8,128)(2,1)S(1)} %copy-done.12), channel_id=1, source_target_pairs={{8,0},{16,8},{24,16},{32,24},{40,32},{48,40},{56,48},{64,56},{72,6... | collective-permute-start | bytes 1658888 | tf_op jit(solution)/shard_map/ppermute | solution.py:476
  133.1 0.8 copy-start.7
  133.1 18.0 %collective-permute-start.21 = (bf16[32,5120]{1,0:T(8,128)(2,1)}, bf16[32,5120]{1,0:T(8,128)(2,1)S(1)}, u32[]{:S(2)}, u32[]{:S(2)}) collective-permute-start(bf16[32,5120]{1,0:T(8,128)(2,1)} %get-tuple-element.71.refs_4_), channel_id=1, source_target_pairs={{0,2},{1,3},{2,4},{3,5},{4,6},{5,7},{6,0},{7,1},{8,10},{9,11},{10,... | collective-permute-start | bytes 983048 | tf_op jit(solution)/shard_map/ppermute | solution.py:27
  136.1 10.6 %copy-start.27 = (bf16[16,5120]{1,0:T(8,128)(2,1)}, bf16[16,5120]{1,0:T(8,128)(2,1)S(1)}, u32[]{:S(2)}) copy-start(bf16[16,5120]{1,0:T(8,128)(2,1)S(1)} %collective-permute-done.22.refs_4_) | copy-start | bytes 491524
  136.1 18.2 %collective-permute-start.28 = (bf16[160,640]{1,0:T(8,128)(2,1)}, bf16[160,640]{1,0:T(8,128)(2,1)S(1)}, u32[]{:S(2)}, u32[]{:S(2)}) collective-permute-start(bf16[160,640]{1,0:T(8,128)(2,1)} %get-tuple-element.72.refs_7_), channel_id=1, source_target_pairs={{0,32},{8,40},{16,48},{24,56},{32,64},{40,72},{48,80},{56,88},{64,... | collective-permute-start | bytes 614408 | tf_op jit(solution)/shard_map/ppermute | solution.py:37
  137.1 9.6 %copy-start.8 = (bf16[320,640]{1,0:T(8,128)(2,1)}, bf16[320,640]{1,0:T(8,128)(2,1)S(1)}, u32[]{:S(2)}) copy-start(bf16[320,640]{1,0:T(8,128)(2,1)S(1)} %collective-permute-done.23.refs_2_.refs_1_) | copy-start | bytes 1228804
  137.1 17.2 %collective-permute-start.29 = (bf16[160,640]{1,0:T(8,128)(2,1)}, bf16[160,640]{1,0:T(8,128)(2,1)S(1)}, u32[]{:S(2)}, u32[]{:S(2)}) collective-permute-start(bf16[160,640]{1,0:T(8,128)(2,1)} %get-tuple-element.85), channel_id=1, source_target_pairs={{0,96},{8,104},{16,112},{24,120},{32,0},{40,8},{48,16},{56,24},{64... | collective-permute-start | bytes 614408 | tf_op jit(solution)/shard_map/ppermute | solution.py:37
  138.1 8.6 %copy-start.9 = (bf16[320,640]{1,0:T(8,128)(2,1)}, bf16[320,640]{1,0:T(8,128)(2,1)S(1)}, u32[]{:S(2)}) copy-start(bf16[320,640]{1,0:T(8,128)(2,1)S(1)} %collective-permute-done.24.refs_3_.refs_2_) | copy-start | bytes 1228804
  138.2 38.9 %collective-permute-start.32 = (bf16[2,360,384]{2,1,0:T(8,128)(2,1)}, bf16[2,360,384]{2,1,0:T(8,128)(2,1)S(1)}, u32[]{:S(2)}, u32[]{:S(2)}) collective-permute-start(bf16[2,360,384]{2,1,0:T(8,128)(2,1)} %get-tuple-element.90), channel_id=1, source_target_pairs={{0,8},{8,16},{16,24},{24,32},{32,40},{40,48},{48,56},{56,64},{64,7... | collective-permute-start | bytes 1658888 | tf_op jit(solution)/shard_map/ppermute | solution.py:477
  154.2 5.2 %copy-start.25 = (bf16[160,640]{1,0:T(8,128)(2,1)S(1)}, bf16[160,640]{1,0:T(8,128)(2,1)}, u32[]{:S(2)}) copy-start(bf16[160,640]{1,0:T(8,128)(2,1)} %get-tuple-element.81.refs_5_) | copy-start | bytes 614404
  154.2 6.5 %copy-start.32 = (bf16[160,640]{1,0:T(8,128)(2,1)S(1)}, bf16[160,640]{1,0:T(8,128)(2,1)}, u32[]{:S(2)}) copy-start(bf16[160,640]{1,0:T(8,128)(2,1)} %get-tuple-element.83) | copy-start | bytes 614404
  154.2 7.8 %copy-start.17 = (bf16[2,360,256]{2,1,0:T(8,128)(2,1)S(1)}, bf16[2,360,256]{2,1,0:T(8,128)(2,1)}, u32[]{:S(2)}) copy-start(bf16[2,360,256]{2,1,0:T(8,128)(2,1)} %get-tuple-element.73.refs_4_) | copy-start | bytes 1105924
  154.2 14.7 %copy-start.1 = (bf16[48,5120]{1,0:T(8,128)(2,1)S(1)}, bf16[48,5120]{1,0:T(8,128)(2,1)}, u32[]{:S(2)}) copy-start(bf16[48,5120]{1,0:T(8,128)(2,1)} %shard_map.124.refs_5_) | copy-start | bytes 1474564
  154.3 0.7 copy-start.24
  157.3 14.4 %collective-permute-start.30 = (bf16[320,640]{1,0:T(8,128)(2,1)}, bf16[320,640]{1,0:T(8,128)(2,1)S(1)}, u32[]{:S(2)}, u32[]{:S(2)}) collective-permute-start(bf16[320,640]{1,0:T(8,128)(2,1)} %shard_map.125.refs_7_), channel_id=1, source_target_pairs={{0,16},{8,24},{16,0},{24,8},{32,48},{40,56},{48,32},{56,40},{64,80... | collective-permute-start | bytes 1228808 | tf_op jit(solution)/shard_map/ppermute | solution.py:37
  159.4 9.5 %collective-permute-start.26 = (bf16[160,640]{1,0:T(8,128)(2,1)S(1)}, bf16[160,640]{1,0:T(8,128)(2,1)}, u32[]{:S(2)}, u32[]{:S(2)}) collective-permute-start(bf16[160,640]{1,0:T(8,128)(2,1)S(1)} %copy-done.25), channel_id=1, source_target_pairs={{0,32},{8,40},{16,48},{24,56},{32,64},{40,72},{48,80},{56,88},{64,... | collective-permute-start | bytes 614408 | tf_op jit(solution)/shard_map/ppermute | solution.py:37
  160.7 9.1 %collective-permute-start.27 = (bf16[160,640]{1,0:T(8,128)(2,1)S(1)}, bf16[160,640]{1,0:T(8,128)(2,1)S(1)}, u32[]{:S(2)}, u32[]{:S(2)}) collective-permute-start(bf16[160,640]{1,0:T(8,128)(2,1)S(1)} %copy-done.32), channel_id=1, source_target_pairs={{0,96},{8,104},{16,112},{24,120},{32,0},{40,8},{48,16},{56,24},{64... | collective-permute-start | bytes 614408 | tf_op jit(solution)/shard_map/ppermute | solution.py:37
  162.0 17.1 %collective-permute-start.33 = (bf16[2,360,256]{2,1,0:T(8,128)(2,1)S(1)}, bf16[2,360,256]{2,1,0:T(8,128)(2,1)S(1)}, u32[]{:S(2)}, u32[]{:S(2)}) collective-permute-start(bf16[2,360,256]{2,1,0:T(8,128)(2,1)S(1)} %copy-done.17), channel_id=1, source_target_pairs={{8,0},{16,8},{24,16},{32,24},{40,32},{48,40},{56,48},{64,56},{72,6... | collective-permute-start | bytes 1105928 | tf_op jit(solution)/shard_map/ppermute | solution.py:476
  169.0 27.1 %collective-permute-start.25 = (bf16[48,5120]{1,0:T(8,128)(2,1)S(1)}, bf16[48,5120]{1,0:T(8,128)(2,1)S(1)}, u32[]{:S(2)}, u32[]{:S(2)}) collective-permute-start(bf16[48,5120]{1,0:T(8,128)(2,1)S(1)} %copy-done.1), channel_id=1, source_target_pairs={{0,1},{1,0},{2,3},{3,2},{4,5},{5,4},{6,7},{7,6},{8,9},{9,8},{10,11... | collective-permute-start | bytes 1474568 | tf_op jit(solution)/shard_map/ppermute | solution.py:27
  169.8 1.9 copy-start.26
  169.8 22.3 %collective-permute-start.34 = (bf16[2,360,256]{2,1,0:T(8,128)(2,1)}, bf16[2,360,256]{2,1,0:T(8,128)(2,1)S(1)}, u32[]{:S(2)}, u32[]{:S(2)}) collective-permute-start(bf16[2,360,256]{2,1,0:T(8,128)(2,1)} %get-tuple-element.92), channel_id=1, source_target_pairs={{0,8},{8,16},{16,24},{24,32},{32,40},{40,48},{48,56},{56,64},{64,7... | collective-permute-start | bytes 1105928 | tf_op jit(solution)/shard_map/ppermute | solution.py:477
  171.7 2.7 %copy-start.16 = (bf16[320,640]{1,0:T(8,128)(2,1)}, bf16[320,640]{1,0:T(8,128)(2,1)S(1)}, u32[]{:S(2)}) copy-start(bf16[320,640]{1,0:T(8,128)(2,1)S(1)} %collective-permute-done.30.refs_5_) | copy-start | bytes 1228804
  171.8 24.3 %collective-permute-start.20 = (bf16[32,5120]{1,0:T(8,128)(2,1)}, bf16[32,5120]{1,0:T(8,128)(2,1)S(1)}, u32[]{:S(2)}, u32[]{:S(2)}) collective-permute-start(bf16[32,5120]{1,0:T(8,128)(2,1)} %get-tuple-element.75), channel_id=1, source_target_pairs={{0,6},{1,7},{2,0},{3,1},{4,2},{5,3},{6,4},{7,5},{8,14},{9,15},{10,... | collective-permute-start | bytes 983048 | tf_op jit(solution)/shard_map/ppermute | solution.py:27
  177.0 15.1 %copy-start.13 = (bf16[2,360,384]{2,1,0:T(8,128)(2,1)}, bf16[2,360,384]{2,1,0:T(8,128)(2,1)S(1)}, u32[]{:S(2)}) copy-start(bf16[2,360,384]{2,1,0:T(8,128)(2,1)S(1)} %collective-permute-done.32.refs_2_) | copy-start | bytes 1658884
  177.0 25.3 %collective-permute-start.35 = (bf16[320,320]{1,0:T(8,128)(2,1)}, bf16[320,320]{1,0:T(8,128)(2,1)S(1)}, u32[]{:S(2)}, u32[]{:S(2)}) collective-permute-start(bf16[320,320]{1,0:T(8,128)(2,1)} %get-tuple-element.93), channel_id=1, source_target_pairs={{0,8},{8,0},{16,24},{24,16},{32,40},{40,32},{48,56},{56,48},{64,72... | collective-permute-start | bytes 614408 | tf_op jit(solution)/shard_map/ppermute | solution.py:37
  179.2 13.0 %copy-start.18 = (bf16[2,360,256]{2,1,0:T(8,128)(2,1)}, bf16[2,360,256]{2,1,0:T(8,128)(2,1)S(1)}, u32[]{:S(2)}) copy-start(bf16[2,360,256]{2,1,0:T(8,128)(2,1)S(1)} %collective-permute-done.33.refs_4_) | copy-start | bytes 1105924
  179.2 16.9 %collective-permute-start.19 = (bf16[16,5120]{1,0:T(8,128)(2,1)}, bf16[16,5120]{1,0:T(8,128)(2,1)S(1)}, u32[]{:S(2)}, u32[]{:S(2)}) collective-permute-start(bf16[16,5120]{1,0:T(8,128)(2,1)} %get-tuple-element.74.refs_4_), channel_id=1, source_target_pairs={{0,2},{1,3},{2,4},{3,5},{4,6},{5,7},{6,0},{7,1},{8,10},{9,11},{10,... | collective-permute-start | bytes 491528 | tf_op jit(solution)/shard_map/ppermute | solution.py:27
  196.1 0.8 copy-start.20
  196.1 0.9 copy-start.15
  (5 other events, 3.5 us)
where the time goes:
time: 208 us; the launch traced here: 207 us
  Pallas kernels  83.2 us (40%)
  starting transfers between devices  64.1 us (31%)
  waiting for transfers between devices  36.3 us (17%)
  local copies, waits for them, and re-layouts  16.9 us (8%)
  other arithmetic  5.23 us (3%)
    pallas_call x17, Pallas kernels, kernel(): pl.pallas_call(run, grid=grid, in_specs=[*specs, *[ANYWHERE] * len(after)...  70.5 us
    ppermute x18, starting transfers between devices, tensor_shift(): return lax.ppermute(value, 'tensor', pairs)  26.3 us
    ppermute x18, waiting for transfers between devices, tensor_shift(): return lax.ppermute(value, 'tensor', pairs)  25.3 us
    ppermute x12, starting transfers between devices, seq_shift(): return lax.ppermute(value, 'seq', pairs)  15.8 us
    pallas_call x2, Pallas kernels, weight_half(): pl.pallas_call(weight_kernel, grid_spec=pltpu.PrefetchScalarGridSpec(num_...  12.7 us
    ppermute x2, waiting for transfers between devices, send_halo(): from_above = lax.ppermute(grad_down, 'seq', onward)  11 us
    unnamed x69, local copies, waits for them, and re-layouts  10.6 us
    ppermute x2, starting transfers between devices, send_halo(): from_below = lax.ppermute(grad_up, 'seq', back)  9.66 us
  transfers between devices with their start and end apart: 36, of which 4 were waited for; matrix products, arithmetic and copies ran while one was open for 7% of the time, Pallas kernels for 36%

commit v1 on v0

v1 whole, which is shorter than its diff:
```python
import jax
import jax.numpy as jnp
import numpy as np
from jax import lax
from jax.experimental import pallas as pl
from jax.experimental.pallas import tpu as pltpu
from jax.sharding import PartitionSpec as P

HEAD_DIM = 128
TILE_W = 8
REACH_W = 3
OFFSETS = 63
SCALE = HEAD_DIM ** (-0.5)
OUTSIDE = -1e30
F32 = jnp.float32
BF16 = jnp.bfloat16


def dot(a, b, dims):
    return lax.dot_general(a, b, (dims, ((), ())), preferred_element_type=F32)


def tensor_shift(value, dx, dy):
    pairs = [
        (x * 2 + y, (x + dx) % 4 * 2 + (y + dy) % 2) for x in range(4) for y in range(2)
    ]
    return lax.ppermute(value, "tensor", pairs)


def seq_shift(value, dz, dy, core=0):
    pairs = [
        ((z * 2 + y) * 2 + c, ((z + dz) % 4 * 2 + (y + dy) % 2) * 2 + (c + core) % 2)
        for z in range(4)
        for y in range(2)
        for c in range(2)
    ]
    return lax.ppermute(value, "seq", pairs)


def added(*terms):
    total = terms[0].astype(F32)
    for term in terms[1:]:
        total = total + term.astype(F32)
    return total


BLOCKS = ((0, 0), (1, 0), (3, 0), (0, 1), (3, 1), (1, 1), (2, 0), (2, 1))


def gathered(own, shift):
    c01 = shift(own, 0, 1)
    c10 = shift(own, -1, 0)
    c30 = shift(own, 1, 0)
    c20 = shift(c10, -1, 0)
    c11 = shift(c01, -1, 0)
    c31 = shift(c01, 1, 0)
    c21 = shift(c31, 1, 0)
    return jnp.concatenate([own, c10, c30, c01, c31, c11, c20, c21], axis=0), [c10, c31]


ANYWHERE = pl.BlockSpec(memory_space=pl.ANY)


def kernel(body, outs, args, specs=None, out_specs=None, grid=(), after=(), flops=0, moved=0, scratch=()):
    count = len(args)

    def run(*refs):
        return body(*refs[:count], *refs[count + len(after) :])

    vector = pl.BlockSpec(memory_space=pltpu.VMEM)
    specs = [vector] * count if specs is None else specs
    out_specs = [vector] * len(outs) if out_specs is None else out_specs
    return pl.pallas_call(
        run,
        grid=grid,
        in_specs=[*specs, *[ANYWHERE] * len(after)],
        out_specs=out_specs,
        out_shape=[jax.ShapeDtypeStruct(shape, kind) for shape, kind in outs],
        scratch_shapes=scratch,
        cost_estimate=pl.CostEstimate(flops=flops, transcendentals=0, bytes_accessed=moved),
    )(*args, *after)


def sum_kernel(*refs):
    refs[-1][...] = added(*[r[...] for r in refs[:-1]]).astype(BF16)


def relay_kernel(a_ref, b_ref, came_a_ref, came_b_ref, out_a_ref, out_b_ref):
    out_a_ref[...] = added(a_ref[...], came_a_ref[...]).astype(BF16)
    out_b_ref[...] = added(b_ref[...], came_b_ref[...]).astype(BF16)


def mixed_kernel(*refs):
    out_ref = refs[-1]
    total = added(*[r[...] for r in refs[:-1]])
    frames, columns, rows, _ = out_ref.shape
    for f in range(frames):
        for c in range(columns):
            start = (f * columns + c) * rows
            out_ref[f, c] = total[start : start + rows].astype(BF16)


SCALAR = pl.BlockSpec(memory_space=pltpu.SMEM)
VECTOR = pl.BlockSpec(memory_space=pltpu.VMEM)


def hop(shift, arrays):
    return [shift(arrays[i], 1 - 2 * i, 0) for i in range(2)]


def forward_kernel(q_ref, own_ref, up_ref, down_ref, bias_ref, hot_ref, perm_ref, p_ref, att_ref):
    qa = jnp.concatenate([q_ref[...], hot_ref[...]], axis=1)
    scores = []
    for b, ref in enumerate((up_ref, own_ref, down_ref)):
        bias = jnp.concatenate([bias_ref[0, b]] * 9, axis=0).astype(BF16)
        ka = jnp.concatenate([ref[0], bias], axis=1)
        scores.append(dot(ka, qa, ((1,), (1,))))
    top = jnp.max(scores[0], axis=0, keepdims=True)
    for s in scores[1:]:
        top = jnp.maximum(top, jnp.max(s, axis=0, keepdims=True))
    weights = [jnp.exp((s - top) * SCALE) for s in scores]
    total = jnp.sum(weights[0], axis=0, keepdims=True)
    for w in weights[1:]:
        total = total + jnp.sum(w, axis=0, keepdims=True)
    inverse = 1.0 / total
    attended = None
    for b, ref in enumerate((up_ref, own_ref, down_ref)):
        probs = (weights[b] * inverse).astype(BF16)
        p_ref[0, b] = probs
        part = dot(ref[1], probs, ((0,), (0,)))
        attended = part if attended is None else attended + part
    attended = attended.astype(BF16)
    att_ref[...] = dot(perm_ref[...], attended, ((1,), (1,))).astype(BF16)


def backward_kernel(
    q_ref, own_ref, up_ref, down_ref, p_ref, ga_ref, perm_ref, gq_ref, gown_ref, gup_ref, gdown_ref
):
    q = q_ref[...]
    g = dot(perm_ref[...], ga_ref[...], ((1,), (0,))).astype(BF16)
    refs = (up_ref, own_ref, down_ref)
    outs = (gup_ref, gown_ref, gdown_ref)
    grads = []
    delta = None
    for b in range(3):
        gp = dot(refs[b][1], g, ((1,), (1,)))
        part = jnp.sum(p_ref[0, b].astype(F32) * gp, axis=0, keepdims=True)
        delta = part if delta is None else delta + part
        grads.append(gp)
    gq = None
    for b in range(3):
        probs = p_ref[0, b]
        ds = (probs.astype(F32) * (grads[b] - delta) * SCALE).astype(BF16)
        outs[b][0] = dot(ds, q, ((1,), (0,))).astype(outs[b].dtype)
        outs[b][1] = dot(probs, g, ((1,), (0,))).astype(outs[b].dtype)
        part = dot(refs[b][0], ds, ((0,), (0,)))
        gq = part if gq is None else gq + part
    gq_ref[...] = gq.T.astype(BF16)


def weight_kernel(order_ref, g_ref, far_g_ref, att_ref, far_att_ref, *outs):
    attended = jnp.concatenate([att_ref[...], far_att_ref[...]], axis=0)
    first = order_ref[len(outs)] == 0
    width = 2 * outs[0].shape[0]
    for i, out_ref in enumerate(outs):
        columns = pl.ds(pl.multiple_of(order_ref[i] * width, width), width)
        g = jnp.concatenate([g_ref[:, columns], far_g_ref[:, columns]], axis=0)
        g = jnp.where(first, g[:, : width // 2], g[:, width // 2 :])
        out_ref[...] = dot(g, attended, ((0,), (0,))).astype(BF16)


def project_kernel(att_ref, w_ref, *outs):
    mixed = dot(att_ref[...], w_ref[...], ((1,), (0,)))
    room = outs[0].shape[0]
    for k, out_ref in enumerate(outs):
        out_ref[...] = mixed[k * room : (k + 1) * room].astype(BF16)


def attn_grad_kernel(w_ref, g_ref, ga_ref, total_ref):
    step = pl.program_id(0)
    part = dot(g_ref[...], w_ref[...], ((1,), (1,)))

    @pl.when(step == 0)
    def _():
        total_ref[...] = part

    @pl.when(step > 0)
    def _():
        total_ref[...] += part

    @pl.when(step == pl.num_programs(0) - 1)
    def _():
        ga_ref[...] = total_ref[...].astype(BF16)


def total_kernel(*refs):
    out_ref = refs[-1]
    start = 0
    for i in range(0, len(refs) - 1, 3):
        part = added(refs[i][...], refs[i + 1][...], refs[i + 2][...]).astype(BF16)
        out_ref[:, :, start : start + part.shape[2]] = part
        start += part.shape[2]


def mask_bias(window, own_mask, seq_place, row_tiles):
    heads = window.shape[0]
    columns = own_mask.shape[0]
    rows = own_mask.reshape(columns, 3, 3, 7)[:, 1]
    query = np.arange(columns)
    delta = query[:, None] - query[None, :]
    pick = (delta[:, :, None] + REACH_W == np.arange(7)).astype(np.int32)
    bits = jnp.sum(rows.transpose(1, 0, 2)[:, None] * pick[None], axis=-1)
    dh = jnp.arange(3, dtype=jnp.int32) - 1
    tile_row = dh + seq_place
    row_ok = (tile_row >= 0) & (tile_row < row_tiles)
    inside = (jnp.abs(dh)[None, :] <= window[:, 1:2]) & row_ok[None, :] & (window[:, :1] >= 0)
    near = np.abs(delta)[None] <= window[:, 2][:, None, None]
    ok = inside[:, :, None, None] & near[:, None] & (bits > 0)[None]
    bias = jnp.where(ok, 0.0, OUTSIDE).astype(F32)
    bias = jnp.pad(bias, ((0, 0), (0, 0), (0, 0), (0, 128 - columns)))
    wide = jnp.broadcast_to(bias[:, :, :, None], (heads, 3, columns, TILE_W, 128))
    return wide.reshape(heads, 3, columns * TILE_W, 128)


def layer(queries, keys_values, out_weight, grad_out, window, block_mask):
    frames, tile_rows, columns, channels = queries.shape
    model_width = grad_out.shape[3]
    local_columns = grad_out.shape[2]
    tokens = frames * tile_rows * columns
    heads = channels // HEAD_DIM
    strips = frames * tile_rows
    row_tiles = lax.axis_size("seq")
    seq_place = lax.axis_index("seq")
    tensor_place = lax.axis_index("tensor")
    spot_z, spot_y, core = seq_place // 4, seq_place // 2 % 2, seq_place % 2
    spot_x, spot_low = tensor_place // 2, tensor_place % 2
    core = core[None].astype(jnp.int32)

    onward = [(i, i + 1) for i in range(row_tiles - 1)]
    back = [(i + 1, i) for i in range(row_tiles - 1)]
    up = lax.ppermute(keys_values, "seq", onward)
    down = lax.ppermute(keys_values, "seq", back)

    piece = strips * local_columns
    room = -(-piece // 16) * 16
    own_grad = grad_out.transpose(0, 2, 1, 3).reshape(piece, model_width)
    own_grad = jnp.pad(own_grad, ((0, room - piece), (0, 0)))
    all_grad, last_hops = gathered(own_grad, tensor_shift)
    slots = 8 * room

    row = np.arange(slots) % room
    ring, pair = (np.repeat([b[i] for b in BLOCKS], room).astype(np.int32) for i in range(2))
    owner = (spot_x + ring) % 4 * 2 + (spot_low + pair) % 2
    strip = row // (local_columns * tile_rows) * tile_rows + row % tile_rows
    place = strip * columns + owner * local_columns + row // tile_rows % local_columns
    place = jnp.where(row < piece, place, -1).astype(jnp.int32)
    cell = lax.iota(jnp.int32, tokens)
    perm = (place[:, None] == cell[None, :]).astype(BF16)
    perm_back = (cell[:, None] == place[None, :]).astype(BF16)
    hot = (cell[:, None] % columns // TILE_W == lax.iota(jnp.int32, 128)[None, :]).astype(BF16)

    own_mask = lax.dynamic_slice_in_dim(block_mask, seq_place, 1, 1).reshape(-1, OFFSETS)
    bias = mask_bias(window, own_mask, seq_place, row_tiles)

    flat_q = queries.reshape(tokens, channels)
    flat = [v.reshape(2, tokens, channels) for v in (keys_values, up, down)]

    def whole(shape):
        return pl.BlockSpec(shape, lambda h: (0,) * len(shape))

    q_spec = pl.BlockSpec((tokens, HEAD_DIM), lambda h: (0, h))
    kv_spec = pl.BlockSpec((2, tokens, HEAD_DIM), lambda h: (0, 0, h))
    pairs = heads * tokens * 3 * tokens
    probs, attended = kernel(
        forward_kernel,
        [((heads, 3, tokens, tokens), BF16), ((slots, channels), BF16)],
        [flat_q, *flat, bias, hot, perm],
        [
            q_spec,
            kv_spec,
            kv_spec,
            kv_spec,
            pl.BlockSpec((1, 3, columns, 128), lambda h: (h, 0, 0, 0)),
            whole((tokens, 128)),
            whole((slots, tokens)),
        ],
        [
            pl.BlockSpec((1, 3, tokens, tokens), lambda h: (h, 0, 0, 0)),
            pl.BlockSpec((slots, HEAD_DIM), lambda h: (0, h)),
        ],
        grid=(heads,),
        after=last_hops,
        flops=pairs * 1500,
        moved=8 << 20,
    )
    far_grad = seq_shift(all_grad, 0, 0, 1)
    far_attended = seq_shift(attended, 0, 0, 1)

    broad = model_width // 4
    mixed = kernel(
        project_kernel,
        [((room, model_width), BF16)] * 8,
        [attended, out_weight],
        [whole((slots, channels)), pl.BlockSpec((channels, broad), lambda i: (0, i))],
        [pl.BlockSpec((room, broad), lambda i: (0, i))] * 8,
        grid=(4,),
        flops=slots * model_width * channels * 3,
        moved=12 << 20,
    )
    mixed = dict(zip(BLOCKS, mixed))
    mixed_far = hop(tensor_shift, (mixed[2, 1], mixed[2, 0]))
    mixed_near = hop(tensor_shift, (mixed[1, 0], mixed[3, 1]))

    narrow = model_width // row_tiles

    def weight_blocks(blocks, after):
        chips = [(spot_z + d) % 4 * 2 + (spot_y + e) % 2 for d, e in blocks]
        order = jnp.stack([*chips, core[0]]).astype(jnp.int32)
        return kernel(
            weight_kernel,
            [((narrow, channels), BF16)] * len(blocks),
            [order, all_grad, far_grad, attended, far_attended],
            [SCALAR] + [VECTOR] * 4,
            after=after,
            flops=slots * model_width * channels * 2,
            moved=6 << 20,
        )

    w21, w20, w10, w31 = weight_blocks([(2, 1), (2, 0), (1, 0), (3, 1)], [mixed[0, 0]])
    weight_far = hop(seq_shift, (w21, w20))
    weight_near = hop(seq_shift, (w10, w31))
    w11, w30, w01, w00 = weight_blocks([(1, 1), (3, 0), (0, 1), (0, 0)], [w21])

    (grad_attn,) = kernel(
        attn_grad_kernel,
        [((slots, channels), BF16)],
        [out_weight, all_grad],
        [
            pl.BlockSpec((channels, broad), lambda i: (0, i)),
            pl.BlockSpec((slots, broad), lambda i: (0, i)),
        ],
        [whole((slots, channels))],
        grid=(4,),
        after=[w11],
        flops=slots * model_width * channels * 3,
        moved=12 << 20,
        scratch=[pltpu.VMEM((slots, channels), F32)],
    )

    def differentiate(first, count, after):
        def spec(shape, at):
            def index(h):
                return tuple(h + first if i == at else 0 for i in range(len(shape)))

            return pl.BlockSpec(shape, index)

        width = count * HEAD_DIM
        kv_in = spec((2, tokens, HEAD_DIM), 2)
        return kernel(
            backward_kernel,
            [
                ((tokens, width), BF16),
                ((2, tokens, width), F32),
                ((2, tokens, width), BF16),
                ((2, tokens, width), BF16),
            ],
            [flat_q, *flat, probs, grad_attn, perm_back],
            [
                spec((tokens, HEAD_DIM), 1),
                kv_in,
                kv_in,
                kv_in,
                spec((1, 3, tokens, tokens), 0),
                spec((slots, HEAD_DIM), 1),
                whole((tokens, slots)),
            ],
            [q_spec, kv_spec, kv_spec, kv_spec],
            grid=(count,),
            after=after,
            flops=pairs * 2000 * count // heads,
            moved=2 * count << 20,
        )

    def send_halo(grad_up, grad_down):
        from_below = lax.ppermute(grad_up, "seq", back)
        from_above = lax.ppermute(grad_down, "seq", onward)
        return from_below, from_above

    def summed(body, shapes, terms, after):
        return kernel(body, [(shape, BF16) for shape in shapes], terms, after=after, moved=2 << 20)

    split = (heads + 1) // 2
    mixed_sums = summed(
        relay_kernel, [own_grad.shape] * 2, [mixed[1, 1], mixed[3, 0], *mixed_far], [grad_attn]
    )
    mark = mixed_sums[0]
    mixed_sums = hop(tensor_shift, mixed_sums)
    gq_a, own_a, up_a, down_a = differentiate(0, split, [mark])
    below_a, above_a = send_halo(up_a, down_a)
    weight_sums = summed(relay_kernel, [w00.shape] * 2, [w11, w30, *weight_far], [up_a])
    mark = weight_sums[0]
    weight_sums = hop(seq_shift, weight_sums)
    gq_b, own_b, up_b, down_b = differentiate(split, heads - split, [mark])
    below_b, above_b = send_halo(up_b, down_b)
    (side,) = summed(
        sum_kernel, [own_grad.shape], [mixed[0, 1], mixed_near[1], mixed_sums[0]], [up_b]
    )
    mixed_side = tensor_shift(side, 0, 1)
    (side,) = summed(sum_kernel, [w00.shape], [w01, weight_near[1], weight_sums[0]], [side])
    weight_side = seq_shift(side, 0, 1)
    (grad_kv,) = summed(
        total_kernel,
        [(2, tokens, channels)],
        [own_a, below_a, above_a, own_b, below_b, above_b],
        [side],
    )
    (layer_out,) = summed(
        mixed_kernel,
        [(frames, local_columns, tile_rows, model_width)],
        [mixed[0, 0], mixed_near[0], mixed_sums[1], mixed_side],
        [grad_kv],
    )
    (grad_weight,) = summed(
        sum_kernel, [w00.shape], [w00, weight_near[0], weight_sums[1], weight_side], [layer_out]
    )
    grad_q = jnp.concatenate([gq_a, gq_b], axis=1)
    return (
        layer_out.transpose(0, 2, 1, 3),
        grad_q.reshape(queries.shape),
        grad_kv.reshape(keys_values.shape),
        grad_weight.T,
    )


def solution(mesh):
    return jax.shard_map(
        layer,
        mesh=mesh,
        in_specs=(
            P(None, "seq", None, "tensor"),
            P(None, None, "seq", None, "tensor"),
            P("tensor", None),
            P(None, "seq", "tensor", None),
            P("tensor", None),
            P(),
        ),
        out_specs=(
            P(None, "seq", "tensor", None),
            P(None, "seq", None, "tensor"),
            P(None, None, "seq", None, "tensor"),
            P("tensor", "seq"),
        ),
        check_vma=False,
    )
```

time: 208 us -> 191 us (0.918)
  the two profiles are of different devices: /device:TPU:32 before, /device:TPU:0 now
where the time goes in v1:
time: 191 us; the launch traced here: 189 us
  Pallas kernels  70.1 us (37%)
  starting transfers between devices  64 us (34%)
  waiting for transfers between devices  33.8 us (18%)
  local copies, waits for them, and re-layouts  14.8 us (8%)
  other arithmetic  4.94 us (3%)
    pallas_call x14, Pallas kernels, kernel(): pl.pallas_call(run, grid=grid, in_specs=[*specs, *[ANYWHERE] * len(after)...  70.1 us
    ppermute x9, starting transfers between devices, seq_shift(): return lax.ppermute(value, 'seq', pairs)  30.9 us
    ppermute x14, waiting for transfers between devices, tensor_shift(): return lax.ppermute(value, 'tensor', pairs)  26.5 us
    ppermute x14, starting transfers between devices, tensor_shift(): return lax.ppermute(value, 'tensor', pairs)  19 us
    unnamed x65, local copies, waits for them, and re-layouts  10.1 us
    ppermute x2, starting transfers between devices, send_halo(): from_above = lax.ppermute(grad_down, 'seq', onward)  7.75 us
    ppermute x9, waiting for transfers between devices, seq_shift(): return lax.ppermute(value, 'seq', pairs)  5.83 us
  transfers between devices with their start and end apart: 29, of which 8 were waited for; matrix products, arithmetic and copies ran while one was open for 6% of the time, Pallas kernels for 36%

profile of v1, /device:TPU:0, one launch (start us, length us, event | category | flops | bytes accessed | tf_op | source)
XLA Modules:
  0.0 188.7 jit_solution(1591228122498306026)
XLA Ops:
  0.6 1.5 reshape.164
  2.2 0.9 constant_dynamic-update-slice_fusion.7
  3.1 1.8 collective-permute-start.3
  4.9 2.8 %collective-permute-start.2 = (bf16[48,5120]{1,0:T(8,128)(2,1)S(1)}, bf16[48,5120]{1,0:T(8,128)(2,1)S(1)}, u32[]{:S(2)}, u32[]{:S(2)}) collective-permute-start(bf16[48,5120]{1,0:T(8,128)(2,1)S(1)} %get-tuple-element.65), channel_id=1, source_target_pairs={{0,6},{1,7},{2,0},{3,1},{4,2},{5,3},{6,4},{7,5},{8,14},{9,15},{10,... | collective-permute-start | bytes 1474568 | tf_op jit(solution)/shard_map/ppermute | solution.py:27
  7.6 8.5 %collective-permute-done.3 = bf16[48,5120]{1,0:T(8,128)(2,1)S(1)} collective-permute-done((bf16[48,5120]{1,0:T(8,128)(2,1)S(1)}, bf16[48,5120]{1,0:T(8,128)(2,1)S(1)}, u32[]{:S(2)}, u32[]{:S(2)}) %collective-permute-start.3) | collective-permute-done | bytes 491552 | tf_op jit(solution)/shard_map/ppermute | solution.py:27
  16.1 1.7 collective-permute-start.4
  17.7 1.6 collective-permute-start.9
  19.3 2.2 %collective-permute-start.10 = (bf16[48,5120]{1,0:T(8,128)(2,1)S(1)}, bf16[48,5120]{1,0:T(8,128)(2,1)S(1)}, u32[]{:S(2)}, u32[]{:S(2)}) collective-permute-start(bf16[48,5120]{1,0:T(8,128)(2,1)S(1)} %collective-permute-done.2.refs_7_), channel_id=1, source_target_pairs={{0,6},{1,7},{2,0},{3,1},{4,2},{5,3},{6,4},{7,5},{8,14},{9,15},{10,... | collective-permute-start | bytes 1474568 | tf_op jit(solution)/shard_map/ppermute | solution.py:27
  21.5 0.8 constant_dynamic-update-slice_fusion.6
  22.9 0.8 constant_dynamic-update-slice_fusion.5
  23.7 0.8 constant_dynamic-update-slice_fusion.4
  24.6 7.2 %collective-permute-done.4.refs_8_ = bf16[48,5120]{1,0:T(8,128)(2,1)S(1)} collective-permute-done((bf16[48,5120]{1,0:T(8,128)(2,1)S(1)}, bf16[48,5120]{1,0:T(8,128)(2,1)S(1)}, u32[]{:S(2)}, u32[]{:S(2)}) %collective-permute-start.4) | collective-permute-done | bytes 491552 | tf_op jit(solution)/shard_map/ppermute | solution.py:27
  31.8 0.9 constant_dynamic-update-slice_fusion.3
  32.6 0.8 constant_dynamic-update-slice_fusion.2
  33.5 6.6 %collective-permute-done.10 = bf16[48,5120]{1,0:T(8,128)(2,1)S(1)} collective-permute-done((bf16[48,5120]{1,0:T(8,128)(2,1)S(1)}, bf16[48,5120]{1,0:T(8,128)(2,1)S(1)}, u32[]{:S(2)}, u32[]{:S(2)}) %collective-permute-start.10) | collective-permute-done | bytes 491552 | tf_op jit(solution)/shard_map/ppermute | solution.py:27
  40.1 0.8 constant_dynamic-update-slice_fusion.1
  40.9 3.6 %collective-permute-done.11 = bf16[48,5120]{1,0:T(8,128)(2,1)S(1)} collective-permute-done((bf16[48,5120]{1,0:T(8,128)(2,1)S(1)}, bf16[48,5120]{1,0:T(8,128)(2,1)S(1)}, u32[]{:S(2)}, u32[]{:S(2)}) %collective-permute-start.11) | collective-permute-done | bytes 491552 | tf_op jit(solution)/shard_map/ppermute | solution.py:27
  44.5 0.8 constant_dynamic-update-slice_fusion.refs_1_
  45.4 2.5 %collective-permute-start = (bf16[2,3,3,40,640]{4,3,2,1,0:T(8,128)(2,1)S(1)}, bf16[2,3,3,40,640]{4,3,2,1,0:T(8,128)(2,1)S(1)}, u32[]{:S(2)}, u32[]{:S(2)}) collective-permute-start(bf16[2,3,3,40,640]{4,3,2,1,0:T(8,128)(2,1)S(1)} %copy-done.1), channel_id=1, source_target_pairs={{0,8},{8,16},{16,24},{24,32},{32,40},{40,48},{48,56},{56,64},{64,7... | collective-permute-start | bytes 2764808 | tf_op jit(solution)/shard_map/ppermute | solution.py:241
  47.8 1.3 collective-permute-start.1
  50.4 0.8 fusion.2.refs_5_
  51.1 0.8 fusion.refs_6_
  52.0 0.7 broadcast_bitcast_fusion.refs_4_
  53.3 0.9 collective-permute-done.1
  54.2 0.9 copy-done.3
  55.1 10.1 %shard_map.156 = (bf16[5,3,360,360]{3,2,1,0:T(8,128)(2,1)}, bf16[384,640]{1,0:T(8,128)(2,1)}) custom-call(bf16[360,640]{1,0:T(8,128)(2,1)} %bitcast.42, bf16[2,360,640]{2,1,0:T(8,128)(2,1)} %bitcast.32, bf16[2,360,640]{2,1,0:T(8,128)(2,1)} %bitcast.35, bf16[2,360,640]{2,1,0:T(8,128)(2,1)} %bitcast.38, f32[5,3,40,128]{3,2,1,0:T(8,128)} %broadcast_bitcast_fusion.refs_4_, ...), custom_call_target="tpu_custom_call" | custom-call | flops 2916000000 | bytes 8388608 | tf_op jit(solution)/shard_map/pallas_call | solution.py:73
  65.2 18.5 %collective-permute-start.13 = (bf16[384,640]{1,0:T(8,128)(2,1)}, bf16[384,640]{1,0:T(8,128)(2,1)S(1)}, u32[]{:S(2)}, u32[]{:S(2)}) collective-permute-start(bf16[384,640]{1,0:T(8,128)(2,1)} %get-tuple-element.34.refs_0_.refs_3_), channel_id=1, source_target_pairs={{0,8},{8,0},{16,24},{24,16},{32,40},{40,32},{48,56},{56,48},{64,72... | collective-permute-start | bytes 1474568 | tf_op jit(solution)/shard_map/ppermute | solution.py:37
  83.7 0.7 stack.39.refs_0_
  84.4 0.7 stack.34.refs_0_
  85.0 7.1 %shard_map.157 = (bf16[48,5120]{1,0:T(8,128)(2,1)}, bf16[48,5120]{1,0:T(8,128)(2,1)}, bf16[48,5120]{1,0:T(8,128)(2,1)}, bf16[48,5120]{1,0:T(8,128)(2,1)}, bf16[4...) custom-call(bf16[384,640]{1,0:T(8,128)(2,1)} %get-tuple-element.34.refs_0_.r, ...), custom_call_target="tpu_custom_call" | custom-call | flops 3774873600 | bytes 12582912 | tf_op jit(solution)/shard_map/pallas_call | solution.py:73
  92.2 3.2 %collective-permute-start.7 = (bf16[48,5120]{1,0:T(8,128)(2,1)}, bf16[48,5120]{1,0:T(8,128)(2,1)S(1)}, u32[]{:S(2)}, u32[]{:S(2)}) collective-permute-start(bf16[48,5120]{1,0:T(8,128)(2,1)} %get-tuple-element.40), channel_id=1, source_target_pairs={{0,6},{1,7},{2,0},{3,1},{4,2},{5,3},{6,4},{7,5},{8,14},{9,15},{10,... | collective-permute-start | bytes 1474568 | tf_op jit(solution)/shard_map/ppermute | solution.py:27
  95.4 2.0 %collective-permute-start.5 = (bf16[48,5120]{1,0:T(8,128)(2,1)}, bf16[48,5120]{1,0:T(8,128)(2,1)S(1)}, u32[]{:S(2)}, u32[]{:S(2)}) collective-permute-start(bf16[48,5120]{1,0:T(8,128)(2,1)} %get-tuple-element.36), channel_id=1, source_target_pairs={{0,2},{1,3},{2,4},{3,5},{4,6},{5,7},{6,0},{7,1},{8,10},{9,11},{10,... | collective-permute-start | bytes 1474568 | tf_op jit(solution)/shard_map/ppermute | solution.py:27
  97.4 6.8 %shard_map.158 = (bf16[320,640]{1,0:T(8,128)(2,1)}, bf16[320,640]{1,0:T(8,128)(2,1)}, bf16[320,640]{1,0:T(8,128)(2,1)}, bf16[320,640]{1,0:T(8,128)(2,1)}) custom-call(s32[5]{0:T(128)} %stack.39.refs_0_, bf16[384,5120]{1,0:T(8,128)(2,1)} %constant_dynamic-update-slice_fusion.refs_1_, bf16[384,5120]{1,0:T(8,128)(2,1)} %collective-permute-done.12.refs_2_, ...), custom_call_target="tpu_custom_call" | custom-call | flops 2516582400 | bytes 6291456 | tf_op jit(solution)/shard_map/pallas_call | solution.py:73
  104.2 1.9 %collective-permute-start.17 = (bf16[320,640]{1,0:T(8,128)(2,1)}, bf16[320,640]{1,0:T(8,128)(2,1)S(1)}, u32[]{:S(2)}, u32[]{:S(2)}) collective-permute-start(bf16[320,640]{1,0:T(8,128)(2,1)} %get-tuple-element.41.refs_5_), channel_id=1, source_target_pairs={{0,32},{8,40},{16,48},{24,56},{32,64},{40,72},{48,80},{56,88},{64,... | collective-permute-start | bytes 1228808 | tf_op jit(solution)/shard_map/ppermute | solution.py:37
  106.1 6.7 %shard_map.159 = (bf16[320,640]{1,0:T(8,128)(2,1)}, bf16[320,640]{1,0:T(8,128)(2,1)}, bf16[320,640]{1,0:T(8,128)(2,1)}, bf16[320,640]{1,0:T(8,128)(2,1)}) custom-call(s32[5]{0:T(128)} %stack.34.refs_0_, bf16[384,5120]{1,0:T(8,128)(2,1)} %constant_dynamic-update-slice_fusion.refs_1_, bf16[384,5120]{1,0:T(8,128)(2,1)} %collective-permute-done.12.refs_2_, ...), custom_call_target="tpu_custom_call" | custom-call | flops 2516582400 | bytes 6291456 | tf_op jit(solution)/shard_map/pallas_call | solution.py:73
  112.8 7.6 %shard_map.160.refs_4_.refs_5_ = bf16[384,640]{1,0:T(8,128)(2,1)} custom-call(bf16[640,5120]{1,0:T(8,128)(2,1)} %refs_0_.1, bf16[384,5120]{1,0:T(8,128)(2,1)} %constant_dynamic-update-slice_fusion.refs_1_, bf16[320,640]{1,0:T(8,128)(2,1)} %get-tuple-element.42.refs_2_.refs_0_), custom_call_target="tpu_custom_call" | custom-call | flops 3774873600 | bytes 12582912 | tf_op jit(solution)/shard_map/pallas_call | solution.py:73
  120.4 1.3 collective-permute-start.18
  121.8 0.8 copy-done.7
  122.5 2.5 %shard_map.161 = (bf16[48,5120]{1,0:T(8,128)(2,1)}, bf16[48,5120]{1,0:T(8,128)(2,1)}) custom-call(bf16[48,5120]{1,0:T(8,128)(2,1)} %get-tuple-element.37.refs_0_, bf16[48,5120]{1,0:T(8,128)(2,1)} %get-tuple-element.38.refs_1_, bf16[48,5120]{1,0:T(8,128)(2,1)} %copy-done.6, bf16[48,5120]{1,0:T(8,128)(2,1)} %copy-done.7, ...), custom_call_target="tpu_custom_call" | custom-call | bytes 2097152 | tf_op jit(solution)/shard_map/pallas_call | solution.py:73
  125.1 0.8 collective-permute-start.16
  125.9 0.8 fusion.1.refs_6_
  126.7 0.9 collective-permute-start.24
  127.6 8.1 %shard_map.162 = (bf16[360,384]{1,0:T(8,128)(2,1)}, f32[2,360,384]{2,1,0:T(8,128)}, bf16[2,360,384]{2,1,0:T(8,128)(2,1)}, bf16[2,360,384]{2,1,0:T(8,128)(2,1)}) custom-call(bf16[360,640]{1,0:T(8,128)(2,1)} %bitcast.43, bf16[2,360,640]{2,1,0:T(8,128)(2,1)} %bitcast.33, bf16[2,360,640]{2,1,0:T(8,128)(2,1)} %bitcast.36, bf16[2,360,640]{2,1,0:T(8,128)(2,1)} %bitcast.39, ...), custom_call_target="tpu_custom_call" | custom-call | flops 2332800000 | bytes 6291456 | tf_op jit(solution)/shard_map/pallas_call | solution.py:73
  135.7 1.3 collective-permute-start.20
  137.0 3.1 %collective-permute-start.21 = (bf16[2,360,384]{2,1,0:T(8,128)(2,1)}, bf16[2,360,384]{2,1,0:T(8,128)(2,1)S(1)}, u32[]{:S(2)}, u32[]{:S(2)}) collective-permute-start(bf16[2,360,384]{2,1,0:T(8,128)(2,1)} %get-tuple-element.54), channel_id=1, source_target_pairs={{0,8},{8,16},{16,24},{24,32},{32,40},{40,48},{48,56},{56,64},{64,7... | collective-permute-start | bytes 1658888 | tf_op jit(solution)/shard_map/ppermute | solution.py:386
  140.1 2.4 %shard_map.163 = (bf16[320,640]{1,0:T(8,128)(2,1)}, bf16[320,640]{1,0:T(8,128)(2,1)}) custom-call(bf16[320,640]{1,0:T(8,128)(2,1)} %get-tuple-element.42.refs_2_.refs_0_, bf16[320,640]{1,0:T(8,128)(2,1)} %get-tuple-element.48.refs_1_, bf16[320,640]{1,0:T(8,128)(2,1)} %copy-done.17, bf16[320,640]{1,0:T(8,128)(2,1)} %collective-permute-done.18.refs_3_, ...), custom_call_target="tpu_custom_call" | custom-call | bytes 2097152 | tf_op jit(solution)/shard_map/pallas_call | solution.py:73
  142.5 2.0 %collective-permute-start.25 = (bf16[320,640]{1,0:T(8,128)(2,1)}, bf16[320,640]{1,0:T(8,128)(2,1)}, u32[]{:S(2)}, u32[]{:S(2)}) collective-permute-start(bf16[320,640]{1,0:T(8,128)(2,1)} %get-tuple-element.51.refs_7_), channel_id=1, source_target_pairs={{0,32},{8,40},{16,48},{24,56},{32,64},{40,72},{48,80},{56,88},{64,... | collective-permute-start | bytes 1228808 | tf_op jit(solution)/shard_map/ppermute | solution.py:37
  144.4 6.2 %shard_map.164 = (bf16[360,256]{1,0:T(8,128)(2,1)}, f32[2,360,256]{2,1,0:T(8,128)}, bf16[2,360,256]{2,1,0:T(8,128)(2,1)}, bf16[2,360,256]{2,1,0:T(8,128)(2,1)}) custom-call(bf16[360,640]{1,0:T(8,128)(2,1)} %bitcast.44, bf16[2,360,640]{2,1,0:T(8,128)(2,1)} %bitcast.34, bf16[2,360,640]{2,1,0:T(8,128)(2,1)} %bitcast.37, bf16[2,360,640]{2,1,0:T(8,128)(2,1)} %bitcast.40, ...), custom_call_target="tpu_custom_call" | custom-call | flops 1555200000 | bytes 4194304 | tf_op jit(solution)/shard_map/pallas_call | solution.py:73
  150.7 1.4 collective-permute-start.22
  152.1 4.7 %collective-permute-start.23 = (bf16[2,360,256]{2,1,0:T(8,128)(2,1)}, bf16[2,360,256]{2,1,0:T(8,128)(2,1)}, u32[]{:S(2)}, u32[]{:S(2)}) collective-permute-start(bf16[2,360,256]{2,1,0:T(8,128)(2,1)} %get-tuple-element.56), channel_id=1, source_target_pairs={{0,8},{8,16},{16,24},{24,32},{32,40},{40,48},{48,56},{56,64},{64,7... | collective-permute-start | bytes 1105928 | tf_op jit(solution)/shard_map/ppermute | solution.py:386
  156.8 2.3 %shard_map.165.refs_3_ = bf16[48,5120]{1,0:T(8,128)(2,1)} custom-call(bf16[48,5120]{1,0:T(8,128)(2,1)} %get-tuple-element.44.refs_0_, bf16[48,5120]{1,0:T(8,128)(2,1)} %copy-done.12, bf16[48,5120]{1,0:T(8,128)(2,1)} %copy-done.13, bf16[2,360,256]{2,1,0:T(8,128)(2,1)} %get-tuple-element.52.refs_3_), custom_call_target="tpu_custom_call" | custom-call | bytes 2097152 | tf_op jit(solution)/shard_map/pallas_call | solution.py:73
  159.1 2.5 %collective-permute-start.14 = (bf16[48,5120]{1,0:T(8,128)(2,1)}, bf16[48,5120]{1,0:T(8,128)(2,1)S(1)}, u32[]{:S(2)}, u32[]{:S(2)}) collective-permute-start(bf16[48,5120]{1,0:T(8,128)(2,1)} %get-tuple-element.43), channel_id=1, source_target_pairs={{0,6},{1,7},{2,0},{3,1},{4,2},{5,3},{6,4},{7,5},{8,14},{9,15},{10,... | collective-permute-start | bytes 1474568 | tf_op jit(solution)/shard_map/ppermute | solution.py:27
  162.1 2.2 %shard_map.166.refs_6_ = bf16[320,640]{1,0:T(8,128)(2,1)} custom-call(bf16[320,640]{1,0:T(8,128)(2,1)} %get-tuple-element.57.refs_0_, bf16[320,640]{1,0:T(8,128)(2,1)} %copy-done.16, bf16[320,640]{1,0:T(8,128)(2,1)} %collective-permute-done.25.refs_2_, bf16[48,5120]{1,0:T(8,128)(2,1)} %shard_map.165.refs_3_), custom_call_target="tpu_custom_call" | custom-call | bytes 2097152 | tf_op jit(solution)/shard_map/pallas_call | solution.py:73
  164.2 2.2 %collective-permute-start.26 = (bf16[320,640]{1,0:T(8,128)(2,1)}, bf16[320,640]{1,0:T(8,128)(2,1)S(1)}, u32[]{:S(2)}, u32[]{:S(2)}) collective-permute-start(bf16[320,640]{1,0:T(8,128)(2,1)} %get-tuple-element.62), channel_id=1, source_target_pairs={{0,32},{8,40},{16,48},{24,56},{32,64},{40,72},{48,80},{56,88},{64,... | collective-permute-start | bytes 1228808 | tf_op jit(solution)/shard_map/ppermute | solution.py:37
  166.5 1.0 collective-permute-start.27
  167.5 3.0 %collective-permute-start.28 = (bf16[320,640]{1,0:T(8,128)(2,1)}, bf16[320,640]{1,0:T(8,128)(2,1)S(1)}, u32[]{:S(2)}, u32[]{:S(2)}) collective-permute-start(bf16[320,640]{1,0:T(8,128)(2,1)} %shard_map.166.refs_6_), channel_id=1, source_target_pairs={{0,16},{8,24},{16,0},{24,8},{32,48},{40,56},{48,32},{56,40},{64,80... | collective-permute-start | bytes 1228808 | tf_op jit(solution)/shard_map/ppermute | solution.py:37
  170.5 1.8 pad_maximum_fusion
  172.3 3.2 %shard_map.167.refs_4_ = bf16[2,360,640]{2,1,0:T(8,128)(2,1)} custom-call(f32[2,360,384]{2,1,0:T(8,128)} %get-tuple-element.53.refs_0_, bf16[2,360,384]{2,1,0:T(8,128)(2,1)} %copy-done.4, bf16[2,360,384]{2,1,0:T(8,128)(2,1)} %copy-done.5, f32[2,360,256]{2,1,0:T(8,128)} %get-tuple-element.55.refs_3_, bf16[2,360,256]{2,1,0:T(8,128)(2,1)} %collective-permute-done.22.refs_4_, ...), custom_call_target="tpu_custom_call" | custom-call | bytes 2097152 | tf_op jit(solution)/shard_map/pallas_call | solution.py:73
  175.5 0.8 copy-done.14
  176.3 0.8 copy-done.15
  177.1 2.7 %shard_map.168.refs_4_ = bf16[3,5,3,5120]{3,2,1,0:T(4,128)(2,1)} custom-call(bf16[48,5120]{1,0:T(8,128)(2,1)} %get-tuple-element.35.refs_5_.refs_0_, bf16[48,5120]{1,0:T(8,128)(2,1)} %copy-done.9, bf16[48,5120]{1,0:T(8,128)(2,1)} %copy-done.14, bf16[48,5120]{1,0:T(8,128)(2,1)} %copy-done.15, bf16[2,360,640]{2,1,0:T(8,128)(2,1)} %shard_map.167.refs_4_), custom_call_target="tpu_custom_call" | custom-call | bytes 2097152 | tf_op jit(solution)/shard_map/pallas_call | solution.py:73
  179.8 5.8 %collective-permute-done.28.refs_3_ = bf16[320,640]{1,0:T(8,128)(2,1)S(1)} collective-permute-done((bf16[320,640]{1,0:T(8,128)(2,1)}, bf16[320,640]{1,0:T(8,128)(2,1)S(1)}, u32[]{:S(2)}, u32[]{:S(2)}) %collective-permute-start.28) | collective-permute-done | bytes 409632 | tf_op jit(solution)/shard_map/ppermute | solution.py:37
  185.6 0.8 copy-done.20
  186.4 2.3 %shard_map.169 = bf16[320,640]{1,0:T(8,128)(2,1)} custom-call(bf16[320,640]{1,0:T(8,128)(2,1)} %get-tuple-element.61.refs_0_, bf16[320,640]{1,0:T(8,128)(2,1)} %copy-done.18, bf16[320,640]{1,0:T(8,128)(2,1)} %copy-done.19, bf16[320,640]{1,0:T(8,128)(2,1)} %copy-done.20, bf16[3,5,3,5120]{3,2,1,0:T(4,128)(2,1)} %shard_map.168.refs_4_), custom_call_target="tpu_custom_call" | custom-call | bytes 2097152 | tf_op jit(solution)/shard_map/pallas_call | solution.py:73
  (98 shorter events, 3.0 us)
Async XLA Ops:
  0.6 48.5 %copy-start = (s32[1,16,5,63]{3,1,2,0:T(8,128)S(1)}, s32[1,16,5,63]{3,1,2,0:T(8,128)}, u32[]{:S(2)}) copy-start(s32[1,16,5,63]{3,1,2,0:T(8,128)} %param.18) | copy-start | bytes 60484
  2.1 43.2 %copy-start.1 = (bf16[2,3,3,40,640]{4,3,2,1,0:T(8,128)(2,1)S(1)}, bf16[2,3,3,40,640]{4,3,2,1,0:T(8,128)(2,1)}, u32[]{:S(2)}) copy-start(bf16[2,3,3,40,640]{4,3,2,1,0:T(8,128)(2,1)} %param.14) | copy-start | bytes 2764804
  2.1 47.1 %copy-start.22 = (s32[5,5,7]{2,1,0:T(8,128)S(1)}, s32[5,5,7]{2,1,0:T(8,128)}, u32[]{:S(2)}) copy-start(s32[5,5,7]{2,1,0:T(8,128)} %constant.194) | copy-start | bytes 2104
  2.1 47.8 %copy-start.28 = (s32[5,3]{0,1:T(4,128)S(1)}, s32[5,3]{0,1:T(4,128)}, u32[]{:S(2)}) copy-start(s32[5,3]{0,1:T(4,128)} %param.17) | copy-start | bytes 184
  2.2 47.9 %copy-start.23 = (s32[5,5]{1,0:T(8,128)S(1)}, s32[5,5]{1,0:T(8,128)}, u32[]{:S(2)}) copy-start(s32[5,5]{1,0:T(8,128)} %constant.193) | copy-start | bytes 304
  3.1 47.3 %copy-start.24 = (s32[384]{0:T(512)S(1)}, s32[384]{0:T(512)}, u32[]{:S(2)}) copy-start(s32[384]{0:T(512)} %constant.178.clone) | copy-start | bytes 4612
  3.1 47.3 %copy-start.25 = (s32[384]{0:T(512)S(1)}, s32[384]{0:T(512)}, u32[]{:S(2)}) copy-start(s32[384]{0:T(512)} %constant.179.clone) | copy-start | bytes 4612
  3.1 47.3 %copy-start.26 = (s32[384]{0:T(512)S(1)}, s32[384]{0:T(512)}, u32[]{:S(2)}) copy-start(s32[384]{0:T(512)} %constant.195) | copy-start | bytes 4612
  3.1 47.3 %copy-start.27 = (pred[384]{0:T(512)(128)(4,1)S(1)}, pred[384]{0:T(512)(128)(4,1)}, u32[]{:S(2)}) copy-start(pred[384]{0:T(512)(128)(4,1)} %constant.182.clone) | copy-start | bytes 1156
  3.1 13.0 %collective-permute-start.3 = (bf16[48,5120]{1,0:T(8,128)(2,1)S(1)}, bf16[48,5120]{1,0:T(8,128)(2,1)S(1)}, u32[]{:S(2)}, u32[]{:S(2)}) collective-permute-start(bf16[48,5120]{1,0:T(8,128)(2,1)S(1)} %get-tuple-element.65), channel_id=1, source_target_pairs={{0,1},{1,0},{2,3},{3,2},{4,5},{5,4},{6,7},{7,6},{8,9},{9,8},{10,11... | collective-permute-start | bytes 1474568 | tf_op jit(solution)/shard_map/ppermute | solution.py:27
  4.9 14.5 %collective-permute-start.2 = (bf16[48,5120]{1,0:T(8,128)(2,1)S(1)}, bf16[48,5120]{1,0:T(8,128)(2,1)S(1)}, u32[]{:S(2)}, u32[]{:S(2)}) collective-permute-start(bf16[48,5120]{1,0:T(8,128)(2,1)S(1)} %get-tuple-element.65), channel_id=1, source_target_pairs={{0,6},{1,7},{2,0},{3,1},{4,2},{5,3},{6,4},{7,5},{8,14},{9,15},{10,... | collective-permute-start | bytes 1474568 | tf_op jit(solution)/shard_map/ppermute | solution.py:27
  7.6 15.3 %collective-permute-start.8 = (bf16[48,5120]{1,0:T(8,128)(2,1)S(1)}, bf16[48,5120]{1,0:T(8,128)(2,1)S(1)}, u32[]{:S(2)}, u32[]{:S(2)}) collective-permute-start(bf16[48,5120]{1,0:T(8,128)(2,1)S(1)} %get-tuple-element.65), channel_id=1, source_target_pairs={{0,2},{1,3},{2,4},{3,5},{4,6},{5,7},{6,0},{7,1},{8,10},{9,11},{10,... | collective-permute-start | bytes 1474568 | tf_op jit(solution)/shard_map/ppermute | solution.py:27
  16.1 15.7 %collective-permute-start.4 = (bf16[48,5120]{1,0:T(8,128)(2,1)S(1)}, bf16[48,5120]{1,0:T(8,128)(2,1)S(1)}, u32[]{:S(2)}, u32[]{:S(2)}) collective-permute-start(bf16[48,5120]{1,0:T(8,128)(2,1)S(1)} %collective-permute-done.3), channel_id=1, source_target_pairs={{0,2},{1,3},{2,4},{3,5},{4,6},{5,7},{6,0},{7,1},{8,10},{9,11},{10,... | collective-permute-start | bytes 1474568 | tf_op jit(solution)/shard_map/ppermute | solution.py:27
  17.7 14.9 %collective-permute-start.9 = (bf16[48,5120]{1,0:T(8,128)(2,1)S(1)}, bf16[48,5120]{1,0:T(8,128)(2,1)S(1)}, u32[]{:S(2)}, u32[]{:S(2)}) collective-permute-start(bf16[48,5120]{1,0:T(8,128)(2,1)S(1)} %collective-permute-done.3), channel_id=1, source_target_pairs={{0,6},{1,7},{2,0},{3,1},{4,2},{5,3},{6,4},{7,5},{8,14},{9,15},{10,... | collective-permute-start | bytes 1474568 | tf_op jit(solution)/shard_map/ppermute | solution.py:27
  19.3 33.4 %copy-start.10 = (bf16[48,5120]{1,0:T(8,128)(2,1)}, bf16[48,5120]{1,0:T(8,128)(2,1)S(1)}, u32[]{:S(2)}) copy-start(bf16[48,5120]{1,0:T(8,128)(2,1)S(1)} %collective-permute-done.2.refs_7_) | copy-start | bytes 1474564
  19.3 20.8 %collective-permute-start.10 = (bf16[48,5120]{1,0:T(8,128)(2,1)S(1)}, bf16[48,5120]{1,0:T(8,128)(2,1)S(1)}, u32[]{:S(2)}, u32[]{:S(2)}) collective-permute-start(bf16[48,5120]{1,0:T(8,128)(2,1)S(1)} %collective-permute-done.2.refs_7_), channel_id=1, source_target_pairs={{0,6},{1,7},{2,0},{3,1},{4,2},{5,3},{6,4},{7,5},{8,14},{9,15},{10,... | collective-permute-start | bytes 1474568 | tf_op jit(solution)/shard_map/ppermute | solution.py:27
  31.8 17.4 %copy-start.11 = (bf16[48,5120]{1,0:T(8,128)(2,1)}, bf16[48,5120]{1,0:T(8,128)(2,1)S(1)}, u32[]{:S(2)}) copy-start(bf16[48,5120]{1,0:T(8,128)(2,1)S(1)} %collective-permute-done.4.refs_8_) | copy-start | bytes 1474564
  31.8 12.8 %collective-permute-start.11 = (bf16[48,5120]{1,0:T(8,128)(2,1)S(1)}, bf16[48,5120]{1,0:T(8,128)(2,1)S(1)}, u32[]{:S(2)}, u32[]{:S(2)}) collective-permute-start(bf16[48,5120]{1,0:T(8,128)(2,1)S(1)} %collective-permute-done.4.refs_8_), channel_id=1, source_target_pairs={{0,2},{1,3},{2,4},{3,5},{4,6},{5,7},{6,0},{7,1},{8,10},{9,11},{10,... | collective-permute-start | bytes 1474568 | tf_op jit(solution)/shard_map/ppermute | solution.py:27
  45.4 52.1 %collective-permute-start.12 = (bf16[384,5120]{1,0:T(8,128)(2,1)}, bf16[384,5120]{1,0:T(8,128)(2,1)}, u32[]{:S(2)}, u32[]{:S(2)}) collective-permute-start(bf16[384,5120]{1,0:T(8,128)(2,1)} %constant_dynamic-update-slice_fusion.refs_1_), channel_id=1, source_target_pairs={{0,8},{8,0},{16,24},{24,16},{32,40},{40,32},{48,56},{56,48},{64,72... | collective-permute-start | bytes 11796488 | tf_op jit(solution)/shard_map/ppermute | solution.py:37
  45.4 7.9 %collective-permute-start = (bf16[2,3,3,40,640]{4,3,2,1,0:T(8,128)(2,1)S(1)}, bf16[2,3,3,40,640]{4,3,2,1,0:T(8,128)(2,1)S(1)}, u32[]{:S(2)}, u32[]{:S(2)}) collective-permute-start(bf16[2,3,3,40,640]{4,3,2,1,0:T(8,128)(2,1)S(1)} %copy-done.1), channel_id=1, source_target_pairs={{0,8},{8,16},{16,24},{24,32},{32,40},{40,48},{48,56},{56,64},{64,7... | collective-permute-start | bytes 2764808 | tf_op jit(solution)/shard_map/ppermute | solution.py:241
  47.8 6.3 %collective-permute-start.1 = (bf16[2,3,3,40,640]{4,3,2,1,0:T(8,128)(2,1)S(1)}, bf16[2,3,3,40,640]{4,3,2,1,0:T(8,128)(2,1)S(1)}, u32[]{:S(2)}, u32[]{:S(2)}) collective-permute-start(bf16[2,3,3,40,640]{4,3,2,1,0:T(8,128)(2,1)S(1)} %copy-done.1), channel_id=1, source_target_pairs={{8,0},{16,8},{24,16},{32,24},{40,32},{48,40},{56,48},{64,56},{72,6... | collective-permute-start | bytes 2764808 | tf_op jit(solution)/shard_map/ppermute | solution.py:242
  53.3 0.9 copy-start.2
  54.2 1.0 copy-start.3
  65.2 30.2 %collective-permute-start.13 = (bf16[384,640]{1,0:T(8,128)(2,1)}, bf16[384,640]{1,0:T(8,128)(2,1)S(1)}, u32[]{:S(2)}, u32[]{:S(2)}) collective-permute-start(bf16[384,640]{1,0:T(8,128)(2,1)} %get-tuple-element.34.refs_0_.refs_3_), channel_id=1, source_target_pairs={{0,8},{8,0},{16,24},{24,16},{32,40},{40,32},{48,56},{56,48},{64,72... | collective-permute-start | bytes 1474568 | tf_op jit(solution)/shard_map/ppermute | solution.py:37
  92.1 28.3 %collective-permute-start.6 = (bf16[48,5120]{1,0:T(8,128)(2,1)}, bf16[48,5120]{1,0:T(8,128)(2,1)S(1)}, u32[]{:S(2)}, u32[]{:S(2)}) collective-permute-start(bf16[48,5120]{1,0:T(8,128)(2,1)} %get-tuple-element.39), channel_id=1, source_target_pairs={{0,2},{1,3},{2,4},{3,5},{4,6},{5,7},{6,0},{7,1},{8,10},{9,11},{10,... | collective-permute-start | bytes 1474568 | tf_op jit(solution)/shard_map/ppermute | solution.py:27
  92.2 29.6 %collective-permute-start.7 = (bf16[48,5120]{1,0:T(8,128)(2,1)}, bf16[48,5120]{1,0:T(8,128)(2,1)S(1)}, u32[]{:S(2)}, u32[]{:S(2)}) collective-permute-start(bf16[48,5120]{1,0:T(8,128)(2,1)} %get-tuple-element.40), channel_id=1, source_target_pairs={{0,6},{1,7},{2,0},{3,1},{4,2},{5,3},{6,4},{7,5},{8,14},{9,15},{10,... | collective-permute-start | bytes 1474568 | tf_op jit(solution)/shard_map/ppermute | solution.py:27
  95.4 31.3 %collective-permute-start.15 = (bf16[48,5120]{1,0:T(8,128)(2,1)}, bf16[48,5120]{1,0:T(8,128)(2,1)S(1)}, u32[]{:S(2)}, u32[]{:S(2)}) collective-permute-start(bf16[48,5120]{1,0:T(8,128)(2,1)} %get-tuple-element.45), channel_id=1, source_target_pairs={{0,6},{1,7},{2,0},{3,1},{4,2},{5,3},{6,4},{7,5},{8,14},{9,15},{10,... | collective-permute-start | bytes 1474568 | tf_op jit(solution)/shard_map/ppermute | solution.py:27
  95.4 2.0 %copy-start.8 = (bf16[384,640]{1,0:T(8,128)(2,1)}, bf16[384,640]{1,0:T(8,128)(2,1)S(1)}, u32[]{:S(2)}) copy-start(bf16[384,640]{1,0:T(8,128)(2,1)S(1)} %collective-permute-done.13.refs_4_) | copy-start | bytes 1474564
  95.4 47.1 %collective-permute-start.5 = (bf16[48,5120]{1,0:T(8,128)(2,1)}, bf16[48,5120]{1,0:T(8,128)(2,1)S(1)}, u32[]{:S(2)}, u32[]{:S(2)}) collective-permute-start(bf16[48,5120]{1,0:T(8,128)(2,1)} %get-tuple-element.36), channel_id=1, source_target_pairs={{0,2},{1,3},{2,4},{3,5},{4,6},{5,7},{6,0},{7,1},{8,10},{9,11},{10,... | collective-permute-start | bytes 1474568 | tf_op jit(solution)/shard_map/ppermute | solution.py:27
  104.2 31.5 %collective-permute-start.17 = (bf16[320,640]{1,0:T(8,128)(2,1)}, bf16[320,640]{1,0:T(8,128)(2,1)S(1)}, u32[]{:S(2)}, u32[]{:S(2)}) collective-permute-start(bf16[320,640]{1,0:T(8,128)(2,1)} %get-tuple-element.41.refs_5_), channel_id=1, source_target_pairs={{0,32},{8,40},{16,48},{24,56},{32,64},{40,72},{48,80},{56,88},{64,... | collective-permute-start | bytes 1228808 | tf_op jit(solution)/shard_map/ppermute | solution.py:37
  120.4 1.4 copy-start.6
  120.4 16.6 %collective-permute-start.18 = (bf16[320,640]{1,0:T(8,128)(2,1)}, bf16[320,640]{1,0:T(8,128)(2,1)}, u32[]{:S(2)}, u32[]{:S(2)}) collective-permute-start(bf16[320,640]{1,0:T(8,128)(2,1)} %get-tuple-element.49), channel_id=1, source_target_pairs={{0,96},{8,104},{16,112},{24,120},{32,0},{40,8},{48,16},{56,24},{64... | collective-permute-start | bytes 1228808 | tf_op jit(solution)/shard_map/ppermute | solution.py:37
  121.7 0.8 copy-start.7
  125.1 27.0 %collective-permute-start.16 = (bf16[48,5120]{1,0:T(8,128)(2,1)}, bf16[48,5120]{1,0:T(8,128)(2,1)S(1)}, u32[]{:S(2)}, u32[]{:S(2)}) collective-permute-start(bf16[48,5120]{1,0:T(8,128)(2,1)} %get-tuple-element.46.refs_7_), channel_id=1, source_target_pairs={{0,2},{1,3},{2,4},{3,5},{4,6},{5,7},{6,0},{7,1},{8,10},{9,11},{10,... | collective-permute-start | bytes 1474568 | tf_op jit(solution)/shard_map/ppermute | solution.py:27
  126.6 9.0 %copy-start.12 = (bf16[48,5120]{1,0:T(8,128)(2,1)}, bf16[48,5120]{1,0:T(8,128)(2,1)S(1)}, u32[]{:S(2)}) copy-start(bf16[48,5120]{1,0:T(8,128)(2,1)S(1)} %collective-permute-done.15.refs_1_) | copy-start | bytes 1474564
  126.7 24.0 %collective-permute-start.24 = (bf16[320,640]{1,0:T(8,128)(2,1)}, bf16[320,640]{1,0:T(8,128)(2,1)S(1)}, u32[]{:S(2)}, u32[]{:S(2)}) collective-permute-start(bf16[320,640]{1,0:T(8,128)(2,1)} %get-tuple-element.58), channel_id=1, source_target_pairs={{0,96},{8,104},{16,112},{24,120},{32,0},{40,8},{48,16},{56,24},{64... | collective-permute-start | bytes 1228808 | tf_op jit(solution)/shard_map/ppermute | solution.py:37
  135.7 1.3 copy-start.17
  135.7 23.4 %collective-permute-start.20 = (bf16[2,360,384]{2,1,0:T(8,128)(2,1)}, bf16[2,360,384]{2,1,0:T(8,128)(2,1)S(1)}, u32[]{:S(2)}, u32[]{:S(2)}) collective-permute-start(bf16[2,360,384]{2,1,0:T(8,128)(2,1)} %get-tuple-element.50.refs_4_), channel_id=1, source_target_pairs={{8,0},{16,8},{24,16},{32,24},{40,32},{48,40},{56,48},{64,56},{72,6... | collective-permute-start | bytes 1658888 | tf_op jit(solution)/shard_map/ppermute | solution.py:385
  137.0 27.2 %collective-permute-start.21 = (bf16[2,360,384]{2,1,0:T(8,128)(2,1)}, bf16[2,360,384]{2,1,0:T(8,128)(2,1)S(1)}, u32[]{:S(2)}, u32[]{:S(2)}) collective-permute-start(bf16[2,360,384]{2,1,0:T(8,128)(2,1)} %get-tuple-element.54), channel_id=1, source_target_pairs={{0,8},{8,16},{16,24},{24,32},{32,40},{40,48},{48,56},{56,64},{64,7... | collective-permute-start | bytes 1658888 | tf_op jit(solution)/shard_map/ppermute | solution.py:386
  142.5 8.2 %copy-start.9 = (bf16[48,5120]{1,0:T(8,128)(2,1)}, bf16[48,5120]{1,0:T(8,128)(2,1)S(1)}, u32[]{:S(2)}) copy-start(bf16[48,5120]{1,0:T(8,128)(2,1)S(1)} %collective-permute-done.5.refs_1_) | copy-start | bytes 1474564
  142.5 19.1 %collective-permute-start.25 = (bf16[320,640]{1,0:T(8,128)(2,1)}, bf16[320,640]{1,0:T(8,128)(2,1)}, u32[]{:S(2)}, u32[]{:S(2)}) collective-permute-start(bf16[320,640]{1,0:T(8,128)(2,1)} %get-tuple-element.51.refs_7_), channel_id=1, source_target_pairs={{0,32},{8,40},{16,48},{24,56},{32,64},{40,72},{48,80},{56,88},{64,... | collective-permute-start | bytes 1228808 | tf_op jit(solution)/shard_map/ppermute | solution.py:37
  150.6 19.8 %copy-start.21 = (bf16[360,256]{1,0:T(8,128)(2,1)S(1)}, bf16[360,256]{1,0:T(8,128)(2,1)}, u32[]{:S(2)}) copy-start(bf16[360,256]{1,0:T(8,128)(2,1)} %get-tuple-element.60) | copy-start | bytes 552964
  150.7 11.4 %copy-start.16 = (bf16[320,640]{1,0:T(8,128)(2,1)}, bf16[320,640]{1,0:T(8,128)(2,1)S(1)}, u32[]{:S(2)}) copy-start(bf16[320,640]{1,0:T(8,128)(2,1)S(1)} %collective-permute-done.24.refs_1_) | copy-start | bytes 1228804
  150.7 15.8 %collective-permute-start.22 = (bf16[2,360,256]{2,1,0:T(8,128)(2,1)}, bf16[2,360,256]{2,1,0:T(8,128)(2,1)}, u32[]{:S(2)}, u32[]{:S(2)}) collective-permute-start(bf16[2,360,256]{2,1,0:T(8,128)(2,1)} %get-tuple-element.52.refs_3_), channel_id=1, source_target_pairs={{8,0},{16,8},{24,16},{32,24},{40,32},{48,40},{56,48},{64,56},{72,6... | collective-permute-start | bytes 1105928 | tf_op jit(solution)/shard_map/ppermute | solution.py:385
  152.1 4.7 %copy-start.13 = (bf16[48,5120]{1,0:T(8,128)(2,1)}, bf16[48,5120]{1,0:T(8,128)(2,1)S(1)}, u32[]{:S(2)}) copy-start(bf16[48,5120]{1,0:T(8,128)(2,1)S(1)} %collective-permute-done.16.refs_2_) | copy-start | bytes 1474564
  152.1 15.3 %collective-permute-start.23 = (bf16[2,360,256]{2,1,0:T(8,128)(2,1)}, bf16[2,360,256]{2,1,0:T(8,128)(2,1)}, u32[]{:S(2)}, u32[]{:S(2)}) collective-permute-start(bf16[2,360,256]{2,1,0:T(8,128)(2,1)} %get-tuple-element.56), channel_id=1, source_target_pairs={{0,8},{8,16},{16,24},{24,32},{32,40},{40,48},{48,56},{56,64},{64,7... | collective-permute-start | bytes 1105928 | tf_op jit(solution)/shard_map/ppermute | solution.py:386
  159.1 13.1 %copy-start.4 = (bf16[2,360,384]{2,1,0:T(8,128)(2,1)}, bf16[2,360,384]{2,1,0:T(8,128)(2,1)S(1)}, u32[]{:S(2)}) copy-start(bf16[2,360,384]{2,1,0:T(8,128)(2,1)S(1)} %collective-permute-done.20.refs_1_) | copy-start | bytes 1658884
  159.1 16.3 %collective-permute-start.14 = (bf16[48,5120]{1,0:T(8,128)(2,1)}, bf16[48,5120]{1,0:T(8,128)(2,1)S(1)}, u32[]{:S(2)}, u32[]{:S(2)}) collective-permute-start(bf16[48,5120]{1,0:T(8,128)(2,1)} %get-tuple-element.43), channel_id=1, source_target_pairs={{0,6},{1,7},{2,0},{3,1},{4,2},{5,3},{6,4},{7,5},{8,14},{9,15},{10,... | collective-permute-start | bytes 1474568 | tf_op jit(solution)/shard_map/ppermute | solution.py:27
  161.6 13.9 %collective-permute-start.19 = (bf16[48,5120]{1,0:T(8,128)(2,1)}, bf16[48,5120]{1,0:T(8,128)(2,1)S(1)}, u32[]{:S(2)}, u32[]{:S(2)}) collective-permute-start(bf16[48,5120]{1,0:T(8,128)(2,1)} %shard_map.165.refs_3_), channel_id=1, source_target_pairs={{0,1},{1,0},{2,3},{3,2},{4,5},{5,4},{6,7},{7,6},{8,9},{9,8},{10,11... | collective-permute-start | bytes 1474568 | tf_op jit(solution)/shard_map/ppermute | solution.py:27
  164.2 8.0 %copy-start.5 = (bf16[2,360,384]{2,1,0:T(8,128)(2,1)}, bf16[2,360,384]{2,1,0:T(8,128)(2,1)S(1)}, u32[]{:S(2)}) copy-start(bf16[2,360,384]{2,1,0:T(8,128)(2,1)S(1)} %collective-permute-done.21.refs_2_) | copy-start | bytes 1658884
  164.2 15.6 %collective-permute-start.26 = (bf16[320,640]{1,0:T(8,128)(2,1)}, bf16[320,640]{1,0:T(8,128)(2,1)S(1)}, u32[]{:S(2)}, u32[]{:S(2)}) collective-permute-start(bf16[320,640]{1,0:T(8,128)(2,1)} %get-tuple-element.62), channel_id=1, source_target_pairs={{0,32},{8,40},{16,48},{24,56},{32,64},{40,72},{48,80},{56,88},{64,... | collective-permute-start | bytes 1228808 | tf_op jit(solution)/shard_map/ppermute | solution.py:37
  166.5 13.3 %collective-permute-start.27 = (bf16[320,640]{1,0:T(8,128)(2,1)}, bf16[320,640]{1,0:T(8,128)(2,1)S(1)}, u32[]{:S(2)}, u32[]{:S(2)}) collective-permute-start(bf16[320,640]{1,0:T(8,128)(2,1)} %get-tuple-element.63), channel_id=1, source_target_pairs={{0,96},{8,104},{16,112},{24,120},{32,0},{40,8},{48,16},{56,24},{64... | collective-permute-start | bytes 1228808 | tf_op jit(solution)/shard_map/ppermute | solution.py:37
  167.5 18.1 %collective-permute-start.28 = (bf16[320,640]{1,0:T(8,128)(2,1)}, bf16[320,640]{1,0:T(8,128)(2,1)S(1)}, u32[]{:S(2)}, u32[]{:S(2)}) collective-permute-start(bf16[320,640]{1,0:T(8,128)(2,1)} %shard_map.166.refs_6_), channel_id=1, source_target_pairs={{0,16},{8,24},{16,0},{24,8},{32,48},{40,56},{48,32},{56,40},{64,80... | collective-permute-start | bytes 1228808 | tf_op jit(solution)/shard_map/ppermute | solution.py:37
  175.5 0.8 copy-start.14
  176.3 0.8 copy-start.15
  179.8 5.8 %copy-start.18 = (bf16[320,640]{1,0:T(8,128)(2,1)}, bf16[320,640]{1,0:T(8,128)(2,1)S(1)}, u32[]{:S(2)}) copy-start(bf16[320,640]{1,0:T(8,128)(2,1)S(1)} %collective-permute-done.26.refs_1_) | copy-start | bytes 1228804
  179.8 5.8 %copy-start.19 = (bf16[320,640]{1,0:T(8,128)(2,1)}, bf16[320,640]{1,0:T(8,128)(2,1)S(1)}, u32[]{:S(2)}) copy-start(bf16[320,640]{1,0:T(8,128)(2,1)S(1)} %collective-permute-done.27.refs_2_) | copy-start | bytes 1228804
  185.6 0.8 copy-start.20

commit v2 on v1

--- a/solution.py
+++ b/solution.py
@@ -58,6 +58,7 @@
     return jnp.concatenate([own, c10, c30, c01, c31, c11, c20, c21], axis=0), [c10, c31]
 
 
+ROOM = 24 << 20
 ANYWHERE = pl.BlockSpec(memory_space=pl.ANY)
 
 
@@ -77,17 +78,9 @@
         out_specs=out_specs,
         out_shape=[jax.ShapeDtypeStruct(shape, kind) for shape, kind in outs],
         scratch_shapes=scratch,
+        compiler_params=pltpu.CompilerParams(vmem_limit_bytes=ROOM),
         cost_estimate=pl.CostEstimate(flops=flops, transcendentals=0, bytes_accessed=moved),
     )(*args, *after)
-
-
-def sum_kernel(*refs):
-    refs[-1][...] = added(*[r[...] for r in refs[:-1]]).astype(BF16)
-
-
-def relay_kernel(a_ref, b_ref, came_a_ref, came_b_ref, out_a_ref, out_b_ref):
-    out_a_ref[...] = added(a_ref[...], came_a_ref[...]).astype(BF16)
-    out_b_ref[...] = added(b_ref[...], came_b_ref[...]).astype(BF16)
 
 
 def mixed_kernel(*refs):
@@ -158,15 +151,21 @@
     gq_ref[...] = gq.T.astype(BF16)
 
 
-def weight_kernel(order_ref, g_ref, far_g_ref, att_ref, far_att_ref, *outs):
+def weight_kernel(order_ref, *refs):
+    parts, (att_ref, far_att_ref), outs = refs[:6], refs[6:8], refs[8:]
     attended = jnp.concatenate([att_ref[...], far_att_ref[...]], axis=0)
-    first = order_ref[len(outs)] == 0
-    width = 2 * outs[0].shape[0]
+    turned = [jnp.concatenate([p[...].T for p in parts[3 * i : 3 * i + 3]], axis=0) for i in range(2)]
+    turned = jnp.concatenate(turned, axis=1)
+    rows = outs[0].shape[0]
+    extra = turned.shape[0] - rows
+    turned = jnp.where(order_ref[len(outs)] == 0, turned[:rows], turned[extra:])
+    grad = dot(turned, attended, ((1,), (0,))).astype(BF16)
+    step = pl.program_id(0)
     for i, out_ref in enumerate(outs):
-        columns = pl.ds(pl.multiple_of(order_ref[i] * width, width), width)
-        g = jnp.concatenate([g_ref[:, columns], far_g_ref[:, columns]], axis=0)
-        g = jnp.where(first, g[:, : width // 2], g[:, width // 2 :])
-        out_ref[...] = dot(g, attended, ((0,), (0,))).astype(BF16)
+
+        @pl.when(step == i)
+        def _(out_ref=out_ref):
+            out_ref[...] = grad
 
 
 def project_kernel(att_ref, w_ref, *outs):
@@ -191,15 +190,6 @@
     @pl.when(step == pl.num_programs(0) - 1)
     def _():
         ga_ref[...] = total_ref[...].astype(BF16)
-
-
-def total_kernel(*refs):
-    out_ref = refs[-1]
-    start = 0
-    for i in range(0, len(refs) - 1, 3):
-        part = added(refs[i][...], refs[i + 1][...], refs[i + 2][...]).astype(BF16)
-        out_ref[:, :, start : start + part.shape[2]] = part
-        start += part.shape[2]
 
 
 def mask_bias(window, own_mask, seq_place, row_tiles):
@@ -270,6 +260,11 @@
 
     q_spec = pl.BlockSpec((tokens, HEAD_DIM), lambda h: (0, h))
     kv_spec = pl.BlockSpec((2, tokens, HEAD_DIM), lambda h: (0, 0, h))
+    weights = ((2, 1), (2, 0), (1, 0), (3, 1), (1, 1), (3, 0), (0, 1), (0, 0))
+    ring, pair = (np.array([w[i] for w in weights], np.int32) for i in range(2))
+    chips = (spot_z + ring) % 4 * 2 + (spot_y + pair) % 2
+    order = jnp.concatenate([chips, core]).astype(jnp.int32)
+
     pairs = heads * tokens * 3 * tokens
     probs, attended = kernel(
         forward_kernel,
@@ -289,7 +284,7 @@
             pl.BlockSpec((slots, HEAD_DIM), lambda h: (0, h)),
         ],
         grid=(heads,),
-        after=last_hops,
+        after=[*last_hops, perm_back, order],
         flops=pairs * 1500,
         moved=8 << 20,
     )
@@ -312,24 +307,32 @@
     mixed_near = hop(tensor_shift, (mixed[1, 0], mixed[3, 1]))
 
     narrow = model_width // row_tiles
-
-    def weight_blocks(blocks, after):
-        chips = [(spot_z + d) % 4 * 2 + (spot_y + e) % 2 for d, e in blocks]
-        order = jnp.stack([*chips, core[0]]).astype(jnp.int32)
-        return kernel(
-            weight_kernel,
-            [((narrow, channels), BF16)] * len(blocks),
-            [order, all_grad, far_grad, attended, far_attended],
-            [SCALAR] + [VECTOR] * 4,
-            after=after,
-            flops=slots * model_width * channels * 2,
-            moved=6 << 20,
-        )
-
-    w21, w20, w10, w31 = weight_blocks([(2, 1), (2, 0), (1, 0), (3, 1)], [mixed[0, 0]])
-    weight_far = hop(seq_shift, (w21, w20))
-    weight_near = hop(seq_shift, (w10, w31))
-    w11, w30, w01, w00 = weight_blocks([(1, 1), (3, 0), (0, 1), (0, 0)], [w21])
+    lanes = 128
+    window_specs = [
+        pl.BlockSpec((slots, lanes), lambda i, o, j=j: (0, o[i] * (2 * narrow // lanes) + 2 * o[8] + j))
+        for j in range(3)
+    ]
+
+    def constant(shape):
+        return pl.BlockSpec(shape, lambda i, o: (0, 0))
+
+    weight = pl.pallas_call(
+        weight_kernel,
+        grid_spec=pltpu.PrefetchScalarGridSpec(
+            num_scalar_prefetch=1,
+            grid=(8,),
+            in_specs=[*window_specs, *window_specs, *[constant((slots, channels))] * 2],
+            out_specs=[constant((narrow, channels))] * 8,
+        ),
+        out_shape=[jax.ShapeDtypeStruct((narrow, channels), BF16)] * 8,
+        compiler_params=pltpu.CompilerParams(vmem_limit_bytes=ROOM),
+        cost_estimate=pl.CostEstimate(
+            flops=slots * model_width * channels * 2, transcendentals=0, bytes_accessed=9 << 20
+        ),
+    )(order, *[all_grad] * 3, *[far_grad] * 3, attended, far_attended)
+    weight = dict(zip(weights, weight))
+    weight_far = hop(seq_shift, (weight[2, 1], weight[2, 0]))
+    weight_near = hop(seq_shift, (weight[1, 0], weight[3, 1]))
 
     (grad_attn,) = kernel(
         attn_grad_kernel,
@@ -341,89 +344,55 @@
         ],
         [whole((slots, channels))],
         grid=(4,),
-        after=[w11],
+        after=[weight[0, 0]],
         flops=slots * model_width * channels * 3,
         moved=12 << 20,
         scratch=[pltpu.VMEM((slots, channels), F32)],
     )
 
-    def differentiate(first, count, after):
-        def spec(shape, at):
-            def index(h):
-                return tuple(h + first if i == at else 0 for i in range(len(shape)))
-
-            return pl.BlockSpec(shape, index)
-
-        width = count * HEAD_DIM
-        kv_in = spec((2, tokens, HEAD_DIM), 2)
-        return kernel(
-            backward_kernel,
-            [
-                ((tokens, width), BF16),
-                ((2, tokens, width), F32),
-                ((2, tokens, width), BF16),
-                ((2, tokens, width), BF16),
-            ],
-            [flat_q, *flat, probs, grad_attn, perm_back],
-            [
-                spec((tokens, HEAD_DIM), 1),
-                kv_in,
-                kv_in,
-                kv_in,
-                spec((1, 3, tokens, tokens), 0),
-                spec((slots, HEAD_DIM), 1),
-                whole((tokens, slots)),
-            ],
-            [q_spec, kv_spec, kv_spec, kv_spec],
-            grid=(count,),
-            after=after,
-            flops=pairs * 2000 * count // heads,
-            moved=2 * count << 20,
-        )
-
-    def send_halo(grad_up, grad_down):
-        from_below = lax.ppermute(grad_up, "seq", back)
-        from_above = lax.ppermute(grad_down, "seq", onward)
-        return from_below, from_above
-
-    def summed(body, shapes, terms, after):
-        return kernel(body, [(shape, BF16) for shape in shapes], terms, after=after, moved=2 << 20)
-
-    split = (heads + 1) // 2
-    mixed_sums = summed(
-        relay_kernel, [own_grad.shape] * 2, [mixed[1, 1], mixed[3, 0], *mixed_far], [grad_attn]
-    )
-    mark = mixed_sums[0]
-    mixed_sums = hop(tensor_shift, mixed_sums)
-    gq_a, own_a, up_a, down_a = differentiate(0, split, [mark])
-    below_a, above_a = send_halo(up_a, down_a)
-    weight_sums = summed(relay_kernel, [w00.shape] * 2, [w11, w30, *weight_far], [up_a])
-    mark = weight_sums[0]
-    weight_sums = hop(seq_shift, weight_sums)
-    gq_b, own_b, up_b, down_b = differentiate(split, heads - split, [mark])
-    below_b, above_b = send_halo(up_b, down_b)
-    (side,) = summed(
-        sum_kernel, [own_grad.shape], [mixed[0, 1], mixed_near[1], mixed_sums[0]], [up_b]
-    )
-    mixed_side = tensor_shift(side, 0, 1)
-    (side,) = summed(sum_kernel, [w00.shape], [w01, weight_near[1], weight_sums[0]], [side])
-    weight_side = seq_shift(side, 0, 1)
-    (grad_kv,) = summed(
-        total_kernel,
-        [(2, tokens, channels)],
-        [own_a, below_a, above_a, own_b, below_b, above_b],
-        [side],
-    )
-    (layer_out,) = summed(
+    wide = ((2, tokens, channels), BF16)
+    grad_q, grad_own, grad_up, grad_down = kernel(
+        backward_kernel,
+        [((tokens, channels), BF16), (wide[0], F32), wide, wide],
+        [flat_q, *flat, probs, grad_attn, perm_back],
+        [
+            q_spec,
+            kv_spec,
+            kv_spec,
+            kv_spec,
+            pl.BlockSpec((1, 3, tokens, tokens), lambda h: (h, 0, 0, 0)),
+            pl.BlockSpec((slots, HEAD_DIM), lambda h: (0, h)),
+            whole((tokens, slots)),
+        ],
+        [q_spec, kv_spec, kv_spec, kv_spec],
+        grid=(heads,),
+        flops=pairs * 2000,
+        moved=12 << 20,
+    )
+
+    def relayed(kept, came, shift):
+        sums = [added(k, c).astype(BF16) for k, c in zip(kept, came)]
+        return hop(shift, sums)
+
+    def side(shift, *terms):
+        total = added(*terms).astype(BF16)
+        return shift(total, 0, 1)
+
+    mixed_sums = relayed((mixed[1, 1], mixed[3, 0]), mixed_far, tensor_shift)
+    weight_sums = relayed((weight[1, 1], weight[3, 0]), weight_far, seq_shift)
+    mixed_side = side(tensor_shift, mixed[0, 1], mixed_near[1], mixed_sums[0])
+    weight_side = side(seq_shift, weight[0, 1], weight_near[1], weight_sums[0])
+    from_below = lax.ppermute(grad_up, "seq", back)
+    from_above = lax.ppermute(grad_down, "seq", onward)
+
+    (layer_out,) = kernel(
         mixed_kernel,
-        [(frames, local_columns, tile_rows, model_width)],
+        [((frames, local_columns, tile_rows, model_width), BF16)],
         [mixed[0, 0], mixed_near[0], mixed_sums[1], mixed_side],
-        [grad_kv],
-    )
-    (grad_weight,) = summed(
-        sum_kernel, [w00.shape], [w00, weight_near[0], weight_sums[1], weight_side], [layer_out]
-    )
-    grad_q = jnp.concatenate([gq_a, gq_b], axis=1)
+        moved=3 << 20,
+    )
+    grad_weight = added(weight[0, 0], weight_near[0], weight_sums[1], weight_side).astype(BF16)
+    grad_kv = added(grad_own, from_below, from_above).astype(BF16)
     return (
         layer_out.transpose(0, 2, 1, 3),
         grad_q.reshape(queries.shape),

time: 191 us -> 175 us (0.916)
  waiting for transfers between devices: 33.8 us -> 75.4 us
  Pallas kernels: 70.1 us -> 39 us
  starting transfers between devices: 64 us -> 39.8 us
  local copies, waits for them, and re-layouts: 14.8 us -> 10.1 us
  other arithmetic: 4.94 us -> 7.72 us
    pallas_call x14 -> x5, Pallas kernels: 70.1 us -> 30.6 us  [kernel(): pl.pallas_call(run, grid=grid, in_specs=[*specs, *[ANYWHERE] * len(after)...]
    ppermute x14, waiting for transfers between devices: 26.5 us -> 51.3 us  [tensor_shift(): return lax.ppermute(value, 'tensor', pairs)]
    ppermute x9, waiting for transfers between devices: 5.83 us -> 24.1 us  [seq_shift(): return lax.ppermute(value, 'seq', pairs)]
    ppermute x9, starting transfers between devices: 30.9 us -> 16.4 us  [seq_shift(): return lax.ppermute(value, 'seq', pairs)]
    pallas_call x0 -> x1, Pallas kernels: none -> 8.4 us  [layer(): pl.pallas_call(weight_kernel, grid_spec=pltpu.PrefetchScalarGridSpec(num_...]
    ppermute x4 -> x2, starting transfers between devices: 10.5 us -> 4.37 us  [the longest x1 3.09 us: layer(): from_above = lax.ppermute(grad_down, 'seq', onward)]
    unnamed x65 -> x19, local copies, waits for them, and re-layouts: 10.1 us -> 6.8 us
    ppermute x14, starting transfers between devices: 19 us -> 16.4 us  [tensor_shift(): return lax.ppermute(value, 'tensor', pairs)]
  transfers between devices with their start and end apart: 29 -> 27, of which waited for: 8 -> 10; matrix products, arithmetic and copies ran while one was open for 6% -> 8% of each run, Pallas kernels for 36% -> 23%
where the time goes in v2:
time: 175 us; the launch traced here: 173 us
  waiting for transfers between devices  75.4 us (43%)
  starting transfers between devices  39.8 us (23%)
  Pallas kernels  39 us (22%)
  local copies, waits for them, and re-layouts  10.1 us (6%)
  other arithmetic  7.72 us (4%)
    ppermute x14, waiting for transfers between devices, tensor_shift(): return lax.ppermute(value, 'tensor', pairs)  51.3 us
    pallas_call x5, Pallas kernels, kernel(): pl.pallas_call(run, grid=grid, in_specs=[*specs, *[ANYWHERE] * len(after)...  30.6 us
    ppermute x9, waiting for transfers between devices, seq_shift(): return lax.ppermute(value, 'seq', pairs)  24.1 us
    ppermute x9, starting transfers between devices, seq_shift(): return lax.ppermute(value, 'seq', pairs)  16.4 us
    ppermute x14, starting transfers between devices, tensor_shift(): return lax.ppermute(value, 'tensor', pairs)  16.4 us
    pallas_call x1, Pallas kernels, layer(): pl.pallas_call(weight_kernel, grid_spec=pltpu.PrefetchScalarGridSpec(num_...  8.4 us
    unnamed x19, local copies, waits for them, and re-layouts  6.8 us
  transfers between devices with their start and end apart: 27, of which 10 were waited for; matrix products, arithmetic and copies ran while one was open for 8% of the time, Pallas kernels for 23%

profile of v2, /device:TPU:0, one launch (start us, length us, event | category | flops | bytes accessed | tf_op | source)
XLA Modules:
  0.0 173.2 jit_solution(3234420391261696956)
XLA Ops:
  0.6 1.5 reshape.164
  2.1 0.8 constant_dynamic-update-slice_fusion.7
  3.0 1.7 collective-permute-start.3
  4.7 2.8 %collective-permute-start.2 = (bf16[48,5120]{1,0:T(8,128)(2,1)S(1)}, bf16[48,5120]{1,0:T(8,128)(2,1)S(1)}, u32[]{:S(2)}, u32[]{:S(2)}) collective-permute-start(bf16[48,5120]{1,0:T(8,128)(2,1)S(1)} %get-tuple-element.49), channel_id=1, source_target_pairs={{0,6},{1,7},{2,0},{3,1},{4,2},{5,3},{6,4},{7,5},{8,14},{9,15},{10,... | collective-permute-start | bytes 1474568 | tf_op jit(solution)/shard_map/ppermute | solution.py:27
  7.4 1.3 collective-permute-start
  8.8 1.3 collective-permute-start.1
  10.1 0.1 collective-permute-start.12
  10.2 0.8 slice_bitcast_fusion.2
  11.0 0.7 compare_bitcast_fusion
  11.7 0.1 reshape_reshape.3
  11.8 1.2 multiply_reduce_fusion
  13.0 0.1 copy.21
  13.2 0.8 broadcast_compare_fusion.1
  14.0 0.1 and_select_fusion
  14.1 0.7 fusion.17
  14.8 0.7 fusion.9
  15.6 0.1 fusion.3.refs_5_
  15.8 1.2 collective-permute-done.3
  17.1 1.6 collective-permute-start.4
  18.7 2.6 %collective-permute-start.13 = (bf16[48,5120]{1,0:T(8,128)(2,1)S(1)}, bf16[48,5120]{1,0:T(8,128)(2,1)S(1)}, u32[]{:S(2)}, u32[]{:S(2)}) collective-permute-start(bf16[48,5120]{1,0:T(8,128)(2,1)S(1)} %collective-permute-done.3), channel_id=1, source_target_pairs={{0,6},{1,7},{2,0},{3,1},{4,2},{5,3},{6,4},{7,5},{8,14},{9,15},{10,... | collective-permute-start | bytes 1474568 | tf_op jit(solution)/shard_map/ppermute | solution.py:27
  21.3 0.8 constant_dynamic-update-slice_fusion.6
  22.1 0.2 collective-permute-done.12
  22.3 0.5 collective-permute-start.14
  22.8 1.9 %constant_dynamic-update-slice_fusion.5 = bf16[384,5120]{1,0:T(8,128)(2,1)} fusion(bf16[384,5120]{1,0:T(8,128)(2,1)} %constant_dynamic-update-slice_fusion.6, bf16[48,5120]{1,0:T(8,128)(2,1)} %collective-permute-done.12), kind=kLoop, calls=%fused_computation.23 | loop fusion | bytes 983040
  24.7 0.8 constant_dynamic-update-slice_fusion.4
  25.5 7.3 %collective-permute-done.4.refs_8_ = bf16[48,5120]{1,0:T(8,128)(2,1)S(1)} collective-permute-done((bf16[48,5120]{1,0:T(8,128)(2,1)S(1)}, bf16[48,5120]{1,0:T(8,128)(2,1)S(1)}, u32[]{:S(2)}, u32[]{:S(2)}) %collective-permute-start.4) | collective-permute-done | bytes 491552 | tf_op jit(solution)/shard_map/ppermute | solution.py:27
  32.7 0.8 constant_dynamic-update-slice_fusion.3
  33.6 0.8 constant_dynamic-update-slice_fusion.2
  34.4 8.3 %collective-permute-done.14 = bf16[48,5120]{1,0:T(8,128)(2,1)S(1)} collective-permute-done((bf16[48,5120]{1,0:T(8,128)(2,1)S(1)}, bf16[48,5120]{1,0:T(8,128)(2,1)S(1)}, u32[]{:S(2)}, u32[]{:S(2)}) %collective-permute-start.14) | collective-permute-done | bytes 491552 | tf_op jit(solution)/shard_map/ppermute | solution.py:27
  42.7 0.8 constant_dynamic-update-slice_fusion.1
  43.5 2.5 %collective-permute-done.15 = bf16[48,5120]{1,0:T(8,128)(2,1)S(1)} collective-permute-done((bf16[48,5120]{1,0:T(8,128)(2,1)S(1)}, bf16[48,5120]{1,0:T(8,128)(2,1)S(1)}, u32[]{:S(2)}, u32[]{:S(2)}) %collective-permute-start.15) | collective-permute-done | bytes 491552 | tf_op jit(solution)/shard_map/ppermute | solution.py:27
  45.9 0.8 constant_dynamic-update-slice_fusion.refs_0_.refs_1_.refs_2_
  46.8 1.9 %collective-permute-start.16 = (bf16[384,5120]{1,0:T(8,128)(2,1)}, bf16[384,5120]{1,0:T(8,128)(2,1)S(1)}, u32[]{:S(2)}, u32[]{:S(2)}) collective-permute-start(bf16[384,5120]{1,0:T(8,128)(2,1)} %constant_dynamic-update-slice_fusion.refs_0_.refs_1_.refs_2_), channel_id=1, source_target_pairs={{0,8},{8,0},{16,24},{24,16},{32,40},{40,32},{48,56},{56,48},{64,72... | collective-permute-start | bytes 11796488 | tf_op jit(solution)/shard_map/ppermute | solution.py:37
  48.7 0.1 pad_add_fusion.refs_10_.order_ref
  48.8 0.1 fusion.refs_6_
  49.0 8.5 %shard_map.174 = (bf16[5,3,360,360]{3,2,1,0:T(8,128)(2,1)S(1)}, bf16[384,640]{1,0:T(8,128)(2,1)S(1)}) custom-call(bf16[360,640]{1,0:T(8,128)(2,1)S(1)} %bitcast.31, bf16[2,360,640]{2,1,0:T(8,128)(2,1)S(1)} %bitcast.25, bf16[2,360,640]{2,1,0:T(8,128)(2,1)S(1)} %bitcast.27, bf16[2,360,640]{2,1,0:T(8,128)(2,1)S(1)} %bitcast.29, ...), custom_call_target="tpu_custom_call" | custom-call | flops 2916000000 | bytes 8388608 | tf_op jit(solution)/shard_map/pallas_call | solution.py:74
  57.5 4.6 %shard_map.175 = (bf16[48,5120]{1,0:T(8,128)(2,1)S(1)}, bf16[48,5120]{1,0:T(8,128)(2,1)S(1)}, bf16[48,5120]{1,0:T(8,128)(2,1)S(1)}, bf16[48,5120]{1,0:T(8,128)(2...) custom-call(bf16[384,640]{1,0:T(8,128)(2,1)S(1)} %get-tuple-element., ...), custom_call_target="tpu_custom_call" | custom-call | flops 3774873600 | bytes 12582912 | tf_op jit(solution)/shard_map/pallas_call | solution.py:74
  62.2 0.1 collective-permute-start.17
  62.3 3.1 %collective-permute-start.8 = (bf16[48,5120]{1,0:T(8,128)(2,1)S(1)}, bf16[48,5120]{1,0:T(8,128)(2,1)S(1)}, u32[]{:S(2)}, u32[]{:S(2)}) collective-permute-start(bf16[48,5120]{1,0:T(8,128)(2,1)S(1)} %get-tuple-element.32), channel_id=1, source_target_pairs={{0,6},{1,7},{2,0},{3,1},{4,2},{5,3},{6,4},{7,5},{8,14},{9,15},{10,... | collective-permute-start | bytes 1474568 | tf_op jit(solution)/shard_map/ppermute | solution.py:27
  65.4 11.1 %collective-permute-done.9 = bf16[48,5120]{1,0:T(8,128)(2,1)S(1)} collective-permute-done((bf16[48,5120]{1,0:T(8,128)(2,1)S(1)}, bf16[48,5120]{1,0:T(8,128)(2,1)S(1)}, u32[]{:S(2)}, u32[]{:S(2)}) %collective-permute-start.9) | collective-permute-done | bytes 491552 | tf_op jit(solution)/shard_map/ppermute | solution.py:27
  76.5 0.1 add_convert_fusion.2
  76.7 10.4 %collective-permute-done.6 = bf16[48,5120]{1,0:T(8,128)(2,1)S(1)} collective-permute-done((bf16[48,5120]{1,0:T(8,128)(2,1)S(1)}, bf16[48,5120]{1,0:T(8,128)(2,1)S(1)}, u32[]{:S(2)}, u32[]{:S(2)}) %collective-permute-start.6) | collective-permute-done | bytes 491552 | tf_op jit(solution)/shard_map/ppermute | solution.py:27
  87.1 0.1 add_convert_fusion.3
  87.2 8.4 %shard_map.177 = (bf16[320,640]{1,0:T(8,128)(2,1)S(1)}, bf16[320,640]{1,0:T(8,128)(2,1)S(1)}, bf16[320,640]{1,0:T(8,128)(2,1)S(1)}, bf16[320,640]{1,0:T(8,128)(2...) custom-call(s32[9]{0:T(128)S(1)} %pad_add_fusion.refs_10_.order_ref,, ...), custom_call_target="tpu_custom_call" | custom-call | flops 2516582400 | bytes 9437184 | tf_op jit(solution)/shard_map/pallas_call | solution.py:319
  95.6 7.8 %collective-permute-start.21 = (bf16[320,640]{1,0:T(8,128)(2,1)S(1)}, bf16[320,640]{1,0:T(8,128)(2,1)S(1)}, u32[]{:S(2)}, u32[]{:S(2)}) collective-permute-start(bf16[320,640]{1,0:T(8,128)(2,1)S(1)} %get-tuple-element.43), channel_id=1, source_target_pairs={{0,96},{8,104},{16,112},{24,120},{32,0},{40,8},{48,16},{56,24},{64... | collective-permute-start | bytes 1228808 | tf_op jit(solution)/shard_map/ppermute | solution.py:37
  103.5 3.2 %collective-permute-start.23 = (bf16[320,640]{1,0:T(8,128)(2,1)S(1)}, bf16[320,640]{1,0:T(8,128)(2,1)S(1)}, u32[]{:S(2)}, u32[]{:S(2)}) collective-permute-start(bf16[320,640]{1,0:T(8,128)(2,1)S(1)} %get-tuple-element.45), channel_id=1, source_target_pairs={{0,96},{8,104},{16,112},{24,120},{32,0},{40,8},{48,16},{56,24},{64... | collective-permute-start | bytes 1228808 | tf_op jit(solution)/shard_map/ppermute | solution.py:37
  106.7 5.0 %shard_map.178.refs_5_ = bf16[384,640]{1,0:T(8,128)(2,1)S(1)} custom-call(bf16[640,5120]{1,0:T(8,128)(2,1)S(1)} %bitcast.24, bf16[384,5120]{1,0:T(8,128)(2,1)S(1)} %copy-done.1, bf16[320,640]{1,0:T(8,128)(2,1)S(1)} %get-tuple-element.36.refs_2_), custom_call_target="tpu_custom_call" | custom-call | flops 3774873600 | bytes 12582912 | tf_op jit(solution)/shard_map/pallas_call | solution.py:74
  111.7 11.3 %shard_map.179 = (bf16[360,640]{1,0:T(8,128)(2,1)}, f32[2,360,640]{2,1,0:T(8,128)S(1)}, bf16[2,360,640]{2,1,0:T(8,128)(2,1)S(1)}, bf16[2,360,640]{2,1,0:T(8,128)(2,1)S(1)}) custom-call(bf16[360,640]{1,0:T(8,128)(2,1)S(1)} %bitcast.32, bf16[2,360,640]{2,1,0:T(8,128)(2,1)S(1)} %bitcast.26, bf16[2,360,640]{2,1,0:T(8,128)(2,1)S(1)} %bitcast.28, ...), custom_call_target="tpu_custom_call" | custom-call | flops 3888000000 | bytes 12582912 | tf_op jit(solution)/shard_map/pallas_call | solution.py:74
  123.0 1.3 collective-permute-start.18
  124.3 0.1 add_convert_fusion.6
  124.4 3.1 %collective-permute-start.19 = (bf16[2,360,640]{2,1,0:T(8,128)(2,1)S(1)}, bf16[2,360,640]{2,1,0:T(8,128)(2,1)S(1)}, u32[]{:S(2)}, u32[]{:S(2)}) collective-permute-start(bf16[2,360,640]{2,1,0:T(8,128)(2,1)S(1)} %get-tuple-element.40), channel_id=1, source_target_pairs={{0,8},{8,16},{16,24},{24,32},{32,40},{40,48},{48,56},{56,64},{64,7... | collective-permute-start | bytes 2764808 | tf_op jit(solution)/shard_map/ppermute | solution.py:386
  127.5 0.1 collective-permute-start.25
  127.6 0.2 add_convert_fusion.1
  127.9 3.7 %collective-permute-start.7 = (bf16[48,5120]{1,0:T(8,128)(2,1)S(1)}, bf16[48,5120]{1,0:T(8,128)(2,1)S(1)}, u32[]{:S(2)}, u32[]{:S(2)}) collective-permute-start(bf16[48,5120]{1,0:T(8,128)(2,1)S(1)} %add_convert_fusion.3), channel_id=1, source_target_pairs={{0,6},{1,7},{2,0},{3,1},{4,2},{5,3},{6,4},{7,5},{8,14},{9,15},{10,... | collective-permute-start | bytes 1474568 | tf_op jit(solution)/shard_map/ppermute | solution.py:27
  131.7 13.5 %collective-permute-done.25 = bf16[320,640]{1,0:T(8,128)(2,1)S(1)} collective-permute-done((bf16[320,640]{1,0:T(8,128)(2,1)S(1)}, bf16[320,640]{1,0:T(8,128)(2,1)S(1)}, u32[]{:S(2)}, u32[]{:S(2)}) %collective-permute-start.25) | collective-permute-done | bytes 409632 | tf_op jit(solution)/shard_map/ppermute | solution.py:37
  145.2 0.1 add_convert_fusion.7
  145.3 0.2 add_convert_fusion.5
  145.4 3.0 %collective-permute-start.20 = (bf16[320,640]{1,0:T(8,128)(2,1)S(1)}, bf16[320,640]{1,0:T(8,128)(2,1)S(1)}, u32[]{:S(2)}, u32[]{:S(2)}) collective-permute-start(bf16[320,640]{1,0:T(8,128)(2,1)S(1)} %get-tuple-element.41), channel_id=1, source_target_pairs={{0,32},{8,40},{16,48},{24,56},{32,64},{40,72},{48,80},{56,88},{64,... | collective-permute-start | bytes 1228808 | tf_op jit(solution)/shard_map/ppermute | solution.py:37
  148.5 0.3 collective-permute-start.22
  148.8 10.4 %collective-permute-done.11.refs_3_ = bf16[48,5120]{1,0:T(8,128)(2,1)S(1)} collective-permute-done((bf16[48,5120]{1,0:T(8,128)(2,1)S(1)}, bf16[48,5120]{1,0:T(8,128)(2,1)S(1)}, u32[]{:S(2)}, u32[]{:S(2)}) %collective-permute-start.11) | collective-permute-done | bytes 491552 | tf_op jit(solution)/shard_map/ppermute | solution.py:27
  159.2 1.2 shard_map.176
  160.4 1.3 add_convert_fusion
  161.7 10.6 %collective-permute-done.26 = bf16[320,640]{1,0:T(8,128)(2,1)S(1)} collective-permute-done((bf16[320,640]{1,0:T(8,128)(2,1)S(1)}, bf16[320,640]{1,0:T(8,128)(2,1)S(1)}, u32[]{:S(2)}, u32[]{:S(2)}) %collective-permute-start.26) | collective-permute-done | bytes 409632 | tf_op jit(solution)/shard_map/ppermute | solution.py:37
  172.2 1.0 fusion.2
  (48 shorter events, 0.6 us)
Async XLA Ops:
  0.6 11.0 %copy-start = (s32[1,16,5,63]{3,1,2,0:T(8,128)S(1)}, s32[1,16,5,63]{3,1,2,0:T(8,128)}, u32[]{:S(2)}) copy-start(s32[1,16,5,63]{3,1,2,0:T(8,128)} %param.20) | copy-start | bytes 60484
  3.0 14.1 %collective-permute-start.3 = (bf16[48,5120]{1,0:T(8,128)(2,1)S(1)}, bf16[48,5120]{1,0:T(8,128)(2,1)S(1)}, u32[]{:S(2)}, u32[]{:S(2)}) collective-permute-start(bf16[48,5120]{1,0:T(8,128)(2,1)S(1)} %get-tuple-element.49), channel_id=1, source_target_pairs={{0,1},{1,0},{2,3},{3,2},{4,5},{5,4},{6,7},{7,6},{8,9},{9,8},{10,11... | collective-permute-start | bytes 1474568 | tf_op jit(solution)/shard_map/ppermute | solution.py:27
  4.7 14.0 %collective-permute-start.2 = (bf16[48,5120]{1,0:T(8,128)(2,1)S(1)}, bf16[48,5120]{1,0:T(8,128)(2,1)S(1)}, u32[]{:S(2)}, u32[]{:S(2)}) collective-permute-start(bf16[48,5120]{1,0:T(8,128)(2,1)S(1)} %get-tuple-element.49), channel_id=1, source_target_pairs={{0,6},{1,7},{2,0},{3,1},{4,2},{5,3},{6,4},{7,5},{8,14},{9,15},{10,... | collective-permute-start | bytes 1474568 | tf_op jit(solution)/shard_map/ppermute | solution.py:27
  7.4 41.5 %collective-permute-start = (bf16[2,3,3,40,640]{4,3,2,1,0:T(8,128)(2,1)}, bf16[2,3,3,40,640]{4,3,2,1,0:T(8,128)(2,1)S(1)}, u32[]{:S(2)}, u32[]{:S(2)}) collective-permute-start(bf16[2,3,3,40,640]{4,3,2,1,0:T(8,128)(2,1)} %param.16), channel_id=1, source_target_pairs={{0,8},{8,16},{16,24},{24,32},{32,40},{40,48},{48,56},{56,64},{64,7... | collective-permute-start | bytes 2764808 | tf_op jit(solution)/shard_map/ppermute | solution.py:231
  8.8 40.2 %collective-permute-start.1 = (bf16[2,3,3,40,640]{4,3,2,1,0:T(8,128)(2,1)}, bf16[2,3,3,40,640]{4,3,2,1,0:T(8,128)(2,1)S(1)}, u32[]{:S(2)}, u32[]{:S(2)}) collective-permute-start(bf16[2,3,3,40,640]{4,3,2,1,0:T(8,128)(2,1)} %param.16), channel_id=1, source_target_pairs={{8,0},{16,8},{24,16},{32,24},{40,32},{48,40},{56,48},{64,56},{72,6... | collective-permute-start | bytes 2764808 | tf_op jit(solution)/shard_map/ppermute | solution.py:232
  10.1 12.2 %collective-permute-start.12 = (bf16[48,5120]{1,0:T(8,128)(2,1)S(1)}, bf16[48,5120]{1,0:T(8,128)(2,1)}, u32[]{:S(2)}, u32[]{:S(2)}) collective-permute-start(bf16[48,5120]{1,0:T(8,128)(2,1)S(1)} %get-tuple-element.49), channel_id=1, source_target_pairs={{0,2},{1,3},{2,4},{3,5},{4,6},{5,7},{6,0},{7,1},{8,10},{9,11},{10,... | collective-permute-start | bytes 1474568 | tf_op jit(solution)/shard_map/ppermute | solution.py:27
  15.7 33.2 %copy-start.2 = (bf16[2,3,3,40,640]{4,3,2,1,0:T(8,128)(2,1)S(1)}, bf16[2,3,3,40,640]{4,3,2,1,0:T(8,128)(2,1)}, u32[]{:S(2)}) copy-start(bf16[2,3,3,40,640]{4,3,2,1,0:T(8,128)(2,1)} %param.16) | copy-start | bytes 2764804
  15.7 33.2 %copy-start.3 = (bf16[3,3,40,640]{3,2,1,0:T(8,128)(2,1)S(1)}, bf16[3,3,40,640]{3,2,1,0:T(8,128)(2,1)}, u32[]{:S(2)}) copy-start(bf16[3,3,40,640]{3,2,1,0:T(8,128)(2,1)} %param.15) | copy-start | bytes 1382404
  17.1 15.7 %collective-permute-start.4 = (bf16[48,5120]{1,0:T(8,128)(2,1)S(1)}, bf16[48,5120]{1,0:T(8,128)(2,1)S(1)}, u32[]{:S(2)}, u32[]{:S(2)}) collective-permute-start(bf16[48,5120]{1,0:T(8,128)(2,1)S(1)} %collective-permute-done.3), channel_id=1, source_target_pairs={{0,2},{1,3},{2,4},{3,5},{4,6},{5,7},{6,0},{7,1},{8,10},{9,11},{10,... | collective-permute-start | bytes 1474568 | tf_op jit(solution)/shard_map/ppermute | solution.py:27
  18.7 14.9 %collective-permute-start.13 = (bf16[48,5120]{1,0:T(8,128)(2,1)S(1)}, bf16[48,5120]{1,0:T(8,128)(2,1)S(1)}, u32[]{:S(2)}, u32[]{:S(2)}) collective-permute-start(bf16[48,5120]{1,0:T(8,128)(2,1)S(1)} %collective-permute-done.3), channel_id=1, source_target_pairs={{0,6},{1,7},{2,0},{3,1},{4,2},{5,3},{6,4},{7,5},{8,14},{9,15},{10,... | collective-permute-start | bytes 1474568 | tf_op jit(solution)/shard_map/ppermute | solution.py:27
  22.3 20.4 %collective-permute-start.14 = (bf16[48,5120]{1,0:T(8,128)(2,1)S(1)}, bf16[48,5120]{1,0:T(8,128)(2,1)S(1)}, u32[]{:S(2)}, u32[]{:S(2)}) collective-permute-start(bf16[48,5120]{1,0:T(8,128)(2,1)S(1)} %collective-permute-done.2.refs_7_), channel_id=1, source_target_pairs={{0,6},{1,7},{2,0},{3,1},{4,2},{5,3},{6,4},{7,5},{8,14},{9,15},{10,... | collective-permute-start | bytes 1474568 | tf_op jit(solution)/shard_map/ppermute | solution.py:27
  32.7 13.2 %collective-permute-start.15 = (bf16[48,5120]{1,0:T(8,128)(2,1)S(1)}, bf16[48,5120]{1,0:T(8,128)(2,1)S(1)}, u32[]{:S(2)}, u32[]{:S(2)}) collective-permute-start(bf16[48,5120]{1,0:T(8,128)(2,1)S(1)} %collective-permute-done.4.refs_8_), channel_id=1, source_target_pairs={{0,2},{1,3},{2,4},{3,5},{4,6},{5,7},{6,0},{7,1},{8,10},{9,11},{10,... | collective-permute-start | bytes 1474568 | tf_op jit(solution)/shard_map/ppermute | solution.py:27
  45.9 11.5 %slice-start = ((s8[6553600]{0:T(1024)(128)(4,1)}), s8[4194304]{0:T(1024)(128)(4,1)S(1)}, s32[]{:S(2)}) async-start(s8[6553600]{0:T(1024)(128)(4,1)} %bitcast.23), calls=%async_computation | async-start | bytes 8388608
  46.8 40.5 %collective-permute-start.16 = (bf16[384,5120]{1,0:T(8,128)(2,1)}, bf16[384,5120]{1,0:T(8,128)(2,1)S(1)}, u32[]{:S(2)}, u32[]{:S(2)}) collective-permute-start(bf16[384,5120]{1,0:T(8,128)(2,1)} %constant_dynamic-update-slice_fusion.refs_0_.refs_1_.refs_2_), channel_id=1, source_target_pairs={{0,8},{8,0},{16,24},{24,16},{32,40},{40,32},{48,56},{56,48},{64,72... | collective-permute-start | bytes 11796488 | tf_op jit(solution)/shard_map/ppermute | solution.py:37
  49.0 8.5 %slice-start.1 = ((s8[6553600]{0:T(1024)(128)(4,1)}), s8[2359296]{0:T(1024)(128)(4,1)S(1)}, s32[]{:S(2)}) async-start(s8[6553600]{0:T(1024)(128)(4,1)} %bitcast.23), calls=%async_computation.1 | async-start | bytes 4718592
  57.5 29.7 %copy-start.1 = (bf16[384,5120]{1,0:T(8,128)(2,1)S(1)}, bf16[384,5120]{1,0:T(8,128)(2,1)}, u32[]{:S(2)}) copy-start(bf16[384,5120]{1,0:T(8,128)(2,1)} %constant_dynamic-update-slice_fusion.refs_0_.refs_1_.refs_2_) | copy-start | bytes 11796484
  62.1 14.4 %collective-permute-start.9 = (bf16[48,5120]{1,0:T(8,128)(2,1)S(1)}, bf16[48,5120]{1,0:T(8,128)(2,1)S(1)}, u32[]{:S(2)}, u32[]{:S(2)}) collective-permute-start(bf16[48,5120]{1,0:T(8,128)(2,1)S(1)} %get-tuple-element.34), channel_id=1, source_target_pairs={{0,2},{1,3},{2,4},{3,5},{4,6},{5,7},{6,0},{7,1},{8,10},{9,11},{10,... | collective-permute-start | bytes 1474568 | tf_op jit(solution)/shard_map/ppermute | solution.py:27
  62.2 25.0 %collective-permute-start.17 = (bf16[384,640]{1,0:T(8,128)(2,1)S(1)}, bf16[384,640]{1,0:T(8,128)(2,1)S(1)}, u32[]{:S(2)}, u32[]{:S(2)}) collective-permute-start(bf16[384,640]{1,0:T(8,128)(2,1)S(1)} %get-tuple-element.26.refs_0_.refs_6_), channel_id=1, source_target_pairs={{0,8},{8,0},{16,24},{24,16},{32,40},{40,32},{48,56},{56,48},{64,72... | collective-permute-start | bytes 1474568 | tf_op jit(solution)/shard_map/ppermute | solution.py:37
  62.3 62.2 %collective-permute-start.8 = (bf16[48,5120]{1,0:T(8,128)(2,1)S(1)}, bf16[48,5120]{1,0:T(8,128)(2,1)S(1)}, u32[]{:S(2)}, u32[]{:S(2)}) collective-permute-start(bf16[48,5120]{1,0:T(8,128)(2,1)S(1)} %get-tuple-element.32), channel_id=1, source_target_pairs={{0,6},{1,7},{2,0},{3,1},{4,2},{5,3},{6,4},{7,5},{8,14},{9,15},{10,... | collective-permute-start | bytes 1474568 | tf_op jit(solution)/shard_map/ppermute | solution.py:27
  65.4 21.7 %collective-permute-start.6 = (bf16[48,5120]{1,0:T(8,128)(2,1)S(1)}, bf16[48,5120]{1,0:T(8,128)(2,1)S(1)}, u32[]{:S(2)}, u32[]{:S(2)}) collective-permute-start(bf16[48,5120]{1,0:T(8,128)(2,1)S(1)} %get-tuple-element.30), channel_id=1, source_target_pairs={{0,6},{1,7},{2,0},{3,1},{4,2},{5,3},{6,4},{7,5},{8,14},{9,15},{10,... | collective-permute-start | bytes 1474568 | tf_op jit(solution)/shard_map/ppermute | solution.py:27
  76.6 50.9 %collective-permute-start.10 = (bf16[48,5120]{1,0:T(8,128)(2,1)S(1)}, bf16[48,5120]{1,0:T(8,128)(2,1)S(1)}, u32[]{:S(2)}, u32[]{:S(2)}) collective-permute-start(bf16[48,5120]{1,0:T(8,128)(2,1)S(1)} %add_convert_fusion.2), channel_id=1, source_target_pairs={{0,2},{1,3},{2,4},{3,5},{4,6},{5,7},{6,0},{7,1},{8,10},{9,11},{10,... | collective-permute-start | bytes 1474568 | tf_op jit(solution)/shard_map/ppermute | solution.py:27
  95.6 32.2 %collective-permute-start.21 = (bf16[320,640]{1,0:T(8,128)(2,1)S(1)}, bf16[320,640]{1,0:T(8,128)(2,1)S(1)}, u32[]{:S(2)}, u32[]{:S(2)}) collective-permute-start(bf16[320,640]{1,0:T(8,128)(2,1)S(1)} %get-tuple-element.43), channel_id=1, source_target_pairs={{0,96},{8,104},{16,112},{24,120},{32,0},{40,8},{48,16},{56,24},{64... | collective-permute-start | bytes 1228808 | tf_op jit(solution)/shard_map/ppermute | solution.py:37
  103.5 19.5 %collective-permute-start.24 = (bf16[320,640]{1,0:T(8,128)(2,1)S(1)}, bf16[320,640]{1,0:T(8,128)(2,1)S(1)}, u32[]{:S(2)}, u32[]{:S(2)}) collective-permute-start(bf16[320,640]{1,0:T(8,128)(2,1)S(1)} %get-tuple-element.47), channel_id=1, source_target_pairs={{0,32},{8,40},{16,48},{24,56},{32,64},{40,72},{48,80},{56,88},{64,... | collective-permute-start | bytes 1228808 | tf_op jit(solution)/shard_map/ppermute | solution.py:37
  103.5 24.4 %collective-permute-start.23 = (bf16[320,640]{1,0:T(8,128)(2,1)S(1)}, bf16[320,640]{1,0:T(8,128)(2,1)S(1)}, u32[]{:S(2)}, u32[]{:S(2)}) collective-permute-start(bf16[320,640]{1,0:T(8,128)(2,1)S(1)} %get-tuple-element.45), channel_id=1, source_target_pairs={{0,96},{8,104},{16,112},{24,120},{32,0},{40,8},{48,16},{56,24},{64... | collective-permute-start | bytes 1228808 | tf_op jit(solution)/shard_map/ppermute | solution.py:37
  123.0 37.4 %collective-permute-start.18 = (bf16[2,360,640]{2,1,0:T(8,128)(2,1)S(1)}, bf16[2,360,640]{2,1,0:T(8,128)(2,1)S(1)}, u32[]{:S(2)}, u32[]{:S(2)}) collective-permute-start(bf16[2,360,640]{2,1,0:T(8,128)(2,1)S(1)} %get-tuple-element.39), channel_id=1, source_target_pairs={{8,0},{16,8},{24,16},{32,24},{40,32},{48,40},{56,48},{64,56},{72,6... | collective-permute-start | bytes 2764808 | tf_op jit(solution)/shard_map/ppermute | solution.py:385
  124.4 36.0 %collective-permute-start.19 = (bf16[2,360,640]{2,1,0:T(8,128)(2,1)S(1)}, bf16[2,360,640]{2,1,0:T(8,128)(2,1)S(1)}, u32[]{:S(2)}, u32[]{:S(2)}) collective-permute-start(bf16[2,360,640]{2,1,0:T(8,128)(2,1)S(1)} %get-tuple-element.40), channel_id=1, source_target_pairs={{0,8},{8,16},{16,24},{24,32},{32,40},{40,48},{48,56},{56,64},{64,7... | collective-permute-start | bytes 2764808 | tf_op jit(solution)/shard_map/ppermute | solution.py:386
  127.5 17.6 %collective-permute-start.25 = (bf16[320,640]{1,0:T(8,128)(2,1)S(1)}, bf16[320,640]{1,0:T(8,128)(2,1)S(1)}, u32[]{:S(2)}, u32[]{:S(2)}) collective-permute-start(bf16[320,640]{1,0:T(8,128)(2,1)S(1)} %add_convert_fusion.6), channel_id=1, source_target_pairs={{0,32},{8,40},{16,48},{24,56},{32,64},{40,72},{48,80},{56,88},{64,... | collective-permute-start | bytes 1228808 | tf_op jit(solution)/shard_map/ppermute | solution.py:37
  127.8 17.6 %collective-permute-start.5 = (bf16[48,5120]{1,0:T(8,128)(2,1)S(1)}, bf16[48,5120]{1,0:T(8,128)(2,1)S(1)}, u32[]{:S(2)}, u32[]{:S(2)}) collective-permute-start(bf16[48,5120]{1,0:T(8,128)(2,1)S(1)} %get-tuple-element.28), channel_id=1, source_target_pairs={{0,2},{1,3},{2,4},{3,5},{4,6},{5,7},{6,0},{7,1},{8,10},{9,11},{10,... | collective-permute-start | bytes 1474568 | tf_op jit(solution)/shard_map/ppermute | solution.py:27
  127.9 20.6 %collective-permute-start.7 = (bf16[48,5120]{1,0:T(8,128)(2,1)S(1)}, bf16[48,5120]{1,0:T(8,128)(2,1)S(1)}, u32[]{:S(2)}, u32[]{:S(2)}) collective-permute-start(bf16[48,5120]{1,0:T(8,128)(2,1)S(1)} %add_convert_fusion.3), channel_id=1, source_target_pairs={{0,6},{1,7},{2,0},{3,1},{4,2},{5,3},{6,4},{7,5},{8,14},{9,15},{10,... | collective-permute-start | bytes 1474568 | tf_op jit(solution)/shard_map/ppermute | solution.py:27
  145.2 14.0 %collective-permute-start.11 = (bf16[48,5120]{1,0:T(8,128)(2,1)S(1)}, bf16[48,5120]{1,0:T(8,128)(2,1)S(1)}, u32[]{:S(2)}, u32[]{:S(2)}) collective-permute-start(bf16[48,5120]{1,0:T(8,128)(2,1)S(1)} %add_convert_fusion.1), channel_id=1, source_target_pairs={{0,1},{1,0},{2,3},{3,2},{4,5},{5,4},{6,7},{7,6},{8,9},{9,8},{10,11... | collective-permute-start | bytes 1474568 | tf_op jit(solution)/shard_map/ppermute | solution.py:27
  145.4 16.2 %collective-permute-start.20 = (bf16[320,640]{1,0:T(8,128)(2,1)S(1)}, bf16[320,640]{1,0:T(8,128)(2,1)S(1)}, u32[]{:S(2)}, u32[]{:S(2)}) collective-permute-start(bf16[320,640]{1,0:T(8,128)(2,1)S(1)} %get-tuple-element.41), channel_id=1, source_target_pairs={{0,32},{8,40},{16,48},{24,56},{32,64},{40,72},{48,80},{56,88},{64,... | collective-permute-start | bytes 1228808 | tf_op jit(solution)/shard_map/ppermute | solution.py:37
  148.5 13.2 %collective-permute-start.22 = (bf16[320,640]{1,0:T(8,128)(2,1)S(1)}, bf16[320,640]{1,0:T(8,128)(2,1)S(1)}, u32[]{:S(2)}, u32[]{:S(2)}) collective-permute-start(bf16[320,640]{1,0:T(8,128)(2,1)S(1)} %add_convert_fusion.7), channel_id=1, source_target_pairs={{0,96},{8,104},{16,112},{24,120},{32,0},{40,8},{48,16},{56,24},{64... | collective-permute-start | bytes 1228808 | tf_op jit(solution)/shard_map/ppermute | solution.py:37
  159.2 13.1 %collective-permute-start.26 = (bf16[320,640]{1,0:T(8,128)(2,1)S(1)}, bf16[320,640]{1,0:T(8,128)(2,1)S(1)}, u32[]{:S(2)}, u32[]{:S(2)}) collective-permute-start(bf16[320,640]{1,0:T(8,128)(2,1)S(1)} %add_convert_fusion.5), channel_id=1, source_target_pairs={{0,16},{8,24},{16,0},{24,8},{32,48},{40,56},{48,32},{56,40},{64,80... | collective-permute-start | bytes 1228808 | tf_op jit(solution)/shard_map/ppermute | solution.py:37

commit v3 on v2

--- a/solution.py
+++ b/solution.py
@@ -101,12 +101,12 @@
     return [shift(arrays[i], 1 - 2 * i, 0) for i in range(2)]
 
 
-def forward_kernel(q_ref, own_ref, up_ref, down_ref, bias_ref, hot_ref, perm_ref, p_ref, att_ref):
+def scores_kernel(q_ref, own_ref, up_ref, down_ref, bias_ref, hot_ref, p_ref):
     qa = jnp.concatenate([q_ref[...], hot_ref[...]], axis=1)
     scores = []
     for b, ref in enumerate((up_ref, own_ref, down_ref)):
         bias = jnp.concatenate([bias_ref[0, b]] * 9, axis=0).astype(BF16)
-        ka = jnp.concatenate([ref[0], bias], axis=1)
+        ka = jnp.concatenate([ref[...], bias], axis=1)
         scores.append(dot(ka, qa, ((1,), (1,))))
     top = jnp.max(scores[0], axis=0, keepdims=True)
     for s in scores[1:]:
@@ -116,27 +116,28 @@
     for w in weights[1:]:
         total = total + jnp.sum(w, axis=0, keepdims=True)
     inverse = 1.0 / total
+    for b in range(3):
+        p_ref[0, b] = (weights[b] * inverse).astype(BF16)
+
+
+def attend_kernel(p_ref, own_ref, up_ref, down_ref, perm_ref, att_ref):
     attended = None
     for b, ref in enumerate((up_ref, own_ref, down_ref)):
-        probs = (weights[b] * inverse).astype(BF16)
-        p_ref[0, b] = probs
-        part = dot(ref[1], probs, ((0,), (0,)))
+        part = dot(ref[...], p_ref[0, b], ((0,), (0,)))
         attended = part if attended is None else attended + part
-    attended = attended.astype(BF16)
-    att_ref[...] = dot(perm_ref[...], attended, ((1,), (1,))).astype(BF16)
-
-
-def backward_kernel(
-    q_ref, own_ref, up_ref, down_ref, p_ref, ga_ref, perm_ref, gq_ref, gown_ref, gup_ref, gdown_ref
-):
+    att_ref[...] = dot(perm_ref[...], attended.astype(BF16), ((1,), (1,))).astype(BF16)
+
+
+def backward_kernel(q_ref, *refs):
+    keys, values = (refs[1], refs[0], refs[2]), (refs[4], refs[3], refs[5])
+    p_ref, ga_ref, perm_ref, gq_ref, gown_ref, gup_ref, gdown_ref = refs[6:]
     q = q_ref[...]
     g = dot(perm_ref[...], ga_ref[...], ((1,), (0,))).astype(BF16)
-    refs = (up_ref, own_ref, down_ref)
     outs = (gup_ref, gown_ref, gdown_ref)
     grads = []
     delta = None
     for b in range(3):
-        gp = dot(refs[b][1], g, ((1,), (1,)))
+        gp = dot(values[b][...], g, ((1,), (1,)))
         part = jnp.sum(p_ref[0, b].astype(F32) * gp, axis=0, keepdims=True)
         delta = part if delta is None else delta + part
         grads.append(gp)
@@ -146,26 +147,32 @@
         ds = (probs.astype(F32) * (grads[b] - delta) * SCALE).astype(BF16)
         outs[b][0] = dot(ds, q, ((1,), (0,))).astype(outs[b].dtype)
         outs[b][1] = dot(probs, g, ((1,), (0,))).astype(outs[b].dtype)
-        part = dot(refs[b][0], ds, ((0,), (0,)))
+        part = dot(keys[b][...], ds, ((0,), (0,)))
         gq = part if gq is None else gq + part
     gq_ref[...] = gq.T.astype(BF16)
 
 
-def weight_kernel(order_ref, *refs):
-    parts, (att_ref, far_att_ref), outs = refs[:6], refs[6:8], refs[8:]
+def total_kernel(*refs):
+    out_ref = refs[-1]
+    start = 0
+    for i in range(0, len(refs) - 1, 3):
+        part = added(refs[i][...], refs[i + 1][...], refs[i + 2][...]).astype(BF16)
+        out_ref[:, :, start : start + part.shape[2]] = part
+        start += part.shape[2]
+
+
+def weight_kernel(order_ref, g_ref, far_g_ref, att_ref, far_att_ref, *outs):
     attended = jnp.concatenate([att_ref[...], far_att_ref[...]], axis=0)
-    turned = [jnp.concatenate([p[...].T for p in parts[3 * i : 3 * i + 3]], axis=0) for i in range(2)]
-    turned = jnp.concatenate(turned, axis=1)
+    core = order_ref[len(outs)]
     rows = outs[0].shape[0]
-    extra = turned.shape[0] - rows
-    turned = jnp.where(order_ref[len(outs)] == 0, turned[:rows], turned[extra:])
-    grad = dot(turned, attended, ((1,), (0,))).astype(BF16)
-    step = pl.program_id(0)
+    lanes = 128
+    wide = -(-rows // lanes) * lanes
     for i, out_ref in enumerate(outs):
-
-        @pl.when(step == i)
-        def _(out_ref=out_ref):
-            out_ref[...] = grad
+        start = order_ref[i] * (2 * rows) + core * (2 * rows - wide)
+        columns = pl.ds(pl.multiple_of(start, lanes), wide)
+        turned = jnp.concatenate([g_ref[:, columns].T, far_g_ref[:, columns].T], axis=1)
+        turned = jnp.where(core == 0, turned[:rows], turned[wide - rows :])
+        out_ref[...] = dot(turned, attended, ((1,), (0,))).astype(BF16)
 
 
 def project_kernel(att_ref, w_ref, *outs):
@@ -228,8 +235,13 @@
 
     onward = [(i, i + 1) for i in range(row_tiles - 1)]
     back = [(i + 1, i) for i in range(row_tiles - 1)]
-    up = lax.ppermute(keys_values, "seq", onward)
-    down = lax.ppermute(keys_values, "seq", back)
+    flat_q = queries.reshape(tokens, channels)
+    flat_kv = keys_values.reshape(2, tokens, channels)
+    halos = []
+    for i in range(2):
+        up = lax.ppermute(flat_kv[i], "seq", onward)
+        down = lax.ppermute(flat_kv[i], "seq", back)
+        halos.append([flat_kv, up, down])
 
     piece = strips * local_columns
     room = -(-piece // 16) * 16
@@ -252,41 +264,46 @@
     own_mask = lax.dynamic_slice_in_dim(block_mask, seq_place, 1, 1).reshape(-1, OFFSETS)
     bias = mask_bias(window, own_mask, seq_place, row_tiles)
 
-    flat_q = queries.reshape(tokens, channels)
-    flat = [v.reshape(2, tokens, channels) for v in (keys_values, up, down)]
-
     def whole(shape):
         return pl.BlockSpec(shape, lambda h: (0,) * len(shape))
 
     q_spec = pl.BlockSpec((tokens, HEAD_DIM), lambda h: (0, h))
     kv_spec = pl.BlockSpec((2, tokens, HEAD_DIM), lambda h: (0, 0, h))
+    key_specs = [pl.BlockSpec((None, tokens, HEAD_DIM), lambda h: (0, 0, h)), q_spec, q_spec]
+    value_specs = [pl.BlockSpec((None, tokens, HEAD_DIM), lambda h: (1, 0, h)), q_spec, q_spec]
+    p_spec = pl.BlockSpec((1, 3, tokens, tokens), lambda h: (h, 0, 0, 0))
     weights = ((2, 1), (2, 0), (1, 0), (3, 1), (1, 1), (3, 0), (0, 1), (0, 0))
     ring, pair = (np.array([w[i] for w in weights], np.int32) for i in range(2))
     chips = (spot_z + ring) % 4 * 2 + (spot_y + pair) % 2
     order = jnp.concatenate([chips, core]).astype(jnp.int32)
 
     pairs = heads * tokens * 3 * tokens
-    probs, attended = kernel(
-        forward_kernel,
-        [((heads, 3, tokens, tokens), BF16), ((slots, channels), BF16)],
-        [flat_q, *flat, bias, hot, perm],
+    (probs,) = kernel(
+        scores_kernel,
+        [((heads, 3, tokens, tokens), BF16)],
+        [flat_q, *halos[0], bias, hot],
         [
             q_spec,
-            kv_spec,
-            kv_spec,
-            kv_spec,
+            *key_specs,
             pl.BlockSpec((1, 3, columns, 128), lambda h: (h, 0, 0, 0)),
             whole((tokens, 128)),
-            whole((slots, tokens)),
         ],
-        [
-            pl.BlockSpec((1, 3, tokens, tokens), lambda h: (h, 0, 0, 0)),
-            pl.BlockSpec((slots, HEAD_DIM), lambda h: (0, h)),
-        ],
+        [p_spec],
         grid=(heads,),
-        after=[*last_hops, perm_back, order],
-        flops=pairs * 1500,
-        moved=8 << 20,
+        after=[perm, perm_back, order],
+        flops=pairs * 1000,
+        moved=6 << 20,
+    )
+    (attended,) = kernel(
+        attend_kernel,
+        [((slots, channels), BF16)],
+        [probs, *halos[1], perm],
+        [p_spec, *value_specs, whole((slots, tokens))],
+        [pl.BlockSpec((slots, HEAD_DIM), lambda h: (0, h))],
+        grid=(heads,),
+        after=last_hops,
+        flops=pairs * 500,
+        moved=6 << 20,
     )
     far_grad = seq_shift(all_grad, 0, 0, 1)
     far_attended = seq_shift(attended, 0, 0, 1)
@@ -307,29 +324,15 @@
     mixed_near = hop(tensor_shift, (mixed[1, 0], mixed[3, 1]))
 
     narrow = model_width // row_tiles
-    lanes = 128
-    window_specs = [
-        pl.BlockSpec((slots, lanes), lambda i, o, j=j: (0, o[i] * (2 * narrow // lanes) + 2 * o[8] + j))
-        for j in range(3)
-    ]
-
-    def constant(shape):
-        return pl.BlockSpec(shape, lambda i, o: (0, 0))
-
-    weight = pl.pallas_call(
+    weight = kernel(
         weight_kernel,
-        grid_spec=pltpu.PrefetchScalarGridSpec(
-            num_scalar_prefetch=1,
-            grid=(8,),
-            in_specs=[*window_specs, *window_specs, *[constant((slots, channels))] * 2],
-            out_specs=[constant((narrow, channels))] * 8,
-        ),
-        out_shape=[jax.ShapeDtypeStruct((narrow, channels), BF16)] * 8,
-        compiler_params=pltpu.CompilerParams(vmem_limit_bytes=ROOM),
-        cost_estimate=pl.CostEstimate(
-            flops=slots * model_width * channels * 2, transcendentals=0, bytes_accessed=9 << 20
-        ),
-    )(order, *[all_grad] * 3, *[far_grad] * 3, attended, far_attended)
+        [((narrow, channels), BF16)] * 8,
+        [order, all_grad, far_grad, attended, far_attended],
+        [SCALAR] + [VECTOR] * 4,
+        after=[mixed[0, 0]],
+        flops=slots * model_width * channels * 2,
+        moved=6 << 20,
+    )
     weight = dict(zip(weights, weight))
     weight_far = hop(seq_shift, (weight[2, 1], weight[2, 0]))
     weight_near = hop(seq_shift, (weight[1, 0], weight[3, 1]))
@@ -350,25 +353,52 @@
         scratch=[pltpu.VMEM((slots, channels), F32)],
     )
 
-    wide = ((2, tokens, channels), BF16)
-    grad_q, grad_own, grad_up, grad_down = kernel(
-        backward_kernel,
-        [((tokens, channels), BF16), (wide[0], F32), wide, wide],
-        [flat_q, *flat, probs, grad_attn, perm_back],
-        [
-            q_spec,
-            kv_spec,
-            kv_spec,
-            kv_spec,
-            pl.BlockSpec((1, 3, tokens, tokens), lambda h: (h, 0, 0, 0)),
-            pl.BlockSpec((slots, HEAD_DIM), lambda h: (0, h)),
-            whole((tokens, slots)),
-        ],
-        [q_spec, kv_spec, kv_spec, kv_spec],
-        grid=(heads,),
-        flops=pairs * 2000,
-        moved=12 << 20,
-    )
+    def differentiate(first, count, after):
+        def spec(shape, at):
+            def index(h):
+                return tuple(h + first if i == at else 0 for i in range(len(shape)))
+
+            return pl.BlockSpec(shape, index)
+
+        def own(which):
+            return pl.BlockSpec((None, tokens, HEAD_DIM), lambda h: (which, 0, h + first))
+
+        width = count * HEAD_DIM
+        one = spec((tokens, HEAD_DIM), 1)
+        halo = ((2, tokens, width), BF16)
+        return kernel(
+            backward_kernel,
+            [((tokens, width), BF16), (halo[0], F32), halo, halo],
+            [flat_q, *halos[0], *halos[1], probs, grad_attn, perm_back],
+            [
+                one,
+                own(0),
+                one,
+                one,
+                own(1),
+                one,
+                one,
+                spec((1, 3, tokens, tokens), 0),
+                spec((slots, HEAD_DIM), 1),
+                whole((tokens, slots)),
+            ],
+            [q_spec, kv_spec, kv_spec, kv_spec],
+            grid=(count,),
+            after=after,
+            flops=pairs * 2000 * count // heads,
+            moved=2 * count << 20,
+        )
+
+    def send_halo(grad_up, grad_down):
+        from_below = lax.ppermute(grad_up, "seq", back)
+        from_above = lax.ppermute(grad_down, "seq", onward)
+        return from_below, from_above
+
+    split = (heads + 1) // 2
+    gq_a, own_a, *ends_a = differentiate(0, split, [])
+    halo_a = send_halo(*ends_a)
+    gq_b, own_b, *ends_b = differentiate(split, heads - split, ends_a[:1])
+    halo_b = send_halo(*ends_b)
 
     def relayed(kept, came, shift):
         sums = [added(k, c).astype(BF16) for k, c in zip(kept, came)]
@@ -382,9 +412,6 @@
     weight_sums = relayed((weight[1, 1], weight[3, 0]), weight_far, seq_shift)
     mixed_side = side(tensor_shift, mixed[0, 1], mixed_near[1], mixed_sums[0])
     weight_side = side(seq_shift, weight[0, 1], weight_near[1], weight_sums[0])
-    from_below = lax.ppermute(grad_up, "seq", back)
-    from_above = lax.ppermute(grad_down, "seq", onward)
-
     (layer_out,) = kernel(
         mixed_kernel,
         [((frames, local_columns, tile_rows, model_width), BF16)],
@@ -392,7 +419,14 @@
         moved=3 << 20,
     )
     grad_weight = added(weight[0, 0], weight_near[0], weight_sums[1], weight_side).astype(BF16)
-    grad_kv = added(grad_own, from_below, from_above).astype(BF16)
+    (grad_kv,) = kernel(
+        total_kernel,
+        [((2, tokens, channels), BF16)],
+        [own_a, *halo_a, own_b, *halo_b],
+        after=[layer_out],
+        moved=5 << 20,
+    )
+    grad_q = jnp.concatenate([gq_a, gq_b], axis=1)
     return (
         layer_out.transpose(0, 2, 1, 3),
         grad_q.reshape(queries.shape),

time: 175 us -> 204 us (1.17)
  starting transfers between devices: 39.8 us -> 58.1 us
  waiting for transfers between devices: 75.4 us -> 92.3 us
  Pallas kernels: 39 us -> 35.6 us
  other arithmetic: 7.72 us -> 5.2 us
    ppermute x14, waiting for transfers between devices: 51.3 us -> 78 us  [tensor_shift(): return lax.ppermute(value, 'tensor', pairs)]
    ppermute x4 -> x8, starting transfers between devices: 7 us -> 18.7 us  [the longest x2 7.11 us: send_halo(): from_above = lax.ppermute(grad_down, 'seq', onward)]
    ppermute x9, waiting for transfers between devices: 24.1 us -> 14.3 us  [seq_shift(): return lax.ppermute(value, 'seq', pairs)]
    pallas_call x1 -> x0, Pallas kernels: 8.4 us -> none  [layer(): pl.pallas_call(weight_kernel, grid_spec=pltpu.PrefetchScalarGridSpec(num_...]
    pallas_call x5 -> x9, Pallas kernels: 30.6 us -> 35.6 us  [kernel(): pl.pallas_call(run, grid=grid, in_specs=[*specs, *[ANYWHERE] * len(after)...]
    ppermute x9, starting transfers between devices: 16.4 us -> 20.6 us  [seq_shift(): return lax.ppermute(value, 'seq', pairs)]
    ppermute x14, starting transfers between devices: 16.4 us -> 18.8 us  [tensor_shift(): return lax.ppermute(value, 'tensor', pairs)]
    unnamed x19 -> x27, local copies, waits for them, and re-layouts: 6.8 us -> 6.92 us
  transfers between devices with their start and end apart: 27 -> 31, of which waited for: 10 -> 12; matrix products, arithmetic and copies ran while one was open for 8% -> 6% of each run, Pallas kernels for 23% -> 17%
where the time goes in v3:
time: 204 us
  waiting for transfers between devices  92.3 us (45%)
  starting transfers between devices  58.1 us (28%)
  Pallas kernels  35.6 us (17%)
  local copies, waits for them, and re-layouts  11.5 us (6%)
  other arithmetic  5.2 us (3%)
    ppermute x14, waiting for transfers between devices, tensor_shift(): return lax.ppermute(value, 'tensor', pairs)  78 us
    pallas_call x9, Pallas kernels, kernel(): pl.pallas_call(run, grid=grid, in_specs=[*specs, *[ANYWHERE] * len(after)...  35.6 us
    ppermute x9, starting transfers between devices, seq_shift(): return lax.ppermute(value, 'seq', pairs)  20.6 us
    ppermute x14, starting transfers between devices, tensor_shift(): return lax.ppermute(value, 'tensor', pairs)  18.8 us
    ppermute x9, waiting for transfers between devices, seq_shift(): return lax.ppermute(value, 'seq', pairs)  14.3 us
    ppermute x2, starting transfers between devices, send_halo(): from_above = lax.ppermute(grad_down, 'seq', onward)  7.11 us
    unnamed x27, local copies, waits for them, and re-layouts  6.92 us
    ppermute x2, starting transfers between devices, layer(): up = lax.ppermute(flat_kv[i], 'seq', onward)  6.45 us
  transfers between devices with their start and end apart: 31, of which 12 were waited for; matrix products, arithmetic and copies ran while one was open for 6% of the time, Pallas kernels for 17%

profile of v3, /device:TPU:0, one launch (start us, length us, event | category | flops | bytes accessed | tf_op | source)
XLA Modules:
  0.0 203.9 jit_solution(10942168781229126635)
XLA Ops:
  0.7 2.0 fusion.22
  2.7 1.3 collective-permute-start.1
  4.0 3.1 %collective-permute-start = (bf16[360,640]{1,0:T(8,128)(2,1)}, bf16[360,640]{1,0:T(8,128)(2,1)S(1)}, u32[]{:S(2)}, u32[]{:S(2)}) collective-permute-start(bf16[360,640]{1,0:T(8,128)(2,1)} %bitcast.2), channel_id=1, source_target_pairs={{0,8},{8,16},{16,24},{24,32},{32,40},{40,48},{48,56},{56,64},{64,7... | collective-permute-start | bytes 1382408 | tf_op jit(solution)/shard_map/ppermute | solution.py:242
  7.1 1.5 reshape.160
  8.5 0.8 constant_dynamic-update-slice_fusion.7
  9.4 1.6 collective-permute-start.14
  11.0 1.6 collective-permute-start.5
  12.6 1.7 collective-permute-start.4
  14.5 0.5 multiply_reduce_fusion
  15.6 0.8 fusion.9
  16.6 9.0 %collective-permute-done.4.refs_5_ = bf16[48,5120]{1,0:T(8,128)(2,1)S(1)} collective-permute-done((bf16[48,5120]{1,0:T(8,128)(2,1)S(1)}, bf16[48,5120]{1,0:T(8,128)(2,1)S(1)}, u32[]{:S(2)}, u32[]{:S(2)}) %collective-permute-start.4) | collective-permute-done | bytes 491552 | tf_op jit(solution)/shard_map/ppermute | solution.py:27
  25.6 1.3 collective-permute-start.3
  26.9 0.8 constant_dynamic-update-slice_fusion.6
  27.8 3.4 %collective-permute-start.2 = (bf16[360,640]{1,0:T(8,128)(2,1)S(1)}, bf16[360,640]{1,0:T(8,128)(2,1)S(1)}, u32[]{:S(2)}, u32[]{:S(2)}) collective-permute-start(bf16[360,640]{1,0:T(8,128)(2,1)S(1)} %bitcast.38), channel_id=1, source_target_pairs={{0,8},{8,16},{16,24},{24,32},{32,40},{40,48},{48,56},{56,64},{64,7... | collective-permute-start | bytes 1382408 | tf_op jit(solution)/shard_map/ppermute | solution.py:242
  31.2 1.6 collective-permute-start.6
  32.7 0.8 constant_dynamic-update-slice_fusion.5
  33.6 0.8 constant_dynamic-update-slice_fusion.4
  34.4 9.9 %collective-permute-done.6.refs_6_ = bf16[48,5120]{1,0:T(8,128)(2,1)S(1)} collective-permute-done((bf16[48,5120]{1,0:T(8,128)(2,1)S(1)}, bf16[48,5120]{1,0:T(8,128)(2,1)S(1)}, u32[]{:S(2)}, u32[]{:S(2)}) %collective-permute-start.6) | collective-permute-done | bytes 491552 | tf_op jit(solution)/shard_map/ppermute | solution.py:27
  44.3 1.8 collective-permute-start.15
  46.1 0.8 constant_dynamic-update-slice_fusion.3
  46.9 10.4 %collective-permute-done.15 = bf16[48,5120]{1,0:T(8,128)(2,1)S(1)} collective-permute-done((bf16[48,5120]{1,0:T(8,128)(2,1)S(1)}, bf16[48,5120]{1,0:T(8,128)(2,1)S(1)}, u32[]{:S(2)}, u32[]{:S(2)}) %collective-permute-start.15) | collective-permute-done | bytes 491552 | tf_op jit(solution)/shard_map/ppermute | solution.py:27
  57.3 3.0 %collective-permute-start.16 = (bf16[48,5120]{1,0:T(8,128)(2,1)S(1)}, bf16[48,5120]{1,0:T(8,128)(2,1)S(1)}, u32[]{:S(2)}, u32[]{:S(2)}) collective-permute-start(bf16[48,5120]{1,0:T(8,128)(2,1)S(1)} %collective-permute-done.4.refs_5_), channel_id=1, source_target_pairs={{0,6},{1,7},{2,0},{3,1},{4,2},{5,3},{6,4},{7,5},{8,14},{9,15},{10,... | collective-permute-start | bytes 1474568 | tf_op jit(solution)/shard_map/ppermute | solution.py:27
  60.3 0.8 constant_dynamic-update-slice_fusion.2
  61.1 10.8 %collective-permute-done.16 = bf16[48,5120]{1,0:T(8,128)(2,1)S(1)} collective-permute-done((bf16[48,5120]{1,0:T(8,128)(2,1)S(1)}, bf16[48,5120]{1,0:T(8,128)(2,1)S(1)}, u32[]{:S(2)}, u32[]{:S(2)}) %collective-permute-start.16) | collective-permute-done | bytes 491552 | tf_op jit(solution)/shard_map/ppermute | solution.py:27
  71.9 0.8 constant_dynamic-update-slice_fusion.1
  72.7 14.3 %collective-permute-done.17 = bf16[48,5120]{1,0:T(8,128)(2,1)S(1)} collective-permute-done((bf16[48,5120]{1,0:T(8,128)(2,1)S(1)}, bf16[48,5120]{1,0:T(8,128)(2,1)S(1)}, u32[]{:S(2)}, u32[]{:S(2)}) %collective-permute-start.17) | collective-permute-done | bytes 491552 | tf_op jit(solution)/shard_map/ppermute | solution.py:27
  87.0 0.8 constant_dynamic-update-slice_fusion.refs_1_
  87.8 0.7 fusion.17
  88.6 5.2 %shard_map.174.refs_0_.refs_7_ = bf16[5,3,360,360]{3,2,1,0:T(8,128)(2,1)S(1)} custom-call(bf16[360,640]{1,0:T(8,128)(2,1)S(1)} %bitcast.29, bf16[2,360,640]{2,1,0:T(8,128)(2,1)S(1)} %bitcast.23, bf16[360,640]{1,0:T(8,128)(2,1)S(1)} %collective-permute-done.refs_2_, bf16[360,640]{1,0:T(8,128)(2,1)S(1)} %collective-permute-done.1.refs_3_, ...), custom_call_target="tpu_custom_call" | custom-call | flops 1944000000 | bytes 6291456 | tf_op jit(solution)/shard_map/pallas_call | solution.py:74
  93.9 3.5 %shard_map.175.refs_0_.refs_3_ = bf16[384,640]{1,0:T(8,128)(2,1)S(1)} custom-call(bf16[5,3,360,360]{3,2,1,0:T(8,128)(2,1)S(1)} %shard_map.174.refs_0_.refs_7_, bf16[2,360,640]{2,1,0:T(8,128)(2,1)S(1)} %bitcast.24, bf16[360,640]{1,0:T(8,128)(2,1)S(1)} %collective-permute-done.2.refs_2_.refs_5_, bf16[360,640]{1,0:T(8,128)(2,1)S(1)} %collective-permute-done.3.refs_3_.refs_6_, ...), custom_call_target="tpu_custom_call" | custom-call | flops 972000000 | bytes 6291456 | tf_op jit(solution)/shard_map/pallas_call | solution.py:74
  97.4 4.6 %shard_map.176 = (bf16[48,5120]{1,0:T(8,128)(2,1)S(1)}, bf16[48,5120]{1,0:T(8,128)(2,1)S(1)}, bf16[48,5120]{1,0:T(8,128)(2,1)S(1)}, bf16[48,5120]{1,0:T(8,128)(2...) custom-call(bf16[384,640]{1,0:T(8,128)(2,1)S(1)} %shard_map.175.refs, ...), custom_call_target="tpu_custom_call" | custom-call | flops 3774873600 | bytes 12582912 | tf_op jit(solution)/shard_map/pallas_call | solution.py:74
  102.1 0.6 collective-permute-start.19
  102.7 0.3 collective-permute-start.7
  103.0 2.9 %collective-permute-start.8 = (bf16[48,5120]{1,0:T(8,128)(2,1)S(1)}, bf16[48,5120]{1,0:T(8,128)(2,1)S(1)}, u32[]{:S(2)}, u32[]{:S(2)}) collective-permute-start(bf16[48,5120]{1,0:T(8,128)(2,1)S(1)} %get-tuple-element.31), channel_id=1, source_target_pairs={{0,6},{1,7},{2,0},{3,1},{4,2},{5,3},{6,4},{7,5},{8,14},{9,15},{10,... | collective-permute-start | bytes 1474568 | tf_op jit(solution)/shard_map/ppermute | solution.py:27
  105.9 11.5 %collective-permute-done.11 = bf16[48,5120]{1,0:T(8,128)(2,1)S(1)} collective-permute-done((bf16[48,5120]{1,0:T(8,128)(2,1)S(1)}, bf16[48,5120]{1,0:T(8,128)(2,1)S(1)}, u32[]{:S(2)}, u32[]{:S(2)}) %collective-permute-start.11) | collective-permute-done | bytes 491552 | tf_op jit(solution)/shard_map/ppermute | solution.py:27
  117.4 0.5 collective-permute-start.10
  118.1 1.6 collective-permute-start.12
  119.7 2.0 collective-permute-start.9
  121.7 3.9 %shard_map.178 = (bf16[320,640]{1,0:T(8,128)(2,1)S(1)}, bf16[320,640]{1,0:T(8,128)(2,1)S(1)}, bf16[320,640]{1,0:T(8,128)(2,1)S(1)}, bf16[320,640]{1,0:T(8,128)(2...) custom-call(s32[9]{0:T(128)S(1)} %pad_add_fusion.refs_8_.refs_0_, ...), custom_call_target="tpu_custom_call" | custom-call | flops 2516582400 | bytes 6291456 | tf_op jit(solution)/shard_map/pallas_call | solution.py:74
  125.7 4.2 %collective-permute-start.28 = (bf16[320,640]{1,0:T(8,128)(2,1)S(1)}, bf16[320,640]{1,0:T(8,128)(2,1)S(1)}, u32[]{:S(2)}, u32[]{:S(2)}) collective-permute-start(bf16[320,640]{1,0:T(8,128)(2,1)S(1)} %get-tuple-element.51), channel_id=1, source_target_pairs={{0,32},{8,40},{16,48},{24,56},{32,64},{40,72},{48,80},{56,88},{64,... | collective-permute-start | bytes 1228808 | tf_op jit(solution)/shard_map/ppermute | solution.py:37
  129.8 1.7 collective-permute-done.10
  131.5 6.5 %collective-permute-done.12 = bf16[48,5120]{1,0:T(8,128)(2,1)S(1)} collective-permute-done((bf16[48,5120]{1,0:T(8,128)(2,1)S(1)}, bf16[48,5120]{1,0:T(8,128)(2,1)S(1)}, u32[]{:S(2)}, u32[]{:S(2)}) %collective-permute-start.12) | collective-permute-done | bytes 491552 | tf_op jit(solution)/shard_map/ppermute | solution.py:27
  138.0 0.2 add_convert_fusion
  138.2 7.0 %collective-permute-start.25 = (bf16[320,640]{1,0:T(8,128)(2,1)S(1)}, bf16[320,640]{1,0:T(8,128)(2,1)S(1)}, u32[]{:S(2)}, u32[]{:S(2)}) collective-permute-start(bf16[320,640]{1,0:T(8,128)(2,1)S(1)} %get-tuple-element.47), channel_id=1, source_target_pairs={{0,96},{8,104},{16,112},{24,120},{32,0},{40,8},{48,16},{56,24},{64... | collective-permute-start | bytes 1228808 | tf_op jit(solution)/shard_map/ppermute | solution.py:37
  145.2 5.0 %shard_map.179.refs_8_ = bf16[384,640]{1,0:T(8,128)(2,1)S(1)} custom-call(bf16[640,5120]{1,0:T(8,128)(2,1)S(1)} %bitcast.34, bf16[384,5120]{1,0:T(8,128)(2,1)S(1)} %copy-done.2, bf16[320,640]{1,0:T(8,128)(2,1)S(1)} %get-tuple-element.36.refs_2_), custom_call_target="tpu_custom_call" | custom-call | flops 3774873600 | bytes 12582912 | tf_op jit(solution)/shard_map/pallas_call | solution.py:74
  150.4 2.0 collective-permute-start.29
  152.4 6.5 %shard_map.180 = (bf16[360,384]{1,0:T(8,128)(2,1)S(1)}, f32[2,360,384]{2,1,0:T(8,128)S(1)}, bf16[2,360,384]{2,1,0:T(8,128)(2,1)S(1)}, bf16[2,360,384]{2,1,0:T(8,128)(2,1)S(1)}) custom-call(bf16[360,640]{1,0:T(8,128)(2,1)S(1)} %bitcast.30, bf16[2,360,640]{2,1,0:T(8,128)(2,1)S(1)} %bitcast.25, bf16[360,640]{1,0:T(8,128)(2,1)S(1)} %collective-permute-done.refs_2_, ...), custom_call_target="tpu_custom_call" | custom-call | flops 2332800000 | bytes 6291456 | tf_op jit(solution)/shard_map/pallas_call | solution.py:74
  158.9 4.4 %shard_map.181 = (bf16[360,256]{1,0:T(8,128)(2,1)S(1)}, f32[2,360,256]{2,1,0:T(8,128)S(1)}, bf16[2,360,256]{2,1,0:T(8,128)(2,1)S(1)}, bf16[2,360,256]{2,1,0:T(8,128)(2,1)S(1)}) custom-call(bf16[360,640]{1,0:T(8,128)(2,1)S(1)} %bitcast.31, bf16[2,360,640]{2,1,0:T(8,128)(2,1)S(1)} %bitcast.27, bf16[360,640]{1,0:T(8,128)(2,1)S(1)} %collective-permute-done.refs_2_, ...), custom_call_target="tpu_custom_call" | custom-call | flops 1555200000 | bytes 4194304 | tf_op jit(solution)/shard_map/pallas_call | solution.py:74
  163.3 0.2 collective-permute-start.13
  163.4 1.3 collective-permute-start.22
  164.7 3.1 %collective-permute-start.23 = (bf16[2,360,256]{2,1,0:T(8,128)(2,1)S(1)}, bf16[2,360,256]{2,1,0:T(8,128)(2,1)S(1)}, u32[]{:S(2)}, u32[]{:S(2)}) collective-permute-start(bf16[2,360,256]{2,1,0:T(8,128)(2,1)S(1)} %get-tuple-element.44), channel_id=1, source_target_pairs={{0,8},{8,16},{16,24},{24,32},{32,40},{40,48},{48,56},{56,64},{64,7... | collective-permute-start | bytes 1105928 | tf_op jit(solution)/shard_map/ppermute | solution.py:394
  167.9 1.3 collective-permute-start.20
  169.2 4.1 %collective-permute-start.21 = (bf16[2,360,384]{2,1,0:T(8,128)(2,1)S(1)}, bf16[2,360,384]{2,1,0:T(8,128)(2,1)S(1)}, u32[]{:S(2)}, u32[]{:S(2)}) collective-permute-start(bf16[2,360,384]{2,1,0:T(8,128)(2,1)S(1)} %get-tuple-element.41), channel_id=1, source_target_pairs={{0,8},{8,16},{16,24},{24,32},{32,40},{40,48},{48,56},{56,64},{64,7... | collective-permute-start | bytes 1658888 | tf_op jit(solution)/shard_map/ppermute | solution.py:394
  173.3 0.2 add_convert_fusion.4
  173.5 4.0 %collective-permute-done.13.refs_3_ = bf16[48,5120]{1,0:T(8,128)(2,1)S(1)} collective-permute-done((bf16[48,5120]{1,0:T(8,128)(2,1)S(1)}, bf16[48,5120]{1,0:T(8,128)(2,1)S(1)}, u32[]{:S(2)}, u32[]{:S(2)}) %collective-permute-start.13) | collective-permute-done | bytes 491552 | tf_op jit(solution)/shard_map/ppermute | solution.py:27
  177.5 6.8 %collective-permute-start.26 = (bf16[320,640]{1,0:T(8,128)(2,1)S(1)}, bf16[320,640]{1,0:T(8,128)(2,1)S(1)}, u32[]{:S(2)}, u32[]{:S(2)}) collective-permute-start(bf16[320,640]{1,0:T(8,128)(2,1)S(1)} %add_convert_fusion.6), channel_id=1, source_target_pairs={{0,96},{8,104},{16,112},{24,120},{32,0},{40,8},{48,16},{56,24},{64... | collective-permute-start | bytes 1228808 | tf_op jit(solution)/shard_map/ppermute | solution.py:37
  184.3 1.2 shard_map.177.refs_6_
  185.5 0.8 pad_maximum_fusion
  186.3 1.1 copy-done.4
  187.4 1.3 shard_map.182
  188.7 4.3 %collective-permute-done.24 = bf16[320,640]{1,0:T(8,128)(2,1)S(1)} collective-permute-done((bf16[320,640]{1,0:T(8,128)(2,1)S(1)}, bf16[320,640]{1,0:T(8,128)(2,1)S(1)}, u32[]{:S(2)}, u32[]{:S(2)}) %collective-permute-start.24) | collective-permute-done | bytes 409632 | tf_op jit(solution)/shard_map/ppermute | solution.py:37
  193.0 0.2 collective-permute-done.26
  193.2 9.7 %collective-permute-done.30 = bf16[320,640]{1,0:T(8,128)(2,1)S(1)} collective-permute-done((bf16[320,640]{1,0:T(8,128)(2,1)S(1)}, bf16[320,640]{1,0:T(8,128)(2,1)S(1)}, u32[]{:S(2)}, u32[]{:S(2)}) %collective-permute-start.30) | collective-permute-done | bytes 409632 | tf_op jit(solution)/shard_map/ppermute | solution.py:37
  202.9 1.0 fusion.2
  (68 shorter events, 1.7 us)
Async XLA Ops:
  0.6 13.8 %copy-start = (s32[1,16,5,63]{3,1,2,0:T(8,128)S(1)}, s32[1,16,5,63]{3,1,2,0:T(8,128)}, u32[]{:S(2)}) copy-start(s32[1,16,5,63]{3,1,2,0:T(8,128)} %param.20) | copy-start | bytes 60484
  0.6 13.9 %copy-start.5 = (s32[5,5,7]{2,1,0:T(8,128)S(1)}, s32[5,5,7]{2,1,0:T(8,128)}, u32[]{:S(2)}) copy-start(s32[5,5,7]{2,1,0:T(8,128)} %constant.168) | copy-start | bytes 2104
  0.7 14.7 %copy-start.6 = (s32[5,5]{1,0:T(8,128)S(1)}, s32[5,5]{1,0:T(8,128)}, u32[]{:S(2)}) copy-start(s32[5,5]{1,0:T(8,128)} %constant.167) | copy-start | bytes 304
  0.7 13.7 %copy-start.7 = (s32[5,3]{0,1:T(4,128)S(1)}, s32[5,3]{0,1:T(4,128)}, u32[]{:S(2)}) copy-start(s32[5,3]{0,1:T(4,128)} %param.19) | copy-start | bytes 184
  2.7 85.9 %collective-permute-start.1 = (bf16[360,640]{1,0:T(8,128)(2,1)}, bf16[360,640]{1,0:T(8,128)(2,1)S(1)}, u32[]{:S(2)}, u32[]{:S(2)}) collective-permute-start(bf16[360,640]{1,0:T(8,128)(2,1)} %bitcast.2), channel_id=1, source_target_pairs={{8,0},{16,8},{24,16},{32,24},{40,32},{48,40},{56,48},{64,56},{72,6... | collective-permute-start | bytes 1382408 | tf_op jit(solution)/shard_map/ppermute | solution.py:243
  4.0 84.6 %collective-permute-start = (bf16[360,640]{1,0:T(8,128)(2,1)}, bf16[360,640]{1,0:T(8,128)(2,1)S(1)}, u32[]{:S(2)}, u32[]{:S(2)}) collective-permute-start(bf16[360,640]{1,0:T(8,128)(2,1)} %bitcast.2), channel_id=1, source_target_pairs={{0,8},{8,16},{16,24},{24,32},{32,40},{40,48},{48,56},{56,64},{64,7... | collective-permute-start | bytes 1382408 | tf_op jit(solution)/shard_map/ppermute | solution.py:242
  9.4 18.4 %collective-permute-start.14 = (bf16[48,5120]{1,0:T(8,128)(2,1)S(1)}, bf16[48,5120]{1,0:T(8,128)(2,1)S(1)}, u32[]{:S(2)}, u32[]{:S(2)}) collective-permute-start(bf16[48,5120]{1,0:T(8,128)(2,1)S(1)} %get-tuple-element.55), channel_id=1, source_target_pairs={{0,2},{1,3},{2,4},{3,5},{4,6},{5,7},{6,0},{7,1},{8,10},{9,11},{10,... | collective-permute-start | bytes 1474568 | tf_op jit(solution)/shard_map/ppermute | solution.py:27
  11.0 20.2 %collective-permute-start.5 = (bf16[48,5120]{1,0:T(8,128)(2,1)S(1)}, bf16[48,5120]{1,0:T(8,128)(2,1)S(1)}, u32[]{:S(2)}, u32[]{:S(2)}) collective-permute-start(bf16[48,5120]{1,0:T(8,128)(2,1)S(1)} %get-tuple-element.55), channel_id=1, source_target_pairs={{0,1},{1,0},{2,3},{3,2},{4,5},{5,4},{6,7},{7,6},{8,9},{9,8},{10,11... | collective-permute-start | bytes 1474568 | tf_op jit(solution)/shard_map/ppermute | solution.py:27
  12.6 13.1 %collective-permute-start.4 = (bf16[48,5120]{1,0:T(8,128)(2,1)S(1)}, bf16[48,5120]{1,0:T(8,128)(2,1)S(1)}, u32[]{:S(2)}, u32[]{:S(2)}) collective-permute-start(bf16[48,5120]{1,0:T(8,128)(2,1)S(1)} %get-tuple-element.55), channel_id=1, source_target_pairs={{0,6},{1,7},{2,0},{3,1},{4,2},{5,3},{6,4},{7,5},{8,14},{9,15},{10,... | collective-permute-start | bytes 1474568 | tf_op jit(solution)/shard_map/ppermute | solution.py:27
  16.4 72.2 %copy-start.1 = (bf16[2,3,3,40,640]{4,3,2,1,0:T(8,128)(2,1)S(1)}, bf16[2,3,3,40,640]{4,3,2,1,0:T(8,128)(2,1)}, u32[]{:S(2)}) copy-start(bf16[2,3,3,40,640]{4,3,2,1,0:T(8,128)(2,1)} %param.16) | copy-start | bytes 2764804
  16.4 72.2 %copy-start.3 = (bf16[3,3,40,640]{3,2,1,0:T(8,128)(2,1)S(1)}, bf16[3,3,40,640]{3,2,1,0:T(8,128)(2,1)}, u32[]{:S(2)}) copy-start(bf16[3,3,40,640]{3,2,1,0:T(8,128)(2,1)} %param.15) | copy-start | bytes 1382404
  25.6 68.2 %collective-permute-start.3 = (bf16[360,640]{1,0:T(8,128)(2,1)S(1)}, bf16[360,640]{1,0:T(8,128)(2,1)S(1)}, u32[]{:S(2)}, u32[]{:S(2)}) collective-permute-start(bf16[360,640]{1,0:T(8,128)(2,1)S(1)} %bitcast.37), channel_id=1, source_target_pairs={{8,0},{16,8},{24,16},{32,24},{40,32},{48,40},{56,48},{64,56},{72,6... | collective-permute-start | bytes 1382408 | tf_op jit(solution)/shard_map/ppermute | solution.py:243
  27.8 66.1 %collective-permute-start.2 = (bf16[360,640]{1,0:T(8,128)(2,1)S(1)}, bf16[360,640]{1,0:T(8,128)(2,1)S(1)}, u32[]{:S(2)}, u32[]{:S(2)}) collective-permute-start(bf16[360,640]{1,0:T(8,128)(2,1)S(1)} %bitcast.38), channel_id=1, source_target_pairs={{0,8},{8,16},{16,24},{24,32},{32,40},{40,48},{48,56},{56,64},{64,7... | collective-permute-start | bytes 1382408 | tf_op jit(solution)/shard_map/ppermute | solution.py:242
  31.2 13.1 %collective-permute-start.6 = (bf16[48,5120]{1,0:T(8,128)(2,1)S(1)}, bf16[48,5120]{1,0:T(8,128)(2,1)S(1)}, u32[]{:S(2)}, u32[]{:S(2)}) collective-permute-start(bf16[48,5120]{1,0:T(8,128)(2,1)S(1)} %collective-permute-done.5), channel_id=1, source_target_pairs={{0,2},{1,3},{2,4},{3,5},{4,6},{5,7},{6,0},{7,1},{8,10},{9,11},{10,... | collective-permute-start | bytes 1474568 | tf_op jit(solution)/shard_map/ppermute | solution.py:27
  44.3 13.0 %collective-permute-start.15 = (bf16[48,5120]{1,0:T(8,128)(2,1)S(1)}, bf16[48,5120]{1,0:T(8,128)(2,1)S(1)}, u32[]{:S(2)}, u32[]{:S(2)}) collective-permute-start(bf16[48,5120]{1,0:T(8,128)(2,1)S(1)} %collective-permute-done.5), channel_id=1, source_target_pairs={{0,6},{1,7},{2,0},{3,1},{4,2},{5,3},{6,4},{7,5},{8,14},{9,15},{10,... | collective-permute-start | bytes 1474568 | tf_op jit(solution)/shard_map/ppermute | solution.py:27
  57.3 14.6 %collective-permute-start.16 = (bf16[48,5120]{1,0:T(8,128)(2,1)S(1)}, bf16[48,5120]{1,0:T(8,128)(2,1)S(1)}, u32[]{:S(2)}, u32[]{:S(2)}) collective-permute-start(bf16[48,5120]{1,0:T(8,128)(2,1)S(1)} %collective-permute-done.4.refs_5_), channel_id=1, source_target_pairs={{0,6},{1,7},{2,0},{3,1},{4,2},{5,3},{6,4},{7,5},{8,14},{9,15},{10,... | collective-permute-start | bytes 1474568 | tf_op jit(solution)/shard_map/ppermute | solution.py:27
  71.9 15.1 %collective-permute-start.17 = (bf16[48,5120]{1,0:T(8,128)(2,1)S(1)}, bf16[48,5120]{1,0:T(8,128)(2,1)S(1)}, u32[]{:S(2)}, u32[]{:S(2)}) collective-permute-start(bf16[48,5120]{1,0:T(8,128)(2,1)S(1)} %collective-permute-done.6.refs_6_), channel_id=1, source_target_pairs={{0,2},{1,3},{2,4},{3,5},{4,6},{5,7},{6,0},{7,1},{8,10},{9,11},{10,... | collective-permute-start | bytes 1474568 | tf_op jit(solution)/shard_map/ppermute | solution.py:27
  87.8 34.0 %collective-permute-start.18 = (bf16[384,5120]{1,0:T(8,128)(2,1)}, bf16[384,5120]{1,0:T(8,128)(2,1)S(1)}, u32[]{:S(2)}, u32[]{:S(2)}) collective-permute-start(bf16[384,5120]{1,0:T(8,128)(2,1)} %constant_dynamic-update-slice_fusion.refs_1_), channel_id=1, source_target_pairs={{0,8},{8,0},{16,24},{24,16},{32,40},{40,32},{48,56},{56,48},{64,72... | collective-permute-start | bytes 11796488 | tf_op jit(solution)/shard_map/ppermute | solution.py:37
  88.6 8.8 %slice-start = ((s8[6553600]{0:T(1024)(128)(4,1)}), s8[4194304]{0:T(1024)(128)(4,1)S(1)}, s32[]{:S(2)}) async-start(s8[6553600]{0:T(1024)(128)(4,1)} %bitcast.33), calls=%async_computation | async-start | bytes 8388608
  93.8 3.6 %slice-start.1 = ((s8[6553600]{0:T(1024)(128)(4,1)}), s8[2359296]{0:T(1024)(128)(4,1)S(1)}, s32[]{:S(2)}) async-start(s8[6553600]{0:T(1024)(128)(4,1)} %bitcast.33), calls=%async_computation.1 | async-start | bytes 4718592
  97.4 24.3 %copy-start.2 = (bf16[384,5120]{1,0:T(8,128)(2,1)S(1)}, bf16[384,5120]{1,0:T(8,128)(2,1)}, u32[]{:S(2)}) copy-start(bf16[384,5120]{1,0:T(8,128)(2,1)} %constant_dynamic-update-slice_fusion.refs_1_) | copy-start | bytes 11796484
  102.0 15.4 %collective-permute-start.11 = (bf16[48,5120]{1,0:T(8,128)(2,1)S(1)}, bf16[48,5120]{1,0:T(8,128)(2,1)S(1)}, u32[]{:S(2)}, u32[]{:S(2)}) collective-permute-start(bf16[48,5120]{1,0:T(8,128)(2,1)S(1)} %get-tuple-element.35), channel_id=1, source_target_pairs={{0,2},{1,3},{2,4},{3,5},{4,6},{5,7},{6,0},{7,1},{8,10},{9,11},{10,... | collective-permute-start | bytes 1474568 | tf_op jit(solution)/shard_map/ppermute | solution.py:27
  102.1 17.6 %collective-permute-start.19 = (bf16[384,640]{1,0:T(8,128)(2,1)S(1)}, bf16[384,640]{1,0:T(8,128)(2,1)S(1)}, u32[]{:S(2)}, u32[]{:S(2)}) collective-permute-start(bf16[384,640]{1,0:T(8,128)(2,1)S(1)} %shard_map.175.refs_0_.refs_3_), channel_id=1, source_target_pairs={{0,8},{8,0},{16,24},{24,16},{32,40},{40,32},{48,56},{56,48},{64,72... | collective-permute-start | bytes 1474568 | tf_op jit(solution)/shard_map/ppermute | solution.py:37
  102.7 60.6 %collective-permute-start.7 = (bf16[48,5120]{1,0:T(8,128)(2,1)S(1)}, bf16[48,5120]{1,0:T(8,128)(2,1)S(1)}, u32[]{:S(2)}, u32[]{:S(2)}) collective-permute-start(bf16[48,5120]{1,0:T(8,128)(2,1)S(1)} %get-tuple-element.29), channel_id=1, source_target_pairs={{0,2},{1,3},{2,4},{3,5},{4,6},{5,7},{6,0},{7,1},{8,10},{9,11},{10,... | collective-permute-start | bytes 1474568 | tf_op jit(solution)/shard_map/ppermute | solution.py:27
  103.0 15.0 %collective-permute-start.8 = (bf16[48,5120]{1,0:T(8,128)(2,1)S(1)}, bf16[48,5120]{1,0:T(8,128)(2,1)S(1)}, u32[]{:S(2)}, u32[]{:S(2)}) collective-permute-start(bf16[48,5120]{1,0:T(8,128)(2,1)S(1)} %get-tuple-element.31), channel_id=1, source_target_pairs={{0,6},{1,7},{2,0},{3,1},{4,2},{5,3},{6,4},{7,5},{8,14},{9,15},{10,... | collective-permute-start | bytes 1474568 | tf_op jit(solution)/shard_map/ppermute | solution.py:27
  117.4 14.1 %collective-permute-start.10 = (bf16[48,5120]{1,0:T(8,128)(2,1)S(1)}, bf16[48,5120]{1,0:T(8,128)(2,1)S(1)}, u32[]{:S(2)}, u32[]{:S(2)}) collective-permute-start(bf16[48,5120]{1,0:T(8,128)(2,1)S(1)} %get-tuple-element.33), channel_id=1, source_target_pairs={{0,6},{1,7},{2,0},{3,1},{4,2},{5,3},{6,4},{7,5},{8,14},{9,15},{10,... | collective-permute-start | bytes 1474568 | tf_op jit(solution)/shard_map/ppermute | solution.py:27
  118.1 19.9 %collective-permute-start.12 = (bf16[48,5120]{1,0:T(8,128)(2,1)S(1)}, bf16[48,5120]{1,0:T(8,128)(2,1)S(1)}, u32[]{:S(2)}, u32[]{:S(2)}) collective-permute-start(bf16[48,5120]{1,0:T(8,128)(2,1)S(1)} %add_convert_fusion.1), channel_id=1, source_target_pairs={{0,2},{1,3},{2,4},{3,5},{4,6},{5,7},{6,0},{7,1},{8,10},{9,11},{10,... | collective-permute-start | bytes 1474568 | tf_op jit(solution)/shard_map/ppermute | solution.py:27
  119.7 43.7 %collective-permute-start.9 = (bf16[48,5120]{1,0:T(8,128)(2,1)S(1)}, bf16[48,5120]{1,0:T(8,128)(2,1)S(1)}, u32[]{:S(2)}, u32[]{:S(2)}) collective-permute-start(bf16[48,5120]{1,0:T(8,128)(2,1)S(1)} %add_convert_fusion.2), channel_id=1, source_target_pairs={{0,6},{1,7},{2,0},{3,1},{4,2},{5,3},{6,4},{7,5},{8,14},{9,15},{10,... | collective-permute-start | bytes 1474568 | tf_op jit(solution)/shard_map/ppermute | solution.py:27
  125.7 24.6 %collective-permute-start.28 = (bf16[320,640]{1,0:T(8,128)(2,1)S(1)}, bf16[320,640]{1,0:T(8,128)(2,1)S(1)}, u32[]{:S(2)}, u32[]{:S(2)}) collective-permute-start(bf16[320,640]{1,0:T(8,128)(2,1)S(1)} %get-tuple-element.51), channel_id=1, source_target_pairs={{0,32},{8,40},{16,48},{24,56},{32,64},{40,72},{48,80},{56,88},{64,... | collective-permute-start | bytes 1228808 | tf_op jit(solution)/shard_map/ppermute | solution.py:37
  138.2 26.6 %collective-permute-start.25 = (bf16[320,640]{1,0:T(8,128)(2,1)S(1)}, bf16[320,640]{1,0:T(8,128)(2,1)S(1)}, u32[]{:S(2)}, u32[]{:S(2)}) collective-permute-start(bf16[320,640]{1,0:T(8,128)(2,1)S(1)} %get-tuple-element.47), channel_id=1, source_target_pairs={{0,96},{8,104},{16,112},{24,120},{32,0},{40,8},{48,16},{56,24},{64... | collective-permute-start | bytes 1228808 | tf_op jit(solution)/shard_map/ppermute | solution.py:37
  145.2 22.8 %collective-permute-start.27 = (bf16[320,640]{1,0:T(8,128)(2,1)S(1)}, bf16[320,640]{1,0:T(8,128)(2,1)S(1)}, u32[]{:S(2)}, u32[]{:S(2)}) collective-permute-start(bf16[320,640]{1,0:T(8,128)(2,1)S(1)} %get-tuple-element.49), channel_id=1, source_target_pairs={{0,96},{8,104},{16,112},{24,120},{32,0},{40,8},{48,16},{56,24},{64... | collective-permute-start | bytes 1228808 | tf_op jit(solution)/shard_map/ppermute | solution.py:37
  150.4 18.9 %collective-permute-start.29 = (bf16[320,640]{1,0:T(8,128)(2,1)S(1)}, bf16[320,640]{1,0:T(8,128)(2,1)S(1)}, u32[]{:S(2)}, u32[]{:S(2)}) collective-permute-start(bf16[320,640]{1,0:T(8,128)(2,1)S(1)} %add_convert_fusion.5), channel_id=1, source_target_pairs={{0,32},{8,40},{16,48},{24,56},{32,64},{40,72},{48,80},{56,88},{64,... | collective-permute-start | bytes 1228808 | tf_op jit(solution)/shard_map/ppermute | solution.py:37
  163.3 14.2 %collective-permute-start.13 = (bf16[48,5120]{1,0:T(8,128)(2,1)S(1)}, bf16[48,5120]{1,0:T(8,128)(2,1)S(1)}, u32[]{:S(2)}, u32[]{:S(2)}) collective-permute-start(bf16[48,5120]{1,0:T(8,128)(2,1)S(1)} %add_convert_fusion), channel_id=1, source_target_pairs={{0,1},{1,0},{2,3},{3,2},{4,5},{5,4},{6,7},{7,6},{8,9},{9,8},{10,11... | collective-permute-start | bytes 1474568 | tf_op jit(solution)/shard_map/ppermute | solution.py:27
  163.4 14.0 %collective-permute-start.22 = (bf16[2,360,256]{2,1,0:T(8,128)(2,1)S(1)}, bf16[2,360,256]{2,1,0:T(8,128)(2,1)S(1)}, u32[]{:S(2)}, u32[]{:S(2)}) collective-permute-start(bf16[2,360,256]{2,1,0:T(8,128)(2,1)S(1)} %get-tuple-element.43), channel_id=1, source_target_pairs={{8,0},{16,8},{24,16},{32,24},{40,32},{48,40},{56,48},{64,56},{72,6... | collective-permute-start | bytes 1105928 | tf_op jit(solution)/shard_map/ppermute | solution.py:393
  164.7 19.5 %collective-permute-start.23 = (bf16[2,360,256]{2,1,0:T(8,128)(2,1)S(1)}, bf16[2,360,256]{2,1,0:T(8,128)(2,1)S(1)}, u32[]{:S(2)}, u32[]{:S(2)}) collective-permute-start(bf16[2,360,256]{2,1,0:T(8,128)(2,1)S(1)} %get-tuple-element.44), channel_id=1, source_target_pairs={{0,8},{8,16},{16,24},{24,32},{32,40},{40,48},{48,56},{56,64},{64,7... | collective-permute-start | bytes 1105928 | tf_op jit(solution)/shard_map/ppermute | solution.py:394
  167.9 18.4 %collective-permute-start.20 = (bf16[2,360,384]{2,1,0:T(8,128)(2,1)S(1)}, bf16[2,360,384]{2,1,0:T(8,128)(2,1)S(1)}, u32[]{:S(2)}, u32[]{:S(2)}) collective-permute-start(bf16[2,360,384]{2,1,0:T(8,128)(2,1)S(1)} %get-tuple-element.38.refs_10_), channel_id=1, source_target_pairs={{8,0},{16,8},{24,16},{32,24},{40,32},{48,40},{56,48},{64,56},{72,6... | collective-permute-start | bytes 1658888 | tf_op jit(solution)/shard_map/ppermute | solution.py:393
  169.2 17.1 %collective-permute-start.21 = (bf16[2,360,384]{2,1,0:T(8,128)(2,1)S(1)}, bf16[2,360,384]{2,1,0:T(8,128)(2,1)S(1)}, u32[]{:S(2)}, u32[]{:S(2)}) collective-permute-start(bf16[2,360,384]{2,1,0:T(8,128)(2,1)S(1)} %get-tuple-element.41), channel_id=1, source_target_pairs={{0,8},{8,16},{16,24},{24,32},{32,40},{40,48},{48,56},{56,64},{64,7... | collective-permute-start | bytes 1658888 | tf_op jit(solution)/shard_map/ppermute | solution.py:394
  177.5 15.5 %collective-permute-start.24 = (bf16[320,640]{1,0:T(8,128)(2,1)S(1)}, bf16[320,640]{1,0:T(8,128)(2,1)S(1)}, u32[]{:S(2)}, u32[]{:S(2)}) collective-permute-start(bf16[320,640]{1,0:T(8,128)(2,1)S(1)} %get-tuple-element.45), channel_id=1, source_target_pairs={{0,32},{8,40},{16,48},{24,56},{32,64},{40,72},{48,80},{56,88},{64,... | collective-permute-start | bytes 1228808 | tf_op jit(solution)/shard_map/ppermute | solution.py:37
  177.5 15.7 %collective-permute-start.26 = (bf16[320,640]{1,0:T(8,128)(2,1)S(1)}, bf16[320,640]{1,0:T(8,128)(2,1)S(1)}, u32[]{:S(2)}, u32[]{:S(2)}) collective-permute-start(bf16[320,640]{1,0:T(8,128)(2,1)S(1)} %add_convert_fusion.6), channel_id=1, source_target_pairs={{0,96},{8,104},{16,112},{24,120},{32,0},{40,8},{48,16},{56,24},{64... | collective-permute-start | bytes 1228808 | tf_op jit(solution)/shard_map/ppermute | solution.py:37
  184.3 18.7 %collective-permute-start.30 = (bf16[320,640]{1,0:T(8,128)(2,1)S(1)}, bf16[320,640]{1,0:T(8,128)(2,1)S(1)}, u32[]{:S(2)}, u32[]{:S(2)}) collective-permute-start(bf16[320,640]{1,0:T(8,128)(2,1)S(1)} %add_convert_fusion.4), channel_id=1, source_target_pairs={{0,16},{8,24},{16,0},{24,8},{32,48},{40,56},{48,32},{56,40},{64,80... | collective-permute-start | bytes 1228808 | tf_op jit(solution)/shard_map/ppermute | solution.py:37
  186.3 1.1 copy-start.4

commit v4 on v3

--- a/solution.py
+++ b/solution.py
@@ -175,28 +175,27 @@
         out_ref[...] = dot(turned, attended, ((1,), (0,))).astype(BF16)
 
 
+STEPS = 4
+
+
 def project_kernel(att_ref, w_ref, *outs):
-    mixed = dot(att_ref[...], w_ref[...], ((1,), (0,)))
     room = outs[0].shape[0]
-    for k, out_ref in enumerate(outs):
-        out_ref[...] = mixed[k * room : (k + 1) * room].astype(BF16)
-
-
-def attn_grad_kernel(w_ref, g_ref, ga_ref, total_ref):
-    step = pl.program_id(0)
-    part = dot(g_ref[...], w_ref[...], ((1,), (1,)))
-
-    @pl.when(step == 0)
-    def _():
-        total_ref[...] = part
-
-    @pl.when(step > 0)
-    def _():
-        total_ref[...] += part
-
-    @pl.when(step == pl.num_programs(0) - 1)
-    def _():
-        ga_ref[...] = total_ref[...].astype(BF16)
+    width = w_ref.shape[1] // STEPS
+    for i in range(STEPS):
+        columns = slice(i * width, (i + 1) * width)
+        mixed = dot(att_ref[...], w_ref[:, columns], ((1,), (0,)))
+        for k, out_ref in enumerate(outs):
+            out_ref[:, columns] = mixed[k * room : (k + 1) * room].astype(BF16)
+
+
+def attn_grad_kernel(w_ref, g_ref, ga_ref):
+    width = w_ref.shape[1] // STEPS
+    total = None
+    for i in range(STEPS):
+        columns = slice(i * width, (i + 1) * width)
+        part = dot(g_ref[:, columns], w_ref[:, columns], ((1,), (1,)))
+        total = part if total is None else total + part
+    ga_ref[...] = total.astype(BF16)
 
 
 def mask_bias(window, own_mask, seq_place, row_tiles):
@@ -308,20 +307,25 @@
     far_grad = seq_shift(all_grad, 0, 0, 1)
     far_attended = seq_shift(attended, 0, 0, 1)
 
-    broad = model_width // 4
     mixed = kernel(
         project_kernel,
         [((room, model_width), BF16)] * 8,
         [attended, out_weight],
-        [whole((slots, channels)), pl.BlockSpec((channels, broad), lambda i: (0, i))],
-        [pl.BlockSpec((room, broad), lambda i: (0, i))] * 8,
-        grid=(4,),
         flops=slots * model_width * channels * 3,
         moved=12 << 20,
     )
     mixed = dict(zip(BLOCKS, mixed))
     mixed_far = hop(tensor_shift, (mixed[2, 1], mixed[2, 0]))
     mixed_near = hop(tensor_shift, (mixed[1, 0], mixed[3, 1]))
+
+    (grad_attn,) = kernel(
+        attn_grad_kernel,
+        [((slots, channels), BF16)],
+        [out_weight, all_grad],
+        after=[mixed[0, 0]],
+        flops=slots * model_width * channels * 3,
+        moved=12 << 20,
+    )
 
     narrow = model_width // row_tiles
     weight = kernel(
@@ -329,29 +333,13 @@
         [((narrow, channels), BF16)] * 8,
         [order, all_grad, far_grad, attended, far_attended],
         [SCALAR] + [VECTOR] * 4,
-        after=[mixed[0, 0]],
+        after=[grad_attn],
         flops=slots * model_width * channels * 2,
         moved=6 << 20,
     )
     weight = dict(zip(weights, weight))
     weight_far = hop(seq_shift, (weight[2, 1], weight[2, 0]))
     weight_near = hop(seq_shift, (weight[1, 0], weight[3, 1]))
-
-    (grad_attn,) = kernel(
-        attn_grad_kernel,
-        [((slots, channels), BF16)],
-        [out_weight, all_grad],
-        [
-            pl.BlockSpec((channels, broad), lambda i: (0, i)),
-            pl.BlockSpec((slots, broad), lambda i: (0, i)),
-        ],
-        [whole((slots, channels))],
-        grid=(4,),
-        after=[weight[0, 0]],
-        flops=slots * model_width * channels * 3,
-        moved=12 << 20,
-        scratch=[pltpu.VMEM((slots, channels), F32)],
-    )
 
     def differentiate(first, count, after):
         def spec(shape, at):
@@ -395,7 +383,7 @@
         return from_below, from_above
 
     split = (heads + 1) // 2
-    gq_a, own_a, *ends_a = differentiate(0, split, [])
+    gq_a, own_a, *ends_a = differentiate(0, split, [weight[0, 0]])
     halo_a = send_halo(*ends_a)
     gq_b, own_b, *ends_b = differentiate(split, heads - split, ends_a[:1])
     halo_b = send_halo(*ends_b)

time: 204 us -> 205 us (level)
  local copies, waits for them, and re-layouts: 11.5 us -> 19.4 us
  waiting for transfers between devices: 92.3 us -> 84.7 us
    ppermute x14, waiting for transfers between devices: 78 us -> 70.4 us  [tensor_shift(): return lax.ppermute(value, 'tensor', pairs)]
    unnamed x27 -> x51, local copies, waits for them, and re-layouts: 6.92 us -> 13.8 us
  transfers between devices with their start and end apart: 31 -> 31, of which waited for: 12 -> 12; matrix products, arithmetic and copies ran while one was open for 6% -> 9% of each run, Pallas kernels for 17% -> 17%
where the time goes in v4:
time: 205 us
  waiting for transfers between devices  84.7 us (41%)
  starting transfers between devices  58.2 us (28%)
  Pallas kernels  34.1 us (17%)
  local copies, waits for them, and re-layouts  19.4 us (9%)
  other arithmetic  7.02 us (3%)
    ppermute x14, waiting for transfers between devices, tensor_shift(): return lax.ppermute(value, 'tensor', pairs)  70.4 us
    pallas_call x9, Pallas kernels, kernel(): pl.pallas_call(run, grid=grid, in_specs=[*specs, *[ANYWHERE] * len(after)...  34.1 us
    ppermute x9, starting transfers between devices, seq_shift(): return lax.ppermute(value, 'seq', pairs)  20.6 us
    ppermute x14, starting transfers between devices, tensor_shift(): return lax.ppermute(value, 'tensor', pairs)  18.8 us
    ppermute x9, waiting for transfers between devices, seq_shift(): return lax.ppermute(value, 'seq', pairs)  14.3 us
    unnamed x51, local copies, waits for them, and re-layouts  13.8 us
    ppermute x2, starting transfers between devices, send_halo(): from_above = lax.ppermute(grad_down, 'seq', onward)  7.1 us
    ppermute x2, starting transfers between devices, layer(): up = lax.ppermute(flat_kv[i], 'seq', onward)  6.45 us
  transfers between devices with their start and end apart: 31, of which 12 were waited for; matrix products, arithmetic and copies ran while one was open for 9% of the time, Pallas kernels for 17%

profile of v4, /device:TPU:0, one launch (start us, length us, event | category | flops | bytes accessed | tf_op | source)
XLA Modules:
  0.0 204.6 jit_solution(3424522349083970163)
XLA Ops:
  0.7 2.3 %fusion.22 = (bf16[1,3,3,40,640]{4,3,2,1,0:T(8,128)(2,1)}, bf16[1,3,3,40,640]{4,3,2,1,0:T(8,128)(2,1)}) fusion(bf16[2,3,3,40,640]{4,3,2,1,0:T(8,128)(2,1)} %param.16), kind=kLoop, calls=%fused_computation.78 | loop fusion | bytes 1843200 | tf_op jit(solution)/shard_map/slice | solution.py:241
  3.0 1.3 collective-permute-start.1
  4.3 3.1 %collective-permute-start = (bf16[360,640]{1,0:T(8,128)(2,1)}, bf16[360,640]{1,0:T(8,128)(2,1)S(1)}, u32[]{:S(2)}, u32[]{:S(2)}) collective-permute-start(bf16[360,640]{1,0:T(8,128)(2,1)} %bitcast.2), channel_id=1, source_target_pairs={{0,8},{8,16},{16,24},{24,32},{32,40},{40,48},{48,56},{56,64},{64,7... | collective-permute-start | bytes 1382408 | tf_op jit(solution)/shard_map/ppermute | solution.py:241
  7.3 1.5 reshape.160
  8.8 1.0 constant_dynamic-update-slice_fusion.7
  9.8 1.6 collective-permute-start.14
  11.5 1.6 collective-permute-start.5
  13.0 1.7 collective-permute-start.4
  15.7 0.8 fusion.3.refs_5_
  16.9 0.9 fusion.refs_6_.refs_4_
  17.7 0.7 broadcast_bitcast_fusion.refs_4_
  18.5 7.8 %collective-permute-done.4.refs_5_ = bf16[48,5120]{1,0:T(8,128)(2,1)S(1)} collective-permute-done((bf16[48,5120]{1,0:T(8,128)(2,1)}, bf16[48,5120]{1,0:T(8,128)(2,1)S(1)}, u32[]{:S(2)}, u32[]{:S(2)}) %collective-permute-start.4) | collective-permute-done | bytes 491552 | tf_op jit(solution)/shard_map/ppermute | solution.py:27
  26.3 0.8 copy-done.6
  27.1 1.4 collective-permute-start.3
  28.5 1.9 constant_dynamic-update-slice_fusion.6
  30.4 3.4 %collective-permute-start.2 = (bf16[360,640]{1,0:T(8,128)(2,1)}, bf16[360,640]{1,0:T(8,128)(2,1)S(1)}, u32[]{:S(2)}, u32[]{:S(2)}) collective-permute-start(bf16[360,640]{1,0:T(8,128)(2,1)} %bitcast.38), channel_id=1, source_target_pairs={{0,8},{8,16},{16,24},{24,32},{32,40},{40,48},{48,56},{56,64},{64,7... | collective-permute-start | bytes 1382408 | tf_op jit(solution)/shard_map/ppermute | solution.py:241
  33.8 1.6 collective-permute-start.6
  35.4 1.8 constant_dynamic-update-slice_fusion.5
  37.2 1.8 constant_dynamic-update-slice_fusion.4
  39.0 8.1 %collective-permute-done.6.refs_6_ = bf16[48,5120]{1,0:T(8,128)(2,1)S(1)} collective-permute-done((bf16[48,5120]{1,0:T(8,128)(2,1)}, bf16[48,5120]{1,0:T(8,128)(2,1)S(1)}, u32[]{:S(2)}, u32[]{:S(2)}) %collective-permute-start.6) | collective-permute-done | bytes 491552 | tf_op jit(solution)/shard_map/ppermute | solution.py:27
  47.1 1.8 collective-permute-start.15
  48.9 0.8 constant_dynamic-update-slice_fusion.3
  49.7 10.6 %collective-permute-done.15 = bf16[48,5120]{1,0:T(8,128)(2,1)S(1)} collective-permute-done((bf16[48,5120]{1,0:T(8,128)(2,1)}, bf16[48,5120]{1,0:T(8,128)(2,1)S(1)}, u32[]{:S(2)}, u32[]{:S(2)}) %collective-permute-start.15) | collective-permute-done | bytes 491552 | tf_op jit(solution)/shard_map/ppermute | solution.py:27
  60.3 3.0 %collective-permute-start.16 = (bf16[48,5120]{1,0:T(8,128)(2,1)S(1)}, bf16[48,5120]{1,0:T(8,128)(2,1)S(1)}, u32[]{:S(2)}, u32[]{:S(2)}) collective-permute-start(bf16[48,5120]{1,0:T(8,128)(2,1)S(1)} %copy-done.7), channel_id=1, source_target_pairs={{0,6},{1,7},{2,0},{3,1},{4,2},{5,3},{6,4},{7,5},{8,14},{9,15},{10,... | collective-permute-start | bytes 1474568 | tf_op jit(solution)/shard_map/ppermute | solution.py:27
  63.3 0.8 constant_dynamic-update-slice_fusion.2
  64.1 10.8 %collective-permute-done.16 = bf16[48,5120]{1,0:T(8,128)(2,1)S(1)} collective-permute-done((bf16[48,5120]{1,0:T(8,128)(2,1)S(1)}, bf16[48,5120]{1,0:T(8,128)(2,1)S(1)}, u32[]{:S(2)}, u32[]{:S(2)}) %collective-permute-start.16) | collective-permute-done | bytes 491552 | tf_op jit(solution)/shard_map/ppermute | solution.py:27
  74.9 0.8 constant_dynamic-update-slice_fusion.1
  75.7 14.3 %collective-permute-done.17 = bf16[48,5120]{1,0:T(8,128)(2,1)S(1)} collective-permute-done((bf16[48,5120]{1,0:T(8,128)(2,1)S(1)}, bf16[48,5120]{1,0:T(8,128)(2,1)S(1)}, u32[]{:S(2)}, u32[]{:S(2)}) %collective-permute-start.17) | collective-permute-done | bytes 491552 | tf_op jit(solution)/shard_map/ppermute | solution.py:27
  90.0 0.9 constant_dynamic-update-slice_fusion.refs_1_
  90.9 1.2 fusion.17
  92.1 0.7 pad_add_fusion.refs_8_.refs_0_
  92.8 1.0 copy-done.4
  93.8 1.0 copy-done.11
  94.8 0.9 copy-done.12
  95.7 5.2 %shard_map.174.refs_0_.refs_7_ = bf16[5,3,360,360]{3,2,1,0:T(8,128)(2,1)S(1)} custom-call(bf16[360,640]{1,0:T(8,128)(2,1)S(1)} %bitcast.29, bf16[2,360,640]{2,1,0:T(8,128)(2,1)S(1)} %bitcast.23, bf16[360,640]{1,0:T(8,128)(2,1)S(1)} %collective-permute-done.refs_2_, bf16[360,640]{1,0:T(8,128)(2,1)S(1)} %collective-permute-done.1.refs_3_, ...), custom_call_target="tpu_custom_call" | custom-call | flops 1944000000 | bytes 6291456 | tf_op jit(solution)/shard_map/pallas_call | solution.py:74
  100.9 3.5 %shard_map.175.refs_0_.refs_3_ = bf16[384,640]{1,0:T(8,128)(2,1)S(1)} custom-call(bf16[5,3,360,360]{3,2,1,0:T(8,128)(2,1)S(1)} %shard_map.174.refs_0_.refs_7_, bf16[2,360,640]{2,1,0:T(8,128)(2,1)S(1)} %bitcast.24, bf16[360,640]{1,0:T(8,128)(2,1)S(1)} %collective-permute-done.2.refs_2_.refs_5_, bf16[360,640]{1,0:T(8,128)(2,1)S(1)} %collective-permute-done.3.refs_3_.refs_6_, ...), custom_call_target="tpu_custom_call" | custom-call | flops 972000000 | bytes 6291456 | tf_op jit(solution)/shard_map/pallas_call | solution.py:74
  104.5 3.3 %shard_map.176 = (bf16[48,5120]{1,0:T(8,128)(2,1)S(1)}, bf16[48,5120]{1,0:T(8,128)(2,1)S(1)}, bf16[48,5120]{1,0:T(8,128)(2,1)S(1)}, bf16[48,5120]{1,0:T(8,128)(2...) custom-call(bf16[384,640]{1,0:T(8,128)(2,1)S(1)} %shard_map.175.refs, ...), custom_call_target="tpu_custom_call" | custom-call | flops 3774873600 | bytes 12582912 | tf_op jit(solution)/shard_map/pallas_call | solution.py:74
  107.8 0.6 collective-permute-start.19
  108.7 2.9 %collective-permute-start.8 = (bf16[48,5120]{1,0:T(8,128)(2,1)S(1)}, bf16[48,5120]{1,0:T(8,128)(2,1)S(1)}, u32[]{:S(2)}, u32[]{:S(2)}) collective-permute-start(bf16[48,5120]{1,0:T(8,128)(2,1)S(1)} %get-tuple-element.31), channel_id=1, source_target_pairs={{0,6},{1,7},{2,0},{3,1},{4,2},{5,3},{6,4},{7,5},{8,14},{9,15},{10,... | collective-permute-start | bytes 1474568 | tf_op jit(solution)/shard_map/ppermute | solution.py:27
  111.7 11.5 %collective-permute-done.11 = bf16[48,5120]{1,0:T(8,128)(2,1)S(1)} collective-permute-done((bf16[48,5120]{1,0:T(8,128)(2,1)S(1)}, bf16[48,5120]{1,0:T(8,128)(2,1)S(1)}, u32[]{:S(2)}, u32[]{:S(2)}) %collective-permute-start.11) | collective-permute-done | bytes 491552 | tf_op jit(solution)/shard_map/ppermute | solution.py:27
  123.1 0.5 collective-permute-start.10
  123.8 1.7 collective-permute-start.12
  125.7 3.2 %shard_map.178.refs_5_.refs_8_ = bf16[384,640]{1,0:T(8,128)(2,1)S(1)} custom-call(bf16[640,5120]{1,0:T(8,128)(2,1)S(1)} %bitcast.34, bf16[384,5120]{1,0:T(8,128)(2,1)S(1)} %copy-done.2, bf16[48,5120]{1,0:T(8,128)(2,1)S(1)} %get-tuple-element.28.refs_0_.refs_2_), custom_call_target="tpu_custom_call" | custom-call | flops 3774873600 | bytes 12582912 | tf_op jit(solution)/shard_map/pallas_call | solution.py:74
  128.9 1.8 collective-permute-start.9
  130.7 5.5 %shard_map.179 = (bf16[320,640]{1,0:T(8,128)(2,1)S(1)}, bf16[320,640]{1,0:T(8,128)(2,1)S(1)}, bf16[320,640]{1,0:T(8,128)(2,1)S(1)}, bf16[320,640]{1,0:T(8,128)(2...) custom-call(s32[9]{0:T(128)S(1)} %pad_add_fusion.refs_8_.refs_0_, ...), custom_call_target="tpu_custom_call" | custom-call | flops 2516582400 | bytes 6291456 | tf_op jit(solution)/shard_map/pallas_call | solution.py:74
  136.2 4.2 %collective-permute-start.28 = (bf16[320,640]{1,0:T(8,128)(2,1)S(1)}, bf16[320,640]{1,0:T(8,128)(2,1)S(1)}, u32[]{:S(2)}, u32[]{:S(2)}) collective-permute-start(bf16[320,640]{1,0:T(8,128)(2,1)S(1)} %get-tuple-element.51), channel_id=1, source_target_pairs={{0,32},{8,40},{16,48},{24,56},{32,64},{40,72},{48,80},{56,88},{64,... | collective-permute-start | bytes 1228808 | tf_op jit(solution)/shard_map/ppermute | solution.py:37
  140.4 3.4 %collective-permute-done.12 = bf16[48,5120]{1,0:T(8,128)(2,1)S(1)} collective-permute-done((bf16[48,5120]{1,0:T(8,128)(2,1)S(1)}, bf16[48,5120]{1,0:T(8,128)(2,1)S(1)}, u32[]{:S(2)}, u32[]{:S(2)}) %collective-permute-start.12) | collective-permute-done | bytes 491552 | tf_op jit(solution)/shard_map/ppermute | solution.py:27
  143.9 7.0 %collective-permute-start.25 = (bf16[320,640]{1,0:T(8,128)(2,1)S(1)}, bf16[320,640]{1,0:T(8,128)(2,1)S(1)}, u32[]{:S(2)}, u32[]{:S(2)}) collective-permute-start(bf16[320,640]{1,0:T(8,128)(2,1)S(1)} %get-tuple-element.47), channel_id=1, source_target_pairs={{0,96},{8,104},{16,112},{24,120},{32,0},{40,8},{48,16},{56,24},{64... | collective-permute-start | bytes 1228808 | tf_op jit(solution)/shard_map/ppermute | solution.py:37
  151.3 1.8 collective-permute-start.29
  153.1 6.5 %shard_map.180 = (bf16[360,384]{1,0:T(8,128)(2,1)S(1)}, f32[2,360,384]{2,1,0:T(8,128)S(1)}, bf16[2,360,384]{2,1,0:T(8,128)(2,1)S(1)}, bf16[2,360,384]{2,1,0:T(8,128)(2,1)S(1)}) custom-call(bf16[360,640]{1,0:T(8,128)(2,1)S(1)} %bitcast.30, bf16[2,360,640]{2,1,0:T(8,128)(2,1)S(1)} %bitcast.25, bf16[360,640]{1,0:T(8,128)(2,1)S(1)} %collective-permute-done.refs_2_, ...), custom_call_target="tpu_custom_call" | custom-call | flops 2332800000 | bytes 6291456 | tf_op jit(solution)/shard_map/pallas_call | solution.py:74
  159.6 4.4 %shard_map.181 = (bf16[360,256]{1,0:T(8,128)(2,1)S(1)}, f32[2,360,256]{2,1,0:T(8,128)S(1)}, bf16[2,360,256]{2,1,0:T(8,128)(2,1)S(1)}, bf16[2,360,256]{2,1,0:T(8,128)(2,1)S(1)}) custom-call(bf16[360,640]{1,0:T(8,128)(2,1)S(1)} %bitcast.31, bf16[2,360,640]{2,1,0:T(8,128)(2,1)S(1)} %bitcast.27, bf16[360,640]{1,0:T(8,128)(2,1)S(1)} %collective-permute-done.refs_2_, ...), custom_call_target="tpu_custom_call" | custom-call | flops 1555200000 | bytes 4194304 | tf_op jit(solution)/shard_map/pallas_call | solution.py:74
  164.2 1.3 collective-permute-start.22
  165.5 3.1 %collective-permute-start.23 = (bf16[2,360,256]{2,1,0:T(8,128)(2,1)S(1)}, bf16[2,360,256]{2,1,0:T(8,128)(2,1)S(1)}, u32[]{:S(2)}, u32[]{:S(2)}) collective-permute-start(bf16[2,360,256]{2,1,0:T(8,128)(2,1)S(1)} %get-tuple-element.44), channel_id=1, source_target_pairs={{0,8},{8,16},{16,24},{24,32},{32,40},{40,48},{48,56},{56,64},{64,7... | collective-permute-start | bytes 1105928 | tf_op jit(solution)/shard_map/ppermute | solution.py:382
  168.7 1.3 collective-permute-start.20
  170.0 4.0 %collective-permute-start.21 = (bf16[2,360,384]{2,1,0:T(8,128)(2,1)S(1)}, bf16[2,360,384]{2,1,0:T(8,128)(2,1)S(1)}, u32[]{:S(2)}, u32[]{:S(2)}) collective-permute-start(bf16[2,360,384]{2,1,0:T(8,128)(2,1)S(1)} %get-tuple-element.41), channel_id=1, source_target_pairs={{0,8},{8,16},{16,24},{24,32},{32,40},{40,48},{48,56},{56,64},{64,7... | collective-permute-start | bytes 1658888 | tf_op jit(solution)/shard_map/ppermute | solution.py:382
  174.2 4.0 %collective-permute-done.13.refs_3_ = bf16[48,5120]{1,0:T(8,128)(2,1)S(1)} collective-permute-done((bf16[48,5120]{1,0:T(8,128)(2,1)S(1)}, bf16[48,5120]{1,0:T(8,128)(2,1)S(1)}, u32[]{:S(2)}, u32[]{:S(2)}) %collective-permute-start.13) | collective-permute-done | bytes 491552 | tf_op jit(solution)/shard_map/ppermute | solution.py:27
  178.2 6.9 %collective-permute-start.26 = (bf16[320,640]{1,0:T(8,128)(2,1)S(1)}, bf16[320,640]{1,0:T(8,128)(2,1)S(1)}, u32[]{:S(2)}, u32[]{:S(2)}) collective-permute-start(bf16[320,640]{1,0:T(8,128)(2,1)S(1)} %add_convert_fusion.6), channel_id=1, source_target_pairs={{0,96},{8,104},{16,112},{24,120},{32,0},{40,8},{48,16},{56,24},{64... | collective-permute-start | bytes 1228808 | tf_op jit(solution)/shard_map/ppermute | solution.py:37
  185.2 1.2 shard_map.177.refs_6_
  186.4 0.8 pad_maximum_fusion
  187.2 1.1 copy-done.5
  188.3 1.3 shard_map.182
  189.5 4.2 %collective-permute-done.24 = bf16[320,640]{1,0:T(8,128)(2,1)S(1)} collective-permute-done((bf16[320,640]{1,0:T(8,128)(2,1)S(1)}, bf16[320,640]{1,0:T(8,128)(2,1)S(1)}, u32[]{:S(2)}, u32[]{:S(2)}) %collective-permute-start.24) | collective-permute-done | bytes 409632 | tf_op jit(solution)/shard_map/ppermute | solution.py:37
  193.9 9.7 %collective-permute-done.30 = bf16[320,640]{1,0:T(8,128)(2,1)S(1)} collective-permute-done((bf16[320,640]{1,0:T(8,128)(2,1)S(1)}, bf16[320,640]{1,0:T(8,128)(2,1)S(1)}, u32[]{:S(2)}, u32[]{:S(2)}) %collective-permute-start.30) | collective-permute-done | bytes 409632 | tf_op jit(solution)/shard_map/ppermute | solution.py:37
  203.7 1.0 fusion.2
  (92 shorter events, 3.2 us)
Async XLA Ops:
  0.6 14.2 %copy-start = (s32[1,16,5,63]{3,1,2,0:T(8,128)S(1)}, s32[1,16,5,63]{3,1,2,0:T(8,128)}, u32[]{:S(2)}) copy-start(s32[1,16,5,63]{3,1,2,0:T(8,128)} %param.20) | copy-start | bytes 60484
  0.6 14.3 %copy-start.13 = (s32[5,5,7]{2,1,0:T(8,128)S(1)}, s32[5,5,7]{2,1,0:T(8,128)}, u32[]{:S(2)}) copy-start(s32[5,5,7]{2,1,0:T(8,128)} %constant.168) | copy-start | bytes 2104
  0.7 15.8 %copy-start.15 = (s32[384]{0:T(512)S(1)}, s32[384]{0:T(512)}, u32[]{:S(2)}) copy-start(s32[384]{0:T(512)} %constant.169) | copy-start | bytes 4612
  0.7 15.8 %copy-start.18 = (pred[384]{0:T(512)(128)(4,1)S(1)}, pred[384]{0:T(512)(128)(4,1)}, u32[]{:S(2)}) copy-start(pred[384]{0:T(512)(128)(4,1)} %constant.154.clone) | copy-start | bytes 1156
  0.7 15.8 %copy-start.16 = (s32[384]{0:T(512)S(1)}, s32[384]{0:T(512)}, u32[]{:S(2)}) copy-start(s32[384]{0:T(512)} %constant.151.clone) | copy-start | bytes 4612
  0.7 15.7 %copy-start.17 = (s32[384]{0:T(512)S(1)}, s32[384]{0:T(512)}, u32[]{:S(2)}) copy-start(s32[384]{0:T(512)} %constant.150.clone) | copy-start | bytes 4612
  0.7 15.9 %copy-start.14 = (s32[5,5]{1,0:T(8,128)S(1)}, s32[5,5]{1,0:T(8,128)}, u32[]{:S(2)}) copy-start(s32[5,5]{1,0:T(8,128)} %constant.167) | copy-start | bytes 304
  0.7 14.1 %copy-start.19 = (s32[5,3]{0,1:T(4,128)S(1)}, s32[5,3]{0,1:T(4,128)}, u32[]{:S(2)}) copy-start(s32[5,3]{0,1:T(4,128)} %param.19) | copy-start | bytes 184
  3.0 89.8 %collective-permute-start.1 = (bf16[360,640]{1,0:T(8,128)(2,1)}, bf16[360,640]{1,0:T(8,128)(2,1)S(1)}, u32[]{:S(2)}, u32[]{:S(2)}) collective-permute-start(bf16[360,640]{1,0:T(8,128)(2,1)} %bitcast.2), channel_id=1, source_target_pairs={{8,0},{16,8},{24,16},{32,24},{40,32},{48,40},{56,48},{64,56},{72,6... | collective-permute-start | bytes 1382408 | tf_op jit(solution)/shard_map/ppermute | solution.py:242
  4.3 88.5 %collective-permute-start = (bf16[360,640]{1,0:T(8,128)(2,1)}, bf16[360,640]{1,0:T(8,128)(2,1)S(1)}, u32[]{:S(2)}, u32[]{:S(2)}) collective-permute-start(bf16[360,640]{1,0:T(8,128)(2,1)} %bitcast.2), channel_id=1, source_target_pairs={{0,8},{8,16},{16,24},{24,32},{32,40},{40,48},{48,56},{56,64},{64,7... | collective-permute-start | bytes 1382408 | tf_op jit(solution)/shard_map/ppermute | solution.py:241
  9.8 20.5 %collective-permute-start.14 = (bf16[48,5120]{1,0:T(8,128)(2,1)}, bf16[48,5120]{1,0:T(8,128)(2,1)}, u32[]{:S(2)}, u32[]{:S(2)}) collective-permute-start(bf16[48,5120]{1,0:T(8,128)(2,1)} %get-tuple-element.55), channel_id=1, source_target_pairs={{0,2},{1,3},{2,4},{3,5},{4,6},{5,7},{6,0},{7,1},{8,10},{9,11},{10,... | collective-permute-start | bytes 1474568 | tf_op jit(solution)/shard_map/ppermute | solution.py:27
  11.5 22.3 %collective-permute-start.5 = (bf16[48,5120]{1,0:T(8,128)(2,1)}, bf16[48,5120]{1,0:T(8,128)(2,1)}, u32[]{:S(2)}, u32[]{:S(2)}) collective-permute-start(bf16[48,5120]{1,0:T(8,128)(2,1)} %get-tuple-element.55), channel_id=1, source_target_pairs={{0,1},{1,0},{2,3},{3,2},{4,5},{5,4},{6,7},{7,6},{8,9},{9,8},{10,11... | collective-permute-start | bytes 1474568 | tf_op jit(solution)/shard_map/ppermute | solution.py:27
  13.0 13.3 %collective-permute-start.4 = (bf16[48,5120]{1,0:T(8,128)(2,1)}, bf16[48,5120]{1,0:T(8,128)(2,1)S(1)}, u32[]{:S(2)}, u32[]{:S(2)}) collective-permute-start(bf16[48,5120]{1,0:T(8,128)(2,1)} %get-tuple-element.55), channel_id=1, source_target_pairs={{0,6},{1,7},{2,0},{3,1},{4,2},{5,3},{6,4},{7,5},{8,14},{9,15},{10,... | collective-permute-start | bytes 1474568 | tf_op jit(solution)/shard_map/ppermute | solution.py:27
  16.5 76.3 %copy-start.1 = (bf16[2,3,3,40,640]{4,3,2,1,0:T(8,128)(2,1)S(1)}, bf16[2,3,3,40,640]{4,3,2,1,0:T(8,128)(2,1)}, u32[]{:S(2)}) copy-start(bf16[2,3,3,40,640]{4,3,2,1,0:T(8,128)(2,1)} %param.16) | copy-start | bytes 2764804
  16.6 76.3 %copy-start.3 = (bf16[3,3,40,640]{3,2,1,0:T(8,128)(2,1)S(1)}, bf16[3,3,40,640]{3,2,1,0:T(8,128)(2,1)}, u32[]{:S(2)}) copy-start(bf16[3,3,40,640]{3,2,1,0:T(8,128)(2,1)} %param.15) | copy-start | bytes 1382404
  26.3 0.8 copy-start.6
  27.1 33.2 %copy-start.7 = (bf16[48,5120]{1,0:T(8,128)(2,1)S(1)}, bf16[48,5120]{1,0:T(8,128)(2,1)}, u32[]{:S(2)}) copy-start(bf16[48,5120]{1,0:T(8,128)(2,1)} %copy-done.6) | copy-start | bytes 1474564
  27.1 73.8 %collective-permute-start.3 = (bf16[360,640]{1,0:T(8,128)(2,1)}, bf16[360,640]{1,0:T(8,128)(2,1)S(1)}, u32[]{:S(2)}, u32[]{:S(2)}) collective-permute-start(bf16[360,640]{1,0:T(8,128)(2,1)} %bitcast.37), channel_id=1, source_target_pairs={{8,0},{16,8},{24,16},{32,24},{40,32},{48,40},{56,48},{64,56},{72,6... | collective-permute-start | bytes 1382408 | tf_op jit(solution)/shard_map/ppermute | solution.py:242
  30.4 70.5 %collective-permute-start.2 = (bf16[360,640]{1,0:T(8,128)(2,1)}, bf16[360,640]{1,0:T(8,128)(2,1)S(1)}, u32[]{:S(2)}, u32[]{:S(2)}) collective-permute-start(bf16[360,640]{1,0:T(8,128)(2,1)} %bitcast.38), channel_id=1, source_target_pairs={{0,8},{8,16},{16,24},{24,32},{32,40},{40,48},{48,56},{56,64},{64,7... | collective-permute-start | bytes 1382408 | tf_op jit(solution)/shard_map/ppermute | solution.py:241
  33.8 13.3 %collective-permute-start.6 = (bf16[48,5120]{1,0:T(8,128)(2,1)}, bf16[48,5120]{1,0:T(8,128)(2,1)S(1)}, u32[]{:S(2)}, u32[]{:S(2)}) collective-permute-start(bf16[48,5120]{1,0:T(8,128)(2,1)} %collective-permute-done.5), channel_id=1, source_target_pairs={{0,2},{1,3},{2,4},{3,5},{4,6},{5,7},{6,0},{7,1},{8,10},{9,11},{10,... | collective-permute-start | bytes 1474568 | tf_op jit(solution)/shard_map/ppermute | solution.py:27
  47.1 27.8 %copy-start.9 = (bf16[48,5120]{1,0:T(8,128)(2,1)}, bf16[48,5120]{1,0:T(8,128)(2,1)S(1)}, u32[]{:S(2)}) copy-start(bf16[48,5120]{1,0:T(8,128)(2,1)S(1)} %collective-permute-done.6.refs_6_) | copy-start | bytes 1474564
  47.1 13.2 %collective-permute-start.15 = (bf16[48,5120]{1,0:T(8,128)(2,1)}, bf16[48,5120]{1,0:T(8,128)(2,1)S(1)}, u32[]{:S(2)}, u32[]{:S(2)}) collective-permute-start(bf16[48,5120]{1,0:T(8,128)(2,1)} %collective-permute-done.5), channel_id=1, source_target_pairs={{0,6},{1,7},{2,0},{3,1},{4,2},{5,3},{6,4},{7,5},{8,14},{9,15},{10,... | collective-permute-start | bytes 1474568 | tf_op jit(solution)/shard_map/ppermute | solution.py:27
  60.3 14.6 %collective-permute-start.16 = (bf16[48,5120]{1,0:T(8,128)(2,1)S(1)}, bf16[48,5120]{1,0:T(8,128)(2,1)S(1)}, u32[]{:S(2)}, u32[]{:S(2)}) collective-permute-start(bf16[48,5120]{1,0:T(8,128)(2,1)S(1)} %copy-done.7), channel_id=1, source_target_pairs={{0,6},{1,7},{2,0},{3,1},{4,2},{5,3},{6,4},{7,5},{8,14},{9,15},{10,... | collective-permute-start | bytes 1474568 | tf_op jit(solution)/shard_map/ppermute | solution.py:27
  74.9 15.1 %collective-permute-start.17 = (bf16[48,5120]{1,0:T(8,128)(2,1)S(1)}, bf16[48,5120]{1,0:T(8,128)(2,1)S(1)}, u32[]{:S(2)}, u32[]{:S(2)}) collective-permute-start(bf16[48,5120]{1,0:T(8,128)(2,1)S(1)} %collective-permute-done.6.refs_6_), channel_id=1, source_target_pairs={{0,2},{1,3},{2,4},{3,5},{4,6},{5,7},{6,0},{7,1},{8,10},{9,11},{10,... | collective-permute-start | bytes 1474568 | tf_op jit(solution)/shard_map/ppermute | solution.py:27
  90.9 39.8 %collective-permute-start.18 = (bf16[384,5120]{1,0:T(8,128)(2,1)}, bf16[384,5120]{1,0:T(8,128)(2,1)}, u32[]{:S(2)}, u32[]{:S(2)}) collective-permute-start(bf16[384,5120]{1,0:T(8,128)(2,1)} %constant_dynamic-update-slice_fusion.refs_1_), channel_id=1, source_target_pairs={{0,8},{8,0},{16,24},{24,16},{32,40},{40,32},{48,56},{56,48},{64,72... | collective-permute-start | bytes 11796488 | tf_op jit(solution)/shard_map/ppermute | solution.py:37
  92.8 1.0 copy-start.4
  93.8 1.0 copy-start.11
  94.8 0.9 copy-start.12
  95.6 5.2 %copy-start.8 = (bf16[48,5120]{1,0:T(8,128)(2,1)S(1)}, bf16[48,5120]{1,0:T(8,128)(2,1)}, u32[]{:S(2)}) copy-start(bf16[48,5120]{1,0:T(8,128)(2,1)} %copy-done.6) | copy-start | bytes 1474564
  95.7 5.2 %copy-start.10 = (bf16[48,5120]{1,0:T(8,128)(2,1)S(1)}, bf16[48,5120]{1,0:T(8,128)(2,1)}, u32[]{:S(2)}) copy-start(bf16[48,5120]{1,0:T(8,128)(2,1)} %copy-done.9) | copy-start | bytes 1474564
  95.7 8.8 %slice-start = ((s8[6553600]{0:T(1024)(128)(4,1)}), s8[4194304]{0:T(1024)(128)(4,1)S(1)}, s32[]{:S(2)}) async-start(s8[6553600]{0:T(1024)(128)(4,1)} %bitcast.33), calls=%async_computation | async-start | bytes 8388608
  100.8 3.6 %slice-start.1 = ((s8[6553600]{0:T(1024)(128)(4,1)}), s8[2359296]{0:T(1024)(128)(4,1)S(1)}, s32[]{:S(2)}) async-start(s8[6553600]{0:T(1024)(128)(4,1)} %bitcast.33), calls=%async_computation.1 | async-start | bytes 4718592
  104.4 21.2 %copy-start.2 = (bf16[384,5120]{1,0:T(8,128)(2,1)S(1)}, bf16[384,5120]{1,0:T(8,128)(2,1)}, u32[]{:S(2)}) copy-start(bf16[384,5120]{1,0:T(8,128)(2,1)} %constant_dynamic-update-slice_fusion.refs_1_) | copy-start | bytes 11796484
  107.8 15.4 %collective-permute-start.11 = (bf16[48,5120]{1,0:T(8,128)(2,1)S(1)}, bf16[48,5120]{1,0:T(8,128)(2,1)S(1)}, u32[]{:S(2)}, u32[]{:S(2)}) collective-permute-start(bf16[48,5120]{1,0:T(8,128)(2,1)S(1)} %get-tuple-element.35), channel_id=1, source_target_pairs={{0,2},{1,3},{2,4},{3,5},{4,6},{5,7},{6,0},{7,1},{8,10},{9,11},{10,... | collective-permute-start | bytes 1474568 | tf_op jit(solution)/shard_map/ppermute | solution.py:27
  107.8 21.1 %collective-permute-start.19 = (bf16[384,640]{1,0:T(8,128)(2,1)S(1)}, bf16[384,640]{1,0:T(8,128)(2,1)S(1)}, u32[]{:S(2)}, u32[]{:S(2)}) collective-permute-start(bf16[384,640]{1,0:T(8,128)(2,1)S(1)} %shard_map.175.refs_0_.refs_3_), channel_id=1, source_target_pairs={{0,8},{8,0},{16,24},{24,16},{32,40},{40,32},{48,56},{56,48},{64,72... | collective-permute-start | bytes 1474568 | tf_op jit(solution)/shard_map/ppermute | solution.py:37
  108.4 55.6 %collective-permute-start.7 = (bf16[48,5120]{1,0:T(8,128)(2,1)S(1)}, bf16[48,5120]{1,0:T(8,128)(2,1)S(1)}, u32[]{:S(2)}, u32[]{:S(2)}) collective-permute-start(bf16[48,5120]{1,0:T(8,128)(2,1)S(1)} %get-tuple-element.29), channel_id=1, source_target_pairs={{0,2},{1,3},{2,4},{3,5},{4,6},{5,7},{6,0},{7,1},{8,10},{9,11},{10,... | collective-permute-start | bytes 1474568 | tf_op jit(solution)/shard_map/ppermute | solution.py:27
  108.7 15.1 %collective-permute-start.8 = (bf16[48,5120]{1,0:T(8,128)(2,1)S(1)}, bf16[48,5120]{1,0:T(8,128)(2,1)S(1)}, u32[]{:S(2)}, u32[]{:S(2)}) collective-permute-start(bf16[48,5120]{1,0:T(8,128)(2,1)S(1)} %get-tuple-element.31), channel_id=1, source_target_pairs={{0,6},{1,7},{2,0},{3,1},{4,2},{5,3},{6,4},{7,5},{8,14},{9,15},{10,... | collective-permute-start | bytes 1474568 | tf_op jit(solution)/shard_map/ppermute | solution.py:27
  123.1 17.2 %collective-permute-start.10 = (bf16[48,5120]{1,0:T(8,128)(2,1)S(1)}, bf16[48,5120]{1,0:T(8,128)(2,1)S(1)}, u32[]{:S(2)}, u32[]{:S(2)}) collective-permute-start(bf16[48,5120]{1,0:T(8,128)(2,1)S(1)} %get-tuple-element.33), channel_id=1, source_target_pairs={{0,6},{1,7},{2,0},{3,1},{4,2},{5,3},{6,4},{7,5},{8,14},{9,15},{10,... | collective-permute-start | bytes 1474568 | tf_op jit(solution)/shard_map/ppermute | solution.py:27
  123.8 19.9 %collective-permute-start.12 = (bf16[48,5120]{1,0:T(8,128)(2,1)S(1)}, bf16[48,5120]{1,0:T(8,128)(2,1)S(1)}, u32[]{:S(2)}, u32[]{:S(2)}) collective-permute-start(bf16[48,5120]{1,0:T(8,128)(2,1)S(1)} %add_convert_fusion.1), channel_id=1, source_target_pairs={{0,2},{1,3},{2,4},{3,5},{4,6},{5,7},{6,0},{7,1},{8,10},{9,11},{10,... | collective-permute-start | bytes 1474568 | tf_op jit(solution)/shard_map/ppermute | solution.py:27
  128.9 35.3 %collective-permute-start.9 = (bf16[48,5120]{1,0:T(8,128)(2,1)S(1)}, bf16[48,5120]{1,0:T(8,128)(2,1)S(1)}, u32[]{:S(2)}, u32[]{:S(2)}) collective-permute-start(bf16[48,5120]{1,0:T(8,128)(2,1)S(1)} %add_convert_fusion.2), channel_id=1, source_target_pairs={{0,6},{1,7},{2,0},{3,1},{4,2},{5,3},{6,4},{7,5},{8,14},{9,15},{10,... | collective-permute-start | bytes 1474568 | tf_op jit(solution)/shard_map/ppermute | solution.py:27
  136.2 15.0 %collective-permute-start.28 = (bf16[320,640]{1,0:T(8,128)(2,1)S(1)}, bf16[320,640]{1,0:T(8,128)(2,1)S(1)}, u32[]{:S(2)}, u32[]{:S(2)}) collective-permute-start(bf16[320,640]{1,0:T(8,128)(2,1)S(1)} %get-tuple-element.51), channel_id=1, source_target_pairs={{0,32},{8,40},{16,48},{24,56},{32,64},{40,72},{48,80},{56,88},{64,... | collective-permute-start | bytes 1228808 | tf_op jit(solution)/shard_map/ppermute | solution.py:37
  143.9 21.6 %collective-permute-start.25 = (bf16[320,640]{1,0:T(8,128)(2,1)S(1)}, bf16[320,640]{1,0:T(8,128)(2,1)S(1)}, u32[]{:S(2)}, u32[]{:S(2)}) collective-permute-start(bf16[320,640]{1,0:T(8,128)(2,1)S(1)} %get-tuple-element.47), channel_id=1, source_target_pairs={{0,96},{8,104},{16,112},{24,120},{32,0},{40,8},{48,16},{56,24},{64... | collective-permute-start | bytes 1228808 | tf_op jit(solution)/shard_map/ppermute | solution.py:37
  150.9 17.8 %collective-permute-start.27 = (bf16[320,640]{1,0:T(8,128)(2,1)S(1)}, bf16[320,640]{1,0:T(8,128)(2,1)S(1)}, u32[]{:S(2)}, u32[]{:S(2)}) collective-permute-start(bf16[320,640]{1,0:T(8,128)(2,1)S(1)} %get-tuple-element.49), channel_id=1, source_target_pairs={{0,96},{8,104},{16,112},{24,120},{32,0},{40,8},{48,16},{56,24},{64... | collective-permute-start | bytes 1228808 | tf_op jit(solution)/shard_map/ppermute | solution.py:37
  151.3 18.7 %collective-permute-start.29 = (bf16[320,640]{1,0:T(8,128)(2,1)S(1)}, bf16[320,640]{1,0:T(8,128)(2,1)S(1)}, u32[]{:S(2)}, u32[]{:S(2)}) collective-permute-start(bf16[320,640]{1,0:T(8,128)(2,1)S(1)} %add_convert_fusion.5), channel_id=1, source_target_pairs={{0,32},{8,40},{16,48},{24,56},{32,64},{40,72},{48,80},{56,88},{64,... | collective-permute-start | bytes 1228808 | tf_op jit(solution)/shard_map/ppermute | solution.py:37
  164.0 14.2 %collective-permute-start.13 = (bf16[48,5120]{1,0:T(8,128)(2,1)S(1)}, bf16[48,5120]{1,0:T(8,128)(2,1)S(1)}, u32[]{:S(2)}, u32[]{:S(2)}) collective-permute-start(bf16[48,5120]{1,0:T(8,128)(2,1)S(1)} %add_convert_fusion), channel_id=1, source_target_pairs={{0,1},{1,0},{2,3},{3,2},{4,5},{5,4},{6,7},{7,6},{8,9},{9,8},{10,11... | collective-permute-start | bytes 1474568 | tf_op jit(solution)/shard_map/ppermute | solution.py:27
  164.2 14.0 %collective-permute-start.22 = (bf16[2,360,256]{2,1,0:T(8,128)(2,1)S(1)}, bf16[2,360,256]{2,1,0:T(8,128)(2,1)S(1)}, u32[]{:S(2)}, u32[]{:S(2)}) collective-permute-start(bf16[2,360,256]{2,1,0:T(8,128)(2,1)S(1)} %get-tuple-element.43), channel_id=1, source_target_pairs={{8,0},{16,8},{24,16},{32,24},{40,32},{48,40},{56,48},{64,56},{72,6... | collective-permute-start | bytes 1105928 | tf_op jit(solution)/shard_map/ppermute | solution.py:381
  165.5 19.7 %collective-permute-start.23 = (bf16[2,360,256]{2,1,0:T(8,128)(2,1)S(1)}, bf16[2,360,256]{2,1,0:T(8,128)(2,1)S(1)}, u32[]{:S(2)}, u32[]{:S(2)}) collective-permute-start(bf16[2,360,256]{2,1,0:T(8,128)(2,1)S(1)} %get-tuple-element.44), channel_id=1, source_target_pairs={{0,8},{8,16},{16,24},{24,32},{32,40},{40,48},{48,56},{56,64},{64,7... | collective-permute-start | bytes 1105928 | tf_op jit(solution)/shard_map/ppermute | solution.py:382
  168.7 18.5 %collective-permute-start.20 = (bf16[2,360,384]{2,1,0:T(8,128)(2,1)S(1)}, bf16[2,360,384]{2,1,0:T(8,128)(2,1)S(1)}, u32[]{:S(2)}, u32[]{:S(2)}) collective-permute-start(bf16[2,360,384]{2,1,0:T(8,128)(2,1)S(1)} %get-tuple-element.38.refs_10_), channel_id=1, source_target_pairs={{8,0},{16,8},{24,16},{32,24},{40,32},{48,40},{56,48},{64,56},{72,6... | collective-permute-start | bytes 1658888 | tf_op jit(solution)/shard_map/ppermute | solution.py:381
  170.0 17.2 %collective-permute-start.21 = (bf16[2,360,384]{2,1,0:T(8,128)(2,1)S(1)}, bf16[2,360,384]{2,1,0:T(8,128)(2,1)S(1)}, u32[]{:S(2)}, u32[]{:S(2)}) collective-permute-start(bf16[2,360,384]{2,1,0:T(8,128)(2,1)S(1)} %get-tuple-element.41), channel_id=1, source_target_pairs={{0,8},{8,16},{16,24},{24,32},{32,40},{40,48},{48,56},{56,64},{64,7... | collective-permute-start | bytes 1658888 | tf_op jit(solution)/shard_map/ppermute | solution.py:382
  178.2 15.5 %collective-permute-start.24 = (bf16[320,640]{1,0:T(8,128)(2,1)S(1)}, bf16[320,640]{1,0:T(8,128)(2,1)S(1)}, u32[]{:S(2)}, u32[]{:S(2)}) collective-permute-start(bf16[320,640]{1,0:T(8,128)(2,1)S(1)} %get-tuple-element.45), channel_id=1, source_target_pairs={{0,32},{8,40},{16,48},{24,56},{32,64},{40,72},{48,80},{56,88},{64,... | collective-permute-start | bytes 1228808 | tf_op jit(solution)/shard_map/ppermute | solution.py:37
  178.2 15.7 %collective-permute-start.26 = (bf16[320,640]{1,0:T(8,128)(2,1)S(1)}, bf16[320,640]{1,0:T(8,128)(2,1)S(1)}, u32[]{:S(2)}, u32[]{:S(2)}) collective-permute-start(bf16[320,640]{1,0:T(8,128)(2,1)S(1)} %add_convert_fusion.6), channel_id=1, source_target_pairs={{0,96},{8,104},{16,112},{24,120},{32,0},{40,8},{48,16},{56,24},{64... | collective-permute-start | bytes 1228808 | tf_op jit(solution)/shard_map/ppermute | solution.py:37
  185.2 18.5 %collective-permute-start.30 = (bf16[320,640]{1,0:T(8,128)(2,1)S(1)}, bf16[320,640]{1,0:T(8,128)(2,1)S(1)}, u32[]{:S(2)}, u32[]{:S(2)}) collective-permute-start(bf16[320,640]{1,0:T(8,128)(2,1)S(1)} %add_convert_fusion.4), channel_id=1, source_target_pairs={{0,16},{8,24},{16,0},{24,8},{32,48},{40,56},{48,32},{56,40},{64,80... | collective-permute-start | bytes 1228808 | tf_op jit(solution)/shard_map/ppermute | solution.py:37
  187.2 1.1 copy-start.5

commit v5 on v4

--- a/solution.py
+++ b/solution.py
@@ -326,20 +326,6 @@
         flops=slots * model_width * channels * 3,
         moved=12 << 20,
     )
-
-    narrow = model_width // row_tiles
-    weight = kernel(
-        weight_kernel,
-        [((narrow, channels), BF16)] * 8,
-        [order, all_grad, far_grad, attended, far_attended],
-        [SCALAR] + [VECTOR] * 4,
-        after=[grad_attn],
-        flops=slots * model_width * channels * 2,
-        moved=6 << 20,
-    )
-    weight = dict(zip(weights, weight))
-    weight_far = hop(seq_shift, (weight[2, 1], weight[2, 0]))
-    weight_near = hop(seq_shift, (weight[1, 0], weight[3, 1]))
 
     def differentiate(first, count, after):
         def spec(shape, at):
@@ -383,9 +369,23 @@
         return from_below, from_above
 
     split = (heads + 1) // 2
-    gq_a, own_a, *ends_a = differentiate(0, split, [weight[0, 0]])
+    gq_a, own_a, *ends_a = differentiate(0, split, [])
     halo_a = send_halo(*ends_a)
-    gq_b, own_b, *ends_b = differentiate(split, heads - split, ends_a[:1])
+    narrow = model_width // row_tiles
+    weight = kernel(
+        weight_kernel,
+        [((narrow, channels), BF16)] * 8,
+        [order, all_grad, far_grad, attended, far_attended],
+        [SCALAR] + [VECTOR] * 4,
+        after=ends_a[:1],
+        flops=slots * model_width * channels * 2,
+        moved=6 << 20,
+    )
+    weight = dict(zip(weights, weight))
+    weight_far = hop(seq_shift, (weight[2, 1], weight[2, 0]))
+    weight_near = hop(seq_shift, (weight[1, 0], weight[3, 1]))
+
+    gq_b, own_b, *ends_b = differentiate(split, heads - split, [weight[0, 0]])
     halo_b = send_halo(*ends_b)
 
     def relayed(kept, came, shift):

time: 205 us -> 210 us (1.024)
  the two profiles are of different devices: /device:TPU:0 before, /device:TPU:32 now
where the time goes in v5:
time: 210 us; the launch traced here: 209 us
  waiting for transfers between devices  82.6 us (39%)
  starting transfers between devices  71.4 us (34%)
  Pallas kernels  34 us (16%)
  local copies, waits for them, and re-layouts  16 us (8%)
  other arithmetic  3.76 us (2%)
    ppermute x14, waiting for transfers between devices, tensor_shift(): return lax.ppermute(value, 'tensor', pairs)  51.8 us
    pallas_call x9, Pallas kernels, kernel(): pl.pallas_call(run, grid=grid, in_specs=[*specs, *[ANYWHERE] * len(after)...  34 us
    ppermute x14, starting transfers between devices, tensor_shift(): return lax.ppermute(value, 'tensor', pairs)  17.8 us
    ppermute x9, starting transfers between devices, seq_shift(): return lax.ppermute(value, 'seq', pairs)  17.1 us
    ppermute x9, waiting for transfers between devices, seq_shift(): return lax.ppermute(value, 'seq', pairs)  15.9 us
    ppermute x2, waiting for transfers between devices, send_halo(): from_above = lax.ppermute(grad_down, 'seq', onward)  14.7 us
    ppermute x2, starting transfers between devices, layer(): down = lax.ppermute(flat_kv[i], 'seq', back)  12.1 us
    ppermute x2, starting transfers between devices, send_halo(): from_below = lax.ppermute(grad_up, 'seq', back)  11.9 us
  transfers between devices with their start and end apart: 31, of which 12 were waited for; matrix products, arithmetic and copies ran while one was open for 7% of the time, Pallas kernels for 16%

profile of v5, /device:TPU:32, one launch (start us, length us, event | category | flops | bytes accessed | tf_op | source)
XLA Modules:
  0.0 209.1 jit_solution(16926641175724586713)
XLA Ops:
  0.7 2.2 %fusion.22 = (bf16[1,3,3,40,640]{4,3,2,1,0:T(8,128)(2,1)}, bf16[1,3,3,40,640]{4,3,2,1,0:T(8,128)(2,1)}) fusion(bf16[2,3,3,40,640]{4,3,2,1,0:T(8,128)(2,1)} %param.16), kind=kLoop, calls=%fused_computation.78 | loop fusion | bytes 1843200 | tf_op jit(solution)/shard_map/slice | solution.py:241
  2.9 1.9 collective-permute-start
  4.8 6.0 %collective-permute-start.1 = (bf16[360,640]{1,0:T(8,128)(2,1)}, bf16[360,640]{1,0:T(8,128)(2,1)S(1)}, u32[]{:S(2)}, u32[]{:S(2)}) collective-permute-start(bf16[360,640]{1,0:T(8,128)(2,1)} %bitcast.2), channel_id=1, source_target_pairs={{8,0},{16,8},{24,16},{32,24},{40,32},{48,40},{56,48},{64,56},{72,6... | collective-permute-start | bytes 1382408 | tf_op jit(solution)/shard_map/ppermute | solution.py:242
  10.9 1.5 reshape.160
  12.3 1.0 constant_dynamic-update-slice_fusion.7
  13.4 2.8 %collective-permute-start.4 = (bf16[48,5120]{1,0:T(8,128)(2,1)}, bf16[48,5120]{1,0:T(8,128)(2,1)S(1)}, u32[]{:S(2)}, u32[]{:S(2)}) collective-permute-start(bf16[48,5120]{1,0:T(8,128)(2,1)} %get-tuple-element.55), channel_id=1, source_target_pairs={{0,6},{1,7},{2,0},{3,1},{4,2},{5,3},{6,4},{7,5},{8,14},{9,15},{10,... | collective-permute-start | bytes 1474568 | tf_op jit(solution)/shard_map/ppermute | solution.py:27
  16.2 1.6 collective-permute-start.5
  18.0 0.5 multiply_reduce_fusion
  18.7 0.1 copy.21
  19.1 7.2 %collective-permute-done.4.refs_5_ = bf16[48,5120]{1,0:T(8,128)(2,1)S(1)} collective-permute-done((bf16[48,5120]{1,0:T(8,128)(2,1)}, bf16[48,5120]{1,0:T(8,128)(2,1)S(1)}, u32[]{:S(2)}, u32[]{:S(2)}) %collective-permute-start.4) | collective-permute-done | bytes 491552 | tf_op jit(solution)/shard_map/ppermute | solution.py:27
  26.3 0.8 copy-done.5
  27.1 2.0 collective-permute-start.2
  29.2 2.0 constant_dynamic-update-slice_fusion.6
  31.2 6.0 %collective-permute-start.3 = (bf16[360,640]{1,0:T(8,128)(2,1)}, bf16[360,640]{1,0:T(8,128)(2,1)S(1)}, u32[]{:S(2)}, u32[]{:S(2)}) collective-permute-start(bf16[360,640]{1,0:T(8,128)(2,1)} %bitcast.10), channel_id=1, source_target_pairs={{8,0},{16,8},{24,16},{32,24},{40,32},{48,40},{56,48},{64,56},{72,6... | collective-permute-start | bytes 1382408 | tf_op jit(solution)/shard_map/ppermute | solution.py:242
  37.2 1.2 collective-permute-start.6
  38.4 1.9 constant_dynamic-update-slice_fusion.5
  40.3 1.9 constant_dynamic-update-slice_fusion.4
  42.1 8.0 %collective-permute-done.6.refs_6_ = bf16[48,5120]{1,0:T(8,128)(2,1)S(1)} collective-permute-done((bf16[48,5120]{1,0:T(8,128)(2,1)}, bf16[48,5120]{1,0:T(8,128)(2,1)S(1)}, u32[]{:S(2)}, u32[]{:S(2)}) %collective-permute-start.6) | collective-permute-done | bytes 491552 | tf_op jit(solution)/shard_map/ppermute | solution.py:27
  50.1 1.7 collective-permute-start.15
  51.9 0.8 constant_dynamic-update-slice_fusion.3
  52.7 9.0 %collective-permute-done.15 = bf16[48,5120]{1,0:T(8,128)(2,1)S(1)} collective-permute-done((bf16[48,5120]{1,0:T(8,128)(2,1)}, bf16[48,5120]{1,0:T(8,128)(2,1)S(1)}, u32[]{:S(2)}, u32[]{:S(2)}) %collective-permute-start.15) | collective-permute-done | bytes 491552 | tf_op jit(solution)/shard_map/ppermute | solution.py:27
  61.7 1.7 collective-permute-start.16
  63.5 0.8 constant_dynamic-update-slice_fusion.2
  64.3 6.8 %collective-permute-done.16 = bf16[48,5120]{1,0:T(8,128)(2,1)S(1)} collective-permute-done((bf16[48,5120]{1,0:T(8,128)(2,1)S(1)}, bf16[48,5120]{1,0:T(8,128)(2,1)S(1)}, u32[]{:S(2)}, u32[]{:S(2)}) %collective-permute-start.16) | collective-permute-done | bytes 491552 | tf_op jit(solution)/shard_map/ppermute | solution.py:27
  71.1 0.8 constant_dynamic-update-slice_fusion.1
  71.9 9.2 %collective-permute-done.17 = bf16[48,5120]{1,0:T(8,128)(2,1)S(1)} collective-permute-done((bf16[48,5120]{1,0:T(8,128)(2,1)S(1)}, bf16[48,5120]{1,0:T(8,128)(2,1)S(1)}, u32[]{:S(2)}, u32[]{:S(2)}) %collective-permute-start.17) | collective-permute-done | bytes 491552 | tf_op jit(solution)/shard_map/ppermute | solution.py:27
  81.1 0.8 constant_dynamic-update-slice_fusion.refs_1_
  82.5 5.2 %shard_map.174.refs_0_.refs_7_ = bf16[5,3,360,360]{3,2,1,0:T(8,128)(2,1)S(1)} custom-call(bf16[360,640]{1,0:T(8,128)(2,1)S(1)} %bitcast.29, bf16[2,360,640]{2,1,0:T(8,128)(2,1)S(1)} %bitcast.23, bf16[360,640]{1,0:T(8,128)(2,1)S(1)} %collective-permute-done.refs_2_, bf16[360,640]{1,0:T(8,128)(2,1)S(1)} %collective-permute-done.1.refs_3_, ...), custom_call_target="tpu_custom_call" | custom-call | flops 1944000000 | bytes 6291456 | tf_op jit(solution)/shard_map/pallas_call | solution.py:74
  87.7 3.5 %shard_map.175.refs_0_.refs_3_ = bf16[384,640]{1,0:T(8,128)(2,1)S(1)} custom-call(bf16[5,3,360,360]{3,2,1,0:T(8,128)(2,1)S(1)} %shard_map.174.refs_0_.refs_7_, bf16[2,360,640]{2,1,0:T(8,128)(2,1)S(1)} %bitcast.24, bf16[360,640]{1,0:T(8,128)(2,1)S(1)} %collective-permute-done.2.refs_2_.refs_5_, bf16[360,640]{1,0:T(8,128)(2,1)S(1)} %collective-permute-done.3.refs_3_.refs_6_, ...), custom_call_target="tpu_custom_call" | custom-call | flops 972000000 | bytes 6291456 | tf_op jit(solution)/shard_map/pallas_call | solution.py:74
  91.3 3.3 %shard_map.176 = (bf16[48,5120]{1,0:T(8,128)(2,1)S(1)}, bf16[48,5120]{1,0:T(8,128)(2,1)S(1)}, bf16[48,5120]{1,0:T(8,128)(2,1)S(1)}, bf16[48,5120]{1,0:T(8,128)(2...) custom-call(bf16[384,640]{1,0:T(8,128)(2,1)S(1)} %shard_map.175.refs, ...), custom_call_target="tpu_custom_call" | custom-call | flops 3774873600 | bytes 12582912 | tf_op jit(solution)/shard_map/pallas_call | solution.py:74
  94.7 0.6 collective-permute-start.19
  95.3 3.2 %collective-permute-start.8 = (bf16[48,5120]{1,0:T(8,128)(2,1)S(1)}, bf16[48,5120]{1,0:T(8,128)(2,1)S(1)}, u32[]{:S(2)}, u32[]{:S(2)}) collective-permute-start(bf16[48,5120]{1,0:T(8,128)(2,1)S(1)} %get-tuple-element.31), channel_id=1, source_target_pairs={{0,6},{1,7},{2,0},{3,1},{4,2},{5,3},{6,4},{7,5},{8,14},{9,15},{10,... | collective-permute-start | bytes 1474568 | tf_op jit(solution)/shard_map/ppermute | solution.py:27
  98.5 11.5 %collective-permute-done.11 = bf16[48,5120]{1,0:T(8,128)(2,1)S(1)} collective-permute-done((bf16[48,5120]{1,0:T(8,128)(2,1)S(1)}, bf16[48,5120]{1,0:T(8,128)(2,1)S(1)}, u32[]{:S(2)}, u32[]{:S(2)}) %collective-permute-start.11) | collective-permute-done | bytes 491552 | tf_op jit(solution)/shard_map/ppermute | solution.py:27
  110.0 0.3 collective-permute-start.10
  110.3 3.2 %shard_map.178.refs_8_ = bf16[384,640]{1,0:T(8,128)(2,1)S(1)} custom-call(bf16[640,5120]{1,0:T(8,128)(2,1)S(1)} %bitcast.34, bf16[384,5120]{1,0:T(8,128)(2,1)S(1)} %copy-done.2, bf16[48,5120]{1,0:T(8,128)(2,1)S(1)} %get-tuple-element.28.refs_0_.refs_2_), custom_call_target="tpu_custom_call" | custom-call | flops 3774873600 | bytes 12582912 | tf_op jit(solution)/shard_map/pallas_call | solution.py:74
  113.6 6.5 %shard_map.179 = (bf16[360,384]{1,0:T(8,128)(2,1)S(1)}, f32[2,360,384]{2,1,0:T(8,128)S(1)}, bf16[2,360,384]{2,1,0:T(8,128)(2,1)S(1)}, bf16[2,360,384]{2,1,0:T(8,128)(2,1)S(1)}) custom-call(bf16[360,640]{1,0:T(8,128)(2,1)S(1)} %bitcast.30, bf16[2,360,640]{2,1,0:T(8,128)(2,1)S(1)} %bitcast.25, bf16[360,640]{1,0:T(8,128)(2,1)S(1)} %collective-permute-done.refs_2_, ...), custom_call_target="tpu_custom_call" | custom-call | flops 2332800000 | bytes 6291456 | tf_op jit(solution)/shard_map/pallas_call | solution.py:74
  120.1 1.8 collective-permute-start.12
  122.0 8.9 %collective-permute-start.20 = (bf16[2,360,384]{2,1,0:T(8,128)(2,1)S(1)}, bf16[2,360,384]{2,1,0:T(8,128)(2,1)S(1)}, u32[]{:S(2)}, u32[]{:S(2)}) collective-permute-start(bf16[2,360,384]{2,1,0:T(8,128)(2,1)S(1)} %get-tuple-element.37.refs_5_), channel_id=1, source_target_pairs={{8,0},{16,8},{24,16},{32,24},{40,32},{48,40},{56,48},{64,56},{72,6... | collective-permute-start | bytes 1658888 | tf_op jit(solution)/shard_map/ppermute | solution.py:367
  130.9 5.5 %shard_map.180 = (bf16[320,640]{1,0:T(8,128)(2,1)S(1)}, bf16[320,640]{1,0:T(8,128)(2,1)S(1)}, bf16[320,640]{1,0:T(8,128)(2,1)S(1)}, bf16[320,640]{1,0:T(8,128)(2...) custom-call(s32[9]{0:T(128)S(1)} %pad_add_fusion.refs_8_.refs_0_, ...), custom_call_target="tpu_custom_call" | custom-call | flops 2516582400 | bytes 6291456 | tf_op jit(solution)/shard_map/pallas_call | solution.py:74
  136.4 2.0 collective-permute-start.28
  138.5 9.6 %collective-permute-done.28 = bf16[320,640]{1,0:T(8,128)(2,1)S(1)} collective-permute-done((bf16[320,640]{1,0:T(8,128)(2,1)S(1)}, bf16[320,640]{1,0:T(8,128)(2,1)S(1)}, u32[]{:S(2)}, u32[]{:S(2)}) %collective-permute-start.28) | collective-permute-done | bytes 409632 | tf_op jit(solution)/shard_map/ppermute | solution.py:37
  148.1 0.9 collective-permute-start.27
  149.1 3.5 %collective-permute-start.25 = (bf16[320,640]{1,0:T(8,128)(2,1)S(1)}, bf16[320,640]{1,0:T(8,128)(2,1)S(1)}, u32[]{:S(2)}, u32[]{:S(2)}) collective-permute-start(bf16[320,640]{1,0:T(8,128)(2,1)S(1)} %get-tuple-element.47), channel_id=1, source_target_pairs={{0,96},{8,104},{16,112},{24,120},{32,0},{40,8},{48,16},{56,24},{64... | collective-permute-start | bytes 1228808 | tf_op jit(solution)/shard_map/ppermute | solution.py:37
  152.6 0.2 add_convert_fusion
  152.8 3.7 %collective-permute-done.27 = bf16[320,640]{1,0:T(8,128)(2,1)S(1)} collective-permute-done((bf16[320,640]{1,0:T(8,128)(2,1)S(1)}, bf16[320,640]{1,0:T(8,128)(2,1)S(1)}, u32[]{:S(2)}, u32[]{:S(2)}) %collective-permute-start.27) | collective-permute-done | bytes 409632 | tf_op jit(solution)/shard_map/ppermute | solution.py:37
  156.5 1.8 collective-permute-start.9
  158.3 2.6 %collective-permute-done.25 = bf16[320,640]{1,0:T(8,128)(2,1)S(1)} collective-permute-done((bf16[320,640]{1,0:T(8,128)(2,1)S(1)}, bf16[320,640]{1,0:T(8,128)(2,1)S(1)}, u32[]{:S(2)}, u32[]{:S(2)}) %collective-permute-start.25) | collective-permute-done | bytes 409632 | tf_op jit(solution)/shard_map/ppermute | solution.py:37
  160.9 1.9 collective-permute-start.21
  162.8 1.5 collective-permute-start.13
  164.4 0.2 add_convert_fusion.4
  164.6 0.7 collective-permute-start.24
  165.3 1.4 collective-permute-start.26
  166.7 8.1 %collective-permute-start.30 = (bf16[320,640]{1,0:T(8,128)(2,1)S(1)}, bf16[320,640]{1,0:T(8,128)(2,1)S(1)}, u32[]{:S(2)}, u32[]{:S(2)}) collective-permute-start(bf16[320,640]{1,0:T(8,128)(2,1)S(1)} %add_convert_fusion.4), channel_id=1, source_target_pairs={{0,16},{8,24},{16,0},{24,8},{32,48},{40,56},{48,32},{56,40},{64,80... | collective-permute-start | bytes 1228808 | tf_op jit(solution)/shard_map/ppermute | solution.py:37
  174.8 4.4 %shard_map.181 = (bf16[360,256]{1,0:T(8,128)(2,1)S(1)}, f32[2,360,256]{2,1,0:T(8,128)S(1)}, bf16[2,360,256]{2,1,0:T(8,128)(2,1)S(1)}, bf16[2,360,256]{2,1,0:T(8,128)(2,1)S(1)}) custom-call(bf16[360,640]{1,0:T(8,128)(2,1)S(1)} %bitcast.31, bf16[2,360,640]{2,1,0:T(8,128)(2,1)S(1)} %bitcast.27, bf16[360,640]{1,0:T(8,128)(2,1)S(1)} %collective-permute-done.refs_2_, ...), custom_call_target="tpu_custom_call" | custom-call | flops 1555200000 | bytes 4194304 | tf_op jit(solution)/shard_map/pallas_call | solution.py:74
  179.2 3.3 %collective-permute-done.21.refs_2_ = bf16[2,360,384]{2,1,0:T(8,128)(2,1)S(1)} collective-permute-done((bf16[2,360,384]{2,1,0:T(8,128)(2,1)S(1)}, bf16[2,360,384]{2,1,0:T(8,128)(2,1)S(1)}, u32[]{:S(2)}, u32[]{:S(2)}) %collective-permute-start.21) | collective-permute-done | bytes 552992 | tf_op jit(solution)/shard_map/ppermute | solution.py:368
  182.5 2.9 %collective-permute-start.22 = (bf16[2,360,256]{2,1,0:T(8,128)(2,1)S(1)}, bf16[2,360,256]{2,1,0:T(8,128)(2,1)S(1)}, u32[]{:S(2)}, u32[]{:S(2)}) collective-permute-start(bf16[2,360,256]{2,1,0:T(8,128)(2,1)S(1)} %get-tuple-element.43), channel_id=1, source_target_pairs={{8,0},{16,8},{24,16},{32,24},{40,32},{48,40},{56,48},{64,56},{72,6... | collective-permute-start | bytes 1105928 | tf_op jit(solution)/shard_map/ppermute | solution.py:367
  185.5 6.7 %collective-permute-start.23 = (bf16[2,360,256]{2,1,0:T(8,128)(2,1)S(1)}, bf16[2,360,256]{2,1,0:T(8,128)(2,1)S(1)}, u32[]{:S(2)}, u32[]{:S(2)}) collective-permute-start(bf16[2,360,256]{2,1,0:T(8,128)(2,1)S(1)} %get-tuple-element.44), channel_id=1, source_target_pairs={{0,8},{8,16},{16,24},{24,32},{32,40},{40,48},{48,56},{56,64},{64,7... | collective-permute-start | bytes 1105928 | tf_op jit(solution)/shard_map/ppermute | solution.py:368
  192.2 1.2 shard_map.177.refs_6_
  193.4 0.8 pad_maximum_fusion
  194.3 0.1 collective-permute-done.22.refs_4_
  194.4 11.4 %collective-permute-done.23.refs_5_ = bf16[2,360,256]{2,1,0:T(8,128)(2,1)S(1)} collective-permute-done((bf16[2,360,256]{2,1,0:T(8,128)(2,1)S(1)}, bf16[2,360,256]{2,1,0:T(8,128)(2,1)S(1)}, u32[]{:S(2)}, u32[]{:S(2)}) %collective-permute-start.23) | collective-permute-done | bytes 368672 | tf_op jit(solution)/shard_map/ppermute | solution.py:368
  205.8 1.1 copy-done.4
  206.9 1.2 shard_map.182
  208.1 1.0 fusion.2
  (90 shorter events, 1.6 us)
Async XLA Ops:
  0.6 17.2 %copy-start = (s32[1,16,5,63]{3,1,2,0:T(8,128)S(1)}, s32[1,16,5,63]{3,1,2,0:T(8,128)}, u32[]{:S(2)}) copy-start(s32[1,16,5,63]{3,1,2,0:T(8,128)} %param.20) | copy-start | bytes 60484
  0.6 17.3 %copy-start.10 = (s32[5,5,7]{2,1,0:T(8,128)S(1)}, s32[5,5,7]{2,1,0:T(8,128)}, u32[]{:S(2)}) copy-start(s32[5,5,7]{2,1,0:T(8,128)} %constant.168) | copy-start | bytes 2104
  0.7 17.9 %copy-start.11 = (s32[5,5]{1,0:T(8,128)S(1)}, s32[5,5]{1,0:T(8,128)}, u32[]{:S(2)}) copy-start(s32[5,5]{1,0:T(8,128)} %constant.167) | copy-start | bytes 304
  0.7 17.1 %copy-start.18 = (s32[5,3]{0,1:T(4,128)S(1)}, s32[5,3]{0,1:T(4,128)}, u32[]{:S(2)}) copy-start(s32[5,3]{0,1:T(4,128)} %param.19) | copy-start | bytes 184
  2.9 79.5 %collective-permute-start = (bf16[360,640]{1,0:T(8,128)(2,1)}, bf16[360,640]{1,0:T(8,128)(2,1)S(1)}, u32[]{:S(2)}, u32[]{:S(2)}) collective-permute-start(bf16[360,640]{1,0:T(8,128)(2,1)} %bitcast.2), channel_id=1, source_target_pairs={{0,8},{8,16},{16,24},{24,32},{32,40},{40,48},{48,56},{56,64},{64,7... | collective-permute-start | bytes 1382408 | tf_op jit(solution)/shard_map/ppermute | solution.py:241
  4.8 77.6 %collective-permute-start.1 = (bf16[360,640]{1,0:T(8,128)(2,1)}, bf16[360,640]{1,0:T(8,128)(2,1)S(1)}, u32[]{:S(2)}, u32[]{:S(2)}) collective-permute-start(bf16[360,640]{1,0:T(8,128)(2,1)} %bitcast.2), channel_id=1, source_target_pairs={{8,0},{16,8},{24,16},{32,24},{40,32},{48,40},{56,48},{64,56},{72,6... | collective-permute-start | bytes 1382408 | tf_op jit(solution)/shard_map/ppermute | solution.py:242
  13.4 68.6 %copy-start.12 = (s32[384]{0:T(512)S(1)}, s32[384]{0:T(512)}, u32[]{:S(2)}) copy-start(s32[384]{0:T(512)} %constant.169) | copy-start | bytes 4612
  13.4 68.6 %copy-start.13 = (s32[384]{0:T(512)S(1)}, s32[384]{0:T(512)}, u32[]{:S(2)}) copy-start(s32[384]{0:T(512)} %constant.151.clone) | copy-start | bytes 4612
  13.4 68.6 %copy-start.14 = (s32[384]{0:T(512)S(1)}, s32[384]{0:T(512)}, u32[]{:S(2)}) copy-start(s32[384]{0:T(512)} %constant.150.clone) | copy-start | bytes 4612
  13.4 68.6 %copy-start.17 = (pred[384]{0:T(512)(128)(4,1)S(1)}, pred[384]{0:T(512)(128)(4,1)}, u32[]{:S(2)}) copy-start(pred[384]{0:T(512)(128)(4,1)} %constant.154.clone) | copy-start | bytes 1156
  13.4 13.0 %collective-permute-start.4 = (bf16[48,5120]{1,0:T(8,128)(2,1)}, bf16[48,5120]{1,0:T(8,128)(2,1)S(1)}, u32[]{:S(2)}, u32[]{:S(2)}) collective-permute-start(bf16[48,5120]{1,0:T(8,128)(2,1)} %get-tuple-element.55), channel_id=1, source_target_pairs={{0,6},{1,7},{2,0},{3,1},{4,2},{5,3},{6,4},{7,5},{8,14},{9,15},{10,... | collective-permute-start | bytes 1474568 | tf_op jit(solution)/shard_map/ppermute | solution.py:27
  16.2 15.0 %collective-permute-start.5 = (bf16[48,5120]{1,0:T(8,128)(2,1)}, bf16[48,5120]{1,0:T(8,128)(2,1)}, u32[]{:S(2)}, u32[]{:S(2)}) collective-permute-start(bf16[48,5120]{1,0:T(8,128)(2,1)} %get-tuple-element.55), channel_id=1, source_target_pairs={{0,1},{1,0},{2,3},{3,2},{4,5},{5,4},{6,7},{7,6},{8,9},{9,8},{10,11... | collective-permute-start | bytes 1474568 | tf_op jit(solution)/shard_map/ppermute | solution.py:27
  17.8 19.4 %collective-permute-start.14 = (bf16[48,5120]{1,0:T(8,128)(2,1)}, bf16[48,5120]{1,0:T(8,128)(2,1)}, u32[]{:S(2)}, u32[]{:S(2)}) collective-permute-start(bf16[48,5120]{1,0:T(8,128)(2,1)} %get-tuple-element.55), channel_id=1, source_target_pairs={{0,2},{1,3},{2,4},{3,5},{4,6},{5,7},{6,0},{7,1},{8,10},{9,11},{10,... | collective-permute-start | bytes 1474568 | tf_op jit(solution)/shard_map/ppermute | solution.py:27
  18.0 64.3 %copy-start.15 = (s32[8]{0:T(128)S(1)}, s32[8]{0:T(128)}, u32[]{:S(2)}) copy-start(s32[8]{0:T(128)} %constant.157.clone) | copy-start | bytes 100
  18.0 64.3 %copy-start.16 = (s32[8]{0:T(128)S(1)}, s32[8]{0:T(128)}, u32[]{:S(2)}) copy-start(s32[8]{0:T(128)} %constant.158.clone) | copy-start | bytes 100
  26.3 0.8 copy-start.5
  27.1 34.6 %copy-start.6 = (bf16[48,5120]{1,0:T(8,128)(2,1)S(1)}, bf16[48,5120]{1,0:T(8,128)(2,1)}, u32[]{:S(2)}) copy-start(bf16[48,5120]{1,0:T(8,128)(2,1)} %copy-done.5) | copy-start | bytes 1474564
  27.1 60.6 %collective-permute-start.2 = (bf16[360,640]{1,0:T(8,128)(2,1)}, bf16[360,640]{1,0:T(8,128)(2,1)S(1)}, u32[]{:S(2)}, u32[]{:S(2)}) collective-permute-start(bf16[360,640]{1,0:T(8,128)(2,1)} %bitcast.10), channel_id=1, source_target_pairs={{0,8},{8,16},{16,24},{24,32},{32,40},{40,48},{48,56},{56,64},{64,7... | collective-permute-start | bytes 1382408 | tf_op jit(solution)/shard_map/ppermute | solution.py:241
  29.2 53.3 %copy-start.1 = (bf16[2,3,3,40,640]{4,3,2,1,0:T(8,128)(2,1)S(1)}, bf16[2,3,3,40,640]{4,3,2,1,0:T(8,128)(2,1)}, u32[]{:S(2)}) copy-start(bf16[2,3,3,40,640]{4,3,2,1,0:T(8,128)(2,1)} %param.16) | copy-start | bytes 2764804
  29.2 53.3 %copy-start.3 = (bf16[3,3,40,640]{3,2,1,0:T(8,128)(2,1)S(1)}, bf16[3,3,40,640]{3,2,1,0:T(8,128)(2,1)}, u32[]{:S(2)}) copy-start(bf16[3,3,40,640]{3,2,1,0:T(8,128)(2,1)} %param.15) | copy-start | bytes 1382404
  31.2 56.5 %collective-permute-start.3 = (bf16[360,640]{1,0:T(8,128)(2,1)}, bf16[360,640]{1,0:T(8,128)(2,1)S(1)}, u32[]{:S(2)}, u32[]{:S(2)}) collective-permute-start(bf16[360,640]{1,0:T(8,128)(2,1)} %bitcast.10), channel_id=1, source_target_pairs={{8,0},{16,8},{24,16},{32,24},{40,32},{48,40},{56,48},{64,56},{72,6... | collective-permute-start | bytes 1382408 | tf_op jit(solution)/shard_map/ppermute | solution.py:242
  37.2 12.9 %collective-permute-start.6 = (bf16[48,5120]{1,0:T(8,128)(2,1)}, bf16[48,5120]{1,0:T(8,128)(2,1)S(1)}, u32[]{:S(2)}, u32[]{:S(2)}) collective-permute-start(bf16[48,5120]{1,0:T(8,128)(2,1)} %collective-permute-done.5), channel_id=1, source_target_pairs={{0,2},{1,3},{2,4},{3,5},{4,6},{5,7},{6,0},{7,1},{8,10},{9,11},{10,... | collective-permute-start | bytes 1474568 | tf_op jit(solution)/shard_map/ppermute | solution.py:27
  50.1 21.0 %copy-start.8 = (bf16[48,5120]{1,0:T(8,128)(2,1)}, bf16[48,5120]{1,0:T(8,128)(2,1)S(1)}, u32[]{:S(2)}) copy-start(bf16[48,5120]{1,0:T(8,128)(2,1)S(1)} %collective-permute-done.6.refs_6_) | copy-start | bytes 1474564
  50.1 11.6 %collective-permute-start.15 = (bf16[48,5120]{1,0:T(8,128)(2,1)}, bf16[48,5120]{1,0:T(8,128)(2,1)S(1)}, u32[]{:S(2)}, u32[]{:S(2)}) collective-permute-start(bf16[48,5120]{1,0:T(8,128)(2,1)} %collective-permute-done.5), channel_id=1, source_target_pairs={{0,6},{1,7},{2,0},{3,1},{4,2},{5,3},{6,4},{7,5},{8,14},{9,15},{10,... | collective-permute-start | bytes 1474568 | tf_op jit(solution)/shard_map/ppermute | solution.py:27
  61.7 9.4 %collective-permute-start.16 = (bf16[48,5120]{1,0:T(8,128)(2,1)S(1)}, bf16[48,5120]{1,0:T(8,128)(2,1)S(1)}, u32[]{:S(2)}, u32[]{:S(2)}) collective-permute-start(bf16[48,5120]{1,0:T(8,128)(2,1)S(1)} %copy-done.6), channel_id=1, source_target_pairs={{0,6},{1,7},{2,0},{3,1},{4,2},{5,3},{6,4},{7,5},{8,14},{9,15},{10,... | collective-permute-start | bytes 1474568 | tf_op jit(solution)/shard_map/ppermute | solution.py:27
  71.1 10.0 %collective-permute-start.17 = (bf16[48,5120]{1,0:T(8,128)(2,1)S(1)}, bf16[48,5120]{1,0:T(8,128)(2,1)S(1)}, u32[]{:S(2)}, u32[]{:S(2)}) collective-permute-start(bf16[48,5120]{1,0:T(8,128)(2,1)S(1)} %collective-permute-done.6.refs_6_), channel_id=1, source_target_pairs={{0,2},{1,3},{2,4},{3,5},{4,6},{5,7},{6,0},{7,1},{8,10},{9,11},{10,... | collective-permute-start | bytes 1474568 | tf_op jit(solution)/shard_map/ppermute | solution.py:27
  82.0 40.0 %collective-permute-start.18 = (bf16[384,5120]{1,0:T(8,128)(2,1)}, bf16[384,5120]{1,0:T(8,128)(2,1)}, u32[]{:S(2)}, u32[]{:S(2)}) collective-permute-start(bf16[384,5120]{1,0:T(8,128)(2,1)} %constant_dynamic-update-slice_fusion.refs_1_), channel_id=1, source_target_pairs={{0,8},{8,0},{16,24},{24,16},{32,40},{40,32},{48,56},{56,48},{64,72... | collective-permute-start | bytes 11796488 | tf_op jit(solution)/shard_map/ppermute | solution.py:37
  82.4 5.3 %copy-start.7 = (bf16[48,5120]{1,0:T(8,128)(2,1)S(1)}, bf16[48,5120]{1,0:T(8,128)(2,1)}, u32[]{:S(2)}) copy-start(bf16[48,5120]{1,0:T(8,128)(2,1)} %copy-done.5) | copy-start | bytes 1474564
  82.4 5.3 %copy-start.9 = (bf16[48,5120]{1,0:T(8,128)(2,1)S(1)}, bf16[48,5120]{1,0:T(8,128)(2,1)}, u32[]{:S(2)}) copy-start(bf16[48,5120]{1,0:T(8,128)(2,1)} %copy-done.8) | copy-start | bytes 1474564
  82.5 8.8 %slice-start = ((s8[6553600]{0:T(1024)(128)(4,1)}), s8[4194304]{0:T(1024)(128)(4,1)S(1)}, s32[]{:S(2)}) async-start(s8[6553600]{0:T(1024)(128)(4,1)} %bitcast.33), calls=%async_computation | async-start | bytes 8388608
  87.7 3.6 %slice-start.1 = ((s8[6553600]{0:T(1024)(128)(4,1)}), s8[2359296]{0:T(1024)(128)(4,1)S(1)}, s32[]{:S(2)}) async-start(s8[6553600]{0:T(1024)(128)(4,1)} %bitcast.33), calls=%async_computation.1 | async-start | bytes 4718592
  91.3 19.0 %copy-start.2 = (bf16[384,5120]{1,0:T(8,128)(2,1)S(1)}, bf16[384,5120]{1,0:T(8,128)(2,1)}, u32[]{:S(2)}) copy-start(bf16[384,5120]{1,0:T(8,128)(2,1)} %constant_dynamic-update-slice_fusion.refs_1_) | copy-start | bytes 11796484
  94.6 15.4 %collective-permute-start.11 = (bf16[48,5120]{1,0:T(8,128)(2,1)S(1)}, bf16[48,5120]{1,0:T(8,128)(2,1)S(1)}, u32[]{:S(2)}, u32[]{:S(2)}) collective-permute-start(bf16[48,5120]{1,0:T(8,128)(2,1)S(1)} %get-tuple-element.35), channel_id=1, source_target_pairs={{0,2},{1,3},{2,4},{3,5},{4,6},{5,7},{6,0},{7,1},{8,10},{9,11},{10,... | collective-permute-start | bytes 1474568 | tf_op jit(solution)/shard_map/ppermute | solution.py:27
  94.7 25.4 %collective-permute-start.19 = (bf16[384,640]{1,0:T(8,128)(2,1)S(1)}, bf16[384,640]{1,0:T(8,128)(2,1)S(1)}, u32[]{:S(2)}, u32[]{:S(2)}) collective-permute-start(bf16[384,640]{1,0:T(8,128)(2,1)S(1)} %shard_map.175.refs_0_.refs_3_), channel_id=1, source_target_pairs={{0,8},{8,0},{16,24},{24,16},{32,40},{40,32},{48,56},{56,48},{64,72... | collective-permute-start | bytes 1474568 | tf_op jit(solution)/shard_map/ppermute | solution.py:37
  95.2 69.4 %collective-permute-start.7 = (bf16[48,5120]{1,0:T(8,128)(2,1)S(1)}, bf16[48,5120]{1,0:T(8,128)(2,1)S(1)}, u32[]{:S(2)}, u32[]{:S(2)}) collective-permute-start(bf16[48,5120]{1,0:T(8,128)(2,1)S(1)} %get-tuple-element.29), channel_id=1, source_target_pairs={{0,2},{1,3},{2,4},{3,5},{4,6},{5,7},{6,0},{7,1},{8,10},{9,11},{10,... | collective-permute-start | bytes 1474568 | tf_op jit(solution)/shard_map/ppermute | solution.py:27
  95.3 41.1 %collective-permute-start.8 = (bf16[48,5120]{1,0:T(8,128)(2,1)S(1)}, bf16[48,5120]{1,0:T(8,128)(2,1)S(1)}, u32[]{:S(2)}, u32[]{:S(2)}) collective-permute-start(bf16[48,5120]{1,0:T(8,128)(2,1)S(1)} %get-tuple-element.31), channel_id=1, source_target_pairs={{0,6},{1,7},{2,0},{3,1},{4,2},{5,3},{6,4},{7,5},{8,14},{9,15},{10,... | collective-permute-start | bytes 1474568 | tf_op jit(solution)/shard_map/ppermute | solution.py:27
  110.0 39.1 %collective-permute-start.10 = (bf16[48,5120]{1,0:T(8,128)(2,1)S(1)}, bf16[48,5120]{1,0:T(8,128)(2,1)S(1)}, u32[]{:S(2)}, u32[]{:S(2)}) collective-permute-start(bf16[48,5120]{1,0:T(8,128)(2,1)S(1)} %get-tuple-element.33), channel_id=1, source_target_pairs={{0,6},{1,7},{2,0},{3,1},{4,2},{5,3},{6,4},{7,5},{8,14},{9,15},{10,... | collective-permute-start | bytes 1474568 | tf_op jit(solution)/shard_map/ppermute | solution.py:27
  120.1 32.5 %collective-permute-start.12 = (bf16[48,5120]{1,0:T(8,128)(2,1)S(1)}, bf16[48,5120]{1,0:T(8,128)(2,1)S(1)}, u32[]{:S(2)}, u32[]{:S(2)}) collective-permute-start(bf16[48,5120]{1,0:T(8,128)(2,1)S(1)} %add_convert_fusion.1), channel_id=1, source_target_pairs={{0,2},{1,3},{2,4},{3,5},{4,6},{5,7},{6,0},{7,1},{8,10},{9,11},{10,... | collective-permute-start | bytes 1474568 | tf_op jit(solution)/shard_map/ppermute | solution.py:27
  122.0 44.8 %collective-permute-start.20 = (bf16[2,360,384]{2,1,0:T(8,128)(2,1)S(1)}, bf16[2,360,384]{2,1,0:T(8,128)(2,1)S(1)}, u32[]{:S(2)}, u32[]{:S(2)}) collective-permute-start(bf16[2,360,384]{2,1,0:T(8,128)(2,1)S(1)} %get-tuple-element.37.refs_5_), channel_id=1, source_target_pairs={{8,0},{16,8},{24,16},{32,24},{40,32},{48,40},{56,48},{64,56},{72,6... | collective-permute-start | bytes 1658888 | tf_op jit(solution)/shard_map/ppermute | solution.py:367
  136.4 11.7 %collective-permute-start.28 = (bf16[320,640]{1,0:T(8,128)(2,1)S(1)}, bf16[320,640]{1,0:T(8,128)(2,1)S(1)}, u32[]{:S(2)}, u32[]{:S(2)}) collective-permute-start(bf16[320,640]{1,0:T(8,128)(2,1)S(1)} %get-tuple-element.51), channel_id=1, source_target_pairs={{0,32},{8,40},{16,48},{24,56},{32,64},{40,72},{48,80},{56,88},{64,... | collective-permute-start | bytes 1228808 | tf_op jit(solution)/shard_map/ppermute | solution.py:37
  148.1 8.4 %collective-permute-start.27 = (bf16[320,640]{1,0:T(8,128)(2,1)S(1)}, bf16[320,640]{1,0:T(8,128)(2,1)S(1)}, u32[]{:S(2)}, u32[]{:S(2)}) collective-permute-start(bf16[320,640]{1,0:T(8,128)(2,1)S(1)} %get-tuple-element.49), channel_id=1, source_target_pairs={{0,96},{8,104},{16,112},{24,120},{32,0},{40,8},{48,16},{56,24},{64... | collective-permute-start | bytes 1228808 | tf_op jit(solution)/shard_map/ppermute | solution.py:37
  149.1 11.8 %collective-permute-start.25 = (bf16[320,640]{1,0:T(8,128)(2,1)S(1)}, bf16[320,640]{1,0:T(8,128)(2,1)S(1)}, u32[]{:S(2)}, u32[]{:S(2)}) collective-permute-start(bf16[320,640]{1,0:T(8,128)(2,1)S(1)} %get-tuple-element.47), channel_id=1, source_target_pairs={{0,96},{8,104},{16,112},{24,120},{32,0},{40,8},{48,16},{56,24},{64... | collective-permute-start | bytes 1228808 | tf_op jit(solution)/shard_map/ppermute | solution.py:37
  152.6 10.2 %collective-permute-start.29 = (bf16[320,640]{1,0:T(8,128)(2,1)S(1)}, bf16[320,640]{1,0:T(8,128)(2,1)S(1)}, u32[]{:S(2)}, u32[]{:S(2)}) collective-permute-start(bf16[320,640]{1,0:T(8,128)(2,1)S(1)} %add_convert_fusion.5), channel_id=1, source_target_pairs={{0,32},{8,40},{16,48},{24,56},{32,64},{40,72},{48,80},{56,88},{64,... | collective-permute-start | bytes 1228808 | tf_op jit(solution)/shard_map/ppermute | solution.py:37
  156.5 8.8 %collective-permute-start.9 = (bf16[48,5120]{1,0:T(8,128)(2,1)S(1)}, bf16[48,5120]{1,0:T(8,128)(2,1)S(1)}, u32[]{:S(2)}, u32[]{:S(2)}) collective-permute-start(bf16[48,5120]{1,0:T(8,128)(2,1)S(1)} %add_convert_fusion.2), channel_id=1, source_target_pairs={{0,6},{1,7},{2,0},{3,1},{4,2},{5,3},{6,4},{7,5},{8,14},{9,15},{10,... | collective-permute-start | bytes 1474568 | tf_op jit(solution)/shard_map/ppermute | solution.py:27
  160.9 21.6 %collective-permute-start.21 = (bf16[2,360,384]{2,1,0:T(8,128)(2,1)S(1)}, bf16[2,360,384]{2,1,0:T(8,128)(2,1)S(1)}, u32[]{:S(2)}, u32[]{:S(2)}) collective-permute-start(bf16[2,360,384]{2,1,0:T(8,128)(2,1)S(1)} %get-tuple-element.41), channel_id=1, source_target_pairs={{0,8},{8,16},{16,24},{24,32},{32,40},{40,48},{48,56},{56,64},{64,7... | collective-permute-start | bytes 1658888 | tf_op jit(solution)/shard_map/ppermute | solution.py:368
  162.8 22.6 %collective-permute-start.13 = (bf16[48,5120]{1,0:T(8,128)(2,1)S(1)}, bf16[48,5120]{1,0:T(8,128)(2,1)S(1)}, u32[]{:S(2)}, u32[]{:S(2)}) collective-permute-start(bf16[48,5120]{1,0:T(8,128)(2,1)S(1)} %add_convert_fusion), channel_id=1, source_target_pairs={{0,1},{1,0},{2,3},{3,2},{4,5},{5,4},{6,7},{7,6},{8,9},{9,8},{10,11... | collective-permute-start | bytes 1474568 | tf_op jit(solution)/shard_map/ppermute | solution.py:27
  164.6 43.5 %collective-permute-start.24 = (bf16[320,640]{1,0:T(8,128)(2,1)S(1)}, bf16[320,640]{1,0:T(8,128)(2,1)S(1)}, u32[]{:S(2)}, u32[]{:S(2)}) collective-permute-start(bf16[320,640]{1,0:T(8,128)(2,1)S(1)} %get-tuple-element.45), channel_id=1, source_target_pairs={{0,32},{8,40},{16,48},{24,56},{32,64},{40,72},{48,80},{56,88},{64,... | collective-permute-start | bytes 1228808 | tf_op jit(solution)/shard_map/ppermute | solution.py:37
  165.3 42.8 %collective-permute-start.26 = (bf16[320,640]{1,0:T(8,128)(2,1)S(1)}, bf16[320,640]{1,0:T(8,128)(2,1)S(1)}, u32[]{:S(2)}, u32[]{:S(2)}) collective-permute-start(bf16[320,640]{1,0:T(8,128)(2,1)S(1)} %add_convert_fusion.6), channel_id=1, source_target_pairs={{0,96},{8,104},{16,112},{24,120},{32,0},{40,8},{48,16},{56,24},{64... | collective-permute-start | bytes 1228808 | tf_op jit(solution)/shard_map/ppermute | solution.py:37
  166.7 41.4 %collective-permute-start.30 = (bf16[320,640]{1,0:T(8,128)(2,1)S(1)}, bf16[320,640]{1,0:T(8,128)(2,1)S(1)}, u32[]{:S(2)}, u32[]{:S(2)}) collective-permute-start(bf16[320,640]{1,0:T(8,128)(2,1)S(1)} %add_convert_fusion.4), channel_id=1, source_target_pairs={{0,16},{8,24},{16,0},{24,8},{32,48},{40,56},{48,32},{56,40},{64,80... | collective-permute-start | bytes 1228808 | tf_op jit(solution)/shard_map/ppermute | solution.py:37
  182.5 11.9 %collective-permute-start.22 = (bf16[2,360,256]{2,1,0:T(8,128)(2,1)S(1)}, bf16[2,360,256]{2,1,0:T(8,128)(2,1)S(1)}, u32[]{:S(2)}, u32[]{:S(2)}) collective-permute-start(bf16[2,360,256]{2,1,0:T(8,128)(2,1)S(1)} %get-tuple-element.43), channel_id=1, source_target_pairs={{8,0},{16,8},{24,16},{32,24},{40,32},{48,40},{56,48},{64,56},{72,6... | collective-permute-start | bytes 1105928 | tf_op jit(solution)/shard_map/ppermute | solution.py:367
  185.5 20.3 %collective-permute-start.23 = (bf16[2,360,256]{2,1,0:T(8,128)(2,1)S(1)}, bf16[2,360,256]{2,1,0:T(8,128)(2,1)S(1)}, u32[]{:S(2)}, u32[]{:S(2)}) collective-permute-start(bf16[2,360,256]{2,1,0:T(8,128)(2,1)S(1)} %get-tuple-element.44), channel_id=1, source_target_pairs={{0,8},{8,16},{16,24},{24,32},{32,40},{40,48},{48,56},{56,64},{64,7... | collective-permute-start | bytes 1105928 | tf_op jit(solution)/shard_map/ppermute | solution.py:368
  205.8 1.1 copy-start.4

commit v6 on v5

--- a/solution.py
+++ b/solution.py
@@ -271,12 +271,17 @@
     key_specs = [pl.BlockSpec((None, tokens, HEAD_DIM), lambda h: (0, 0, h)), q_spec, q_spec]
     value_specs = [pl.BlockSpec((None, tokens, HEAD_DIM), lambda h: (1, 0, h)), q_spec, q_spec]
     p_spec = pl.BlockSpec((1, 3, tokens, tokens), lambda h: (h, 0, 0, 0))
-    weights = ((2, 1), (2, 0), (1, 0), (3, 1), (1, 1), (3, 0), (0, 1), (0, 0))
-    ring, pair = (np.array([w[i] for w in weights], np.int32) for i in range(2))
-    chips = (spot_z + ring) % 4 * 2 + (spot_y + pair) % 2
-    order = jnp.concatenate([chips, core]).astype(jnp.int32)
-
+    firsts = ((2, 1), (2, 0))
+    others = ((1, 1), (3, 0), (3, 1), (1, 0), (0, 1), (0, 0))
+
+    def order_of(blocks):
+        ring, pair = (np.array([w[i] for w in blocks], np.int32) for i in range(2))
+        chips = (spot_z + ring) % 4 * 2 + (spot_y + pair) % 2
+        return jnp.concatenate([chips, core]).astype(jnp.int32)
+
+    orders = [order_of(firsts), order_of(others)]
     pairs = heads * tokens * 3 * tokens
+
     (probs,) = kernel(
         scores_kernel,
         [((heads, 3, tokens, tokens), BF16)],
@@ -289,7 +294,7 @@
         ],
         [p_spec],
         grid=(heads,),
-        after=[perm, perm_back, order],
+        after=[perm, perm_back, *orders],
         flops=pairs * 1000,
         moved=6 << 20,
     )
@@ -326,6 +331,21 @@
         flops=slots * model_width * channels * 3,
         moved=12 << 20,
     )
+
+    narrow = model_width // row_tiles
+
+    def weight_blocks(blocks, order, after):
+        return kernel(
+            weight_kernel,
+            [((narrow, channels), BF16)] * len(blocks),
+            [order, all_grad, far_grad, attended, far_attended],
+            [SCALAR] + [VECTOR] * 4,
+            after=after,
+            flops=slots * model_width * channels * 2 * len(blocks) // 8,
+            moved=6 << 20,
+        )
+
+    weight = dict(zip(firsts, weight_blocks(firsts, orders[0], [grad_attn])))
 
     def differentiate(first, count, after):
         def spec(shape, at):
@@ -369,19 +389,9 @@
         return from_below, from_above
 
     split = (heads + 1) // 2
-    gq_a, own_a, *ends_a = differentiate(0, split, [])
+    gq_a, own_a, *ends_a = differentiate(0, split, [weight[2, 1]])
     halo_a = send_halo(*ends_a)
-    narrow = model_width // row_tiles
-    weight = kernel(
-        weight_kernel,
-        [((narrow, channels), BF16)] * 8,
-        [order, all_grad, far_grad, attended, far_attended],
-        [SCALAR] + [VECTOR] * 4,
-        after=ends_a[:1],
-        flops=slots * model_width * channels * 2,
-        moved=6 << 20,
-    )
-    weight = dict(zip(weights, weight))
+    weight.update(zip(others, weight_blocks(others, orders[1], ends_a[:1])))
     weight_far = hop(seq_shift, (weight[2, 1], weight[2, 0]))
     weight_near = hop(seq_shift, (weight[1, 0], weight[3, 1]))
 

time: 210 us -> 201 us (0.957)
  the two profiles are of different devices: /device:TPU:32 before, /device:TPU:0 now
where the time goes in v6:
time: 201 us
  waiting for transfers between devices  83.1 us (41%)
  starting transfers between devices  53.3 us (27%)
  Pallas kernels  36.5 us (18%)
  local copies, waits for them, and re-layouts  16.8 us (8%)
  other arithmetic  9.54 us (5%)
    ppermute x14, waiting for transfers between devices, tensor_shift(): return lax.ppermute(value, 'tensor', pairs)  61.6 us
    pallas_call x10, Pallas kernels, kernel(): pl.pallas_call(run, grid=grid, in_specs=[*specs, *[ANYWHERE] * len(after)...  36.5 us
    ppermute x9, waiting for transfers between devices, seq_shift(): return lax.ppermute(value, 'seq', pairs)  21.5 us
    ppermute x14, starting transfers between devices, tensor_shift(): return lax.ppermute(value, 'tensor', pairs)  19.8 us
    ppermute x9, starting transfers between devices, seq_shift(): return lax.ppermute(value, 'seq', pairs)  17 us
    unnamed x53, local copies, waits for them, and re-layouts  11 us
    ppermute x2, starting transfers between devices, layer(): up = lax.ppermute(flat_kv[i], 'seq', onward)  6.45 us
    ppermute x2, starting transfers between devices, send_halo(): from_above = lax.ppermute(grad_down, 'seq', onward)  4.71 us
  transfers between devices with their start and end apart: 31, of which 11 were waited for; matrix products, arithmetic and copies ran while one was open for 10% of the time, Pallas kernels for 18%

profile of v6, /device:TPU:0, one launch (start us, length us, event | category | flops | bytes accessed | tf_op | source)
XLA Modules:
  0.0 200.5 jit_solution(5212691025134726681)
XLA Ops:
  0.7 2.3 %fusion.24 = (bf16[1,3,3,40,640]{4,3,2,1,0:T(8,128)(2,1)}, bf16[1,3,3,40,640]{4,3,2,1,0:T(8,128)(2,1)}) fusion(bf16[2,3,3,40,640]{4,3,2,1,0:T(8,128)(2,1)} %param.18), kind=kLoop, calls=%fused_computation.84 | loop fusion | bytes 1843200 | tf_op jit(solution)/shard_map/slice | solution.py:241
  3.0 1.3 collective-permute-start.1
  4.3 3.1 %collective-permute-start = (bf16[360,640]{1,0:T(8,128)(2,1)}, bf16[360,640]{1,0:T(8,128)(2,1)S(1)}, u32[]{:S(2)}, u32[]{:S(2)}) collective-permute-start(bf16[360,640]{1,0:T(8,128)(2,1)} %bitcast.2), channel_id=1, source_target_pairs={{0,8},{8,16},{16,24},{24,32},{32,40},{40,48},{48,56},{56,64},{64,7... | collective-permute-start | bytes 1382408 | tf_op jit(solution)/shard_map/ppermute | solution.py:241
  7.3 1.5 reshape.160
  8.8 1.0 constant_dynamic-update-slice_fusion.7
  9.8 1.6 collective-permute-start.14
  11.4 1.6 collective-permute-start.5
  13.0 1.7 collective-permute-start.4
  15.7 0.6 fusion.9
  16.5 0.7 and_select_fusion
  17.2 0.8 fusion.3.refs_5_
  18.0 8.3 %collective-permute-done.4.refs_5_ = bf16[48,5120]{1,0:T(8,128)(2,1)S(1)} collective-permute-done((bf16[48,5120]{1,0:T(8,128)(2,1)}, bf16[48,5120]{1,0:T(8,128)(2,1)S(1)}, u32[]{:S(2)}, u32[]{:S(2)}) %collective-permute-start.4) | collective-permute-done | bytes 491552 | tf_op jit(solution)/shard_map/ppermute | solution.py:27
  26.3 1.3 collective-permute-start.3
  27.6 0.8 constant_dynamic-update-slice_fusion.6
  28.5 3.4 %collective-permute-start.2 = (bf16[360,640]{1,0:T(8,128)(2,1)}, bf16[360,640]{1,0:T(8,128)(2,1)S(1)}, u32[]{:S(2)}, u32[]{:S(2)}) collective-permute-start(bf16[360,640]{1,0:T(8,128)(2,1)} %bitcast.10), channel_id=1, source_target_pairs={{0,8},{8,16},{16,24},{24,32},{32,40},{40,48},{48,56},{56,64},{64,7... | collective-permute-start | bytes 1382408 | tf_op jit(solution)/shard_map/ppermute | solution.py:241
  31.9 1.6 collective-permute-start.6
  33.4 1.8 constant_dynamic-update-slice_fusion.5
  35.3 1.9 constant_dynamic-update-slice_fusion.4
  37.1 8.1 %collective-permute-done.6.refs_6_ = bf16[48,5120]{1,0:T(8,128)(2,1)S(1)} collective-permute-done((bf16[48,5120]{1,0:T(8,128)(2,1)}, bf16[48,5120]{1,0:T(8,128)(2,1)S(1)}, u32[]{:S(2)}, u32[]{:S(2)}) %collective-permute-start.6) | collective-permute-done | bytes 491552 | tf_op jit(solution)/shard_map/ppermute | solution.py:27
  45.2 1.8 collective-permute-start.15
  47.0 0.8 constant_dynamic-update-slice_fusion.3
  47.8 10.6 %collective-permute-done.15 = bf16[48,5120]{1,0:T(8,128)(2,1)S(1)} collective-permute-done((bf16[48,5120]{1,0:T(8,128)(2,1)}, bf16[48,5120]{1,0:T(8,128)(2,1)S(1)}, u32[]{:S(2)}, u32[]{:S(2)}) %collective-permute-start.15) | collective-permute-done | bytes 491552 | tf_op jit(solution)/shard_map/ppermute | solution.py:27
  58.4 3.0 %collective-permute-start.16 = (bf16[48,5120]{1,0:T(8,128)(2,1)}, bf16[48,5120]{1,0:T(8,128)(2,1)S(1)}, u32[]{:S(2)}, u32[]{:S(2)}) collective-permute-start(bf16[48,5120]{1,0:T(8,128)(2,1)} %copy-done.6), channel_id=1, source_target_pairs={{0,6},{1,7},{2,0},{3,1},{4,2},{5,3},{6,4},{7,5},{8,14},{9,15},{10,... | collective-permute-start | bytes 1474568 | tf_op jit(solution)/shard_map/ppermute | solution.py:27
  61.4 0.8 constant_dynamic-update-slice_fusion.2
  62.2 11.1 %collective-permute-done.16 = bf16[48,5120]{1,0:T(8,128)(2,1)S(1)} collective-permute-done((bf16[48,5120]{1,0:T(8,128)(2,1)}, bf16[48,5120]{1,0:T(8,128)(2,1)S(1)}, u32[]{:S(2)}, u32[]{:S(2)}) %collective-permute-start.16) | collective-permute-done | bytes 491552 | tf_op jit(solution)/shard_map/ppermute | solution.py:27
  73.3 0.8 constant_dynamic-update-slice_fusion.1
  74.1 14.2 %collective-permute-done.17 = bf16[48,5120]{1,0:T(8,128)(2,1)S(1)} collective-permute-done((bf16[48,5120]{1,0:T(8,128)(2,1)S(1)}, bf16[48,5120]{1,0:T(8,128)(2,1)S(1)}, u32[]{:S(2)}, u32[]{:S(2)}) %collective-permute-start.17) | collective-permute-done | bytes 491552 | tf_op jit(solution)/shard_map/ppermute | solution.py:27
  88.3 0.9 constant_dynamic-update-slice_fusion.refs_1_
  89.8 0.8 fusion.refs_6_.refs_4_
  90.7 1.2 fusion.19
  91.9 0.7 pad_add_fusion.1.refs_9_.refs_0_
  92.7 0.7 pad_add_fusion.refs_8_.refs_0_
  93.4 0.9 pad.8
  94.4 1.0 copy-done.4
  95.3 0.9 copy-done.10
  96.2 5.2 %shard_map.192.refs_0_.refs_7_ = bf16[5,3,360,360]{3,2,1,0:T(8,128)(2,1)S(1)} custom-call(bf16[360,640]{1,0:T(8,128)(2,1)S(1)} %bitcast.29, bf16[2,360,640]{2,1,0:T(8,128)(2,1)S(1)} %bitcast.23, bf16[360,640]{1,0:T(8,128)(2,1)S(1)} %collective-permute-done.refs_2_, bf16[360,640]{1,0:T(8,128)(2,1)S(1)} %collective-permute-done.1.refs_3_, ...), custom_call_target="tpu_custom_call" | custom-call | flops 1944000000 | bytes 6291456 | tf_op jit(solution)/shard_map/pallas_call | solution.py:74
  101.5 3.5 %shard_map.193.refs_0_.refs_3_ = bf16[384,640]{1,0:T(8,128)(2,1)S(1)} custom-call(bf16[5,3,360,360]{3,2,1,0:T(8,128)(2,1)S(1)} %shard_map.192.refs_0_.refs_7_, bf16[2,360,640]{2,1,0:T(8,128)(2,1)S(1)} %bitcast.24, bf16[360,640]{1,0:T(8,128)(2,1)S(1)} %collective-permute-done.2.refs_2_.refs_5_, bf16[360,640]{1,0:T(8,128)(2,1)S(1)} %collective-permute-done.3.refs_3_.refs_6_, ...), custom_call_target="tpu_custom_call" | custom-call | flops 972000000 | bytes 6291456 | tf_op jit(solution)/shard_map/pallas_call | solution.py:74
  105.0 3.3 %shard_map.194 = (bf16[48,5120]{1,0:T(8,128)(2,1)S(1)}, bf16[48,5120]{1,0:T(8,128)(2,1)S(1)}, bf16[48,5120]{1,0:T(8,128)(2,1)S(1)}, bf16[48,5120]{1,0:T(8,128)(2...) custom-call(bf16[384,640]{1,0:T(8,128)(2,1)S(1)} %shard_map.193.refs, ...), custom_call_target="tpu_custom_call" | custom-call | flops 3774873600 | bytes 12582912 | tf_op jit(solution)/shard_map/pallas_call | solution.py:74
  108.3 1.8 collective-permute-start.8
  110.6 3.0 %collective-permute-start.10 = (bf16[48,5120]{1,0:T(8,128)(2,1)S(1)}, bf16[48,5120]{1,0:T(8,128)(2,1)S(1)}, u32[]{:S(2)}, u32[]{:S(2)}) collective-permute-start(bf16[48,5120]{1,0:T(8,128)(2,1)S(1)} %get-tuple-element.33), channel_id=1, source_target_pairs={{0,6},{1,7},{2,0},{3,1},{4,2},{5,3},{6,4},{7,5},{8,14},{9,15},{10,... | collective-permute-start | bytes 1474568 | tf_op jit(solution)/shard_map/ppermute | solution.py:27
  113.6 8.9 %collective-permute-done.8 = bf16[48,5120]{1,0:T(8,128)(2,1)S(1)} collective-permute-done((bf16[48,5120]{1,0:T(8,128)(2,1)S(1)}, bf16[48,5120]{1,0:T(8,128)(2,1)S(1)}, u32[]{:S(2)}, u32[]{:S(2)}) %collective-permute-start.8) | collective-permute-done | bytes 491552 | tf_op jit(solution)/shard_map/ppermute | solution.py:27
  122.6 3.2 %shard_map.196.refs_5_.refs_8_ = bf16[384,640]{1,0:T(8,128)(2,1)S(1)} custom-call(bf16[640,5120]{1,0:T(8,128)(2,1)S(1)} %bitcast.34, bf16[384,5120]{1,0:T(8,128)(2,1)S(1)} %copy-done.2, bf16[48,5120]{1,0:T(8,128)(2,1)S(1)} %get-tuple-element.28.refs_0_.refs_2_), custom_call_target="tpu_custom_call" | custom-call | flops 3774873600 | bytes 12582912 | tf_op jit(solution)/shard_map/pallas_call | solution.py:74
  125.9 3.3 %collective-permute-start.9 = (bf16[48,5120]{1,0:T(8,128)(2,1)S(1)}, bf16[48,5120]{1,0:T(8,128)(2,1)S(1)}, u32[]{:S(2)}, u32[]{:S(2)}) collective-permute-start(bf16[48,5120]{1,0:T(8,128)(2,1)S(1)} %add_convert_fusion.2), channel_id=1, source_target_pairs={{0,6},{1,7},{2,0},{3,1},{4,2},{5,3},{6,4},{7,5},{8,14},{9,15},{10,... | collective-permute-start | bytes 1474568 | tf_op jit(solution)/shard_map/ppermute | solution.py:27
  129.2 3.1 %shard_map.197 = (bf16[320,640]{1,0:T(8,128)(2,1)S(1)}, bf16[320,640]{1,0:T(8,128)(2,1)S(1)}) custom-call(s32[3]{0:T(128)S(1)} %pad_add_fusion.refs_8_.refs_0_, bf16[384,5120]{1,0:T(8,128)(2,1)S(1)} %copy-done.2, bf16[384,5120]{1,0:T(8,128)(2,1)} %collective-permute-done.18.refs_2_, bf16[384,640]{1,0:T(8,128)(2,1)S(1)} %shard_map.193.refs_0_.refs_3_, ...), custom_call_target="tpu_custom_call" | custom-call | flops 629145600 | bytes 6291456 | tf_op jit(solution)/shard_map/pallas_call | solution.py:74
  132.3 4.1 %collective-permute-start.28 = (bf16[320,640]{1,0:T(8,128)(2,1)S(1)}, bf16[320,640]{1,0:T(8,128)(2,1)S(1)}, u32[]{:S(2)}, u32[]{:S(2)}) collective-permute-start(bf16[320,640]{1,0:T(8,128)(2,1)S(1)} %get-tuple-element.36.refs_10_), channel_id=1, source_target_pairs={{0,32},{8,40},{16,48},{24,56},{32,64},{40,72},{48,80},{56,88},{64,... | collective-permute-start | bytes 1228808 | tf_op jit(solution)/shard_map/ppermute | solution.py:37
  136.7 6.5 %shard_map.198 = (bf16[360,384]{1,0:T(8,128)(2,1)S(1)}, f32[2,360,384]{2,1,0:T(8,128)S(1)}, bf16[2,360,384]{2,1,0:T(8,128)(2,1)S(1)}, bf16[2,360,384]{2,1,0:T(8,128)(2,1)S(1)}) custom-call(bf16[360,640]{1,0:T(8,128)(2,1)S(1)} %bitcast.30, bf16[2,360,640]{2,1,0:T(8,128)(2,1)S(1)} %bitcast.25, bf16[360,640]{1,0:T(8,128)(2,1)S(1)} %collective-permute-done.refs_2_, ...), custom_call_target="tpu_custom_call" | custom-call | flops 2332800000 | bytes 6291456 | tf_op jit(solution)/shard_map/pallas_call | solution.py:74
  143.2 4.7 %shard_map.199 = (bf16[320,640]{1,0:T(8,128)(2,1)S(1)}, bf16[320,640]{1,0:T(8,128)(2,1)S(1)}, bf16[320,640]{1,0:T(8,128)(2,1)S(1)}, bf16[320,640]{1,0:T(8,128)(2...) custom-call(s32[7]{0:T(128)S(1)} %pad_add_fusion.1.refs_9_.refs_0_, bf16[384,5120]{1,0:T(8,128)(2,1)S(1)} %copy-done.2, ...), custom_call_target="tpu_custom_call" | custom-call | flops 1887436800 | bytes 6291456 | tf_op jit(solution)/shard_map/pallas_call | solution.py:74
  147.9 6.5 %collective-permute-start.25 = (bf16[320,640]{1,0:T(8,128)(2,1)S(1)}, bf16[320,640]{1,0:T(8,128)(2,1)S(1)}, u32[]{:S(2)}, u32[]{:S(2)}) collective-permute-start(bf16[320,640]{1,0:T(8,128)(2,1)S(1)} %get-tuple-element.48), channel_id=1, source_target_pairs={{0,96},{8,104},{16,112},{24,120},{32,0},{40,8},{48,16},{56,24},{64... | collective-permute-start | bytes 1228808 | tf_op jit(solution)/shard_map/ppermute | solution.py:37
  154.6 2.0 %collective-permute-start.29 = (bf16[320,640]{1,0:T(8,128)(2,1)S(1)}, bf16[320,640]{1,0:T(8,128)(2,1)S(1)}, u32[]{:S(2)}, u32[]{:S(2)}) collective-permute-start(bf16[320,640]{1,0:T(8,128)(2,1)S(1)} %add_convert_fusion.5), channel_id=1, source_target_pairs={{0,32},{8,40},{16,48},{24,56},{32,64},{40,72},{48,80},{56,88},{64,... | collective-permute-start | bytes 1228808 | tf_op jit(solution)/shard_map/ppermute | solution.py:37
  156.8 4.4 %shard_map.200 = (bf16[360,256]{1,0:T(8,128)(2,1)S(1)}, f32[2,360,256]{2,1,0:T(8,128)S(1)}, bf16[2,360,256]{2,1,0:T(8,128)(2,1)S(1)}, bf16[2,360,256]{2,1,0:T(8,128)(2,1)S(1)}) custom-call(bf16[360,640]{1,0:T(8,128)(2,1)S(1)} %bitcast.31, bf16[2,360,640]{2,1,0:T(8,128)(2,1)S(1)} %bitcast.27, bf16[360,640]{1,0:T(8,128)(2,1)S(1)} %collective-permute-done.refs_2_, ...), custom_call_target="tpu_custom_call" | custom-call | flops 1555200000 | bytes 4194304 | tf_op jit(solution)/shard_map/pallas_call | solution.py:74
  161.4 1.5 collective-permute-start.22
  162.8 1.4 collective-permute-done.25
  164.3 1.6 collective-permute-start.23
  166.0 4.4 %collective-permute-done.27 = bf16[320,640]{1,0:T(8,128)(2,1)S(1)} collective-permute-done((bf16[320,640]{1,0:T(8,128)(2,1)S(1)}, bf16[320,640]{1,0:T(8,128)(2,1)S(1)}, u32[]{:S(2)}, u32[]{:S(2)}) %collective-permute-start.27) | collective-permute-done | bytes 409632 | tf_op jit(solution)/shard_map/ppermute | solution.py:37
  170.4 1.3 collective-permute-start.20
  171.7 3.1 %collective-permute-start.21 = (bf16[2,360,384]{2,1,0:T(8,128)(2,1)S(1)}, bf16[2,360,384]{2,1,0:T(8,128)(2,1)S(1)}, u32[]{:S(2)}, u32[]{:S(2)}) collective-permute-start(bf16[2,360,384]{2,1,0:T(8,128)(2,1)S(1)} %get-tuple-element.42), channel_id=1, source_target_pairs={{0,8},{8,16},{16,24},{24,32},{32,40},{40,48},{48,56},{56,64},{64,7... | collective-permute-start | bytes 1658888 | tf_op jit(solution)/shard_map/ppermute | solution.py:388
  175.3 4.1 %collective-permute-start.26 = (bf16[320,640]{1,0:T(8,128)(2,1)S(1)}, bf16[320,640]{1,0:T(8,128)(2,1)S(1)}, u32[]{:S(2)}, u32[]{:S(2)}) collective-permute-start(bf16[320,640]{1,0:T(8,128)(2,1)S(1)} %add_convert_fusion.6), channel_id=1, source_target_pairs={{0,96},{8,104},{16,112},{24,120},{32,0},{40,8},{48,16},{56,24},{64... | collective-permute-start | bytes 1228808 | tf_op jit(solution)/shard_map/ppermute | solution.py:37
  179.4 1.2 shard_map.195.refs_6_
  180.6 0.8 pad_maximum_fusion
  181.5 1.1 copy-done.5
  182.5 1.3 shard_map.201
  183.8 7.3 %collective-permute-done.24 = bf16[320,640]{1,0:T(8,128)(2,1)S(1)} collective-permute-done((bf16[320,640]{1,0:T(8,128)(2,1)S(1)}, bf16[320,640]{1,0:T(8,128)(2,1)S(1)}, u32[]{:S(2)}, u32[]{:S(2)}) %collective-permute-start.24) | collective-permute-done | bytes 409632 | tf_op jit(solution)/shard_map/ppermute | solution.py:37
  191.2 8.4 %collective-permute-done.30 = bf16[320,640]{1,0:T(8,128)(2,1)S(1)} collective-permute-done((bf16[320,640]{1,0:T(8,128)(2,1)S(1)}, bf16[320,640]{1,0:T(8,128)(2,1)S(1)}, u32[]{:S(2)}, u32[]{:S(2)}) %collective-permute-start.30) | collective-permute-done | bytes 409632 | tf_op jit(solution)/shard_map/ppermute | solution.py:37
  199.5 1.0 fusion.2
  (97 shorter events, 3.8 us)
Async XLA Ops:
  0.6 14.2 %copy-start = (s32[1,16,5,63]{3,1,2,0:T(8,128)S(1)}, s32[1,16,5,63]{3,1,2,0:T(8,128)}, u32[]{:S(2)}) copy-start(s32[1,16,5,63]{3,1,2,0:T(8,128)} %param.22) | copy-start | bytes 60484
  0.6 14.3 %copy-start.11 = (s32[5,5,7]{2,1,0:T(8,128)S(1)}, s32[5,5,7]{2,1,0:T(8,128)}, u32[]{:S(2)}) copy-start(s32[5,5,7]{2,1,0:T(8,128)} %constant.188) | copy-start | bytes 2104
  0.7 14.9 %copy-start.13 = (s32[5,5]{1,0:T(8,128)S(1)}, s32[5,5]{1,0:T(8,128)}, u32[]{:S(2)}) copy-start(s32[5,5]{1,0:T(8,128)} %constant.187) | copy-start | bytes 304
  0.7 15.0 %copy-start.14 = (s32[384]{0:T(512)S(1)}, s32[384]{0:T(512)}, u32[]{:S(2)}) copy-start(s32[384]{0:T(512)} %constant.189) | copy-start | bytes 4612
  0.7 15.0 %copy-start.19 = (pred[384]{0:T(512)(128)(4,1)S(1)}, pred[384]{0:T(512)(128)(4,1)}, u32[]{:S(2)}) copy-start(pred[384]{0:T(512)(128)(4,1)} %constant.172.clone) | copy-start | bytes 1156
  0.7 15.0 %copy-start.15 = (s32[384]{0:T(512)S(1)}, s32[384]{0:T(512)}, u32[]{:S(2)}) copy-start(s32[384]{0:T(512)} %constant.169.clone) | copy-start | bytes 4612
  0.7 15.0 %copy-start.16 = (s32[384]{0:T(512)S(1)}, s32[384]{0:T(512)}, u32[]{:S(2)}) copy-start(s32[384]{0:T(512)} %constant.168.clone) | copy-start | bytes 4612
  0.7 14.1 %copy-start.20 = (s32[5,3]{0,1:T(4,128)S(1)}, s32[5,3]{0,1:T(4,128)}, u32[]{:S(2)}) copy-start(s32[5,3]{0,1:T(4,128)} %param.21) | copy-start | bytes 184
  3.0 91.3 %collective-permute-start.1 = (bf16[360,640]{1,0:T(8,128)(2,1)}, bf16[360,640]{1,0:T(8,128)(2,1)S(1)}, u32[]{:S(2)}, u32[]{:S(2)}) collective-permute-start(bf16[360,640]{1,0:T(8,128)(2,1)} %bitcast.2), channel_id=1, source_target_pairs={{8,0},{16,8},{24,16},{32,24},{40,32},{48,40},{56,48},{64,56},{72,6... | collective-permute-start | bytes 1382408 | tf_op jit(solution)/shard_map/ppermute | solution.py:242
  4.3 90.1 %collective-permute-start = (bf16[360,640]{1,0:T(8,128)(2,1)}, bf16[360,640]{1,0:T(8,128)(2,1)S(1)}, u32[]{:S(2)}, u32[]{:S(2)}) collective-permute-start(bf16[360,640]{1,0:T(8,128)(2,1)} %bitcast.2), channel_id=1, source_target_pairs={{0,8},{8,16},{16,24},{24,32},{32,40},{40,48},{48,56},{56,64},{64,7... | collective-permute-start | bytes 1382408 | tf_op jit(solution)/shard_map/ppermute | solution.py:241
  9.8 79.3 %copy-start.17 = (s32[6]{0:T(128)S(1)}, s32[6]{0:T(128)}, u32[]{:S(2)}) copy-start(s32[6]{0:T(128)} %constant.178.clone) | copy-start | bytes 76
  9.8 79.3 %copy-start.18 = (s32[6]{0:T(128)S(1)}, s32[6]{0:T(128)}, u32[]{:S(2)}) copy-start(s32[6]{0:T(128)} %constant.177.clone) | copy-start | bytes 76
  9.8 18.6 %collective-permute-start.14 = (bf16[48,5120]{1,0:T(8,128)(2,1)}, bf16[48,5120]{1,0:T(8,128)(2,1)}, u32[]{:S(2)}, u32[]{:S(2)}) collective-permute-start(bf16[48,5120]{1,0:T(8,128)(2,1)} %get-tuple-element.55), channel_id=1, source_target_pairs={{0,2},{1,3},{2,4},{3,5},{4,6},{5,7},{6,0},{7,1},{8,10},{9,11},{10,... | collective-permute-start | bytes 1474568 | tf_op jit(solution)/shard_map/ppermute | solution.py:27
  11.4 20.4 %collective-permute-start.5 = (bf16[48,5120]{1,0:T(8,128)(2,1)}, bf16[48,5120]{1,0:T(8,128)(2,1)}, u32[]{:S(2)}, u32[]{:S(2)}) collective-permute-start(bf16[48,5120]{1,0:T(8,128)(2,1)} %get-tuple-element.55), channel_id=1, source_target_pairs={{0,1},{1,0},{2,3},{3,2},{4,5},{5,4},{6,7},{7,6},{8,9},{9,8},{10,11... | collective-permute-start | bytes 1474568 | tf_op jit(solution)/shard_map/ppermute | solution.py:27
  13.0 13.3 %collective-permute-start.4 = (bf16[48,5120]{1,0:T(8,128)(2,1)}, bf16[48,5120]{1,0:T(8,128)(2,1)S(1)}, u32[]{:S(2)}, u32[]{:S(2)}) collective-permute-start(bf16[48,5120]{1,0:T(8,128)(2,1)} %get-tuple-element.55), channel_id=1, source_target_pairs={{0,6},{1,7},{2,0},{3,1},{4,2},{5,3},{6,4},{7,5},{8,14},{9,15},{10,... | collective-permute-start | bytes 1474568 | tf_op jit(solution)/shard_map/ppermute | solution.py:27
  16.5 73.3 %copy-start.12 = (s32[384]{0:T(512)S(1)}, s32[384]{0:T(512)}, u32[]{:S(2)}) copy-start(s32[384]{0:T(512)} %fusion.9) | copy-start | bytes 4612
  26.3 2.1 %copy-start.6 = (bf16[48,5120]{1,0:T(8,128)(2,1)}, bf16[48,5120]{1,0:T(8,128)(2,1)S(1)}, u32[]{:S(2)}) copy-start(bf16[48,5120]{1,0:T(8,128)(2,1)S(1)} %collective-permute-done.4.refs_5_) | copy-start | bytes 1474564
  26.3 75.1 %collective-permute-start.3 = (bf16[360,640]{1,0:T(8,128)(2,1)}, bf16[360,640]{1,0:T(8,128)(2,1)S(1)}, u32[]{:S(2)}, u32[]{:S(2)}) collective-permute-start(bf16[360,640]{1,0:T(8,128)(2,1)} %bitcast.10), channel_id=1, source_target_pairs={{8,0},{16,8},{24,16},{32,24},{40,32},{48,40},{56,48},{64,56},{72,6... | collective-permute-start | bytes 1382408 | tf_op jit(solution)/shard_map/ppermute | solution.py:242
  27.6 66.7 %copy-start.1 = (bf16[2,3,3,40,640]{4,3,2,1,0:T(8,128)(2,1)S(1)}, bf16[2,3,3,40,640]{4,3,2,1,0:T(8,128)(2,1)}, u32[]{:S(2)}) copy-start(bf16[2,3,3,40,640]{4,3,2,1,0:T(8,128)(2,1)} %param.18) | copy-start | bytes 2764804
  27.6 66.7 %copy-start.3 = (bf16[3,3,40,640]{3,2,1,0:T(8,128)(2,1)S(1)}, bf16[3,3,40,640]{3,2,1,0:T(8,128)(2,1)}, u32[]{:S(2)}) copy-start(bf16[3,3,40,640]{3,2,1,0:T(8,128)(2,1)} %param.17) | copy-start | bytes 1382404
  28.5 73.0 %collective-permute-start.2 = (bf16[360,640]{1,0:T(8,128)(2,1)}, bf16[360,640]{1,0:T(8,128)(2,1)S(1)}, u32[]{:S(2)}, u32[]{:S(2)}) collective-permute-start(bf16[360,640]{1,0:T(8,128)(2,1)} %bitcast.10), channel_id=1, source_target_pairs={{0,8},{8,16},{16,24},{24,32},{32,40},{40,48},{48,56},{56,64},{64,7... | collective-permute-start | bytes 1382408 | tf_op jit(solution)/shard_map/ppermute | solution.py:241
  31.9 13.3 %collective-permute-start.6 = (bf16[48,5120]{1,0:T(8,128)(2,1)}, bf16[48,5120]{1,0:T(8,128)(2,1)S(1)}, u32[]{:S(2)}, u32[]{:S(2)}) collective-permute-start(bf16[48,5120]{1,0:T(8,128)(2,1)} %collective-permute-done.5), channel_id=1, source_target_pairs={{0,2},{1,3},{2,4},{3,5},{4,6},{5,7},{6,0},{7,1},{8,10},{9,11},{10,... | collective-permute-start | bytes 1474568 | tf_op jit(solution)/shard_map/ppermute | solution.py:27
  45.2 44.0 %copy-start.8 = (bf16[48,5120]{1,0:T(8,128)(2,1)}, bf16[48,5120]{1,0:T(8,128)(2,1)S(1)}, u32[]{:S(2)}) copy-start(bf16[48,5120]{1,0:T(8,128)(2,1)S(1)} %collective-permute-done.6.refs_6_) | copy-start | bytes 1474564
  45.2 13.2 %collective-permute-start.15 = (bf16[48,5120]{1,0:T(8,128)(2,1)}, bf16[48,5120]{1,0:T(8,128)(2,1)S(1)}, u32[]{:S(2)}, u32[]{:S(2)}) collective-permute-start(bf16[48,5120]{1,0:T(8,128)(2,1)} %collective-permute-done.5), channel_id=1, source_target_pairs={{0,6},{1,7},{2,0},{3,1},{4,2},{5,3},{6,4},{7,5},{8,14},{9,15},{10,... | collective-permute-start | bytes 1474568 | tf_op jit(solution)/shard_map/ppermute | solution.py:27
  58.4 14.8 %collective-permute-start.16 = (bf16[48,5120]{1,0:T(8,128)(2,1)}, bf16[48,5120]{1,0:T(8,128)(2,1)S(1)}, u32[]{:S(2)}, u32[]{:S(2)}) collective-permute-start(bf16[48,5120]{1,0:T(8,128)(2,1)} %copy-done.6), channel_id=1, source_target_pairs={{0,6},{1,7},{2,0},{3,1},{4,2},{5,3},{6,4},{7,5},{8,14},{9,15},{10,... | collective-permute-start | bytes 1474568 | tf_op jit(solution)/shard_map/ppermute | solution.py:27
  73.3 15.0 %collective-permute-start.17 = (bf16[48,5120]{1,0:T(8,128)(2,1)S(1)}, bf16[48,5120]{1,0:T(8,128)(2,1)S(1)}, u32[]{:S(2)}, u32[]{:S(2)}) collective-permute-start(bf16[48,5120]{1,0:T(8,128)(2,1)S(1)} %collective-permute-done.6.refs_6_), channel_id=1, source_target_pairs={{0,2},{1,3},{2,4},{3,5},{4,6},{5,7},{6,0},{7,1},{8,10},{9,11},{10,... | collective-permute-start | bytes 1474568 | tf_op jit(solution)/shard_map/ppermute | solution.py:27
  89.2 40.0 %collective-permute-start.18 = (bf16[384,5120]{1,0:T(8,128)(2,1)}, bf16[384,5120]{1,0:T(8,128)(2,1)}, u32[]{:S(2)}, u32[]{:S(2)}) collective-permute-start(bf16[384,5120]{1,0:T(8,128)(2,1)} %constant_dynamic-update-slice_fusion.refs_1_), channel_id=1, source_target_pairs={{0,8},{8,0},{16,24},{24,16},{32,40},{40,32},{48,56},{56,48},{64,72... | collective-permute-start | bytes 11796488 | tf_op jit(solution)/shard_map/ppermute | solution.py:37
  93.4 8.0 %copy-start.7 = (bf16[48,5120]{1,0:T(8,128)(2,1)S(1)}, bf16[48,5120]{1,0:T(8,128)(2,1)}, u32[]{:S(2)}) copy-start(bf16[48,5120]{1,0:T(8,128)(2,1)} %copy-done.6) | copy-start | bytes 1474564
  94.4 1.0 copy-start.4
  95.3 0.9 copy-start.10
  96.2 5.2 %copy-start.9 = (bf16[48,5120]{1,0:T(8,128)(2,1)S(1)}, bf16[48,5120]{1,0:T(8,128)(2,1)}, u32[]{:S(2)}) copy-start(bf16[48,5120]{1,0:T(8,128)(2,1)} %copy-done.8) | copy-start | bytes 1474564
  96.2 8.8 %slice-start = ((s8[6553600]{0:T(1024)(128)(4,1)}), s8[4194304]{0:T(1024)(128)(4,1)S(1)}, s32[]{:S(2)}) async-start(s8[6553600]{0:T(1024)(128)(4,1)} %bitcast.33), calls=%async_computation | async-start | bytes 8388608
  101.4 3.6 %slice-start.1 = ((s8[6553600]{0:T(1024)(128)(4,1)}), s8[2359296]{0:T(1024)(128)(4,1)S(1)}, s32[]{:S(2)}) async-start(s8[6553600]{0:T(1024)(128)(4,1)} %bitcast.33), calls=%async_computation.1 | async-start | bytes 4718592
  105.0 17.6 %copy-start.2 = (bf16[384,5120]{1,0:T(8,128)(2,1)S(1)}, bf16[384,5120]{1,0:T(8,128)(2,1)}, u32[]{:S(2)}) copy-start(bf16[384,5120]{1,0:T(8,128)(2,1)} %constant_dynamic-update-slice_fusion.refs_1_) | copy-start | bytes 11796484
  108.3 14.2 %collective-permute-start.8 = (bf16[48,5120]{1,0:T(8,128)(2,1)S(1)}, bf16[48,5120]{1,0:T(8,128)(2,1)S(1)}, u32[]{:S(2)}, u32[]{:S(2)}) collective-permute-start(bf16[48,5120]{1,0:T(8,128)(2,1)S(1)} %get-tuple-element.31), channel_id=1, source_target_pairs={{0,6},{1,7},{2,0},{3,1},{4,2},{5,3},{6,4},{7,5},{8,14},{9,15},{10,... | collective-permute-start | bytes 1474568 | tf_op jit(solution)/shard_map/ppermute | solution.py:27
  110.1 15.7 %collective-permute-start.19 = (bf16[384,640]{1,0:T(8,128)(2,1)S(1)}, bf16[384,640]{1,0:T(8,128)(2,1)S(1)}, u32[]{:S(2)}, u32[]{:S(2)}) collective-permute-start(bf16[384,640]{1,0:T(8,128)(2,1)S(1)} %shard_map.193.refs_0_.refs_3_), channel_id=1, source_target_pairs={{0,8},{8,0},{16,24},{24,16},{32,40},{40,32},{48,56},{56,48},{64,72... | collective-permute-start | bytes 1474568 | tf_op jit(solution)/shard_map/ppermute | solution.py:37
  110.3 50.9 %collective-permute-start.7 = (bf16[48,5120]{1,0:T(8,128)(2,1)S(1)}, bf16[48,5120]{1,0:T(8,128)(2,1)S(1)}, u32[]{:S(2)}, u32[]{:S(2)}) collective-permute-start(bf16[48,5120]{1,0:T(8,128)(2,1)S(1)} %get-tuple-element.29), channel_id=1, source_target_pairs={{0,2},{1,3},{2,4},{3,5},{4,6},{5,7},{6,0},{7,1},{8,10},{9,11},{10,... | collective-permute-start | bytes 1474568 | tf_op jit(solution)/shard_map/ppermute | solution.py:27
  110.6 43.9 %collective-permute-start.10 = (bf16[48,5120]{1,0:T(8,128)(2,1)S(1)}, bf16[48,5120]{1,0:T(8,128)(2,1)S(1)}, u32[]{:S(2)}, u32[]{:S(2)}) collective-permute-start(bf16[48,5120]{1,0:T(8,128)(2,1)S(1)} %get-tuple-element.33), channel_id=1, source_target_pairs={{0,6},{1,7},{2,0},{3,1},{4,2},{5,3},{6,4},{7,5},{8,14},{9,15},{10,... | collective-permute-start | bytes 1474568 | tf_op jit(solution)/shard_map/ppermute | solution.py:27
  122.5 14.0 %collective-permute-start.11 = (bf16[48,5120]{1,0:T(8,128)(2,1)S(1)}, bf16[48,5120]{1,0:T(8,128)(2,1)S(1)}, u32[]{:S(2)}, u32[]{:S(2)}) collective-permute-start(bf16[48,5120]{1,0:T(8,128)(2,1)S(1)} %get-tuple-element.35), channel_id=1, source_target_pairs={{0,2},{1,3},{2,4},{3,5},{4,6},{5,7},{6,0},{7,1},{8,10},{9,11},{10,... | collective-permute-start | bytes 1474568 | tf_op jit(solution)/shard_map/ppermute | solution.py:27
  125.9 35.5 %collective-permute-start.9 = (bf16[48,5120]{1,0:T(8,128)(2,1)S(1)}, bf16[48,5120]{1,0:T(8,128)(2,1)S(1)}, u32[]{:S(2)}, u32[]{:S(2)}) collective-permute-start(bf16[48,5120]{1,0:T(8,128)(2,1)S(1)} %add_convert_fusion.2), channel_id=1, source_target_pairs={{0,6},{1,7},{2,0},{3,1},{4,2},{5,3},{6,4},{7,5},{8,14},{9,15},{10,... | collective-permute-start | bytes 1474568 | tf_op jit(solution)/shard_map/ppermute | solution.py:27
  132.3 15.6 %collective-permute-start.28 = (bf16[320,640]{1,0:T(8,128)(2,1)S(1)}, bf16[320,640]{1,0:T(8,128)(2,1)S(1)}, u32[]{:S(2)}, u32[]{:S(2)}) collective-permute-start(bf16[320,640]{1,0:T(8,128)(2,1)S(1)} %get-tuple-element.36.refs_10_), channel_id=1, source_target_pairs={{0,32},{8,40},{16,48},{24,56},{32,64},{40,72},{48,80},{56,88},{64,... | collective-permute-start | bytes 1228808 | tf_op jit(solution)/shard_map/ppermute | solution.py:37
  136.6 18.0 %collective-permute-start.12 = (bf16[48,5120]{1,0:T(8,128)(2,1)S(1)}, bf16[48,5120]{1,0:T(8,128)(2,1)S(1)}, u32[]{:S(2)}, u32[]{:S(2)}) collective-permute-start(bf16[48,5120]{1,0:T(8,128)(2,1)S(1)} %add_convert_fusion.1), channel_id=1, source_target_pairs={{0,2},{1,3},{2,4},{3,5},{4,6},{5,7},{6,0},{7,1},{8,10},{9,11},{10,... | collective-permute-start | bytes 1474568 | tf_op jit(solution)/shard_map/ppermute | solution.py:27
  147.9 16.4 %collective-permute-start.25 = (bf16[320,640]{1,0:T(8,128)(2,1)S(1)}, bf16[320,640]{1,0:T(8,128)(2,1)S(1)}, u32[]{:S(2)}, u32[]{:S(2)}) collective-permute-start(bf16[320,640]{1,0:T(8,128)(2,1)S(1)} %get-tuple-element.48), channel_id=1, source_target_pairs={{0,96},{8,104},{16,112},{24,120},{32,0},{40,8},{48,16},{56,24},{64... | collective-permute-start | bytes 1228808 | tf_op jit(solution)/shard_map/ppermute | solution.py:37
  154.5 15.9 %collective-permute-start.27 = (bf16[320,640]{1,0:T(8,128)(2,1)S(1)}, bf16[320,640]{1,0:T(8,128)(2,1)S(1)}, u32[]{:S(2)}, u32[]{:S(2)}) collective-permute-start(bf16[320,640]{1,0:T(8,128)(2,1)S(1)} %get-tuple-element.50), channel_id=1, source_target_pairs={{0,96},{8,104},{16,112},{24,120},{32,0},{40,8},{48,16},{56,24},{64... | collective-permute-start | bytes 1228808 | tf_op jit(solution)/shard_map/ppermute | solution.py:37
  154.6 17.1 %collective-permute-start.29 = (bf16[320,640]{1,0:T(8,128)(2,1)S(1)}, bf16[320,640]{1,0:T(8,128)(2,1)S(1)}, u32[]{:S(2)}, u32[]{:S(2)}) collective-permute-start(bf16[320,640]{1,0:T(8,128)(2,1)S(1)} %add_convert_fusion.5), channel_id=1, source_target_pairs={{0,32},{8,40},{16,48},{24,56},{32,64},{40,72},{48,80},{56,88},{64,... | collective-permute-start | bytes 1228808 | tf_op jit(solution)/shard_map/ppermute | solution.py:37
  161.2 14.1 %collective-permute-start.13 = (bf16[48,5120]{1,0:T(8,128)(2,1)S(1)}, bf16[48,5120]{1,0:T(8,128)(2,1)S(1)}, u32[]{:S(2)}, u32[]{:S(2)}) collective-permute-start(bf16[48,5120]{1,0:T(8,128)(2,1)S(1)} %add_convert_fusion), channel_id=1, source_target_pairs={{0,1},{1,0},{2,3},{3,2},{4,5},{5,4},{6,7},{7,6},{8,9},{9,8},{10,11... | collective-permute-start | bytes 1474568 | tf_op jit(solution)/shard_map/ppermute | solution.py:27
  161.4 13.9 %collective-permute-start.22 = (bf16[2,360,256]{2,1,0:T(8,128)(2,1)S(1)}, bf16[2,360,256]{2,1,0:T(8,128)(2,1)S(1)}, u32[]{:S(2)}, u32[]{:S(2)}) collective-permute-start(bf16[2,360,256]{2,1,0:T(8,128)(2,1)S(1)} %get-tuple-element.44), channel_id=1, source_target_pairs={{8,0},{16,8},{24,16},{32,24},{40,32},{48,40},{56,48},{64,56},{72,6... | collective-permute-start | bytes 1105928 | tf_op jit(solution)/shard_map/ppermute | solution.py:387
  164.3 15.1 %collective-permute-start.23 = (bf16[2,360,256]{2,1,0:T(8,128)(2,1)S(1)}, bf16[2,360,256]{2,1,0:T(8,128)(2,1)S(1)}, u32[]{:S(2)}, u32[]{:S(2)}) collective-permute-start(bf16[2,360,256]{2,1,0:T(8,128)(2,1)S(1)} %get-tuple-element.45), channel_id=1, source_target_pairs={{0,8},{8,16},{16,24},{24,32},{32,40},{40,48},{48,56},{56,64},{64,7... | collective-permute-start | bytes 1105928 | tf_op jit(solution)/shard_map/ppermute | solution.py:388
  170.4 11.1 %collective-permute-start.20 = (bf16[2,360,384]{2,1,0:T(8,128)(2,1)S(1)}, bf16[2,360,384]{2,1,0:T(8,128)(2,1)S(1)}, u32[]{:S(2)}, u32[]{:S(2)}) collective-permute-start(bf16[2,360,384]{2,1,0:T(8,128)(2,1)S(1)} %get-tuple-element.38.refs_5_), channel_id=1, source_target_pairs={{8,0},{16,8},{24,16},{32,24},{40,32},{48,40},{56,48},{64,56},{72,6... | collective-permute-start | bytes 1658888 | tf_op jit(solution)/shard_map/ppermute | solution.py:387
  171.7 9.8 %collective-permute-start.21 = (bf16[2,360,384]{2,1,0:T(8,128)(2,1)S(1)}, bf16[2,360,384]{2,1,0:T(8,128)(2,1)S(1)}, u32[]{:S(2)}, u32[]{:S(2)}) collective-permute-start(bf16[2,360,384]{2,1,0:T(8,128)(2,1)S(1)} %get-tuple-element.42), channel_id=1, source_target_pairs={{0,8},{8,16},{16,24},{24,32},{32,40},{40,48},{48,56},{56,64},{64,7... | collective-permute-start | bytes 1658888 | tf_op jit(solution)/shard_map/ppermute | solution.py:388
  175.3 15.8 %collective-permute-start.24 = (bf16[320,640]{1,0:T(8,128)(2,1)S(1)}, bf16[320,640]{1,0:T(8,128)(2,1)S(1)}, u32[]{:S(2)}, u32[]{:S(2)}) collective-permute-start(bf16[320,640]{1,0:T(8,128)(2,1)S(1)} %get-tuple-element.46), channel_id=1, source_target_pairs={{0,32},{8,40},{16,48},{24,56},{32,64},{40,72},{48,80},{56,88},{64,... | collective-permute-start | bytes 1228808 | tf_op jit(solution)/shard_map/ppermute | solution.py:37
  175.3 15.8 %collective-permute-start.26 = (bf16[320,640]{1,0:T(8,128)(2,1)S(1)}, bf16[320,640]{1,0:T(8,128)(2,1)S(1)}, u32[]{:S(2)}, u32[]{:S(2)}) collective-permute-start(bf16[320,640]{1,0:T(8,128)(2,1)S(1)} %add_convert_fusion.6), channel_id=1, source_target_pairs={{0,96},{8,104},{16,112},{24,120},{32,0},{40,8},{48,16},{56,24},{64... | collective-permute-start | bytes 1228808 | tf_op jit(solution)/shard_map/ppermute | solution.py:37
  179.4 20.1 %collective-permute-start.30 = (bf16[320,640]{1,0:T(8,128)(2,1)S(1)}, bf16[320,640]{1,0:T(8,128)(2,1)S(1)}, u32[]{:S(2)}, u32[]{:S(2)}) collective-permute-start(bf16[320,640]{1,0:T(8,128)(2,1)S(1)} %add_convert_fusion.4), channel_id=1, source_target_pairs={{0,16},{8,24},{16,0},{24,8},{32,48},{40,56},{48,32},{56,40},{64,80... | collective-permute-start | bytes 1228808 | tf_op jit(solution)/shard_map/ppermute | solution.py:37
  181.5 1.1 copy-start.5

commit v7 on v6

--- a/solution.py
+++ b/solution.py
@@ -55,7 +55,7 @@
     c11 = shift(c01, -1, 0)
     c31 = shift(c01, 1, 0)
     c21 = shift(c31, 1, 0)
-    return jnp.concatenate([own, c10, c30, c01, c31, c11, c20, c21], axis=0), [c10, c31]
+    return [own, c10, c30, c01, c31, c11, c20, c21], [c10, c31]
 
 
 ROOM = 24 << 20
@@ -246,7 +246,7 @@
     room = -(-piece // 16) * 16
     own_grad = grad_out.transpose(0, 2, 1, 3).reshape(piece, model_width)
     own_grad = jnp.pad(own_grad, ((0, room - piece), (0, 0)))
-    all_grad, last_hops = gathered(own_grad, tensor_shift)
+    pieces, last_hops = gathered(own_grad, tensor_shift)
     slots = 8 * room
 
     row = np.arange(slots) % room
@@ -298,6 +298,8 @@
         flops=pairs * 1000,
         moved=6 << 20,
     )
+    *early, probs = lax.optimization_barrier((*pieces[:6], probs))
+    all_grad = jnp.concatenate([*early, *pieces[6:]], axis=0)
     (attended,) = kernel(
         attend_kernel,
         [((slots, channels), BF16)],

time: 201 us -> 172 us (0.86)
  waiting for transfers between devices: 83.1 us -> 34 us
  starting transfers between devices: 53.3 us -> 87.5 us
  local copies, waits for them, and re-layouts: 16.8 us -> 10.4 us
  other arithmetic: 9.54 us -> 4.49 us
  Pallas kernels: 36.5 us -> 33.2 us
    ppermute x14, waiting for transfers between devices: 61.6 us -> 12.7 us  [tensor_shift(): return lax.ppermute(value, 'tensor', pairs)]
    ppermute x9, starting transfers between devices: 17 us -> 53 us  [seq_shift(): return lax.ppermute(value, 'seq', pairs)]
    unnamed x53 -> x41, local copies, waits for them, and re-layouts: 11 us -> 4.65 us
    pallas_call x10, Pallas kernels: 36.5 us -> 33.2 us  [kernel(): pl.pallas_call(run, grid=grid, in_specs=[*specs, *[ANYWHERE] * len(after)...]
    ppermute x9, waiting for transfers between devices: 21.5 us -> 18.6 us  [seq_shift(): return lax.ppermute(value, 'seq', pairs)]
    ppermute x2, waiting for transfers between devices: 0.01 us -> 2.45 us  [layer(): down = lax.ppermute(flat_kv[i], 'seq', back)]
  transfers between devices with their start and end apart: 31 -> 31, of which waited for: 11 -> 10; matrix products, arithmetic and copies ran while one was open for 10% -> 6% of each run, Pallas kernels for 18% -> 19%
where the time goes in v7:
time: 172 us; the launch traced here: 171 us
  starting transfers between devices  87.5 us (51%)
  waiting for transfers between devices  34 us (20%)
  Pallas kernels  33.2 us (19%)
  local copies, waits for them, and re-layouts  10.4 us (6%)
  other arithmetic  4.49 us (3%)
    ppermute x9, starting transfers between devices, seq_shift(): return lax.ppermute(value, 'seq', pairs)  53 us
    pallas_call x10, Pallas kernels, kernel(): pl.pallas_call(run, grid=grid, in_specs=[*specs, *[ANYWHERE] * len(after)...  33.2 us
    ppermute x9, waiting for transfers between devices, seq_shift(): return lax.ppermute(value, 'seq', pairs)  18.6 us
    ppermute x14, starting transfers between devices, tensor_shift(): return lax.ppermute(value, 'tensor', pairs)  18.5 us
    ppermute x14, waiting for transfers between devices, tensor_shift(): return lax.ppermute(value, 'tensor', pairs)  12.7 us
    ppermute x2, starting transfers between devices, layer(): up = lax.ppermute(flat_kv[i], 'seq', onward)  6.12 us
    unnamed x41, local copies, waits for them, and re-layouts  4.65 us
    ppermute x2, starting transfers between devices, send_halo(): from_above = lax.ppermute(grad_down, 'seq', onward)  4.46 us
  transfers between devices with their start and end apart: 31, of which 10 were waited for; matrix products, arithmetic and copies ran while one was open for 6% of the time, Pallas kernels for 19%

profile of v7, /device:TPU:0, one launch (start us, length us, event | category | flops | bytes accessed | tf_op | source)
XLA Modules:
  0.0 170.9 jit_solution(18064250147111646028)
XLA Ops:
  0.8 1.6 reshape.157
  2.4 0.8 pad.8
  3.2 1.7 collective-permute-start.2
  4.9 1.5 collective-permute-start.1
  6.4 1.7 %collective-permute-start = (bf16[48,5120]{1,0:T(8,128)(2,1)}, bf16[48,5120]{1,0:T(8,128)(2,1)S(1)}, u32[]{:S(2)}, u32[]{:S(2)}) collective-permute-start(bf16[48,5120]{1,0:T(8,128)(2,1)} %pad.8), channel_id=1, source_target_pairs={{0,6},{1,7},{2,0},{3,1},{4,2},{5,3},{6,4},{7,5},{8,14},{9,15},{10,... | collective-permute-start | bytes 1474568 | tf_op jit(solution)/shard_map/ppermute | solution.py:27
  8.1 2.2 %fusion.24 = (bf16[1,3,3,40,640]{4,3,2,1,0:T(8,128)(2,1)}, bf16[1,3,3,40,640]{4,3,2,1,0:T(8,128)(2,1)}) fusion(bf16[2,3,3,40,640]{4,3,2,1,0:T(8,128)(2,1)} %param.18), kind=kLoop, calls=%fused_computation.84 | loop fusion | bytes 1843200 | tf_op jit(solution)/shard_map/slice | solution.py:241
  10.3 1.3 collective-permute-start.6
  11.6 3.1 %collective-permute-start.5 = (bf16[360,640]{1,0:T(8,128)(2,1)}, bf16[360,640]{1,0:T(8,128)(2,1)S(1)}, u32[]{:S(2)}, u32[]{:S(2)}) collective-permute-start(bf16[360,640]{1,0:T(8,128)(2,1)} %bitcast.3), channel_id=1, source_target_pairs={{0,8},{8,16},{16,24},{24,32},{32,40},{40,48},{48,56},{56,64},{64,7... | collective-permute-start | bytes 1382408 | tf_op jit(solution)/shard_map/ppermute | solution.py:241
  15.2 0.5 multiply_reduce_fusion
  15.7 0.1 copy.23
  15.9 0.1 fusion.3.refs_5_
  16.2 0.7 and_select_fusion
  16.9 0.8 pad.9
  17.9 1.6 collective-permute-start.4
  19.4 0.5 collective-permute-start.3
  20.0 5.2 %shard_map.192.refs_0_.refs_7_ = bf16[5,3,360,360]{3,2,1,0:T(8,128)(2,1)S(1)} custom-call(bf16[360,640]{1,0:T(8,128)(2,1)S(1)} %bitcast.29, bf16[2,360,640]{2,1,0:T(8,128)(2,1)S(1)} %bitcast.23, bf16[360,640]{1,0:T(8,128)(2,1)S(1)} %collective-permute-done.5.refs_2_, bf16[360,640]{1,0:T(8,128)(2,1)S(1)} %collective-permute-done.6.refs_3_, ...), custom_call_target="tpu_custom_call" | custom-call | flops 1944000000 | bytes 6291456 | tf_op jit(solution)/shard_map/pallas_call | solution.py:74
  25.3 2.8 %collective-permute-start.16 = (bf16[48,5120]{1,0:T(8,128)(2,1)S(1)}, bf16[48,5120]{1,0:T(8,128)(2,1)S(1)}, u32[]{:S(2)}, u32[]{:S(2)}) collective-permute-start(bf16[48,5120]{1,0:T(8,128)(2,1)S(1)} %collective-permute-done.refs_5_), channel_id=1, source_target_pairs={{0,6},{1,7},{2,0},{3,1},{4,2},{5,3},{6,4},{7,5},{8,14},{9,15},{10,... | collective-permute-start | bytes 1474568 | tf_op jit(solution)/shard_map/ppermute | solution.py:27
  28.1 2.6 %collective-permute-done.4 = bf16[48,5120]{1,0:T(8,128)(2,1)S(1)} collective-permute-done((bf16[48,5120]{1,0:T(8,128)(2,1)}, bf16[48,5120]{1,0:T(8,128)(2,1)S(1)}, u32[]{:S(2)}, u32[]{:S(2)}) %collective-permute-start.4) | collective-permute-done | bytes 491552 | tf_op jit(solution)/shard_map/ppermute | solution.py:27
  30.7 1.1 constant_dynamic-update-slice_fusion.7
  31.8 1.1 constant_dynamic-update-slice_fusion.5
  32.9 1.2 constant_dynamic-update-slice_fusion.4
  34.1 0.3 collective-permute-start.17
  34.5 3.6 %collective-permute-done.16 = bf16[48,5120]{1,0:T(8,128)(2,1)S(1)} collective-permute-done((bf16[48,5120]{1,0:T(8,128)(2,1)S(1)}, bf16[48,5120]{1,0:T(8,128)(2,1)S(1)}, u32[]{:S(2)}, u32[]{:S(2)}) %collective-permute-start.16) | collective-permute-done | bytes 491552 | tf_op jit(solution)/shard_map/ppermute | solution.py:27
  38.2 6.5 %collective-permute-done.17 = bf16[48,5120]{1,0:T(8,128)(2,1)S(1)} collective-permute-done((bf16[48,5120]{1,0:T(8,128)(2,1)S(1)}, bf16[48,5120]{1,0:T(8,128)(2,1)S(1)}, u32[]{:S(2)}, u32[]{:S(2)}) %collective-permute-start.17) | collective-permute-done | bytes 491552 | tf_op jit(solution)/shard_map/ppermute | solution.py:27
  44.7 4.7 %collective-permute-start.18 = (bf16[384,5120]{1,0:T(8,128)(2,1)S(1)}, bf16[384,5120]{1,0:T(8,128)(2,1)S(1)}, u32[]{:S(2)}, u32[]{:S(2)}) collective-permute-start(bf16[384,5120]{1,0:T(8,128)(2,1)S(1)} %constant_dynamic-update-slice_fusion.refs_1_), channel_id=1, source_target_pairs={{0,8},{8,0},{16,24},{24,16},{32,40},{40,32},{48,56},{56,48},{64,72... | collective-permute-start | bytes 11796488 | tf_op jit(solution)/shard_map/ppermute | solution.py:37
  49.4 1.4 collective-permute-start.8
  50.9 3.1 %collective-permute-start.7 = (bf16[360,640]{1,0:T(8,128)(2,1)S(1)}, bf16[360,640]{1,0:T(8,128)(2,1)S(1)}, u32[]{:S(2)}, u32[]{:S(2)}) collective-permute-start(bf16[360,640]{1,0:T(8,128)(2,1)S(1)} %bitcast.38), channel_id=1, source_target_pairs={{0,8},{8,16},{16,24},{24,32},{32,40},{40,48},{48,56},{56,64},{64,7... | collective-permute-start | bytes 1382408 | tf_op jit(solution)/shard_map/ppermute | solution.py:241
  53.9 2.4 %collective-permute-done.8.refs_3_.refs_6_ = bf16[360,640]{1,0:T(8,128)(2,1)S(1)} collective-permute-done((bf16[360,640]{1,0:T(8,128)(2,1)S(1)}, bf16[360,640]{1,0:T(8,128)(2,1)S(1)}, u32[]{:S(2)}, u32[]{:S(2)}) %collective-permute-start.8) | collective-permute-done | bytes 460832 | tf_op jit(solution)/shard_map/ppermute | solution.py:242
  56.4 0.1 collective-permute-done.7.refs_2_.refs_5_
  56.5 3.5 %shard_map.193.refs_0_.refs_3_ = bf16[384,640]{1,0:T(8,128)(2,1)S(1)} custom-call(bf16[5,3,360,360]{3,2,1,0:T(8,128)(2,1)S(1)} %shard_map.192.refs_0_.refs_7_, bf16[2,360,640]{2,1,0:T(8,128)(2,1)S(1)} %bitcast.24, bf16[360,640]{1,0:T(8,128)(2,1)S(1)} %collective-permute-done.7.refs_2_.refs_5_, bf16[360,640]{1,0:T(8,128)(2,1)S(1)} %collective-permute-done.8.refs_3_.refs_6_, ...), custom_call_target="tpu_custom_call" | custom-call | flops 972000000 | bytes 6291456 | tf_op jit(solution)/shard_map/pallas_call | solution.py:74
  60.0 3.2 %shard_map.194 = (bf16[48,5120]{1,0:T(8,128)(2,1)S(1)}, bf16[48,5120]{1,0:T(8,128)(2,1)S(1)}, bf16[48,5120]{1,0:T(8,128)(2,1)S(1)}, bf16[48,5120]{1,0:T(8,128)(2...) custom-call(bf16[384,640]{1,0:T(8,128)(2,1)S(1)} %shard_map.193.refs, ...), custom_call_target="tpu_custom_call" | custom-call | flops 3774873600 | bytes 12582912 | tf_op jit(solution)/shard_map/pallas_call | solution.py:74
  63.3 1.6 collective-permute-start.10
  64.9 11.9 %collective-permute-start.19 = (bf16[384,640]{1,0:T(8,128)(2,1)S(1)}, bf16[384,640]{1,0:T(8,128)(2,1)S(1)}, u32[]{:S(2)}, u32[]{:S(2)}) collective-permute-start(bf16[384,640]{1,0:T(8,128)(2,1)S(1)} %shard_map.193.refs_0_.refs_3_), channel_id=1, source_target_pairs={{0,8},{8,0},{16,24},{24,16},{32,40},{40,32},{48,56},{56,48},{64,72... | collective-permute-start | bytes 1474568 | tf_op jit(solution)/shard_map/ppermute | solution.py:37
  76.8 0.9 collective-permute-start.9
  77.7 2.3 %collective-permute-start.12 = (bf16[48,5120]{1,0:T(8,128)(2,1)S(1)}, bf16[48,5120]{1,0:T(8,128)(2,1)S(1)}, u32[]{:S(2)}, u32[]{:S(2)}) collective-permute-start(bf16[48,5120]{1,0:T(8,128)(2,1)S(1)} %get-tuple-element.41), channel_id=1, source_target_pairs={{0,6},{1,7},{2,0},{3,1},{4,2},{5,3},{6,4},{7,5},{8,14},{9,15},{10,... | collective-permute-start | bytes 1474568 | tf_op jit(solution)/shard_map/ppermute | solution.py:27
  80.0 0.1 add_convert_fusion.2
  80.1 3.2 %shard_map.196.refs_5_.refs_8_ = bf16[384,640]{1,0:T(8,128)(2,1)S(1)} custom-call(bf16[640,5120]{1,0:T(8,128)(2,1)S(1)} %bitcast.34, bf16[384,5120]{1,0:T(8,128)(2,1)S(1)} %constant_dynamic-update-slice_fusion.refs_1_, bf16[48,5120]{1,0:T(8,128)(2,1)S(1)} %get-tuple-element.36.refs_0_.refs_2_), custom_call_target="tpu_custom_call" | custom-call | flops 3774873600 | bytes 12582912 | tf_op jit(solution)/shard_map/pallas_call | solution.py:74
  83.4 3.3 %collective-permute-start.11 = (bf16[48,5120]{1,0:T(8,128)(2,1)S(1)}, bf16[48,5120]{1,0:T(8,128)(2,1)S(1)}, u32[]{:S(2)}, u32[]{:S(2)}) collective-permute-start(bf16[48,5120]{1,0:T(8,128)(2,1)S(1)} %add_convert_fusion.2), channel_id=1, source_target_pairs={{0,6},{1,7},{2,0},{3,1},{4,2},{5,3},{6,4},{7,5},{8,14},{9,15},{10,... | collective-permute-start | bytes 1474568 | tf_op jit(solution)/shard_map/ppermute | solution.py:27
  86.7 1.5 shard_map.197
  88.2 16.2 %collective-permute-start.28 = (bf16[320,640]{1,0:T(8,128)(2,1)S(1)}, bf16[320,640]{1,0:T(8,128)(2,1)S(1)}, u32[]{:S(2)}, u32[]{:S(2)}) collective-permute-start(bf16[320,640]{1,0:T(8,128)(2,1)S(1)} %get-tuple-element.50.refs_10_), channel_id=1, source_target_pairs={{0,32},{8,40},{16,48},{24,56},{32,64},{40,72},{48,80},{56,88},{64,... | collective-permute-start | bytes 1228808 | tf_op jit(solution)/shard_map/ppermute | solution.py:37
  104.6 6.5 %shard_map.198 = (bf16[360,384]{1,0:T(8,128)(2,1)S(1)}, f32[2,360,384]{2,1,0:T(8,128)S(1)}, bf16[2,360,384]{2,1,0:T(8,128)(2,1)S(1)}, bf16[2,360,384]{2,1,0:T(8,128)(2,1)S(1)}) custom-call(bf16[360,640]{1,0:T(8,128)(2,1)S(1)} %bitcast.30, bf16[2,360,640]{2,1,0:T(8,128)(2,1)S(1)} %bitcast.25, bf16[360,640]{1,0:T(8,128)(2,1)S(1)} %collective-permute-done.5.refs_2_, ...), custom_call_target="tpu_custom_call" | custom-call | flops 2332800000 | bytes 6291456 | tf_op jit(solution)/shard_map/pallas_call | solution.py:74
  111.2 3.1 %shard_map.199 = (bf16[320,640]{1,0:T(8,128)(2,1)S(1)}, bf16[320,640]{1,0:T(8,128)(2,1)S(1)}, bf16[320,640]{1,0:T(8,128)(2,1)S(1)}, bf16[320,640]{1,0:T(8,128)(2...) custom-call(s32[7]{0:T(128)S(1)} %pad_add_fusion.1.refs_9_.refs_0_, ...), custom_call_target="tpu_custom_call" | custom-call | flops 1887436800 | bytes 6291456 | tf_op jit(solution)/shard_map/pallas_call | solution.py:74
  114.3 7.1 %collective-permute-start.25 = (bf16[320,640]{1,0:T(8,128)(2,1)S(1)}, bf16[320,640]{1,0:T(8,128)(2,1)S(1)}, u32[]{:S(2)}, u32[]{:S(2)}) collective-permute-start(bf16[320,640]{1,0:T(8,128)(2,1)S(1)} %get-tuple-element.62), channel_id=1, source_target_pairs={{0,96},{8,104},{16,112},{24,120},{32,0},{40,8},{48,16},{56,24},{64... | collective-permute-start | bytes 1228808 | tf_op jit(solution)/shard_map/ppermute | solution.py:37
  121.6 2.0 %collective-permute-start.29 = (bf16[320,640]{1,0:T(8,128)(2,1)S(1)}, bf16[320,640]{1,0:T(8,128)(2,1)S(1)}, u32[]{:S(2)}, u32[]{:S(2)}) collective-permute-start(bf16[320,640]{1,0:T(8,128)(2,1)S(1)} %add_convert_fusion.5), channel_id=1, source_target_pairs={{0,32},{8,40},{16,48},{24,56},{32,64},{40,72},{48,80},{56,88},{64,... | collective-permute-start | bytes 1228808 | tf_op jit(solution)/shard_map/ppermute | solution.py:37
  123.6 0.2 add_convert_fusion
  123.8 4.4 %shard_map.200 = (bf16[360,256]{1,0:T(8,128)(2,1)S(1)}, f32[2,360,256]{2,1,0:T(8,128)S(1)}, bf16[2,360,256]{2,1,0:T(8,128)(2,1)S(1)}, bf16[2,360,256]{2,1,0:T(8,128)(2,1)S(1)}) custom-call(bf16[360,640]{1,0:T(8,128)(2,1)S(1)} %bitcast.31, bf16[2,360,640]{2,1,0:T(8,128)(2,1)S(1)} %bitcast.27, bf16[360,640]{1,0:T(8,128)(2,1)S(1)} %collective-permute-done.5.refs_2_, ...), custom_call_target="tpu_custom_call" | custom-call | flops 1555200000 | bytes 4194304 | tf_op jit(solution)/shard_map/pallas_call | solution.py:74
  128.3 1.5 collective-permute-start.22
  129.8 1.4 collective-permute-done.25
  131.3 1.4 collective-permute-start.23
  132.8 3.8 %collective-permute-done.27 = bf16[320,640]{1,0:T(8,128)(2,1)S(1)} collective-permute-done((bf16[320,640]{1,0:T(8,128)(2,1)S(1)}, bf16[320,640]{1,0:T(8,128)(2,1)S(1)}, u32[]{:S(2)}, u32[]{:S(2)}) %collective-permute-start.27) | collective-permute-done | bytes 409632 | tf_op jit(solution)/shard_map/ppermute | solution.py:37
  136.6 1.3 collective-permute-start.20
  137.9 3.1 %collective-permute-start.21 = (bf16[2,360,384]{2,1,0:T(8,128)(2,1)S(1)}, bf16[2,360,384]{2,1,0:T(8,128)(2,1)S(1)}, u32[]{:S(2)}, u32[]{:S(2)}) collective-permute-start(bf16[2,360,384]{2,1,0:T(8,128)(2,1)S(1)} %get-tuple-element.56), channel_id=1, source_target_pairs={{0,8},{8,16},{16,24},{24,32},{32,40},{40,48},{48,56},{56,64},{64,7... | collective-permute-start | bytes 1658888 | tf_op jit(solution)/shard_map/ppermute | solution.py:390
  141.0 0.2 add_convert_fusion.4
  141.2 2.9 %collective-permute-start.24 = (bf16[320,640]{1,0:T(8,128)(2,1)S(1)}, bf16[320,640]{1,0:T(8,128)(2,1)S(1)}, u32[]{:S(2)}, u32[]{:S(2)}) collective-permute-start(bf16[320,640]{1,0:T(8,128)(2,1)S(1)} %get-tuple-element.60), channel_id=1, source_target_pairs={{0,32},{8,40},{16,48},{24,56},{32,64},{40,72},{48,80},{56,88},{64,... | collective-permute-start | bytes 1228808 | tf_op jit(solution)/shard_map/ppermute | solution.py:37
  144.1 7.8 %collective-permute-start.26 = (bf16[320,640]{1,0:T(8,128)(2,1)S(1)}, bf16[320,640]{1,0:T(8,128)(2,1)S(1)}, u32[]{:S(2)}, u32[]{:S(2)}) collective-permute-start(bf16[320,640]{1,0:T(8,128)(2,1)S(1)} %add_convert_fusion.6), channel_id=1, source_target_pairs={{0,96},{8,104},{16,112},{24,120},{32,0},{40,8},{48,16},{56,24},{64... | collective-permute-start | bytes 1228808 | tf_op jit(solution)/shard_map/ppermute | solution.py:37
  151.9 0.3 collective-permute-start.30
  152.2 1.2 shard_map.195.refs_6_
  153.4 0.8 pad_maximum_fusion
  154.2 1.1 copy-done.3
  155.3 1.3 shard_map.201
  156.6 4.6 %collective-permute-done.24 = bf16[320,640]{1,0:T(8,128)(2,1)S(1)} collective-permute-done((bf16[320,640]{1,0:T(8,128)(2,1)S(1)}, bf16[320,640]{1,0:T(8,128)(2,1)S(1)}, u32[]{:S(2)}, u32[]{:S(2)}) %collective-permute-start.24) | collective-permute-done | bytes 409632 | tf_op jit(solution)/shard_map/ppermute | solution.py:37
  161.2 0.3 collective-permute-done.26
  161.5 8.5 %collective-permute-done.30 = bf16[320,640]{1,0:T(8,128)(2,1)S(1)} collective-permute-done((bf16[320,640]{1,0:T(8,128)(2,1)S(1)}, bf16[320,640]{1,0:T(8,128)(2,1)S(1)}, u32[]{:S(2)}, u32[]{:S(2)}) %collective-permute-start.30) | collective-permute-done | bytes 409632 | tf_op jit(solution)/shard_map/ppermute | solution.py:37
  169.9 1.0 fusion.2
  (86 shorter events, 1.6 us)
Async XLA Ops:
  0.6 14.4 %copy-start = (s32[1,16,5,63]{3,1,2,0:T(8,128)S(1)}, s32[1,16,5,63]{3,1,2,0:T(8,128)}, u32[]{:S(2)}) copy-start(s32[1,16,5,63]{3,1,2,0:T(8,128)} %param.22) | copy-start | bytes 60484
  0.6 14.1 %copy-start.7 = (s32[384]{0:T(512)S(1)}, s32[384]{0:T(512)}, u32[]{:S(2)}) copy-start(s32[384]{0:T(512)} %constant.189) | copy-start | bytes 4612
  0.7 14.1 %copy-start.12 = (pred[384]{0:T(512)(128)(4,1)S(1)}, pred[384]{0:T(512)(128)(4,1)}, u32[]{:S(2)}) copy-start(pred[384]{0:T(512)(128)(4,1)} %constant.172.clone) | copy-start | bytes 1156
  0.7 14.1 %copy-start.8 = (s32[384]{0:T(512)S(1)}, s32[384]{0:T(512)}, u32[]{:S(2)}) copy-start(s32[384]{0:T(512)} %constant.169.clone) | copy-start | bytes 4612
  0.7 14.1 %copy-start.9 = (s32[384]{0:T(512)S(1)}, s32[384]{0:T(512)}, u32[]{:S(2)}) copy-start(s32[384]{0:T(512)} %constant.168.clone) | copy-start | bytes 4612
  0.7 14.5 %copy-start.5 = (s32[5,5,7]{2,1,0:T(8,128)S(1)}, s32[5,5,7]{2,1,0:T(8,128)}, u32[]{:S(2)}) copy-start(s32[5,5,7]{2,1,0:T(8,128)} %constant.188) | copy-start | bytes 2104
  0.7 15.3 %copy-start.6 = (s32[5,5]{1,0:T(8,128)S(1)}, s32[5,5]{1,0:T(8,128)}, u32[]{:S(2)}) copy-start(s32[5,5]{1,0:T(8,128)} %constant.187) | copy-start | bytes 304
  0.7 16.2 %copy-start.10 = (s32[6]{0:T(128)S(1)}, s32[6]{0:T(128)}, u32[]{:S(2)}) copy-start(s32[6]{0:T(128)} %constant.178.clone) | copy-start | bytes 76
  0.7 16.2 %copy-start.11 = (s32[6]{0:T(128)S(1)}, s32[6]{0:T(128)}, u32[]{:S(2)}) copy-start(s32[6]{0:T(128)} %constant.177.clone) | copy-start | bytes 76
  0.7 16.2 %copy-start.14 = (s32[2]{0:T(128)S(1)}, s32[2]{0:T(128)}, u32[]{:S(2)}) copy-start(s32[2]{0:T(128)} %constant.176.clone) | copy-start | bytes 28
  0.8 19.3 %copy-start.1 = (bf16[2,3,3,40,640]{4,3,2,1,0:T(8,128)(2,1)S(1)}, bf16[2,3,3,40,640]{4,3,2,1,0:T(8,128)(2,1)}, u32[]{:S(2)}) copy-start(bf16[2,3,3,40,640]{4,3,2,1,0:T(8,128)(2,1)} %param.18) | copy-start | bytes 2764804
  0.8 13.9 %copy-start.13 = (s32[5,3]{0,1:T(4,128)S(1)}, s32[5,3]{0,1:T(4,128)}, u32[]{:S(2)}) copy-start(s32[5,3]{0,1:T(4,128)} %param.21) | copy-start | bytes 184
  0.8 19.3 %copy-start.2 = (bf16[3,3,40,640]{3,2,1,0:T(8,128)(2,1)S(1)}, bf16[3,3,40,640]{3,2,1,0:T(8,128)(2,1)}, u32[]{:S(2)}) copy-start(bf16[3,3,40,640]{3,2,1,0:T(8,128)(2,1)} %param.17) | copy-start | bytes 1382404
  3.2 14.7 %collective-permute-start.2 = (bf16[48,5120]{1,0:T(8,128)(2,1)}, bf16[48,5120]{1,0:T(8,128)(2,1)}, u32[]{:S(2)}, u32[]{:S(2)}) collective-permute-start(bf16[48,5120]{1,0:T(8,128)(2,1)} %pad.8), channel_id=1, source_target_pairs={{0,1},{1,0},{2,3},{3,2},{4,5},{5,4},{6,7},{7,6},{8,9},{9,8},{10,11... | collective-permute-start | bytes 1474568 | tf_op jit(solution)/shard_map/ppermute | solution.py:27
  4.9 23.2 %collective-permute-start.1 = (bf16[48,5120]{1,0:T(8,128)(2,1)}, bf16[48,5120]{1,0:T(8,128)(2,1)}, u32[]{:S(2)}, u32[]{:S(2)}) collective-permute-start(bf16[48,5120]{1,0:T(8,128)(2,1)} %pad.8), channel_id=1, source_target_pairs={{0,2},{1,3},{2,4},{3,5},{4,6},{5,7},{6,0},{7,1},{8,10},{9,11},{10,... | collective-permute-start | bytes 1474568 | tf_op jit(solution)/shard_map/ppermute | solution.py:27
  6.4 18.9 %collective-permute-start = (bf16[48,5120]{1,0:T(8,128)(2,1)}, bf16[48,5120]{1,0:T(8,128)(2,1)S(1)}, u32[]{:S(2)}, u32[]{:S(2)}) collective-permute-start(bf16[48,5120]{1,0:T(8,128)(2,1)} %pad.8), channel_id=1, source_target_pairs={{0,6},{1,7},{2,0},{3,1},{4,2},{5,3},{6,4},{7,5},{8,14},{9,15},{10,... | collective-permute-start | bytes 1474568 | tf_op jit(solution)/shard_map/ppermute | solution.py:27
  10.3 9.2 %collective-permute-start.6 = (bf16[360,640]{1,0:T(8,128)(2,1)}, bf16[360,640]{1,0:T(8,128)(2,1)S(1)}, u32[]{:S(2)}, u32[]{:S(2)}) collective-permute-start(bf16[360,640]{1,0:T(8,128)(2,1)} %bitcast.3), channel_id=1, source_target_pairs={{8,0},{16,8},{24,16},{32,24},{40,32},{48,40},{56,48},{64,56},{72,6... | collective-permute-start | bytes 1382408 | tf_op jit(solution)/shard_map/ppermute | solution.py:242
  11.6 8.5 %collective-permute-start.5 = (bf16[360,640]{1,0:T(8,128)(2,1)}, bf16[360,640]{1,0:T(8,128)(2,1)S(1)}, u32[]{:S(2)}, u32[]{:S(2)}) collective-permute-start(bf16[360,640]{1,0:T(8,128)(2,1)} %bitcast.3), channel_id=1, source_target_pairs={{0,8},{8,16},{16,24},{24,32},{32,40},{40,48},{48,56},{56,64},{64,7... | collective-permute-start | bytes 1382408 | tf_op jit(solution)/shard_map/ppermute | solution.py:241
  17.9 12.8 %collective-permute-start.4 = (bf16[48,5120]{1,0:T(8,128)(2,1)}, bf16[48,5120]{1,0:T(8,128)(2,1)S(1)}, u32[]{:S(2)}, u32[]{:S(2)}) collective-permute-start(bf16[48,5120]{1,0:T(8,128)(2,1)} %collective-permute-done.2), channel_id=1, source_target_pairs={{0,6},{1,7},{2,0},{3,1},{4,2},{5,3},{6,4},{7,5},{8,14},{9,15},{10,... | collective-permute-start | bytes 1474568 | tf_op jit(solution)/shard_map/ppermute | solution.py:27
  19.4 11.2 %collective-permute-start.3 = (bf16[48,5120]{1,0:T(8,128)(2,1)}, bf16[48,5120]{1,0:T(8,128)(2,1)S(1)}, u32[]{:S(2)}, u32[]{:S(2)}) collective-permute-start(bf16[48,5120]{1,0:T(8,128)(2,1)} %collective-permute-done.2), channel_id=1, source_target_pairs={{0,2},{1,3},{2,4},{3,5},{4,6},{5,7},{6,0},{7,1},{8,10},{9,11},{10,... | collective-permute-start | bytes 1474568 | tf_op jit(solution)/shard_map/ppermute | solution.py:27
  25.2 24.2 %copy-start.4 = (bf16[1,3,3,40,640]{4,3,2,1,0:T(8,128)(2,1)S(1)}, bf16[1,3,3,40,640]{4,3,2,1,0:T(8,128)(2,1)}, u32[]{:S(2)}) copy-start(bf16[1,3,3,40,640]{4,3,2,1,0:T(8,128)(2,1)} %get-tuple-element.66) | copy-start | bytes 1382404
  25.3 12.9 %collective-permute-start.16 = (bf16[48,5120]{1,0:T(8,128)(2,1)S(1)}, bf16[48,5120]{1,0:T(8,128)(2,1)S(1)}, u32[]{:S(2)}, u32[]{:S(2)}) collective-permute-start(bf16[48,5120]{1,0:T(8,128)(2,1)S(1)} %collective-permute-done.refs_5_), channel_id=1, source_target_pairs={{0,6},{1,7},{2,0},{3,1},{4,2},{5,3},{6,4},{7,5},{8,14},{9,15},{10,... | collective-permute-start | bytes 1474568 | tf_op jit(solution)/shard_map/ppermute | solution.py:27
  32.8 27.2 %slice-start = ((s8[6553600]{0:T(1024)(128)(4,1)}), s8[4194304]{0:T(1024)(128)(4,1)S(1)}, s32[]{:S(2)}) async-start(s8[6553600]{0:T(1024)(128)(4,1)} %bitcast.33), calls=%async_computation | async-start | bytes 8388608
  34.1 10.5 %collective-permute-start.17 = (bf16[48,5120]{1,0:T(8,128)(2,1)S(1)}, bf16[48,5120]{1,0:T(8,128)(2,1)S(1)}, u32[]{:S(2)}, u32[]{:S(2)}) collective-permute-start(bf16[48,5120]{1,0:T(8,128)(2,1)S(1)} %collective-permute-done.3.refs_6_), channel_id=1, source_target_pairs={{0,2},{1,3},{2,4},{3,5},{4,6},{5,7},{6,0},{7,1},{8,10},{9,11},{10,... | collective-permute-start | bytes 1474568 | tf_op jit(solution)/shard_map/ppermute | solution.py:27
  44.7 42.0 %collective-permute-start.18 = (bf16[384,5120]{1,0:T(8,128)(2,1)S(1)}, bf16[384,5120]{1,0:T(8,128)(2,1)S(1)}, u32[]{:S(2)}, u32[]{:S(2)}) collective-permute-start(bf16[384,5120]{1,0:T(8,128)(2,1)S(1)} %constant_dynamic-update-slice_fusion.refs_1_), channel_id=1, source_target_pairs={{0,8},{8,0},{16,24},{24,16},{32,40},{40,32},{48,56},{56,48},{64,72... | collective-permute-start | bytes 11796488 | tf_op jit(solution)/shard_map/ppermute | solution.py:37
  49.4 10.6 %slice-start.1 = ((s8[6553600]{0:T(1024)(128)(4,1)}), s8[2359296]{0:T(1024)(128)(4,1)S(1)}, s32[]{:S(2)}) async-start(s8[6553600]{0:T(1024)(128)(4,1)} %bitcast.33), calls=%async_computation.1 | async-start | bytes 4718592
  49.4 6.9 %collective-permute-start.8 = (bf16[360,640]{1,0:T(8,128)(2,1)S(1)}, bf16[360,640]{1,0:T(8,128)(2,1)S(1)}, u32[]{:S(2)}, u32[]{:S(2)}) collective-permute-start(bf16[360,640]{1,0:T(8,128)(2,1)S(1)} %bitcast.37), channel_id=1, source_target_pairs={{8,0},{16,8},{24,16},{32,24},{40,32},{48,40},{56,48},{64,56},{72,6... | collective-permute-start | bytes 1382408 | tf_op jit(solution)/shard_map/ppermute | solution.py:242
  50.9 5.6 %collective-permute-start.7 = (bf16[360,640]{1,0:T(8,128)(2,1)S(1)}, bf16[360,640]{1,0:T(8,128)(2,1)S(1)}, u32[]{:S(2)}, u32[]{:S(2)}) collective-permute-start(bf16[360,640]{1,0:T(8,128)(2,1)S(1)} %bitcast.38), channel_id=1, source_target_pairs={{0,8},{8,16},{16,24},{24,32},{32,40},{40,48},{48,56},{56,64},{64,7... | collective-permute-start | bytes 1382408 | tf_op jit(solution)/shard_map/ppermute | solution.py:241
  63.3 16.8 %collective-permute-start.10 = (bf16[48,5120]{1,0:T(8,128)(2,1)S(1)}, bf16[48,5120]{1,0:T(8,128)(2,1)S(1)}, u32[]{:S(2)}, u32[]{:S(2)}) collective-permute-start(bf16[48,5120]{1,0:T(8,128)(2,1)S(1)} %get-tuple-element.39), channel_id=1, source_target_pairs={{0,6},{1,7},{2,0},{3,1},{4,2},{5,3},{6,4},{7,5},{8,14},{9,15},{10,... | collective-permute-start | bytes 1474568 | tf_op jit(solution)/shard_map/ppermute | solution.py:27
  64.9 18.5 %collective-permute-start.19 = (bf16[384,640]{1,0:T(8,128)(2,1)S(1)}, bf16[384,640]{1,0:T(8,128)(2,1)S(1)}, u32[]{:S(2)}, u32[]{:S(2)}) collective-permute-start(bf16[384,640]{1,0:T(8,128)(2,1)S(1)} %shard_map.193.refs_0_.refs_3_), channel_id=1, source_target_pairs={{0,8},{8,0},{16,24},{24,16},{32,40},{40,32},{48,56},{56,48},{64,72... | collective-permute-start | bytes 1474568 | tf_op jit(solution)/shard_map/ppermute | solution.py:37
  76.8 51.4 %collective-permute-start.9 = (bf16[48,5120]{1,0:T(8,128)(2,1)S(1)}, bf16[48,5120]{1,0:T(8,128)(2,1)S(1)}, u32[]{:S(2)}, u32[]{:S(2)}) collective-permute-start(bf16[48,5120]{1,0:T(8,128)(2,1)S(1)} %get-tuple-element.37), channel_id=1, source_target_pairs={{0,2},{1,3},{2,4},{3,5},{4,6},{5,7},{6,0},{7,1},{8,10},{9,11},{10,... | collective-permute-start | bytes 1474568 | tf_op jit(solution)/shard_map/ppermute | solution.py:27
  77.7 43.8 %collective-permute-start.12 = (bf16[48,5120]{1,0:T(8,128)(2,1)S(1)}, bf16[48,5120]{1,0:T(8,128)(2,1)S(1)}, u32[]{:S(2)}, u32[]{:S(2)}) collective-permute-start(bf16[48,5120]{1,0:T(8,128)(2,1)S(1)} %get-tuple-element.41), channel_id=1, source_target_pairs={{0,6},{1,7},{2,0},{3,1},{4,2},{5,3},{6,4},{7,5},{8,14},{9,15},{10,... | collective-permute-start | bytes 1474568 | tf_op jit(solution)/shard_map/ppermute | solution.py:27
  80.0 24.4 %collective-permute-start.13 = (bf16[48,5120]{1,0:T(8,128)(2,1)S(1)}, bf16[48,5120]{1,0:T(8,128)(2,1)S(1)}, u32[]{:S(2)}, u32[]{:S(2)}) collective-permute-start(bf16[48,5120]{1,0:T(8,128)(2,1)S(1)} %get-tuple-element.43), channel_id=1, source_target_pairs={{0,2},{1,3},{2,4},{3,5},{4,6},{5,7},{6,0},{7,1},{8,10},{9,11},{10,... | collective-permute-start | bytes 1474568 | tf_op jit(solution)/shard_map/ppermute | solution.py:27
  83.4 44.9 %collective-permute-start.11 = (bf16[48,5120]{1,0:T(8,128)(2,1)S(1)}, bf16[48,5120]{1,0:T(8,128)(2,1)S(1)}, u32[]{:S(2)}, u32[]{:S(2)}) collective-permute-start(bf16[48,5120]{1,0:T(8,128)(2,1)S(1)} %add_convert_fusion.2), channel_id=1, source_target_pairs={{0,6},{1,7},{2,0},{3,1},{4,2},{5,3},{6,4},{7,5},{8,14},{9,15},{10,... | collective-permute-start | bytes 1474568 | tf_op jit(solution)/shard_map/ppermute | solution.py:27
  88.2 26.0 %collective-permute-start.28 = (bf16[320,640]{1,0:T(8,128)(2,1)S(1)}, bf16[320,640]{1,0:T(8,128)(2,1)S(1)}, u32[]{:S(2)}, u32[]{:S(2)}) collective-permute-start(bf16[320,640]{1,0:T(8,128)(2,1)S(1)} %get-tuple-element.50.refs_10_), channel_id=1, source_target_pairs={{0,32},{8,40},{16,48},{24,56},{32,64},{40,72},{48,80},{56,88},{64,... | collective-permute-start | bytes 1228808 | tf_op jit(solution)/shard_map/ppermute | solution.py:37
  104.5 17.1 %collective-permute-start.14 = (bf16[48,5120]{1,0:T(8,128)(2,1)S(1)}, bf16[48,5120]{1,0:T(8,128)(2,1)S(1)}, u32[]{:S(2)}, u32[]{:S(2)}) collective-permute-start(bf16[48,5120]{1,0:T(8,128)(2,1)S(1)} %add_convert_fusion.1), channel_id=1, source_target_pairs={{0,2},{1,3},{2,4},{3,5},{4,6},{5,7},{6,0},{7,1},{8,10},{9,11},{10,... | collective-permute-start | bytes 1474568 | tf_op jit(solution)/shard_map/ppermute | solution.py:27
  114.3 17.0 %collective-permute-start.25 = (bf16[320,640]{1,0:T(8,128)(2,1)S(1)}, bf16[320,640]{1,0:T(8,128)(2,1)S(1)}, u32[]{:S(2)}, u32[]{:S(2)}) collective-permute-start(bf16[320,640]{1,0:T(8,128)(2,1)S(1)} %get-tuple-element.62), channel_id=1, source_target_pairs={{0,96},{8,104},{16,112},{24,120},{32,0},{40,8},{48,16},{56,24},{64... | collective-permute-start | bytes 1228808 | tf_op jit(solution)/shard_map/ppermute | solution.py:37
  121.5 15.1 %collective-permute-start.27 = (bf16[320,640]{1,0:T(8,128)(2,1)S(1)}, bf16[320,640]{1,0:T(8,128)(2,1)S(1)}, u32[]{:S(2)}, u32[]{:S(2)}) collective-permute-start(bf16[320,640]{1,0:T(8,128)(2,1)S(1)} %get-tuple-element.64), channel_id=1, source_target_pairs={{0,96},{8,104},{16,112},{24,120},{32,0},{40,8},{48,16},{56,24},{64... | collective-permute-start | bytes 1228808 | tf_op jit(solution)/shard_map/ppermute | solution.py:37
  121.6 16.3 %collective-permute-start.29 = (bf16[320,640]{1,0:T(8,128)(2,1)S(1)}, bf16[320,640]{1,0:T(8,128)(2,1)S(1)}, u32[]{:S(2)}, u32[]{:S(2)}) collective-permute-start(bf16[320,640]{1,0:T(8,128)(2,1)S(1)} %add_convert_fusion.5), channel_id=1, source_target_pairs={{0,32},{8,40},{16,48},{24,56},{32,64},{40,72},{48,80},{56,88},{64,... | collective-permute-start | bytes 1228808 | tf_op jit(solution)/shard_map/ppermute | solution.py:37
  128.2 13.0 %collective-permute-start.15 = (bf16[48,5120]{1,0:T(8,128)(2,1)S(1)}, bf16[48,5120]{1,0:T(8,128)(2,1)S(1)}, u32[]{:S(2)}, u32[]{:S(2)}) collective-permute-start(bf16[48,5120]{1,0:T(8,128)(2,1)S(1)} %add_convert_fusion), channel_id=1, source_target_pairs={{0,1},{1,0},{2,3},{3,2},{4,5},{5,4},{6,7},{7,6},{8,9},{9,8},{10,11... | collective-permute-start | bytes 1474568 | tf_op jit(solution)/shard_map/ppermute | solution.py:27
  128.3 15.7 %collective-permute-start.22 = (bf16[2,360,256]{2,1,0:T(8,128)(2,1)S(1)}, bf16[2,360,256]{2,1,0:T(8,128)(2,1)S(1)}, u32[]{:S(2)}, u32[]{:S(2)}) collective-permute-start(bf16[2,360,256]{2,1,0:T(8,128)(2,1)S(1)} %get-tuple-element.58), channel_id=1, source_target_pairs={{8,0},{16,8},{24,16},{32,24},{40,32},{48,40},{56,48},{64,56},{72,6... | collective-permute-start | bytes 1105928 | tf_op jit(solution)/shard_map/ppermute | solution.py:389
  131.3 20.6 %collective-permute-start.23 = (bf16[2,360,256]{2,1,0:T(8,128)(2,1)S(1)}, bf16[2,360,256]{2,1,0:T(8,128)(2,1)S(1)}, u32[]{:S(2)}, u32[]{:S(2)}) collective-permute-start(bf16[2,360,256]{2,1,0:T(8,128)(2,1)S(1)} %get-tuple-element.59), channel_id=1, source_target_pairs={{0,8},{8,16},{16,24},{24,32},{32,40},{40,48},{48,56},{56,64},{64,7... | collective-permute-start | bytes 1105928 | tf_op jit(solution)/shard_map/ppermute | solution.py:390
  136.6 17.6 %collective-permute-start.20 = (bf16[2,360,384]{2,1,0:T(8,128)(2,1)S(1)}, bf16[2,360,384]{2,1,0:T(8,128)(2,1)S(1)}, u32[]{:S(2)}, u32[]{:S(2)}) collective-permute-start(bf16[2,360,384]{2,1,0:T(8,128)(2,1)S(1)} %get-tuple-element.52.refs_5_), channel_id=1, source_target_pairs={{8,0},{16,8},{24,16},{32,24},{40,32},{48,40},{56,48},{64,56},{72,6... | collective-permute-start | bytes 1658888 | tf_op jit(solution)/shard_map/ppermute | solution.py:389
  137.9 16.3 %collective-permute-start.21 = (bf16[2,360,384]{2,1,0:T(8,128)(2,1)S(1)}, bf16[2,360,384]{2,1,0:T(8,128)(2,1)S(1)}, u32[]{:S(2)}, u32[]{:S(2)}) collective-permute-start(bf16[2,360,384]{2,1,0:T(8,128)(2,1)S(1)} %get-tuple-element.56), channel_id=1, source_target_pairs={{0,8},{8,16},{16,24},{24,32},{32,40},{40,48},{48,56},{56,64},{64,7... | collective-permute-start | bytes 1658888 | tf_op jit(solution)/shard_map/ppermute | solution.py:390
  141.2 20.0 %collective-permute-start.24 = (bf16[320,640]{1,0:T(8,128)(2,1)S(1)}, bf16[320,640]{1,0:T(8,128)(2,1)S(1)}, u32[]{:S(2)}, u32[]{:S(2)}) collective-permute-start(bf16[320,640]{1,0:T(8,128)(2,1)S(1)} %get-tuple-element.60), channel_id=1, source_target_pairs={{0,32},{8,40},{16,48},{24,56},{32,64},{40,72},{48,80},{56,88},{64,... | collective-permute-start | bytes 1228808 | tf_op jit(solution)/shard_map/ppermute | solution.py:37
  144.1 17.4 %collective-permute-start.26 = (bf16[320,640]{1,0:T(8,128)(2,1)S(1)}, bf16[320,640]{1,0:T(8,128)(2,1)S(1)}, u32[]{:S(2)}, u32[]{:S(2)}) collective-permute-start(bf16[320,640]{1,0:T(8,128)(2,1)S(1)} %add_convert_fusion.6), channel_id=1, source_target_pairs={{0,96},{8,104},{16,112},{24,120},{32,0},{40,8},{48,16},{56,24},{64... | collective-permute-start | bytes 1228808 | tf_op jit(solution)/shard_map/ppermute | solution.py:37
  151.9 18.1 %collective-permute-start.30 = (bf16[320,640]{1,0:T(8,128)(2,1)S(1)}, bf16[320,640]{1,0:T(8,128)(2,1)S(1)}, u32[]{:S(2)}, u32[]{:S(2)}) collective-permute-start(bf16[320,640]{1,0:T(8,128)(2,1)S(1)} %add_convert_fusion.4), channel_id=1, source_target_pairs={{0,16},{8,24},{16,0},{24,8},{32,48},{40,56},{48,32},{56,40},{64,80... | collective-permute-start | bytes 1228808 | tf_op jit(solution)/shard_map/ppermute | solution.py:37
  154.2 1.1 copy-start.3
